TPU v7x, 32 devices: a whole 2x2x4 slice. The times are simulated.
32 devices in a mesh: batch: 8 (over z, y), seq: 4 (over x, core).
Axes of the slice: x: 2, y: 2, z: 4, core: 2. Of those that a mesh axis runs over, the one named last changes fastest.
Arguments:
- inputs: bfloat16 [16, 1024, 768], P('batch', 'seq'), may hold values from -6 to 6
- segments: int32 [16, 1024], P('batch'), may hold values from 0 to 7, never falling along the last dimension, each value on 1 to 512 neighbouring positions
- qkv_weight: bfloat16 [768, 2304], replicated, may hold values from -0.21875 to 0.21875
- query_bias: bfloat16 [768], replicated, may hold values from -3 to 3
- value_bias: bfloat16 [768], replicated, may hold values from -3 to 3
- out_weight: bfloat16 [768, 768], replicated, may hold values from -1.75 to 1.75
- out_bias: bfloat16 [768], replicated, may hold values from -3 to 3
- norm1_gain: bfloat16 [768], replicated, may hold values from 0.099609375 to 1.8984375
- norm1_shift: bfloat16 [768], replicated, may hold values from -3 to 3
- up_weight: bfloat16 [768, 3072], replicated, may hold values from -0.21875 to 0.21875
- up_bias: bfloat16 [3072], replicated, may hold values from -3 to 3
- down_weight: bfloat16 [3072, 768], replicated, may hold values from -0.109375 to 0.109375
- down_bias: bfloat16 [768], replicated, may hold values from -3 to 3
- norm2_gain: bfloat16 [768], replicated, may hold values from 0.099609375 to 1.8984375
- norm2_shift: bfloat16 [768], replicated, may hold values from -3 to 3
- cotangent: bfloat16 [16, 1024, 768], P('batch', 'seq'), may hold values from -6 to 6
Outputs:
- outputs: bfloat16 [16, 1024, 768], P('batch', 'seq')
- input_grad: float32 [16, 1024, 768], P('batch', 'seq')
- qkv_weight_grad: float32 [768, 2304], P('batch', 'seq')
- query_bias_grad: float32 [768], replicated
- value_bias_grad: float32 [768], replicated
- out_weight_grad: float32 [768, 768], P('batch', 'seq')
- out_bias_grad: float32 [768], replicated
- norm1_gain_grad: float32 [768], replicated
- norm1_shift_grad: float32 [768], replicated
- up_weight_grad: float32 [768, 3072], P('batch', 'seq')
- up_bias_grad: float32 [3072], replicated
- down_weight_grad: float32 [3072, 768], P('batch', 'seq')
- down_bias_grad: float32 [768], replicated
- norm2_gain_grad: float32 [768], replicated
- norm2_shift_grad: float32 [768], replicated
Inputs may be any that keep to these rules, and one draw needn't show every extreme that they name: `segments`: in each packed row the passage numbers never fall, every number below 8 occurs, each passage holds 1 to 512 positions, and one passage in each row holds exactly 512.
All inputs are finite; a program needn't handle non-finite values.
Results may differ from a plain program's by a relative error of at most 0.013.
The roundings to bfloat16 on the way count: a program that leaves them out, or rounds other values in their place, can miss the bound.
Values may be sent and summed in bfloat16 or wider, within the bound.
No kernel may reach another device: no remote copies, remote signals or barrier semaphores. Data moves between devices by JAX's collectives and lax.ppermute only.
A program may use at most 192 MiB of HBM per device.

v0:
```python
import functools

import jax
import jax.numpy as jnp
from jax import lax
from jax.experimental import pallas as pl
from jax.experimental.pallas import tpu as pltpu
from jax.sharding import PartitionSpec as P

DH = 64
EPS = 1e-05
NEG = -1000000000.0
F32 = jnp.float32
LOW = jnp.bfloat16
PAIR = 2 * DH
SCALE = DH**-0.5
BLOCK = 256
ROOT_HALF = 0.5**0.5
ROOT_TWO_PI = 0.3989422804014327


def shaped(shape, dtype):
    return jax.ShapeDtypeStruct(shape, dtype)


def dot_nn(left, right):
    return jnp.dot(left, right, preferred_element_type=F32)


def dot_nt(left, right):
    return lax.dot_general(left, right, (((1,), (1,)), ((), ())), preferred_element_type=F32)


def params(mib):
    return pltpu.CompilerParams(vmem_limit_bytes=mib << 20, dimension_semantics=("arbitrary",))


def full(shape):
    return pl.BlockSpec(shape, lambda *_: (0,) * len(shape))


def one_head(array, head):
    lane = lax.broadcasted_iota(jnp.int32, array.shape, 1)
    return jnp.where((lane < DH) if head == 0 else (lane >= DH), array, jnp.zeros_like(array))


def mask_columns(seg_col, seg_row):
    return jnp.where(seg_col == seg_row, 0.0, NEG)


def forward_kernel(
    info, x0, x1, x2, x3, wq, wk, wv, bq, bv, seg_col, seg_row,
    q_out, k_out, v_out, c0, c1, c2, c3, lse_out,
    xs, bias, qs, vt, ctx,
):
    place = info[0]
    tokens = xs.shape[0]
    quarter = tokens // 4
    blocks = tokens // BLOCK

    @pl.when(pl.program_id(0) == 0)
    def _():
        for j, ref in enumerate((x0, x1, x2, x3)):
            xs[pl.ds(pl.multiple_of((place ^ j) * quarter, quarter), quarter), :] = ref[...]
        for b in range(blocks):
            row = seg_row[:, b * BLOCK : (b + 1) * BLOCK]
            bias[b] = mask_columns(seg_col[...], row)

    weights = jnp.concatenate([wq[...], wk[...], wv[...]], axis=1)
    projected = dot_nn(xs[...], weights)
    query = (projected[:, :PAIR] + bq[...].astype(F32)).astype(LOW)
    key = projected[:, PAIR : 2 * PAIR].astype(LOW)
    value = (projected[:, 2 * PAIR :] + bv[...].astype(F32)).astype(LOW)
    q_out[...] = query
    k_out[...] = key
    v_out[...] = value
    qs[...] = query * jnp.asarray(SCALE, LOW)
    vt[...] = value.T

    def step(b, _):
        start = pl.multiple_of(b * BLOCK, BLOCK)
        q_block = qs[pl.ds(start, BLOCK), :]
        sides = []
        for head in range(2):
            scores = dot_nt(k_out[...], one_head(q_block, head)) + bias[b]
            top = jnp.max(scores, axis=0, keepdims=True)
            expo = jnp.exp(scores - top)
            total = jnp.sum(expo, axis=0, keepdims=True)
            probs = (expo * (1.0 / total)).astype(LOW)
            sides.append(dot_nn(vt[head * DH : (head + 1) * DH, :], probs))
            lse_out[0, head, pl.ds(b, 1), :] = top + jnp.log(total)
        ctx[pl.ds(start, BLOCK), :] = jnp.concatenate(sides, axis=0).T.astype(LOW)
        return 0

    lax.fori_loop(0, blocks, step, 0)
    for j, ref in enumerate((c0, c1, c2, c3)):
        ref[...] = ctx[pl.ds(pl.multiple_of((place ^ j) * quarter, quarter), quarter), :]


def attend_forward(info, quarters, qkv_weight, query_bias, value_bias, seg):
    quarter, width = quarters[0].shape
    tokens, half = 4 * quarter, width // 2
    pairs = half // PAIR

    def weight_spec(t):
        return pl.BlockSpec((width, PAIR), lambda p, i: (0, (2 * t + i[1]) * pairs + p))

    def bias_spec():
        return pl.BlockSpec((1, PAIR), lambda p, i: (0, i[1] * pairs + p))

    col = pl.BlockSpec((tokens, PAIR), lambda p, i: (0, p))
    part = pl.BlockSpec((quarter, PAIR), lambda p, i: (0, p))
    blocks = tokens // BLOCK
    return pl.pallas_call(
        forward_kernel,
        grid_spec=pltpu.PrefetchScalarGridSpec(
            num_scalar_prefetch=1,
            grid=(pairs,),
            in_specs=[full((quarter, width))] * 4
            + [weight_spec(0), weight_spec(1), weight_spec(2), bias_spec(), bias_spec()]
            + [full((tokens, 1)), full((1, tokens))],
            out_specs=[col] * 3
            + [part] * 4
            + [pl.BlockSpec((1, 2, blocks, BLOCK), lambda p, i: (p, 0, 0, 0))],
            scratch_shapes=[
                pltpu.VMEM((tokens, width), LOW),
                pltpu.VMEM((blocks, tokens, BLOCK), F32),
                pltpu.VMEM((tokens, PAIR), LOW),
                pltpu.VMEM((PAIR, tokens), LOW),
                pltpu.VMEM((tokens, PAIR), LOW),
            ],
        ),
        out_shape=[shaped((tokens, half), LOW)] * 3
        + [shaped((quarter, half), LOW)] * 4
        + [shaped((pairs, 2, blocks, BLOCK), F32)],
        compiler_params=params(56),
        name="attend_forward",
    )(
        info,
        *quarters,
        qkv_weight,
        qkv_weight,
        qkv_weight,
        query_bias[None],
        value_bias[None],
        seg[:, None],
        seg[None],
    )


def backward_kernel(
    info, q_in, k_in, v_in, o0, o1, o2, o3, lse, seg_col, seg_row,
    dq_out, dk_out, dv_out, bias_out,
    bias, qs, do, kt, dk, dv,
):
    place = info[0]
    tokens = q_in.shape[0]
    quarter = tokens // 4
    blocks = tokens // BLOCK

    @pl.when(pl.program_id(0) == 0)
    def _():
        for b in range(blocks):
            row = seg_row[:, b * BLOCK : (b + 1) * BLOCK]
            bias[b] = mask_columns(seg_col[...], row)

    for j, ref in enumerate((o0, o1, o2, o3)):
        do[pl.ds(pl.multiple_of((place ^ j) * quarter, quarter), quarter), :] = ref[...]
    qs[...] = q_in[...] * jnp.asarray(SCALE, LOW)
    kt[...] = k_in[...].T
    dk[...] = jnp.zeros_like(dk)
    dv[...] = jnp.zeros_like(dv)

    def step(b, dq_sum):
        start = pl.multiple_of(b * BLOCK, BLOCK)
        q_block = qs[pl.ds(start, BLOCK), :]
        o_block = do[pl.ds(start, BLOCK), :]
        sides, probs_low, d_scores_low, q_heads, o_heads = [], [], [], [], []
        for head in range(2):
            q_head, o_head = one_head(q_block, head), one_head(o_block, head)
            scores = dot_nt(k_in[...], q_head) + bias[b]
            probs = jnp.exp(scores - lse[0, head, pl.ds(b, 1), :])
            d_probs = dot_nt(v_in[...], o_head)
            delta = jnp.sum(probs * d_probs, axis=0, keepdims=True)
            d_scores = (probs * (d_probs - delta)).astype(LOW)
            sides.append(dot_nn(kt[head * DH : (head + 1) * DH, :], d_scores))
            probs_low.append(probs.astype(LOW))
            d_scores_low.append(d_scores)
            q_heads.append(q_head)
            o_heads.append(o_head)
        dk[...] += dot_nn(jnp.concatenate(d_scores_low, axis=1), jnp.concatenate(q_heads, axis=0))
        dv[...] += dot_nn(jnp.concatenate(probs_low, axis=1), jnp.concatenate(o_heads, axis=0))
        d_query = (jnp.concatenate(sides, axis=0).T * SCALE).astype(LOW)
        dq_out[pl.ds(start, BLOCK), :] = d_query
        return dq_sum + jnp.sum(d_query.astype(F32), axis=0, keepdims=True)

    dq_sum = lax.fori_loop(0, blocks, step, jnp.zeros((1, PAIR), F32))
    dk_out[...] = dk[...].astype(LOW)
    d_value = dv[...].astype(LOW)
    dv_out[...] = d_value
    bias_out[0, 0:1, :] = dq_sum
    bias_out[0, 1:2, :] = jnp.sum(d_value.astype(F32), axis=0, keepdims=True)


def attend_backward(info, query, key, value, parts, lse, seg):
    tokens, half = query.shape
    quarter, pairs, blocks = tokens // 4, half // PAIR, tokens // BLOCK
    col = pl.BlockSpec((tokens, PAIR), lambda p, i: (0, p))
    part = pl.BlockSpec((quarter, PAIR), lambda p, i: (0, p))
    return pl.pallas_call(
        backward_kernel,
        grid_spec=pltpu.PrefetchScalarGridSpec(
            num_scalar_prefetch=1,
            grid=(pairs,),
            in_specs=[col] * 3
            + [part] * 4
            + [pl.BlockSpec((1, 2, blocks, BLOCK), lambda p, i: (p, 0, 0, 0))]
            + [full((tokens, 1)), full((1, tokens))],
            out_specs=[col] * 3 + [pl.BlockSpec((1, 2, PAIR), lambda p, i: (p, 0, 0))],
            scratch_shapes=[
                pltpu.VMEM((blocks, tokens, BLOCK), F32),
                pltpu.VMEM((tokens, PAIR), LOW),
                pltpu.VMEM((tokens, PAIR), LOW),
                pltpu.VMEM((PAIR, tokens), LOW),
                pltpu.VMEM((tokens, PAIR), F32),
                pltpu.VMEM((tokens, PAIR), F32),
            ],
        ),
        out_shape=[shaped((tokens, half), LOW)] * 3 + [shaped((pairs, 2, PAIR), F32)],
        compiler_params=params(56),
        name="attend_backward",
    )(info, query, key, value, *parts, lse, seg[:, None], seg[None])


def normalise(values):
    centred = values - jnp.mean(values, axis=1, keepdims=True)
    root = lax.rsqrt(jnp.mean(centred * centred, axis=1, keepdims=True) + EPS)
    return centred * root, root


def norm_back(grad, gain, normal, root):
    e = grad * gain
    along = jnp.mean(e * normal, axis=1, keepdims=True)
    return root * (e - jnp.mean(e, axis=1, keepdims=True) - normal * along)


def column_sum(values):
    return jnp.sum(values, axis=0, keepdims=True)


def store_columns(place, flipped, mine, send):
    size = flipped.shape[0] // 4
    for b in range(4):
        rel = place ^ b

        @pl.when(rel % 2 == 0)
        def _():
            mine[pl.ds(rel // 2, 1)] = flipped[b * size : (b + 1) * size][None]

        @pl.when(rel % 2 == 1)
        def _():
            send[pl.ds(rel // 2, 1)] = flipped[b * size : (b + 1) * size][None]


def middle_forward_kernel(
    info, p0, p1, p2, p3, x_in, cot, wo, bo, g1, s1, up, bup, down, bdown, g2, s2,
    out, d_res, n1, r1, hid_t, ctx_t, act, slope, mine, send, vec,
    hid, hid_low, branch,
):
    place, core, chip = info[0], info[1], info[2]
    step = pl.program_id(0)
    quarter = p0.shape[0]

    @pl.when(step == 0)
    def _():
        first = core == 0

        def sides(a, b):
            a, b = a[...], b[...]
            return jnp.concatenate([jnp.where(first, a, b), jnp.where(first, b, a)], axis=1)

        ctx = jnp.concatenate([sides(p0, p1), sides(p2, p3)], axis=0)
        ctx_t[...] = ctx.T
        x = jnp.concatenate([x_in[chip], x_in[1 - chip]], axis=0).astype(F32)
        summed = x + dot_nn(ctx, wo[...]) + bo[...].astype(F32)
        normal, root = normalise(summed)
        n1[...] = normal
        r1[...] = root
        hidden = normal * g1[...].astype(F32) + s1[...].astype(F32)
        hid[...] = hidden
        low = hidden.astype(LOW)
        hid_low[...] = low
        hid_t[...] = low.T
        branch[...] = jnp.zeros_like(branch)

    pre = dot_nn(hid_low[...], up[...]) + bup[...].astype(F32)
    phi = 0.5 + 0.5 * lax.erf(pre * ROOT_HALF)
    low = (pre * phi).astype(LOW)
    act[...] = low
    slope[...] = phi + pre * (jnp.exp(-0.5 * pre * pre) * ROOT_TWO_PI)
    branch[...] += dot_nn(low, down[...])

    @pl.when(step == pl.num_programs(0) - 1)
    def _():
        normal, root = normalise(hid[...] + branch[...] + bdown[...].astype(F32))
        final = (normal * g2[...].astype(F32) + s2[...].astype(F32)).astype(LOW)
        out[pl.ds(chip, 1)] = final[:quarter][None]
        out[pl.ds(1 - chip, 1)] = final[quarter:][None]
        grad = jnp.concatenate([cot[chip], cot[1 - chip]], axis=0).astype(F32)
        back = norm_back(grad, g2[...].astype(F32), normal, root)
        d_res[...] = back
        vec[0:1, :] = column_sum(back)
        vec[1:2, :] = column_sum(grad * normal)
        vec[2:3, :] = column_sum(grad)
        store_columns(place, back.astype(LOW).T, mine, send)


def middle_forward(info, parts, inputs, cotangent, wo, bo, g1, s1, up, bup, down, bdown, g2, s2):
    quarter, half = parts[0].shape
    width, inner = 2 * half, up.shape[1]
    count, steps = 2 * quarter, 4
    chunk = inner // steps
    vector = full((1, width))
    tokens = full((count, width))
    turned = full((2, width // 4, count))
    return pl.pallas_call(
        middle_forward_kernel,
        grid_spec=pltpu.PrefetchScalarGridSpec(
            num_scalar_prefetch=1,
            grid=(steps,),
            in_specs=[full((quarter, half))] * 4
            + [full((2, quarter, width))] * 2
            + [full((width, width)), vector, vector, vector]
            + [
                pl.BlockSpec((width, chunk), lambda c, i: (0, c)),
                pl.BlockSpec((1, chunk), lambda c, i: (0, c)),
                pl.BlockSpec((chunk, width), lambda c, i: (c, 0)),
            ]
            + [vector] * 3,
            out_specs=[full((2, quarter, width)), tokens, tokens, full((count, 1))]
            + [full((width, count))] * 2
            + [pl.BlockSpec((count, chunk), lambda c, i: (0, c))] * 2
            + [turned, turned, full((8, width))],
            scratch_shapes=[
                pltpu.VMEM((count, width), F32),
                pltpu.VMEM((count, width), LOW),
                pltpu.VMEM((count, width), F32),
            ],
        ),
        out_shape=[
            shaped((2, quarter, width), LOW),
            shaped((count, width), F32),
            shaped((count, width), F32),
            shaped((count, 1), F32),
            shaped((width, count), LOW),
            shaped((width, count), LOW),
            shaped((count, inner), LOW),
            shaped((count, inner), F32),
            shaped((2, width // 4, count), LOW),
            shaped((2, width // 4, count), LOW),
            shaped((8, width), F32),
        ],
        compiler_params=params(60),
        name="middle_forward",
    )(
        info, *parts, inputs, cotangent, wo, bo[None], g1[None], s1[None],
        up, bup[None], down, bdown[None], g2[None], s2[None],
    )


def middle_backward_kernel(
    info, d_res, slope, down, up, wo, n1, r1, g1,
    send_pre, mine_pre, d_up_bias, d_summed, q0, q1, q2, q3, mine, send, vec,
    d_branch, d_hidden,
):
    place, core = info[0], info[1]
    step = pl.program_id(0)
    quarter = q0.shape[0]
    half = q0.shape[1]

    @pl.when(step == 0)
    def _():
        d_branch[...] = d_res[...].astype(LOW)
        d_hidden[...] = d_res[...]

    d_pre = (dot_nt(d_branch[...], down[...]) * slope[...]).astype(LOW)
    d_up_bias[...] = column_sum(d_pre.astype(F32))
    d_hidden[...] += dot_nt(d_pre, up[...])

    @pl.when(step < 2)
    def _():
        send_pre[0] = d_pre

    @pl.when(step >= 2)
    def _():
        mine_pre[0] = d_pre

    @pl.when(step == pl.num_programs(0) - 1)
    def _():
        grad = d_hidden[...]
        normal = n1[...]
        back = norm_back(grad, g1[...].astype(F32), normal, r1[...])
        d_summed[...] = back
        vec[0:1, :] = column_sum(back)
        vec[1:2, :] = column_sum(grad * normal)
        vec[2:3, :] = column_sum(grad)
        low = back.astype(LOW)
        store_columns(place, low.T, mine, send)
        d_ctx = dot_nt(low, wo[...]).astype(LOW)
        first = core == 0
        left, right = d_ctx[:, :half], d_ctx[:, half:]
        same = jnp.where(first, left, right)
        other = jnp.where(first, right, left)
        q0[...] = same[:quarter]
        q1[...] = other[:quarter]
        q2[...] = same[quarter:]
        q3[...] = other[quarter:]


def middle_backward(info, d_res, slope, down, up, wo, n1, r1, g1):
    count, width = d_res.shape
    inner, quarter, half = up.shape[1], count // 2, width // 2
    steps = 4
    chunk = inner // steps

    def block(c, i):
        return i[0] ^ (1 - c // 2 + 2 * (c % 2))

    tokens = full((count, width))
    turned = full((2, width // 4, count))
    return pl.pallas_call(
        middle_backward_kernel,
        grid_spec=pltpu.PrefetchScalarGridSpec(
            num_scalar_prefetch=1,
            grid=(steps,),
            in_specs=[
                tokens,
                pl.BlockSpec((count, chunk), lambda c, i: (0, block(c, i))),
                pl.BlockSpec((chunk, width), lambda c, i: (block(c, i), 0)),
                pl.BlockSpec((width, chunk), lambda c, i: (0, block(c, i))),
                full((width, width)),
                tokens,
                full((count, 1)),
                full((1, width)),
            ],
            out_specs=[
                pl.BlockSpec((1, count, chunk), lambda c, i: (jnp.minimum(c, 1), 0, 0)),
                pl.BlockSpec((1, count, chunk), lambda c, i: (jnp.maximum(c - 2, 0), 0, 0)),
                pl.BlockSpec((1, chunk), lambda c, i: (0, block(c, i))),
                tokens,
            ]
            + [full((quarter, half))] * 4
            + [turned, turned, full((8, width))],
            scratch_shapes=[pltpu.VMEM((count, width), LOW), pltpu.VMEM((count, width), F32)],
        ),
        out_shape=[
            shaped((2, count, chunk), LOW),
            shaped((2, count, chunk), LOW),
            shaped((1, inner), F32),
            shaped((count, width), F32),
        ]
        + [shaped((quarter, half), LOW)] * 4
        + [
            shaped((2, width // 4, count), LOW),
            shaped((2, width // 4, count), LOW),
            shaped((8, width), F32),
        ],
        compiler_params=params(60),
        name="middle_backward",
    )(info, d_res, slope, down, up, wo, n1, r1, g1[None])


def spot(rel, flip_x, order):
    bits = {"y": rel % 2, "z": (rel // 2) % 2, "w": rel // 4, "x": flip_x}
    index = 0
    for axis in order[1:]:
        index = index * 2 + bits[axis]
    return bits[order[0]], index


def put(value, rel, flip_x, order, send, keep):
    sent, index = spot(rel, flip_x, order)
    if isinstance(sent, int):
        if sent:
            send[pl.ds(index, 1)] = value.astype(LOW)[None]
        else:
            keep[pl.ds(index, 1)] = value[None]
        return

    @pl.when(sent == 1)
    def _():
        send[pl.ds(index, 1)] = value.astype(LOW)[None]

    @pl.when(sent == 0)
    def _():
        keep[pl.ds(index, 1)] = value[None]


DOWN_ORDERS = ("yzxw", "zyxw", "xyzw")


def down_kernel(info, mine, theirs, act, act_pair, *outs):
    rel = pl.program_id(0)
    size = mine.shape[1]
    left = jnp.concatenate([mine[0], mine[1]], axis=0)
    left_pair = jnp.concatenate([theirs[0], theirs[1]], axis=0)
    grad = dot_nn(left, act[...]) + dot_nn(left_pair, act_pair[...])
    wide = grad.shape[1] // len(DOWN_ORDERS)
    for n, order in enumerate(DOWN_ORDERS):
        for flip in range(2):
            value = grad[flip * size : (flip + 1) * size, n * wide : (n + 1) * wide]
            put(value, rel, flip, order, outs[2 * n], outs[2 * n + 1])


def down_grad(info, mine, theirs, act, act_pair):
    _, size, count = mine.shape
    block = act.shape[1] // 8
    wide = block // len(DOWN_ORDERS)
    part = full((8, size, wide))
    shapes = [shaped((8, size, wide), LOW), shaped((8, size, wide), F32)]
    spec = pl.BlockSpec((count, block), lambda r, i: (0, r ^ i[3]))
    return pl.pallas_call(
        down_kernel,
        grid_spec=pltpu.PrefetchScalarGridSpec(
            num_scalar_prefetch=1,
            grid=(8,),
            in_specs=[full((2, size, count))] * 2 + [spec, spec],
            out_specs=[part] * 2 * len(DOWN_ORDERS),
        ),
        out_shape=shapes * len(DOWN_ORDERS),
        compiler_params=params(48),
        name="down_grad",
    )(info, mine, theirs, act, act_pair)


UP_ORDERS = ("zyxw", "xyzw", "yzxw")


def up_kernel(info, left, left_pair, mine, theirs, *outs):
    me = info[3]
    step = pl.program_id(0)
    n_parts = len(UP_ORDERS)
    grad = dot_nn(left[...], mine[0]) + dot_nn(left_pair[...], theirs[0])
    deep = grad.shape[0] // 8
    flip = step // n_parts
    for n, order in enumerate(UP_ORDERS):

        @pl.when(step % n_parts == n)
        def _():
            for b in range(8):
                value = grad[b * deep : (b + 1) * deep]
                put(value, me ^ b, flip, order, outs[2 * n], outs[2 * n + 1])


def up_grad(info, left, left_pair, mine, theirs):
    width, count = left.shape
    n_parts = len(UP_ORDERS)
    wide = mine.shape[2] // n_parts
    part = full((8, width // 8, wide))
    shapes = [shaped((8, width // 8, wide), LOW), shaped((8, width // 8, wide), F32)]
    spec = pl.BlockSpec((1, count, wide), lambda s, i: (s // n_parts, 0, s % n_parts))
    return pl.pallas_call(
        up_kernel,
        grid_spec=pltpu.PrefetchScalarGridSpec(
            num_scalar_prefetch=1,
            grid=(2 * n_parts,),
            in_specs=[full((width, count))] * 2 + [spec, spec],
            out_specs=[part] * 2 * n_parts,
        ),
        out_shape=shapes * n_parts,
        compiler_params=params(48),
        name="up_grad",
    )(info, left, left_pair, mine, theirs)


def out_kernel(info, left, left_pair, mine, theirs, send, keep):
    me = info[3]
    right = jnp.concatenate([mine[0], mine[1]], axis=0)
    right_pair = jnp.concatenate([theirs[0], theirs[1]], axis=0)
    grad = dot_nt(left[...], right) + dot_nt(left_pair[...], right_pair)
    deep = grad.shape[0] // 8
    for b in range(8):
        put(grad[b * deep : (b + 1) * deep], me ^ b, 0, "yzw", send, keep)


def out_grad(info, left, left_pair, mine, theirs):
    width, count = left.shape
    wide = 2 * mine.shape[1]
    part = full((4, width // 8, wide))
    return pl.pallas_call(
        out_kernel,
        grid_spec=pltpu.PrefetchScalarGridSpec(
            num_scalar_prefetch=1,
            grid=(1,),
            in_specs=[full((width, count))] * 2 + [full(mine.shape)] * 2,
            out_specs=[part, part],
        ),
        out_shape=[shaped((4, width // 8, wide), LOW), shaped((4, width // 8, wide), F32)],
        compiler_params=params(48),
        name="out_grad",
    )(info, left, left_pair, mine, theirs)


QKV_ORDERS = ("yzw", "zyw", "ywz")


def qkv_kernel(info, x_t, dq, dk, dv, *outs):
    me = info[3]
    step = pl.program_id(0)
    for n, (ref, order) in enumerate(zip((dq, dk, dv), QKV_ORDERS)):

        @pl.when(step == n)
        def _():
            grad = dot_nn(x_t[...], ref[...])
            deep = grad.shape[0] // 8
            for b in range(8):
                value = grad[b * deep : (b + 1) * deep]
                put(value, me ^ b, 0, order, outs[2 * n], outs[2 * n + 1])


def qkv_grad(info, x_t, dq, dk, dv):
    width, tokens = x_t.shape
    half = dq.shape[1]
    part = full((4, width // 8, half))
    shapes = [shaped((4, width // 8, half), LOW), shaped((4, width // 8, half), F32)]
    return pl.pallas_call(
        qkv_kernel,
        grid_spec=pltpu.PrefetchScalarGridSpec(
            num_scalar_prefetch=1,
            grid=(3,),
            in_specs=[full((width, tokens))] + [full((tokens, half))] * 3,
            out_specs=[part] * 6,
        ),
        out_shape=shapes * 3,
        compiler_params=params(48),
        name="qkv_grad",
    )(info, x_t, dq, dk, dv)


def input_kernel(info, dq, dk, dv, wq, wk, wv, keep, send):
    rel = pl.program_id(0)
    grad = dot_nt(dq[...], wq[...]) + dot_nt(dk[...], wk[...]) + dot_nt(dv[...], wv[...])

    @pl.when(rel < 2)
    def _():
        send[0] = grad

    @pl.when(rel >= 2)
    def _():
        keep[0] = grad


def input_part(info, dq, dk, dv, qkv_weight):
    tokens, half = dq.shape
    quarter, width = tokens // 4, 2 * half

    rows = pl.BlockSpec((quarter, half), lambda c, i: (i[0] ^ (1 - c // 2 + 2 * (c % 2)), 0))

    def weight(t):
        return pl.BlockSpec((width, half), lambda c, i: (0, 2 * t + i[1]))

    return pl.pallas_call(
        input_kernel,
        grid_spec=pltpu.PrefetchScalarGridSpec(
            num_scalar_prefetch=1,
            grid=(4,),
            in_specs=[rows] * 3 + [weight(0), weight(1), weight(2)],
            out_specs=[
                pl.BlockSpec((1, quarter, width), lambda c, i: (jnp.maximum(c - 2, 0), 0, 0)),
                pl.BlockSpec((1, quarter, width), lambda c, i: (jnp.minimum(c, 1), 0, 0)),
            ],
        ),
        out_shape=[shaped((2, quarter, width), F32)] * 2,
        compiler_params=params(48),
        name="input_part",
    )(info, dq, dk, dv, qkv_weight, qkv_weight, qkv_weight)


def turn_kernel(info, x0, x1, x2, x3, x_t):
    quarter = x0.shape[0]
    for j, ref in enumerate((x0, x1, x2, x3)):
        at = pl.multiple_of((info[0] ^ j) * quarter, quarter)
        x_t[:, pl.ds(at, quarter)] = ref[...].T


def turn(info, quarters):
    quarter, width = quarters[0].shape
    return pl.pallas_call(
        turn_kernel,
        grid_spec=pltpu.PrefetchScalarGridSpec(
            num_scalar_prefetch=1,
            grid=(1,),
            in_specs=[full((quarter, width))] * 4,
            out_specs=full((width, 4 * quarter)),
        ),
        out_shape=shaped((width, 4 * quarter), LOW),
        compiler_params=params(48),
        name="turn",
    )(info, *quarters)


def body(
    inputs,
    segments,
    qkv_weight,
    query_bias,
    value_bias,
    out_weight,
    out_bias,
    norm1_gain,
    norm1_shift,
    up_weight,
    up_bias,
    down_weight,
    down_bias,
    norm2_gain,
    norm2_shift,
    cotangent,
):
    rows, quarter, width = inputs.shape
    half = width // 2
    seq_size = lax.axis_size("seq")
    batch_size = lax.axis_size("batch")
    fine = batch_size // 8
    place = lax.axis_index("seq")
    chip, core = place // 2, place % 2
    info = jnp.stack([place, core, chip, lax.axis_index("batch") // fine]).astype(jnp.int32)

    def over_seq(array, flip):
        return lax.ppermute(array, "seq", [(i, i ^ flip) for i in range(seq_size)])

    def over_batch(array, flip):
        return lax.ppermute(array, "batch", [(i, i ^ flip) for i in range(batch_size)])

    def swap(array, axis):
        if axis == "x":
            return over_seq(array, 2)
        return over_batch(array, fine << "yzw".index(axis))

    def pick(array, index, axis=0):
        return lax.dynamic_index_in_dim(array, index, axis, keepdims=False)

    def settle(sent, kept, order):
        for axis in order:
            total = kept + swap(sent, axis).astype(F32)
            middle = total.shape[0] // 2
            if middle:
                kept, sent = total[:middle], total[middle:].astype(LOW)
        return total[0]

    def finish(grad):
        if fine > 1:
            groups = [[i * fine + j for j in range(fine)] for i in range(8)]
            grad = lax.psum_scatter(
                grad, "batch", scatter_dimension=0, axis_index_groups=groups, tiled=True
            )
        return grad

    own = pick(inputs, chip)
    far = over_seq(pick(inputs, 1 - chip), 2)
    near = over_seq(own, 1)
    across = over_seq(far, 1)
    quarters = (own, near, far, across)
    segment = pick(segments, chip)

    query, key, value, *parts, lse = attend_forward(
        info, quarters, qkv_weight, query_bias, value_bias, segment
    )
    parts = [parts[0]] + [over_seq(parts[j], j) for j in (1, 2, 3)]
    x_t = turn(info, quarters)

    outputs, d_res, n1, r1, hid_t, ctx_t, act, slope, mine, send, vec_two = middle_forward(
        info, parts, inputs, cotangent, out_weight, out_bias, norm1_gain, norm1_shift,
        up_weight, up_bias, down_weight, down_bias, norm2_gain, norm2_shift,
    )
    hid_pair, ctx_pair, act_pair = over_seq(hid_t, 1), over_seq(ctx_t, 1), over_seq(act, 1)
    downs = down_grad(info, mine, over_seq(send, 1), act, act_pair)
    down_total = [
        settle(downs[2 * n], downs[2 * n + 1], order) for n, order in enumerate(DOWN_ORDERS)
    ]
    down_total = finish(jnp.concatenate(down_total, axis=1).T)

    send_pre, mine_pre, d_up_bias, d_summed, q0, q1, q2, q3, mine, send, vec_one = middle_backward(
        info, d_res, slope, down_weight, up_weight, out_weight, n1, r1, norm1_gain
    )
    d_parts = [q0, over_seq(q1, 1), over_seq(q2, 2), over_seq(q3, 3)]
    ups = up_grad(info, hid_t, hid_pair, mine_pre, over_seq(send_pre, 1))
    up_total = [settle(ups[2 * n], ups[2 * n + 1], order) for n, order in enumerate(UP_ORDERS)]
    up_total = finish(jnp.concatenate(up_total, axis=1))
    outs = out_grad(info, ctx_t, ctx_pair, mine, over_seq(send, 1))
    out_total = settle(outs[0], outs[1], "yzw")
    wide = out_total.shape[1] // 2
    out_total = out_total[:, :wide] + over_seq(out_total[:, wide:].astype(LOW), 2).astype(F32)
    out_total = finish(out_total)

    def spread(vector):
        for flip in (1, 2):
            vector = vector + over_seq(vector, flip)
        flip = 1
        while flip < batch_size:
            vector = vector + over_batch(vector, flip)
            flip *= 2
        return vector

    early = spread(jnp.concatenate([vec_one[:3], vec_two[:3], d_up_bias.reshape(-1, width)]))

    dq, dk, dv, bias_part = attend_backward(info, query, key, value, d_parts, lse, segment)
    bias_part = bias_part.transpose(1, 0, 2).reshape(2, 1, half)
    late = spread(
        jnp.concatenate(
            [jnp.where(core == 0, bias_part, 0.0), jnp.where(core == 1, bias_part, 0.0)], axis=1
        ).reshape(2, width)
    )

    qkvs = qkv_grad(info, x_t, dq, dk, dv)
    d_qkv = [settle(qkvs[2 * n], qkvs[2 * n + 1], order) for n, order in enumerate(QKV_ORDERS)]
    unit = half // 2
    units = [part[:, side * unit : (side + 1) * unit] for part in d_qkv for side in range(2)]
    first = core == 0
    sent = [jnp.where(first, units[a], units[b]) for a, b in ((2, 0), (3, 2), (5, 3))]
    kept = [jnp.where(first, units[a], units[b]) for a, b in ((0, 1), (1, 4), (4, 5))]
    swapped = over_seq(jnp.stack(sent), 1)
    chip_zero = jnp.stack(
        [kept[0], jnp.where(first, kept[1], swapped[0]), jnp.where(first, swapped[0], swapped[1])]
    )
    chip_one = jnp.stack(
        [jnp.where(first, swapped[1], swapped[2]), jnp.where(first, swapped[2], kept[1]), kept[2]]
    )
    stay = jnp.where(chip == 0, chip_zero, chip_one)
    leave = jnp.where(chip == 0, chip_one, chip_zero)
    total = stay + over_seq(leave.astype(LOW), 2).astype(F32)
    qkv_total = finish(total.transpose(1, 0, 2).reshape(-1, 3 * unit))

    keep, send = input_part(info, dq, dk, dv, qkv_weight)
    d_row = keep + over_seq(send, 1)
    d_near = d_summed[:quarter] + d_row[0]
    d_far = d_summed[quarter:] + over_seq(d_row[1].astype(LOW), 2).astype(F32)
    d_inputs = jnp.stack([jnp.where(chip == 0, d_near, d_far), jnp.where(chip == 0, d_far, d_near)])
    return (
        outputs,
        d_inputs,
        qkv_total,
        late[0],
        late[1],
        out_total,
        early[0],
        early[1],
        early[2],
        up_total,
        early[6:].reshape(-1),
        down_total,
        early[3],
        early[4],
        early[5],
    )


def solution(mesh):
    whole, split = P(), P("batch", "seq")
    tokens = P("batch", "seq", None)
    return jax.shard_map(
        body,
        mesh=mesh,
        in_specs=(tokens, P("batch", None)) + (whole,) * 13 + (tokens,),
        out_specs=(tokens, tokens, split, whole, whole, split)
        + (whole,) * 3
        + (split, whole, split)
        + (whole,) * 3,
        check_vma=False,
    )
```

profile of v0, /device:TPU:0, one launch (start us, length us, event | category | flops | bytes accessed | tf_op | source)
XLA Modules:
  0.0 350.2 jit_solution(10352273914897290873)
XLA Ops:
  1.9 3.0 collective-permute-start.1
  4.9 9.1 %collective-permute-done.1.x2 = bf16[256,768]{1,0:T(8,128)(2,1)S(1)} collective-permute-done((bf16[256,768]{1,0:T(8,128)(2,1)S(1)}, bf16[256,768]{1,0:T(8,128)(2,1)S(1)}, u32[]{:S(2)}, u32[]{:S(2)}) %collective-permute-start.1) | collective-permute-done | bytes 393248 | tf_op jit(solution)/shard_map/ppermute | solution.py:730
  19.1 29.8 %attend_forward.1 = (bf16[1024,384]{1,0:T(8,128)(2,1)}, bf16[1024,384]{1,0:T(8,128)(2,1)}, bf16[1024,384]{1,0:T(8,128)(2,1)}, bf16[256,384]{1,0:T(8,128)(2,1)}, ...) custom-call(s32[4]{0:T(128)} %pad_add_fusion.info, ...), custom_call_target="tpu_custom_call" | custom-call | tf_op jit(solution)/shard_map/attend_forward/pallas_call | solution.py:114
  49.4 1.7 collective-permute-start.4
  55.3 2.1 collective-permute-done.4.p2
  57.4 2.7 collective-permute-done.5.p3
  60.8 18.1 %middle_forward.1 = (bf16[2,256,768]{2,1,0:T(8,128)(2,1)}, f32[512,768]{1,0:T(8,128)}, f32[512,768]{1,0:T(8,128)}, f32[512,1]{1,0:T(8,128)}, bf16[768,512]{1,0:T...) custom-call(s32[4]{0:T(128)} %pad_add_fusion.info, ...), custom_call_target="tpu_custom_call" | custom-call | tf_op jit(solution)/shard_map/middle_forward/pallas_call | solution.py:326
  79.0 16.5 %middle_backward.1 = (bf16[2,512,768]{2,1,0:T(8,128)(2,1)}, bf16[2,512,768]{2,1,0:T(8,128)(2,1)}, f32[1,3072]{1,0:T(1,128)}, f32[512,768]{1,0:T(8,128)}, bf16[25...) custom-call(s32[4]{0:T(128)} %pad_add_fusion.info, ...), custom_call_target="tpu_custom_call" | custom-call | tf_op jit(solution)/shard_map/middle_backward/pallas_call | solution.py:431
  98.8 1.8 collective-permute-start.7
  100.7 1.8 collective-permute-start.34
  102.5 9.1 %collective-permute-done.34 = f32[10,768]{1,0:T(8,128)S(1)} collective-permute-done((f32[10,768]{1,0:T(8,128)S(1)}, f32[10,768]{1,0:T(8,128)S(1)}, u32[]{:S(2)}, u32[]{:S(2)}) %collective-permute-start.34) | collective-permute-done | bytes 30752 | tf_op jit(solution)/shard_map/ppermute | solution.py:730
  111.6 1.8 collective-permute-start.35
  113.4 2.3 collective-permute-done.35
  115.7 1.9 collective-permute-start.36
  120.5 2.8 collective-permute-start.37
  124.1 30.3 %attend_backward.1 = (bf16[1024,384]{1,0:T(8,128)(2,1)}, bf16[1024,384]{1,0:T(8,128)(2,1)}, bf16[1024,384]{1,0:T(8,128)(2,1)}, f32[3,2,128]{2,1,0:T(2,128)}) custom-call(s32[4]{0:T(128)} %pad_add_fusion.info, bf16[1024,384]{1,0:T(8,128)(2,1)} %get-tuple-element.81.q_in, bf16[1024,384]{1,0:T(8,128)(2,1)} %get-tuple-element.82.k_in, ...), custom_call_target="tpu_custom_call" | custom-call | tf_op jit(solution)/shard_map/attend_backward/pallas_call | solution.py:210
  157.8 6.2 %qkv_grad.1 = (bf16[4,96,384]{2,1,0:T(8,128)(2,1)S(1)}, f32[4,96,384]{2,1,0:T(8,128)S(1)}, bf16[4,96,384]{2,1,0:T(8,128)(2,1)}, f32[4,96,384]{2,1,0:T(8,128)S(1)...) custom-call(s32[4]{0:T(128)S(1)} %copy-done.23, bf16[768,1024]{1,0:T(8,128)(2,1)} %copy-done.2, ...), custom_call_target="tpu_custom_call" | custom-call | tf_op jit(solution)/shard_map/qkv_grad/pallas_call | solution.py:626
  164.1 1.6 collective-permute-start.17
  168.4 1.5 collective-permute-start.23
  169.9 2.1 collective-permute-done.23
  172.5 3.1 collective-permute-done.24
  177.5 1.9 collective-permute-done.25
  183.7 6.4 %collective-permute-done.14 = bf16[4,96,384]{2,1,0:T(8,128)(2,1)S(1)} collective-permute-done((bf16[4,96,384]{2,1,0:T(8,128)(2,1)S(1)}, bf16[4,96,384]{2,1,0:T(8,128)(2,1)S(1)}, u32[]{:S(2)}, u32[]{:S(2)}) %collective-permute-start.14) | collective-permute-done | bytes 294944 | tf_op jit(solution)/shard_map/ppermute | solution.py:733
  190.7 4.9 %collective-permute-done.18 = bf16[2,96,384]{2,1,0:T(8,128)(2,1)S(1)} collective-permute-done((bf16[2,96,384]{2,1,0:T(8,128)(2,1)S(1)}, bf16[2,96,384]{2,1,0:T(8,128)(2,1)S(1)}, u32[]{:S(2)}, u32[]{:S(2)}) %collective-permute-start.18) | collective-permute-done | bytes 147488 | tf_op jit(solution)/shard_map/ppermute | solution.py:733
  196.1 4.6 %collective-permute-done.12 = bf16[2,96,384]{2,1,0:T(8,128)(2,1)S(1)} collective-permute-done((bf16[2,96,384]{2,1,0:T(8,128)(2,1)S(1)}, bf16[2,96,384]{2,1,0:T(8,128)(2,1)S(1)}, u32[]{:S(2)}, u32[]{:S(2)}) %collective-permute-start.12) | collective-permute-done | bytes 147488 | tf_op jit(solution)/shard_map/ppermute | solution.py:733
  201.1 8.6 %collective-permute-done.15 = bf16[2,96,384]{2,1,0:T(8,128)(2,1)S(1)} collective-permute-done((bf16[2,96,384]{2,1,0:T(8,128)(2,1)S(1)}, bf16[2,96,384]{2,1,0:T(8,128)(2,1)S(1)}, u32[]{:S(2)}, u32[]{:S(2)}) %collective-permute-start.15) | collective-permute-done | bytes 147488 | tf_op jit(solution)/shard_map/ppermute | solution.py:733
  209.8 5.1 %collective-permute-done.19 = bf16[1,96,384]{2,1,0:T(8,128)(2,1)S(1)} collective-permute-done((bf16[1,96,384]{2,1,0:T(8,128)(2,1)S(1)}, bf16[1,96,384]{2,1,0:T(8,128)(2,1)S(1)}, u32[]{:S(2)}, u32[]{:S(2)}) %collective-permute-start.19) | collective-permute-done | bytes 73760 | tf_op jit(solution)/shard_map/ppermute | solution.py:733
  215.2 5.0 %collective-permute-done.13 = bf16[1,96,384]{2,1,0:T(8,128)(2,1)S(1)} collective-permute-done((bf16[1,96,384]{2,1,0:T(8,128)(2,1)S(1)}, bf16[1,96,384]{2,1,0:T(8,128)(2,1)S(1)}, u32[]{:S(2)}, u32[]{:S(2)}) %collective-permute-start.13) | collective-permute-done | bytes 73760 | tf_op jit(solution)/shard_map/ppermute | solution.py:733
  220.3 4.3 %collective-permute-done.16 = bf16[1,96,384]{2,1,0:T(8,128)(2,1)S(1)} collective-permute-done((bf16[1,96,384]{2,1,0:T(8,128)(2,1)S(1)}, bf16[1,96,384]{2,1,0:T(8,128)(2,1)S(1)}, u32[]{:S(2)}, u32[]{:S(2)}) %collective-permute-start.16) | collective-permute-done | bytes 73760 | tf_op jit(solution)/shard_map/ppermute | solution.py:733
  227.3 6.3 %input_part.1 = (f32[2,256,768]{2,1,0:T(8,128)S(1)}, f32[2,256,768]{2,1,0:T(8,128)}) custom-call(s32[4]{0:T(128)S(1)} %copy-done.23, bf16[1024,384]{1,0:T(8,128)(2,1)S(1)} %copy-done.6, bf16[1024,384]{1,0:T(8,128)(2,1)S(1)} %copy-done.8, bf16[1024,384]{1,0:T(8,128)(2,1)S(1)} %copy-done.10, bf16[768,2304]{1,0:T(8,128)(2,1)} %wv.3, bf16[768,2304]{1,0:T(8,128)(2,1)} %wv.3, ...), custom_call_target="tpu_custom_call" | custom-call | tf_op jit(solution)/shard_map/input_part/pallas_call | solution.py:662
  236.1 3.1 out_grad.1
  241.7 7.0 %collective-permute-done.29 = bf16[4,96,384]{2,1,0:T(8,128)(2,1)S(1)} collective-permute-done((bf16[4,96,384]{2,1,0:T(8,128)(2,1)S(1)}, bf16[4,96,384]{2,1,0:T(8,128)(2,1)S(1)}, u32[]{:S(2)}, u32[]{:S(2)}) %collective-permute-start.29) | collective-permute-done | bytes 294944 | tf_op jit(solution)/shard_map/ppermute | solution.py:733
  249.8 4.4 %collective-permute-done.30 = bf16[2,96,384]{2,1,0:T(8,128)(2,1)S(1)} collective-permute-done((bf16[2,96,384]{2,1,0:T(8,128)(2,1)S(1)}, bf16[2,96,384]{2,1,0:T(8,128)(2,1)S(1)}, u32[]{:S(2)}, u32[]{:S(2)}) %collective-permute-start.30) | collective-permute-done | bytes 147488 | tf_op jit(solution)/shard_map/ppermute | solution.py:733
  254.6 5.5 %collective-permute-done.31 = bf16[1,96,384]{2,1,0:T(8,128)(2,1)S(1)} collective-permute-done((bf16[1,96,384]{2,1,0:T(8,128)(2,1)S(1)}, bf16[1,96,384]{2,1,0:T(8,128)(2,1)S(1)}, u32[]{:S(2)}, u32[]{:S(2)}) %collective-permute-start.31) | collective-permute-done | bytes 73760 | tf_op jit(solution)/shard_map/ppermute | solution.py:733
  261.8 4.0 %collective-permute-done.21 = bf16[3,96,192]{2,1,0:T(8,128)(2,1)S(1)} collective-permute-done((bf16[3,96,192]{2,1,0:T(8,128)(2,1)S(1)}, bf16[3,96,192]{2,1,0:T(8,128)(2,1)S(1)}, u32[]{:S(2)}, u32[]{:S(2)}) %collective-permute-start.21) | collective-permute-done | bytes 110624 | tf_op jit(solution)/shard_map/ppermute | solution.py:730
  268.4 7.5 %up_grad.1 = (bf16[8,96,256]{2,1,0:T(8,128)(2,1)S(1)}, f32[8,96,256]{2,1,0:T(8,128)S(1)}, bf16[8,96,256]{2,1,0:T(8,128)(2,1)S(1)}, f32[8,96,256]{2,1,0:T(8,128)S...) custom-call(s32[4]{0:T(128)S(1)} %copy-done.23, bf16[768,512]{1,0:T(8,128)(2,1)S(1)} %copy-done.19, ...), custom_call_target="tpu_custom_call" | custom-call | tf_op jit(solution)/shard_map/up_grad/pallas_call | solution.py:562
  277.6 1.6 add.172
  279.3 8.2 %collective-permute-done.48 = bf16[8,96,256]{2,1,0:T(8,128)(2,1)S(1)} collective-permute-done((bf16[8,96,256]{2,1,0:T(8,128)(2,1)S(1)}, bf16[8,96,256]{2,1,0:T(8,128)(2,1)S(1)}, u32[]{:S(2)}, u32[]{:S(2)}) %collective-permute-start.48) | collective-permute-done | bytes 393248 | tf_op jit(solution)/shard_map/ppermute | solution.py:733
  290.2 4.3 %collective-permute-done.49 = bf16[4,96,256]{2,1,0:T(8,128)(2,1)S(1)} collective-permute-done((bf16[4,96,256]{2,1,0:T(8,128)(2,1)S(1)}, bf16[4,96,256]{2,1,0:T(8,128)(2,1)S(1)}, u32[]{:S(2)}, u32[]{:S(2)}) %collective-permute-start.49) | collective-permute-done | bytes 196640 | tf_op jit(solution)/shard_map/ppermute | solution.py:733
  296.8 3.4 collective-permute-done.41
  304.9 1.9 collective-permute-start.47
  309.1 1.6 copy-done.24
  310.7 8.4 %down_grad.1 = (bf16[8,192,128]{2,1,0:T(8,128)(2,1)S(1)}, f32[8,192,128]{2,1,0:T(8,128)S(1)}, bf16[8,192,128]{2,1,0:T(8,128)(2,1)S(1)}, f32[8,192,128]{2,1,0:T(8...) custom-call(s32[4]{0:T(128)S(1)} %copy-done.23, bf16[2,192,512]{2,1,0:T(8,128)(2,1)S(1)} %copy-done.20, ...), custom_call_target="tpu_custom_call" | custom-call | tf_op jit(solution)/shard_map/down_grad/pallas_call | solution.py:522
  322.0 1.6 collective-permute-start.54
  323.5 3.4 collective-permute-done.62
  330.0 3.2 collective-permute-done.54
  342.7 1.6 collective-permute-start.61
  346.3 2.0 collective-permute-done.61
  (302 shorter events, 79.0 us)
Async XLA Ops:
  1.9 12.1 %collective-permute-start.1 = (bf16[256,768]{1,0:T(8,128)(2,1)S(1)}, bf16[256,768]{1,0:T(8,128)(2,1)S(1)}, u32[]{:S(2)}, u32[]{:S(2)}) collective-permute-start(bf16[256,768]{1,0:T(8,128)(2,1)S(1)} %get-tuple-element.152), channel_id=1, source_target_pairs={{0,2},{1,3},{2,0},{3,1},{4,6},{5,7},{6,4},{7,5},{8,10},{9,11},{10,... | collective-permute-start | bytes 1179656 | tf_op jit(solution)/shard_map/ppermute | solution.py:730
  4.9 12.7 %collective-permute-start = (bf16[256,768]{1,0:T(8,128)(2,1)S(1)}, bf16[256,768]{1,0:T(8,128)(2,1)S(1)}, u32[]{:S(2)}, u32[]{:S(2)}) collective-permute-start(bf16[256,768]{1,0:T(8,128)(2,1)S(1)} %get-tuple-element.153.x0), channel_id=1, source_target_pairs={{0,1},{1,0},{2,3},{3,2},{4,5},{5,4},{6,7},{7,6},{8,9},{9,8},{10,11... | collective-permute-start | bytes 1179656 | tf_op jit(solution)/shard_map/ppermute | solution.py:730
  48.9 6.4 %collective-permute-start.3 = (bf16[256,384]{1,0:T(8,128)(2,1)}, bf16[256,384]{1,0:T(8,128)(2,1)S(1)}, u32[]{:S(2)}, u32[]{:S(2)}) collective-permute-start(bf16[256,384]{1,0:T(8,128)(2,1)} %get-tuple-element.72), channel_id=1, source_target_pairs={{0,1},{1,0},{2,3},{3,2},{4,5},{5,4},{6,7},{7,6},{8,9},{9,8},{10,11... | collective-permute-start | bytes 589832 | tf_op jit(solution)/shard_map/ppermute | solution.py:730
  49.4 8.0 %collective-permute-start.4 = (bf16[256,384]{1,0:T(8,128)(2,1)}, bf16[256,384]{1,0:T(8,128)(2,1)S(1)}, u32[]{:S(2)}, u32[]{:S(2)}) collective-permute-start(bf16[256,384]{1,0:T(8,128)(2,1)} %get-tuple-element.73), channel_id=1, source_target_pairs={{0,2},{1,3},{2,0},{3,1},{4,6},{5,7},{6,4},{7,5},{8,10},{9,11},{10,... | collective-permute-start | bytes 589832 | tf_op jit(solution)/shard_map/ppermute | solution.py:730
  51.2 8.9 %collective-permute-start.5 = (bf16[256,384]{1,0:T(8,128)(2,1)}, bf16[256,384]{1,0:T(8,128)(2,1)S(1)}, u32[]{:S(2)}, u32[]{:S(2)}) collective-permute-start(bf16[256,384]{1,0:T(8,128)(2,1)} %get-tuple-element.74), channel_id=1, source_target_pairs={{0,3},{1,2},{2,1},{3,0},{4,7},{5,6},{6,5},{7,4},{8,11},{9,10},{10,... | collective-permute-start | bytes 589832 | tf_op jit(solution)/shard_map/ppermute | solution.py:730
  98.7 24.6 %collective-permute-start.6 = (bf16[256,384]{1,0:T(8,128)(2,1)}, bf16[256,384]{1,0:T(8,128)(2,1)S(1)}, u32[]{:S(2)}, u32[]{:S(2)}) collective-permute-start(bf16[256,384]{1,0:T(8,128)(2,1)} %get-tuple-element.85), channel_id=1, source_target_pairs={{0,1},{1,0},{2,3},{3,2},{4,5},{5,4},{6,7},{7,6},{8,9},{9,8},{10,11... | collective-permute-start | bytes 589832 | tf_op jit(solution)/shard_map/ppermute | solution.py:730
  98.8 24.5 %collective-permute-start.7 = (bf16[256,384]{1,0:T(8,128)(2,1)}, bf16[256,384]{1,0:T(8,128)(2,1)S(1)}, u32[]{:S(2)}, u32[]{:S(2)}) collective-permute-start(bf16[256,384]{1,0:T(8,128)(2,1)} %get-tuple-element.86), channel_id=1, source_target_pairs={{0,2},{1,3},{2,0},{3,1},{4,6},{5,7},{6,4},{7,5},{8,10},{9,11},{10,... | collective-permute-start | bytes 589832 | tf_op jit(solution)/shard_map/ppermute | solution.py:730
  100.6 22.8 %collective-permute-start.8 = (bf16[256,384]{1,0:T(8,128)(2,1)}, bf16[256,384]{1,0:T(8,128)(2,1)S(1)}, u32[]{:S(2)}, u32[]{:S(2)}) collective-permute-start(bf16[256,384]{1,0:T(8,128)(2,1)} %get-tuple-element.87), channel_id=1, source_target_pairs={{0,3},{1,2},{2,1},{3,0},{4,7},{5,6},{6,5},{7,4},{8,11},{9,10},{10,... | collective-permute-start | bytes 589832 | tf_op jit(solution)/shard_map/ppermute | solution.py:730
  100.7 10.9 %collective-permute-start.34 = (f32[10,768]{1,0:T(8,128)S(1)}, f32[10,768]{1,0:T(8,128)S(1)}, u32[]{:S(2)}, u32[]{:S(2)}) collective-permute-start(f32[10,768]{1,0:T(8,128)S(1)} %fusion.14), channel_id=1, source_target_pairs={{0,2},{1,3},{2,0},{3,1},{4,6},{5,7},{6,4},{7,5},{8,10},{9,11},{10,... | collective-permute-start | bytes 92168 | tf_op jit(solution)/shard_map/ppermute | solution.py:730
  120.5 55.6 %collective-permute-start.37 = (f32[10,768]{1,0:T(8,128)}, f32[10,768]{1,0:T(8,128)}, u32[]{:S(2)}, u32[]{:S(2)}) collective-permute-start(f32[10,768]{1,0:T(8,128)} %add.197), channel_id=1, source_target_pairs={{0,16},{4,20},{8,24},{12,28},{16,0},{20,4},{24,8},{28,12},{1,17},{... | collective-permute-start | bytes 92168 | tf_op jit(solution)/shard_map/ppermute | solution.py:733
  164.1 16.6 %collective-permute-start.17 = (bf16[4,96,384]{2,1,0:T(8,128)(2,1)}, bf16[4,96,384]{2,1,0:T(8,128)(2,1)}, u32[]{:S(2)}, u32[]{:S(2)}) collective-permute-start(bf16[4,96,384]{2,1,0:T(8,128)(2,1)} %get-tuple-element.99), channel_id=1, source_target_pairs={{0,8},{4,12},{8,0},{12,4},{16,24},{20,28},{24,16},{28,20},{1,9},{5... | collective-permute-start | bytes 884744 | tf_op jit(solution)/shard_map/ppermute | solution.py:733
  165.6 16.6 %collective-permute-start.11 = (bf16[4,96,384]{2,1,0:T(8,128)(2,1)S(1)}, bf16[4,96,384]{2,1,0:T(8,128)(2,1)}, u32[]{:S(2)}, u32[]{:S(2)}) collective-permute-start(bf16[4,96,384]{2,1,0:T(8,128)(2,1)S(1)} %get-tuple-element.95), channel_id=1, source_target_pairs={{0,4},{4,0},{8,12},{12,8},{16,20},{20,16},{24,28},{28,24},{1,5},{5... | collective-permute-start | bytes 884744 | tf_op jit(solution)/shard_map/ppermute | solution.py:733
  176.1 60.0 %collective-permute-start.27 = (bf16[768,512]{1,0:T(8,128)(2,1)}, bf16[768,512]{1,0:T(8,128)(2,1)}, u32[]{:S(2)}, u32[]{:S(2)}) collective-permute-start(bf16[768,512]{1,0:T(8,128)(2,1)} %get-tuple-element.101.left), channel_id=1, source_target_pairs={{0,1},{1,0},{2,3},{3,2},{4,5},{5,4},{6,7},{7,6},{8,9},{9,8},{10,11... | collective-permute-start | bytes 2359304 | tf_op jit(solution)/shard_map/ppermute | solution.py:730
  176.1 59.9 %collective-permute-start.28 = (bf16[2,192,512]{2,1,0:T(8,128)(2,1)}, bf16[2,192,512]{2,1,0:T(8,128)(2,1)S(1)}, u32[]{:S(2)}, u32[]{:S(2)}) collective-permute-start(bf16[2,192,512]{2,1,0:T(8,128)(2,1)} %get-tuple-element.103), channel_id=1, source_target_pairs={{0,1},{1,0},{2,3},{3,2},{4,5},{5,4},{6,7},{7,6},{8,9},{9,8},{10,11... | collective-permute-start | bytes 1179656 | tf_op jit(solution)/shard_map/ppermute | solution.py:730
  179.4 89.0 %collective-permute-start.38 = (bf16[768,512]{1,0:T(8,128)(2,1)S(1)}, bf16[768,512]{1,0:T(8,128)(2,1)}, u32[]{:S(2)}, u32[]{:S(2)}) collective-permute-start(bf16[768,512]{1,0:T(8,128)(2,1)S(1)} %copy-done.19), channel_id=1, source_target_pairs={{0,1},{1,0},{2,3},{3,2},{4,5},{5,4},{6,7},{7,6},{8,9},{9,8},{10,11... | collective-permute-start | bytes 2359304 | tf_op jit(solution)/shard_map/ppermute | solution.py:730
  180.7 9.4 %collective-permute-start.14 = (bf16[4,96,384]{2,1,0:T(8,128)(2,1)S(1)}, bf16[4,96,384]{2,1,0:T(8,128)(2,1)S(1)}, u32[]{:S(2)}, u32[]{:S(2)}) collective-permute-start(bf16[4,96,384]{2,1,0:T(8,128)(2,1)S(1)} %get-tuple-element.97), channel_id=1, source_target_pairs={{0,4},{4,0},{8,12},{12,8},{16,20},{20,16},{24,28},{28,24},{1,5},{5... | collective-permute-start | bytes 884744 | tf_op jit(solution)/shard_map/ppermute | solution.py:733
  182.3 52.5 %collective-permute-start.26 = (f32[2,768]{1,0:T(2,128)}, f32[2,768]{1,0:T(2,128)}, u32[]{:S(2)}, u32[]{:S(2)}) collective-permute-start(f32[2,768]{1,0:T(2,128)} %add.188), channel_id=1, source_target_pairs={{0,16},{4,20},{8,24},{12,28},{16,0},{20,4},{24,8},{28,12},{1,17},{... | collective-permute-start | bytes 18440 | tf_op jit(solution)/shard_map/ppermute | solution.py:733
  190.1 5.5 %collective-permute-start.18 = (bf16[2,96,384]{2,1,0:T(8,128)(2,1)S(1)}, bf16[2,96,384]{2,1,0:T(8,128)(2,1)S(1)}, u32[]{:S(2)}, u32[]{:S(2)}) collective-permute-start(bf16[2,96,384]{2,1,0:T(8,128)(2,1)S(1)} %slice.552), channel_id=1, source_target_pairs={{0,4},{4,0},{8,12},{12,8},{16,20},{20,16},{24,28},{28,24},{1,5},{5... | collective-permute-start | bytes 442376 | tf_op jit(solution)/shard_map/ppermute | solution.py:733
  200.7 9.0 %collective-permute-start.15 = (bf16[2,96,384]{2,1,0:T(8,128)(2,1)S(1)}, bf16[2,96,384]{2,1,0:T(8,128)(2,1)S(1)}, u32[]{:S(2)}, u32[]{:S(2)}) collective-permute-start(bf16[2,96,384]{2,1,0:T(8,128)(2,1)S(1)} %slice.553), channel_id=1, source_target_pairs={{0,16},{4,20},{8,24},{12,28},{16,0},{20,4},{24,8},{28,12},{1,17},{... | collective-permute-start | bytes 442376 | tf_op jit(solution)/shard_map/ppermute | solution.py:733
  226.0 14.4 %collective-permute-start.20 = (f32[3,96,192]{2,1,0:T(8,128)}, f32[3,96,192]{2,1,0:T(8,128)}, u32[]{:S(2)}, u32[]{:S(2)}) collective-permute-start(f32[3,96,192]{2,1,0:T(8,128)} %pad_maximum_fusion.1), channel_id=1, source_target_pairs={{0,1},{1,0},{2,3},{3,2},{4,5},{5,4},{6,7},{7,6},{8,9},{9,8},{10,11... | collective-permute-start | bytes 663560 | tf_op jit(solution)/shard_map/ppermute | solution.py:730
  234.8 33.6 %collective-permute-start.39 = (bf16[2,512,768]{2,1,0:T(8,128)(2,1)}, bf16[2,512,768]{2,1,0:T(8,128)(2,1)}, u32[]{:S(2)}, u32[]{:S(2)}) collective-permute-start(bf16[2,512,768]{2,1,0:T(8,128)(2,1)} %get-tuple-element.111), channel_id=1, source_target_pairs={{0,1},{1,0},{2,3},{3,2},{4,5},{5,4},{6,7},{7,6},{8,9},{9,8},{10,11... | collective-permute-start | bytes 4718600 | tf_op jit(solution)/shard_map/ppermute | solution.py:730
  236.0 73.0 %collective-permute-start.52 = (bf16[2,192,512]{2,1,0:T(8,128)(2,1)}, bf16[2,192,512]{2,1,0:T(8,128)(2,1)S(1)}, u32[]{:S(2)}, u32[]{:S(2)}) collective-permute-start(bf16[2,192,512]{2,1,0:T(8,128)(2,1)} %get-tuple-element.119), channel_id=1, source_target_pairs={{0,1},{1,0},{2,3},{3,2},{4,5},{5,4},{6,7},{7,6},{8,9},{9,8},{10,11... | collective-permute-start | bytes 1179656 | tf_op jit(solution)/shard_map/ppermute | solution.py:730
  239.2 9.4 %collective-permute-start.29 = (bf16[4,96,384]{2,1,0:T(8,128)(2,1)S(1)}, bf16[4,96,384]{2,1,0:T(8,128)(2,1)S(1)}, u32[]{:S(2)}, u32[]{:S(2)}) collective-permute-start(bf16[4,96,384]{2,1,0:T(8,128)(2,1)S(1)} %get-tuple-element.105), channel_id=1, source_target_pairs={{0,4},{4,0},{8,12},{12,8},{16,20},{20,16},{24,28},{28,24},{1,5},{5... | collective-permute-start | bytes 884744 | tf_op jit(solution)/shard_map/ppermute | solution.py:733
  240.4 37.2 %collective-permute-start.9 = (f32[2,256,768]{2,1,0:T(8,128)}, f32[2,256,768]{2,1,0:T(8,128)}, u32[]{:S(2)}, u32[]{:S(2)}) collective-permute-start(f32[2,256,768]{2,1,0:T(8,128)} %get-tuple-element.93), channel_id=1, source_target_pairs={{0,1},{1,0},{2,3},{3,2},{4,5},{5,4},{6,7},{7,6},{8,9},{9,8},{10,11... | collective-permute-start | bytes 4718600 | tf_op jit(solution)/shard_map/ppermute | solution.py:730
  248.7 5.5 %collective-permute-start.30 = (bf16[2,96,384]{2,1,0:T(8,128)(2,1)S(1)}, bf16[2,96,384]{2,1,0:T(8,128)(2,1)S(1)}, u32[]{:S(2)}, u32[]{:S(2)}) collective-permute-start(bf16[2,96,384]{2,1,0:T(8,128)(2,1)S(1)} %slice.551), channel_id=1, source_target_pairs={{0,8},{4,12},{8,0},{12,4},{16,24},{20,28},{24,16},{28,20},{1,9},{5... | collective-permute-start | bytes 442376 | tf_op jit(solution)/shard_map/ppermute | solution.py:733
  254.3 5.8 %collective-permute-start.31 = (bf16[1,96,384]{2,1,0:T(8,128)(2,1)S(1)}, bf16[1,96,384]{2,1,0:T(8,128)(2,1)S(1)}, u32[]{:S(2)}, u32[]{:S(2)}) collective-permute-start(bf16[1,96,384]{2,1,0:T(8,128)(2,1)S(1)} %slice.561), channel_id=1, source_target_pairs={{0,16},{4,20},{8,24},{12,28},{16,0},{20,4},{24,8},{28,12},{1,17},{... | collective-permute-start | bytes 221192 | tf_op jit(solution)/shard_map/ppermute | solution.py:733
  260.1 5.7 %collective-permute-start.21 = (bf16[3,96,192]{2,1,0:T(8,128)(2,1)S(1)}, bf16[3,96,192]{2,1,0:T(8,128)(2,1)S(1)}, u32[]{:S(2)}, u32[]{:S(2)}) collective-permute-start(bf16[3,96,192]{2,1,0:T(8,128)(2,1)S(1)} %select_convert_fusion), channel_id=1, source_target_pairs={{0,2},{1,3},{2,0},{3,1},{4,6},{5,7},{6,4},{7,5},{8,10},{9,11},{10,... | collective-permute-start | bytes 331784 | tf_op jit(solution)/shard_map/ppermute | solution.py:730
  265.8 10.7 %collective-permute-start.32 = (bf16[96,192]{1,0:T(8,128)(2,1)S(1)}, bf16[96,192]{1,0:T(8,128)(2,1)S(1)}, u32[]{:S(2)}, u32[]{:S(2)}) collective-permute-start(bf16[96,192]{1,0:T(8,128)(2,1)S(1)} %slice.571), channel_id=1, source_target_pairs={{0,2},{1,3},{2,0},{3,1},{4,6},{5,7},{6,4},{7,5},{8,10},{9,11},{10,... | collective-permute-start | bytes 110600 | tf_op jit(solution)/shard_map/ppermute | solution.py:730
  268.4 40.7 %collective-permute-start.53 = (bf16[512,3072]{1,0:T(8,128)(2,1)}, bf16[512,3072]{1,0:T(8,128)(2,1)S(1)}, u32[]{:S(2)}, u32[]{:S(2)}) collective-permute-start(bf16[512,3072]{1,0:T(8,128)(2,1)} %get-tuple-element.120.act), channel_id=1, source_target_pairs={{0,1},{1,0},{2,3},{3,2},{4,5},{5,4},{6,7},{7,6},{8,9},{9,8},{10,11... | collective-permute-start | bytes 9437192 | tf_op jit(solution)/shard_map/ppermute | solution.py:730
  275.9 11.6 %collective-permute-start.48 = (bf16[8,96,256]{2,1,0:T(8,128)(2,1)S(1)}, bf16[8,96,256]{2,1,0:T(8,128)(2,1)S(1)}, u32[]{:S(2)}, u32[]{:S(2)}) collective-permute-start(bf16[8,96,256]{2,1,0:T(8,128)(2,1)S(1)} %get-tuple-element.117), channel_id=1, source_target_pairs={{0,4},{4,0},{8,12},{12,8},{16,20},{20,16},{24,28},{28,24},{1,5},{5... | collective-permute-start | bytes 1179656 | tf_op jit(solution)/shard_map/ppermute | solution.py:733
  277.1 11.2 %collective-permute-start.44 = (bf16[8,96,256]{2,1,0:T(8,128)(2,1)S(1)}, bf16[8,96,256]{2,1,0:T(8,128)(2,1)S(1)}, u32[]{:S(2)}, u32[]{:S(2)}) collective-permute-start(bf16[8,96,256]{2,1,0:T(8,128)(2,1)S(1)} %get-tuple-element.115), channel_id=1, source_target_pairs={{0,2},{1,3},{2,0},{3,1},{4,6},{5,7},{6,4},{7,5},{8,10},{9,11},{10,... | collective-permute-start | bytes 1179656 | tf_op jit(solution)/shard_map/ppermute | solution.py:730
  277.6 11.0 %collective-permute-start.40 = (bf16[8,96,256]{2,1,0:T(8,128)(2,1)S(1)}, bf16[8,96,256]{2,1,0:T(8,128)(2,1)S(1)}, u32[]{:S(2)}, u32[]{:S(2)}) collective-permute-start(bf16[8,96,256]{2,1,0:T(8,128)(2,1)S(1)} %get-tuple-element.113), channel_id=1, source_target_pairs={{0,8},{4,12},{8,0},{12,4},{16,24},{20,28},{24,16},{28,20},{1,9},{5... | collective-permute-start | bytes 1179656 | tf_op jit(solution)/shard_map/ppermute | solution.py:733
  287.5 13.3 %collective-permute-start.10 = (bf16[256,768]{1,0:T(8,128)(2,1)S(1)}, bf16[256,768]{1,0:T(8,128)(2,1)S(1)}, u32[]{:S(2)}, u32[]{:S(2)}) collective-permute-start(bf16[256,768]{1,0:T(8,128)(2,1)S(1)} %fusion.1), channel_id=1, source_target_pairs={{0,2},{1,3},{2,0},{3,1},{4,6},{5,7},{6,4},{7,5},{8,10},{9,11},{10,... | collective-permute-start | bytes 1179656 | tf_op jit(solution)/shard_map/ppermute | solution.py:730
  288.4 6.2 %collective-permute-start.49 = (bf16[4,96,256]{2,1,0:T(8,128)(2,1)S(1)}, bf16[4,96,256]{2,1,0:T(8,128)(2,1)S(1)}, u32[]{:S(2)}, u32[]{:S(2)}) collective-permute-start(bf16[4,96,256]{2,1,0:T(8,128)(2,1)S(1)} %slice.548), channel_id=1, source_target_pairs={{0,8},{4,12},{8,0},{12,4},{16,24},{20,28},{24,16},{28,20},{1,9},{5... | collective-permute-start | bytes 589832 | tf_op jit(solution)/shard_map/ppermute | solution.py:733
  288.6 7.6 %collective-permute-start.45 = (bf16[4,96,256]{2,1,0:T(8,128)(2,1)S(1)}, bf16[4,96,256]{2,1,0:T(8,128)(2,1)S(1)}, u32[]{:S(2)}, u32[]{:S(2)}) collective-permute-start(bf16[4,96,256]{2,1,0:T(8,128)(2,1)S(1)} %slice.549), channel_id=1, source_target_pairs={{0,4},{4,0},{8,12},{12,8},{16,20},{20,16},{24,28},{28,24},{1,5},{5... | collective-permute-start | bytes 589832 | tf_op jit(solution)/shard_map/ppermute | solution.py:733
  294.6 5.7 %collective-permute-start.41 = (bf16[4,96,256]{2,1,0:T(8,128)(2,1)S(1)}, bf16[4,96,256]{2,1,0:T(8,128)(2,1)S(1)}, u32[]{:S(2)}, u32[]{:S(2)}) collective-permute-start(bf16[4,96,256]{2,1,0:T(8,128)(2,1)S(1)} %slice.550), channel_id=1, source_target_pairs={{0,4},{4,0},{8,12},{12,8},{16,20},{20,16},{24,28},{28,24},{1,5},{5... | collective-permute-start | bytes 589832 | tf_op jit(solution)/shard_map/ppermute | solution.py:733
  296.1 7.5 %collective-permute-start.50 = (bf16[2,96,256]{2,1,0:T(8,128)(2,1)S(1)}, bf16[2,96,256]{2,1,0:T(8,128)(2,1)S(1)}, u32[]{:S(2)}, u32[]{:S(2)}) collective-permute-start(bf16[2,96,256]{2,1,0:T(8,128)(2,1)S(1)} %slice.558), channel_id=1, source_target_pairs={{0,2},{1,3},{2,0},{3,1},{4,6},{5,7},{6,4},{7,5},{8,10},{9,11},{10,... | collective-permute-start | bytes 294920 | tf_op jit(solution)/shard_map/ppermute | solution.py:730
  300.8 6.0 %collective-permute-start.42 = (bf16[2,96,256]{2,1,0:T(8,128)(2,1)S(1)}, bf16[2,96,256]{2,1,0:T(8,128)(2,1)S(1)}, u32[]{:S(2)}, u32[]{:S(2)}) collective-permute-start(bf16[2,96,256]{2,1,0:T(8,128)(2,1)S(1)} %slice.560), channel_id=1, source_target_pairs={{0,2},{1,3},{2,0},{3,1},{4,6},{5,7},{6,4},{7,5},{8,10},{9,11},{10,... | collective-permute-start | bytes 294920 | tf_op jit(solution)/shard_map/ppermute | solution.py:730
  304.9 15.3 %collective-permute-start.47 = (bf16[1,96,256]{2,1,0:T(8,128)(2,1)S(1)}, bf16[1,96,256]{2,1,0:T(8,128)(2,1)S(1)}, u32[]{:S(2)}, u32[]{:S(2)}) collective-permute-start(bf16[1,96,256]{2,1,0:T(8,128)(2,1)S(1)} %slice.569), channel_id=1, source_target_pairs={{0,16},{4,20},{8,24},{12,28},{16,0},{20,4},{24,8},{28,12},{1,17},{... | collective-permute-start | bytes 147464 | tf_op jit(solution)/shard_map/ppermute | solution.py:733
  306.9 13.4 %collective-permute-start.43 = (bf16[1,96,256]{2,1,0:T(8,128)(2,1)S(1)}, bf16[1,96,256]{2,1,0:T(8,128)(2,1)S(1)}, u32[]{:S(2)}, u32[]{:S(2)}) collective-permute-start(bf16[1,96,256]{2,1,0:T(8,128)(2,1)S(1)} %slice.570), channel_id=1, source_target_pairs={{0,16},{4,20},{8,24},{12,28},{16,0},{20,4},{24,8},{28,12},{1,17},{... | collective-permute-start | bytes 147464 | tf_op jit(solution)/shard_map/ppermute | solution.py:733
  319.1 7.8 %collective-permute-start.62 = (bf16[8,192,128]{2,1,0:T(8,128)(2,1)S(1)}, bf16[8,192,128]{2,1,0:T(8,128)(2,1)S(1)}, u32[]{:S(2)}, u32[]{:S(2)}) collective-permute-start(bf16[8,192,128]{2,1,0:T(8,128)(2,1)S(1)} %get-tuple-element.126), channel_id=1, source_target_pairs={{0,2},{1,3},{2,0},{3,1},{4,6},{5,7},{6,4},{7,5},{8,10},{9,11},{10,... | collective-permute-start | bytes 1179656 | tf_op jit(solution)/shard_map/ppermute | solution.py:730
  320.2 8.8 %collective-permute-start.58 = (bf16[8,192,128]{2,1,0:T(8,128)(2,1)S(1)}, bf16[8,192,128]{2,1,0:T(8,128)(2,1)S(1)}, u32[]{:S(2)}, u32[]{:S(2)}) collective-permute-start(bf16[8,192,128]{2,1,0:T(8,128)(2,1)S(1)} %get-tuple-element.124), channel_id=1, source_target_pairs={{0,8},{4,12},{8,0},{12,4},{16,24},{20,28},{24,16},{28,20},{1,9},{5... | collective-permute-start | bytes 1179656 | tf_op jit(solution)/shard_map/ppermute | solution.py:733
  322.0 11.2 %collective-permute-start.54 = (bf16[8,192,128]{2,1,0:T(8,128)(2,1)S(1)}, bf16[8,192,128]{2,1,0:T(8,128)(2,1)S(1)}, u32[]{:S(2)}, u32[]{:S(2)}) collective-permute-start(bf16[8,192,128]{2,1,0:T(8,128)(2,1)S(1)} %get-tuple-element.122), channel_id=1, source_target_pairs={{0,4},{4,0},{8,12},{12,8},{16,20},{20,16},{24,28},{28,24},{1,5},{5... | collective-permute-start | bytes 1179656 | tf_op jit(solution)/shard_map/ppermute | solution.py:733
  327.1 8.2 %collective-permute-start.63 = (bf16[4,192,128]{2,1,0:T(8,128)(2,1)S(1)}, bf16[4,192,128]{2,1,0:T(8,128)(2,1)S(1)}, u32[]{:S(2)}, u32[]{:S(2)}) collective-permute-start(bf16[4,192,128]{2,1,0:T(8,128)(2,1)S(1)} %slice.545), channel_id=1, source_target_pairs={{0,4},{4,0},{8,12},{12,8},{16,20},{20,16},{24,28},{28,24},{1,5},{5... | collective-permute-start | bytes 589832 | tf_op jit(solution)/shard_map/ppermute | solution.py:733
  329.1 8.3 %collective-permute-start.59 = (bf16[4,192,128]{2,1,0:T(8,128)(2,1)S(1)}, bf16[4,192,128]{2,1,0:T(8,128)(2,1)S(1)}, u32[]{:S(2)}, u32[]{:S(2)}) collective-permute-start(bf16[4,192,128]{2,1,0:T(8,128)(2,1)S(1)} %slice.546), channel_id=1, source_target_pairs={{0,4},{4,0},{8,12},{12,8},{16,20},{20,16},{24,28},{28,24},{1,5},{5... | collective-permute-start | bytes 589832 | tf_op jit(solution)/shard_map/ppermute | solution.py:733
  333.3 6.3 %collective-permute-start.55 = (bf16[4,192,128]{2,1,0:T(8,128)(2,1)S(1)}, bf16[4,192,128]{2,1,0:T(8,128)(2,1)S(1)}, u32[]{:S(2)}, u32[]{:S(2)}) collective-permute-start(bf16[4,192,128]{2,1,0:T(8,128)(2,1)S(1)} %slice.547), channel_id=1, source_target_pairs={{0,8},{4,12},{8,0},{12,4},{16,24},{20,28},{24,16},{28,20},{1,9},{5... | collective-permute-start | bytes 589832 | tf_op jit(solution)/shard_map/ppermute | solution.py:733
  335.4 5.8 %collective-permute-start.64 = (bf16[2,192,128]{2,1,0:T(8,128)(2,1)S(1)}, bf16[2,192,128]{2,1,0:T(8,128)(2,1)S(1)}, u32[]{:S(2)}, u32[]{:S(2)}) collective-permute-start(bf16[2,192,128]{2,1,0:T(8,128)(2,1)S(1)} %slice.555), channel_id=1, source_target_pairs={{0,8},{4,12},{8,0},{12,4},{16,24},{20,28},{24,16},{28,20},{1,9},{5... | collective-permute-start | bytes 294920 | tf_op jit(solution)/shard_map/ppermute | solution.py:733
  342.7 5.6 %collective-permute-start.61 = (bf16[1,192,128]{2,1,0:T(8,128)(2,1)S(1)}, bf16[1,192,128]{2,1,0:T(8,128)(2,1)S(1)}, u32[]{:S(2)}, u32[]{:S(2)}) collective-permute-start(bf16[1,192,128]{2,1,0:T(8,128)(2,1)S(1)} %slice.566), channel_id=1, source_target_pairs={{0,16},{4,20},{8,24},{12,28},{16,0},{20,4},{24,8},{28,12},{1,17},{... | collective-permute-start | bytes 147464 | tf_op jit(solution)/shard_map/ppermute | solution.py:733
  (65 other events, 794.4 us)
where the time goes:
time: 351 us; the launch traced here: 350 us
  Pallas kernels  127 us (36%)
  waiting for transfers between devices  126 us (36%)
  starting transfers between devices  54.4 us (15%)
  local copies, waits for them, and re-layouts  23.7 us (7%)
  other arithmetic  17 us (5%)
    ppermute x36, waiting for transfers between devices, over_batch(): lax.ppermute(array, 'batch', [(i, i ^ flip) for i in range(batch_size)])  92.1 us
    ppermute x30, waiting for transfers between devices, over_seq(): return lax.ppermute(array, 'seq', [(i, i ^ flip) for i in range(seq_size)])  34.1 us
    ppermute x36, starting transfers between devices, over_batch(): lax.ppermute(array, 'batch', [(i, i ^ flip) for i in range(batch_size)])  32.9 us
    pallas_call x1, Pallas kernels, attend_backward(): pl.pallas_call(backward_kernel, grid_spec=pltpu.PrefetchScalarGridSpec(nu...  30.3 us
    pallas_call x1, Pallas kernels, attend_forward(): pl.pallas_call(forward_kernel, grid_spec=pltpu.PrefetchScalarGridSpec(num...  29.8 us
    ppermute x30, starting transfers between devices, over_seq(): return lax.ppermute(array, 'seq', [(i, i ^ flip) for i in range(seq_size)])  21.4 us
    pallas_call x1, Pallas kernels, middle_forward(): pl.pallas_call(middle_forward_kernel, grid_spec=pltpu.PrefetchScalarGridS...  18.1 us
    pallas_call x1, Pallas kernels, middle_backward(): pl.pallas_call(middle_backward_kernel, grid_spec=pltpu.PrefetchScalarGrid...  16.5 us
  transfers between devices with their start and end apart: 66, of which 38 were waited for; matrix products, arithmetic and copies ran while one was open for 7% of the time, Pallas kernels for 18%

commit v1 on v0

v1 whole, which is shorter than its diff:
```python
import functools

import jax
import jax.numpy as jnp
from jax import lax
from jax.experimental import pallas as pl
from jax.experimental.pallas import tpu as pltpu
from jax.sharding import PartitionSpec as P

DH = 64
EPS = 1e-05
NEG = -1000000000.0
F32 = jnp.float32
LOW = jnp.bfloat16
PAIR = 2 * DH
SCALE = DH**-0.5
BLOCK = 128
SIZES = (2, 3, 4, 5, 6, 8)
VMEM = 60
ROOT_HALF = 0.5**0.5
ROOT_TWO_PI = 0.3989422804014327


def shaped(shape, dtype):
    return jax.ShapeDtypeStruct(shape, dtype)


def dot_nn(left, right):
    return jnp.dot(left, right, preferred_element_type=F32)


def dot_nt(left, right):
    return lax.dot_general(left, right, (((1,), (1,)), ((), ())), preferred_element_type=F32)


def params(mib):
    return pltpu.CompilerParams(vmem_limit_bytes=mib << 20, dimension_semantics=("arbitrary",))


def full(shape):
    return pl.BlockSpec(shape, lambda *_: (0,) * len(shape))


def cost(micros):
    return pl.CostEstimate(flops=int(micros * 1.15e9), transcendentals=0, bytes_accessed=0)


def column_sum(values):
    return jnp.sum(values, axis=0, keepdims=True)


def spot(rel, flip_x, order):
    bits = {"y": rel % 2, "z": (rel // 2) % 2, "w": rel // 4, "x": flip_x}
    index = 0
    for axis in order[1:]:
        index = index * 2 + bits[axis]
    return bits[order[0]], index


def put(value, rel, flip_x, order, send, keep):
    sent, index = spot(rel, flip_x, order)

    @pl.when(sent == 1)
    def _():
        send[pl.ds(index, 1)] = value.astype(LOW)[None]

    @pl.when(sent == 0)
    def _():
        keep[pl.ds(index, 1)] = value[None]


def put_rows(grad, rows, me, flip_x, order, send, keep):
    deep = grad.shape[0] // 8
    for b in range(8):
        rows[b] = grad[b * deep : (b + 1) * deep]
    for rel in range(8):
        sent, index = spot(rel, flip_x, order)
        value = rows[me ^ rel]
        if sent:
            send[index] = value.astype(LOW)
        else:
            keep[index] = value


def join_kernel(segments, routes, *refs):
    ins, outs = refs[: 2 * len(segments)], list(refs[2 * len(segments) :])
    for route in routes:
        send = outs.pop(0) if any(segments[m][n] > 1 for m, n in route) else None
        keep = outs.pop(0)
        sent = filled = 0
        for m, n in route:
            start, size = sum(segments[m][:n]), segments[m][n]
            total = ins[2 * m][start : start + size]
            total = total + ins[2 * m + 1][start : start + size].astype(F32)
            if size > 1:
                size //= 2
                send[sent : sent + size] = total[size:].astype(LOW)
                sent += size
            keep[filled : filled + size] = total[:size]
            filled += size


def join(messages, routes):
    segments = [list(message[0]) for message in messages]
    tail = messages[0][1].shape[1:]
    shapes, results = [], []
    for route in routes:
        sizes = [segments[m][n] for m, n in route]
        left = [size // 2 for size in sizes if size > 1]
        results.append(left)
        if left:
            shapes.append(shaped((sum(left),) + tail, LOW))
        shapes.append(shaped((sum(max(size // 2, 1) for size in sizes),) + tail, F32))
    operands = [array for message in messages for array in message[1:]]
    arrays = pl.pallas_call(
        functools.partial(join_kernel, segments, routes),
        grid=(1,),
        in_specs=[full(array.shape) for array in operands],
        out_specs=[full(shape.shape) for shape in shapes],
        out_shape=shapes,
        compiler_params=params(VMEM),
        cost_estimate=cost(1),
        name="join",
    )(*operands)
    arrays = list(arrays)
    return [(left, arrays.pop(0) if left else None, arrays.pop(0)) for left in results]


def each_window(info, block, run):
    start = pl.multiple_of(info[4 + block], BLOCK)
    kind = info[4 + (info.shape[0] - 4) // 2 + block]
    for n, size in enumerate(SIZES):

        @pl.when(kind == n)
        def _():
            run(pl.ds(start, size * BLOCK), size * BLOCK)


def windows(segment):
    tokens = segment.shape[0]
    rows = segment.reshape(tokens // BLOCK, BLOCK)
    first = jnp.sum((segment[None] < rows[:, :1]).astype(jnp.int32), axis=1) // BLOCK
    last = (jnp.sum((segment[None] <= rows[:, -1:]).astype(jnp.int32), axis=1) - 1) // BLOCK
    need = last - first + 1
    kind = sum((need > size).astype(jnp.int32) for size in SIZES[:-1])
    size = sum(
        jnp.where(kind == n, size, 0).astype(jnp.int32) for n, size in enumerate(SIZES)
    )
    return [jnp.minimum(first, tokens // BLOCK - size) * BLOCK, kind]


def both_heads(array):
    lane = lax.broadcasted_iota(jnp.int32, array.shape, 1)
    zero = jnp.zeros_like(array)
    return jnp.concatenate(
        [jnp.where(lane < DH, array, zero), jnp.where(lane < DH, zero, array)], axis=0
    )


def own_heads(turned):
    return jnp.concatenate([turned[:DH, :BLOCK], turned[DH:, BLOCK:]], axis=0)


def fill_segments(seg_row, seg_col):
    seg_col[...] = jnp.broadcast_to(seg_row[...].astype(F32), (BLOCK, seg_row.shape[1])).T


def masked_scores(key, query, seg_col, seg_row):
    same = seg_col == seg_row
    return jnp.where(jnp.concatenate([same, same], axis=1), dot_nt(key, query), NEG)


def forward_kernel(
    info, x0, x1, x2, x3, wq, wk, wv, bq, bv, seg_row,
    q_out, k_out, v_out, c0, c1, c2, c3, o_out, lse_out,
    xs, seg_col, qs, vt, ctx,
):
    place = info[0]
    tokens = xs.shape[0]
    quarter = tokens // 4

    @pl.when(pl.program_id(0) == 0)
    def _():
        for j, ref in enumerate((x0, x1, x2, x3)):
            xs[pl.ds(pl.multiple_of((place ^ j) * quarter, quarter), quarter), :] = ref[...]
        fill_segments(seg_row, seg_col)

    weights = jnp.concatenate([wq[...], wk[...], wv[...]], axis=1)
    projected = dot_nn(xs[...], weights)
    query = (projected[:, :PAIR] + bq[...].astype(F32)).astype(LOW)
    key = projected[:, PAIR : 2 * PAIR].astype(LOW)
    value = (projected[:, 2 * PAIR :] + bv[...].astype(F32)).astype(LOW)
    q_out[...] = query
    k_out[...] = key
    v_out[...] = value
    qs[...] = query * jnp.asarray(SCALE, LOW)
    vt[...] = value.T

    def step(b, _):
        start = pl.multiple_of(b * BLOCK, BLOCK)
        rows = pl.ds(start, BLOCK)

        def run(window, size):
            row = seg_row[:, rows].astype(F32)
            scores = masked_scores(k_out[window, :], both_heads(qs[rows, :]), seg_col[window, :], row)
            top = jnp.max(scores, axis=0, keepdims=True)
            expo = jnp.exp(scores - top)
            total = jnp.sum(expo, axis=0, keepdims=True)
            mixed = dot_nn(vt[:, window], expo.astype(LOW)) * (1.0 / total)
            lse_out[0, pl.ds(b, 1), :] = top + jnp.log(total)
            mixed = own_heads(mixed)
            o_out[:, rows] = mixed
            ctx[rows, :] = mixed.T.astype(LOW)

        each_window(info, b, run)
        return 0

    lax.fori_loop(0, tokens // BLOCK, step, 0)
    for j, ref in enumerate((c0, c1, c2, c3)):
        ref[...] = ctx[pl.ds(pl.multiple_of((place ^ j) * quarter, quarter), quarter), :]


def attend_forward(info, quarters, qkv_weight, query_bias, value_bias, seg):
    quarter, width = quarters[0].shape
    tokens, half = 4 * quarter, width // 2
    pairs = half // PAIR

    def weight_spec(t):
        return pl.BlockSpec((width, PAIR), lambda p, i: (0, (2 * t + i[1]) * pairs + p))

    def bias_spec():
        return pl.BlockSpec((1, PAIR), lambda p, i: (0, i[1] * pairs + p))

    col = pl.BlockSpec((tokens, PAIR), lambda p, i: (0, p))
    part = pl.BlockSpec((quarter, PAIR), lambda p, i: (0, p))
    blocks = tokens // BLOCK
    return pl.pallas_call(
        forward_kernel,
        grid_spec=pltpu.PrefetchScalarGridSpec(
            num_scalar_prefetch=1,
            grid=(pairs,),
            in_specs=[full((quarter, width))] * 4
            + [weight_spec(0), weight_spec(1), weight_spec(2), bias_spec(), bias_spec()]
            + [full((1, tokens))],
            out_specs=[col] * 3
            + [part] * 4
            + [pl.BlockSpec((PAIR, tokens), lambda p, i: (p, 0))]
            + [pl.BlockSpec((1, blocks, 2 * BLOCK), lambda p, i: (p, 0, 0))],
            scratch_shapes=[
                pltpu.VMEM((tokens, width), LOW),
                pltpu.VMEM((tokens, BLOCK), F32),
                pltpu.VMEM((tokens, PAIR), LOW),
                pltpu.VMEM((PAIR, tokens), LOW),
                pltpu.VMEM((tokens, PAIR), LOW),
            ],
        ),
        out_shape=[shaped((tokens, half), LOW)] * 3
        + [shaped((quarter, half), LOW)] * 4
        + [shaped((half, tokens), F32), shaped((pairs, blocks, 2 * BLOCK), F32)],
        compiler_params=params(VMEM),
        cost_estimate=cost(16),
        name="attend_forward",
    )(info, *quarters, qkv_weight, qkv_weight, qkv_weight, query_bias[None], value_bias[None], seg)


QKV_ORDERS = ("yzw", "zyw", "yzw")


def backward_kernel(
    order, info, q_in, k_in, v_in, o0, o1, o1b, o2, o3, o_in, lse, seg_row, x_t,
    dq_out, dk_out, dv_out, bias_out, w_send, w_keep,
    seg_col, qs, do, kt, dk, dv, w_rows,
):
    place, me = info[0], info[3]
    tokens = q_in.shape[0]
    quarter = tokens // 4
    fill_segments(seg_row, seg_col)
    for j, ref in enumerate((o0, None, o2, o3)):
        if ref is None:
            at = pl.multiple_of((place ^ 1) * quarter, quarter)
            do[pl.ds(at, quarter // 2), :] = o1[...]
            do[pl.ds(at + quarter // 2, quarter // 2), :] = o1b[...]
            continue
        do[pl.ds(pl.multiple_of((place ^ j) * quarter, quarter), quarter), :] = ref[...]
    qs[...] = q_in[...] * jnp.asarray(SCALE, LOW)
    kt[...] = k_in[...].T
    dk[...] = jnp.zeros_like(dk)
    dv[...] = jnp.zeros_like(dv)

    def step(b, _):
        start = pl.multiple_of(b * BLOCK, BLOCK)
        rows = pl.ds(start, BLOCK)

        def run(window, size):
            row = seg_row[:, rows].astype(F32)
            o_block = do[rows, :]
            query, grad = both_heads(qs[rows, :]), both_heads(o_block)
            along = o_block.T.astype(F32) * o_in[:, rows]
            delta = jnp.concatenate([column_sum(along[:DH]), column_sum(along[DH:])], axis=1)
            scores = masked_scores(k_in[window, :], query, seg_col[window, :], row)
            probs = jnp.exp(scores - lse[0, pl.ds(b, 1), :])
            d_scores = (probs * (dot_nt(v_in[window, :], grad) - delta)).astype(LOW)
            dv[window, :] += dot_nn(probs.astype(LOW), grad)
            dk[window, :] += dot_nn(d_scores, query)
            d_query = own_heads(dot_nn(kt[:, window], d_scores)) * SCALE
            dq_out[rows, :] = d_query.T.astype(LOW)

        each_window(info, b, run)
        return 0

    lax.fori_loop(0, tokens // BLOCK, step, 0)
    dk_out[...] = dk[...].astype(LOW)
    dv_out[...] = dv[...].astype(LOW)
    bias_out[0:1, :] = column_sum(dq_out[...].astype(F32))
    bias_out[1:2, :] = column_sum(dv_out[...].astype(F32))
    grad = jnp.concatenate([dq_out[...], dk_out[...], dv_out[...]], axis=1)
    grad = dot_nn(x_t[...], grad)
    put_rows(grad, w_rows, me, 0, order, w_send, w_keep)


def attend_backward(info, n, query, key, value, parts, context, lse, seg, x_t):
    tokens, half = query.shape
    quarter, blocks, width = tokens // 4, tokens // BLOCK, x_t.shape[0]
    col = pl.BlockSpec((tokens, PAIR), lambda p, i: (0, n))
    pairs = half // PAIR
    part = pl.BlockSpec((quarter, PAIR), lambda p, i: (0, n))
    first = pl.BlockSpec((None, quarter, PAIR), lambda p, i: (0, 0, n))
    packed = quarter // 2
    low, high = [
        pl.BlockSpec((packed, PAIR), lambda p, i, at=at: (half // packed, at * pairs + n))
        for at in range(2)
    ]
    weight = (4, width // 8, 3 * PAIR)
    return pl.pallas_call(
        functools.partial(backward_kernel, QKV_ORDERS[n]),
        grid_spec=pltpu.PrefetchScalarGridSpec(
            num_scalar_prefetch=1,
            grid=(1,),
            in_specs=[col] * 3
            + [part, low, high, first, part]
            + [pl.BlockSpec((PAIR, tokens), lambda p, i: (n, 0))]
            + [pl.BlockSpec((1, blocks, 2 * BLOCK), lambda p, i: (n, 0, 0))]
            + [full((1, tokens)), full((width, tokens))],
            out_specs=[full((tokens, PAIR))] * 3 + [full((2, PAIR))] + [full(weight)] * 2,
            scratch_shapes=[
                pltpu.VMEM((tokens, BLOCK), F32),
                pltpu.VMEM((tokens, PAIR), LOW),
                pltpu.VMEM((tokens, PAIR), LOW),
                pltpu.VMEM((PAIR, tokens), LOW),
                pltpu.VMEM((tokens, PAIR), F32),
                pltpu.VMEM((tokens, PAIR), F32),
                pltpu.VMEM((8, width // 8, 3 * PAIR), F32),
            ],
        ),
        out_shape=[shaped((tokens, PAIR), LOW)] * 3
        + [shaped((2, PAIR), F32), shaped(weight, LOW), shaped(weight, F32)],
        compiler_params=params(VMEM),
        cost_estimate=cost(8),
        name="attend_backward",
    )(info, query, key, value, *parts, context, lse, seg, x_t)


def normalise(values):
    centred = values - jnp.mean(values, axis=1, keepdims=True)
    root = lax.rsqrt(jnp.mean(centred * centred, axis=1, keepdims=True) + EPS)
    return centred * root, root


def norm_back(grad, gain, normal, root):
    e = grad * gain
    along = jnp.mean(e * normal, axis=1, keepdims=True)
    return root * (e - jnp.mean(e, axis=1, keepdims=True) - normal * along)


def store_columns(place, flipped, mine, send):
    size, count = flipped.shape[0] // 4, flipped.shape[1]
    for b in range(4):
        rel = place ^ b

        @pl.when(rel % 2 == 0)
        def _():
            mine[pl.ds(rel // 2, 1)] = flipped[b * size : (b + 1) * size][None]

        @pl.when(rel % 2 == 1)
        def _():
            rows = pl.ds(pl.multiple_of(rel // 2 * size, size), size)
            send[rows, :count] = flipped[b * size : (b + 1) * size]


def middle_forward_kernel(
    info, p0, p1, p2, p3, x_in, cot, wo, bo, g1, s1, up, bup, down, bdown, g2, s2,
    out, d_res, n1, r1, turned, act, slope, mine, send, vec,
    hid, hid_low, branch,
):
    place, core, chip = info[0], info[1], info[2]
    step = pl.program_id(0)
    quarter = p0.shape[0]

    @pl.when(step == 0)
    def _():
        first = core == 0

        def sides(a, b):
            a, b = a[...], b[...]
            return jnp.concatenate([jnp.where(first, a, b), jnp.where(first, b, a)], axis=1)

        ctx = jnp.concatenate([sides(p0, p1), sides(p2, p3)], axis=0)
        turned[1] = ctx.T
        x = jnp.concatenate([x_in[chip], x_in[1 - chip]], axis=0).astype(F32)
        summed = x + dot_nn(ctx, wo[...]) + bo[...].astype(F32)
        normal, root = normalise(summed)
        n1[...] = normal
        r1[...] = root
        hidden = normal * g1[...].astype(F32) + s1[...].astype(F32)
        hid[...] = hidden
        low = hidden.astype(LOW)
        hid_low[...] = low
        turned[0] = low.T
        branch[...] = jnp.zeros_like(branch)

    pre = dot_nn(hid_low[...], up[...]) + bup[...].astype(F32)
    phi = 0.5 + 0.5 * lax.erf(pre * ROOT_HALF)
    low = (pre * phi).astype(LOW)
    act[...] = low
    slope[...] = phi + pre * (jnp.exp(-0.5 * pre * pre) * ROOT_TWO_PI)
    branch[...] += dot_nn(low, down[...])

    @pl.when(step == pl.num_programs(0) - 1)
    def _():
        normal, root = normalise(hid[...] + branch[...] + bdown[...].astype(F32))
        final = (normal * g2[...].astype(F32) + s2[...].astype(F32)).astype(LOW)
        out[pl.ds(chip, 1)] = final[:quarter][None]
        out[pl.ds(1 - chip, 1)] = final[quarter:][None]
        grad = jnp.concatenate([cot[chip], cot[1 - chip]], axis=0).astype(F32)
        back = norm_back(grad, g2[...].astype(F32), normal, root)
        d_res[...] = back
        vec[0:1, :] = column_sum(back)
        vec[1:2, :] = column_sum(grad * normal)
        vec[2:3, :] = column_sum(grad)
        store_columns(place, back.astype(LOW).T, mine, send)


def middle_forward(info, parts, inputs, cotangent, wo, bo, g1, s1, up, bup, down, bdown, g2, s2):
    quarter, half = parts[0].shape
    width, inner = 2 * half, up.shape[1]
    count, steps = 2 * quarter, 4
    chunk = inner // steps
    vector = full((1, width))
    tokens = full((count, width))
    turned = full((2, width // 4, count))
    return pl.pallas_call(
        middle_forward_kernel,
        grid_spec=pltpu.PrefetchScalarGridSpec(
            num_scalar_prefetch=1,
            grid=(steps,),
            in_specs=[full((quarter, half))] * 4
            + [full((2, quarter, width))] * 2
            + [full((width, width)), vector, vector, vector]
            + [
                pl.BlockSpec((width, chunk), lambda c, i: (0, c)),
                pl.BlockSpec((1, chunk), lambda c, i: (0, c)),
                pl.BlockSpec((chunk, width), lambda c, i: (c, 0)),
            ]
            + [vector] * 3,
            out_specs=[full((2, quarter, width)), tokens, tokens, full((count, 1))]
            + [full((2, width, count))]
            + [pl.BlockSpec((count, chunk), lambda c, i: (0, c))] * 2
            + [turned, full((width // 2, count)), full((8, width))],
            scratch_shapes=[
                pltpu.VMEM((count, width), F32),
                pltpu.VMEM((count, width), LOW),
                pltpu.VMEM((count, width), F32),
            ],
        ),
        out_shape=[
            shaped((2, quarter, width), LOW),
            shaped((count, width), F32),
            shaped((count, width), F32),
            shaped((count, 1), F32),
            shaped((2, width, count), LOW),
            shaped((count, inner), LOW),
            shaped((count, inner), F32),
            shaped((2, width // 4, count), LOW),
            shaped((width // 2, count), LOW),
            shaped((8, width), F32),
        ],
        compiler_params=params(VMEM),
        cost_estimate=cost(18),
        name="middle_forward",
    )(
        info, *parts, inputs, cotangent, wo, bo[None], g1[None], s1[None],
        up, bup[None], down, bdown[None], g2[None], s2[None],
    )


def middle_backward_kernel(
    info, d_res, slope, down, up, wo, n1, r1, g1,
    to_core, mine_pre, d_up_bias, d_summed, q0, to_chip, mine, vec,
    d_branch, d_hidden,
):
    place, core = info[0], info[1]
    step = pl.program_id(0)
    quarter = q0.shape[0]
    half = q0.shape[1]
    count = d_res.shape[0]

    @pl.when(step == 0)
    def _():
        d_branch[...] = d_res[...].astype(LOW)
        d_hidden[...] = d_res[...]

    d_pre = (dot_nt(d_branch[...], down[...]) * slope[...]).astype(LOW)
    d_up_bias[...] = column_sum(d_pre.astype(F32))
    d_hidden[...] += dot_nt(d_pre, up[...])

    @pl.when(step < 2)
    def _():
        at = pl.multiple_of((1 + step) * count, count)
        to_core[pl.ds(at, count), :] = d_pre

    @pl.when(step >= 2)
    def _():
        mine_pre[0] = d_pre

    @pl.when(step == pl.num_programs(0) - 1)
    def _():
        grad = d_hidden[...]
        normal = n1[...]
        back = norm_back(grad, g1[...].astype(F32), normal, r1[...])
        d_summed[...] = back
        vec[0:1, :] = column_sum(back)
        vec[1:2, :] = column_sum(grad * normal)
        vec[2:3, :] = column_sum(grad)
        low = back.astype(LOW)
        store_columns(place, low.T, mine, to_core)
        d_ctx = dot_nt(low, wo[...]).astype(LOW)
        first = core == 0
        left, right = d_ctx[:, :half], d_ctx[:, half:]
        same = jnp.where(first, left, right)
        other = jnp.where(first, right, left)
        q0[...] = same[:quarter]
        packed = quarter // 2
        to_core[half : half + packed, :] = jnp.concatenate(
            [other[:packed], other[packed:quarter]], axis=1
        )
        to_chip[0] = same[quarter:]
        to_chip[1] = other[quarter:]


def middle_backward(info, d_res, slope, down, up, wo, n1, r1, g1):
    count, width = d_res.shape
    inner, quarter, half = up.shape[1], count // 2, width // 2
    steps = 4
    chunk = inner // steps

    def block(c, i):
        return i[0] ^ (1 - c // 2 + 2 * (c % 2))

    tokens = full((count, width))
    turned = full((2, width // 4, count))
    return pl.pallas_call(
        middle_backward_kernel,
        grid_spec=pltpu.PrefetchScalarGridSpec(
            num_scalar_prefetch=1,
            grid=(steps,),
            in_specs=[
                tokens,
                pl.BlockSpec((count, chunk), lambda c, i: (0, block(c, i))),
                pl.BlockSpec((chunk, width), lambda c, i: (block(c, i), 0)),
                pl.BlockSpec((width, chunk), lambda c, i: (0, block(c, i))),
                full((width, width)),
                tokens,
                full((count, 1)),
                full((1, width)),
            ],
            out_specs=[
                full((3 * count, width)),
                pl.BlockSpec((1, count, chunk), lambda c, i: (jnp.maximum(c - 2, 0), 0, 0)),
                pl.BlockSpec((1, chunk), lambda c, i: (0, block(c, i))),
                tokens,
            ]
            + [full((quarter, half)), full((2, quarter, half)), turned, full((8, width))],
            scratch_shapes=[pltpu.VMEM((count, width), LOW), pltpu.VMEM((count, width), F32)],
        ),
        out_shape=[
            shaped((3 * count, width), LOW),
            shaped((2, count, chunk), LOW),
            shaped((1, inner), F32),
            shaped((count, width), F32),
        ]
        + [
            shaped((quarter, half), LOW),
            shaped((2, quarter, half), LOW),
            shaped((2, width // 4, count), LOW),
            shaped((8, width), F32),
        ],
        compiler_params=params(VMEM),
        cost_estimate=cost(16),
        name="middle_backward",
    )(info, d_res, slope, down, up, wo, n1, r1, g1[None])


DOWN_ORDERS = ("zxyw", "xzyw")


def down_kernel(info, mine, theirs, act, act_pair, *outs):
    rel = pl.program_id(0)
    left = jnp.concatenate([mine[0], mine[1]], axis=0)
    grad = dot_nn(left, act[...]) + dot_nn(theirs[...], act_pair[...])
    size = grad.shape[0] // 4
    for n, order in enumerate(DOWN_ORDERS):
        for flip in range(2):
            start = (2 * flip + n) * size
            put(grad[start : start + size], rel, flip, order, outs[2 * n], outs[2 * n + 1])


def down_grad(info, mine, theirs, act, act_pair):
    _, size, count = mine.shape
    block = act.shape[1] // 8
    part = (8, size // 2, block)
    spec = pl.BlockSpec((count, block), lambda r, i: (0, r ^ i[3]))
    return pl.pallas_call(
        down_kernel,
        grid_spec=pltpu.PrefetchScalarGridSpec(
            num_scalar_prefetch=1,
            grid=(8,),
            in_specs=[full(mine.shape), full(theirs.shape), spec, spec],
            out_specs=[full(part)] * 4,
        ),
        out_shape=[shaped(part, LOW), shaped(part, F32)] * 2,
        compiler_params=params(VMEM),
        cost_estimate=cost(8),
        name="down_grad",
    )(info, mine, theirs, act, act_pair)


UP_ORDERS = ("xyzw", "yxzw")


def up_kernel(
    info, left, left_pair, mine, theirs, mine_d, theirs_d, send_a, keep_a, send_b, keep_b, rows
):
    me = info[3]
    step = pl.program_id(0)

    @pl.when(step < 4)
    def _():
        grad = dot_nn(left[0], mine[0]) + dot_nn(left_pair[0], theirs[...])
        for n, flip in ((0, 0), (1, 0), (0, 1), (1, 1)):

            @pl.when(step == 2 * flip + n)
            def _():
                send, keep = ((send_a, keep_a), (send_b, keep_b))[n]
                put_rows(grad, rows, me, flip, UP_ORDERS[n], send, keep)

    @pl.when(step == 4)
    def _():
        right = jnp.concatenate([mine_d[0], mine_d[1]], axis=0)
        grad = dot_nt(left[1], right) + dot_nt(left_pair[1], theirs_d[...])
        deep, wide = grad.shape[0] // 8, grad.shape[1] // 2
        for b in range(8):
            rows[b] = grad[b * deep : (b + 1) * deep]
        for rel in range(4):
            near, far = rows[me ^ rel], rows[me ^ (rel + 4)]
            for flip in range(2):
                cut = slice(flip * wide, (flip + 1) * wide)
                value = jnp.concatenate([near[:, cut], far[:, cut]], axis=1)
                index = 8 + 2 * flip + rel // 2
                if rel % 2:
                    send_b[index] = value.astype(LOW)
                else:
                    keep_b[index] = value


def up_grad(info, left, left_pair, mine, from_core, mine_d):
    _, width, count = left.shape
    half = width // 2

    def at(s):
        return jnp.minimum(s, 3)

    shapes = [
        shaped((lead, width // 8, half), dtype) for lead in (8, 12) for dtype in (LOW, F32)
    ]
    return pl.pallas_call(
        up_kernel,
        grid_spec=pltpu.PrefetchScalarGridSpec(
            num_scalar_prefetch=1,
            grid=(5,),
            in_specs=[full(left.shape)] * 2
            + [
                pl.BlockSpec((1, count, half), lambda s, i: (at(s) // 2, 0, at(s) % 2)),
                pl.BlockSpec((count, half), lambda s, i: (1 + at(s) // 2, at(s) % 2)),
                full(mine_d.shape),
                pl.BlockSpec((half, count), lambda s, i: (0, 0)),
            ],
            out_specs=[full(shape.shape) for shape in shapes],
            scratch_shapes=[pltpu.VMEM((8, width // 8, half), F32)],
        ),
        out_shape=shapes,
        compiler_params=params(VMEM),
        cost_estimate=cost(10),
        name="up_grad",
    )(info, left, left_pair, mine, from_core, mine_d, from_core)


def input_kernel(info, *refs):
    grads, weights, (keep, send) = refs[:9], refs[9:12], refs[12:]
    rel = pl.program_id(0)
    total = sum(
        dot_nt(jnp.concatenate([ref[...] for ref in grads[t::3]], axis=1), weights[t][...])
        for t in range(3)
    )

    @pl.when(rel < 2)
    def _():
        send[0] = total

    @pl.when(rel >= 2)
    def _():
        keep[0] = total


def input_part(info, grads, qkv_weight):
    tokens = grads[0].shape[0]
    width = qkv_weight.shape[0]
    quarter, half = tokens // 4, width // 2

    rows = pl.BlockSpec((quarter, PAIR), lambda c, i: (i[0] ^ (1 - c // 2 + 2 * (c % 2)), 0))

    def weight(t):
        return pl.BlockSpec((width, half), lambda c, i: (0, 2 * t + i[1]))

    return pl.pallas_call(
        input_kernel,
        grid_spec=pltpu.PrefetchScalarGridSpec(
            num_scalar_prefetch=1,
            grid=(4,),
            in_specs=[rows] * 9 + [weight(0), weight(1), weight(2)],
            out_specs=[
                pl.BlockSpec((1, quarter, width), lambda c, i: (jnp.maximum(c - 2, 0), 0, 0)),
                pl.BlockSpec((1, quarter, width), lambda c, i: (jnp.minimum(c, 1), 0, 0)),
            ],
        ),
        out_shape=[shaped((2, quarter, width), F32)] * 2,
        compiler_params=params(VMEM),
        cost_estimate=cost(6),
        name="input_part",
    )(info, *grads, qkv_weight, qkv_weight, qkv_weight)


UNITS = (((0, 1), (2, 3), (4,), (5,)), ((0,), (1,), (2, 3), (4, 5)))


def share_kernel(info, *refs):
    place, core = info[0], info[1]
    kept, got, (own, one, two, three) = refs[:3], refs[3:6], refs[6:]
    total = [kept[n][0] + got[n][0].astype(F32) for n in range(3)]
    units = []
    for t in range(3):
        part = jnp.concatenate([pair[:, t * PAIR : (t + 1) * PAIR] for pair in total], axis=1)
        units += jnp.split(part, 2, axis=1)
    for side in range(2):
        for target in range(4):
            for flip, ref in enumerate((own, one, two, three)):

                @pl.when(jnp.logical_and(core == side, place ^ target == flip))
                def _():
                    for n in range(2):
                        unit = units[UNITS[side][target][n % len(UNITS[side][target])]]
                        ref[n] = unit.astype(ref.dtype)


def share(info, kept, got):
    unit = (2, kept[0].shape[1], kept[0].shape[2] // 2)
    return pl.pallas_call(
        share_kernel,
        grid_spec=pltpu.PrefetchScalarGridSpec(
            num_scalar_prefetch=1,
            grid=(1,),
            in_specs=[full(kept[0].shape)] * 6,
            out_specs=[full(unit)] * 4,
        ),
        out_shape=[shaped(unit, F32)] + [shaped(unit, LOW)] * 3,
        compiler_params=params(VMEM),
        cost_estimate=cost(1),
        name="share",
    )(info, *kept, *got)


def gather_kernel(info, own, one, two, three, out):
    place = info[0]
    same = own[...] + two[...].astype(F32)
    other = one[...].astype(F32) + three[...].astype(F32)
    for target in range(4):

        @pl.when(place == target)
        def _():
            sides = (same, other) if target % 2 == 0 else (other, same)
            pieces = [
                (side_unit, sides[side][n])
                for side in range(2)
                for n, side_unit in enumerate(
                    unit % 2 + 4 * (unit // 2) + 2 * side for unit in UNITS[side][target]
                )
            ]
            pieces.sort(key=lambda piece: piece[0])
            out[...] = jnp.concatenate([piece[1] for piece in pieces], axis=1)


def gather(info, own, *others):
    shape = (own.shape[1], 3 * own.shape[2])
    return pl.pallas_call(
        gather_kernel,
        grid_spec=pltpu.PrefetchScalarGridSpec(
            num_scalar_prefetch=1,
            grid=(1,),
            in_specs=[full(own.shape)] * 4,
            out_specs=full(shape),
        ),
        out_shape=shaped(shape, F32),
        compiler_params=params(VMEM),
        cost_estimate=cost(1),
        name="gather",
    )(info, own, *others)


def turn_kernel(info, x0, x1, x2, x3, x_t):
    quarter = x0.shape[0]
    for j, ref in enumerate((x0, x1, x2, x3)):
        at = pl.multiple_of((info[0] ^ j) * quarter, quarter)
        x_t[:, pl.ds(at, quarter)] = ref[...].T


def turn(info, quarters):
    quarter, width = quarters[0].shape
    return pl.pallas_call(
        turn_kernel,
        grid_spec=pltpu.PrefetchScalarGridSpec(
            num_scalar_prefetch=1,
            grid=(1,),
            in_specs=[full((quarter, width))] * 4,
            out_specs=full((width, 4 * quarter)),
        ),
        out_shape=shaped((width, 4 * quarter), LOW),
        compiler_params=params(VMEM),
        cost_estimate=cost(1),
        name="turn",
    )(info, *quarters)


def body(
    inputs,
    segments,
    qkv_weight,
    query_bias,
    value_bias,
    out_weight,
    out_bias,
    norm1_gain,
    norm1_shift,
    up_weight,
    up_bias,
    down_weight,
    down_bias,
    norm2_gain,
    norm2_shift,
    cotangent,
):
    rows, quarter, width = inputs.shape
    half = width // 2
    seq_size = lax.axis_size("seq")
    batch_size = lax.axis_size("batch")
    fine = batch_size // 8
    place = lax.axis_index("seq")
    chip, core = place // 2, place % 2
    segment = lax.dynamic_index_in_dim(segments, chip, 0)
    info = jnp.stack([place, core, chip, lax.axis_index("batch") // fine]).astype(jnp.int32)
    info = jnp.concatenate([info] + windows(segment[0]))

    def over_seq(array, flip):
        return lax.ppermute(array, "seq", [(i, i ^ flip) for i in range(seq_size)])

    def over_batch(array, flip):
        return lax.ppermute(array, "batch", [(i, i ^ flip) for i in range(batch_size)])

    def swap(array, axis):
        if axis == "x":
            return over_seq(array, 2)
        return over_batch(array, fine << "yzw".index(axis))

    def pick(array, index, axis=0):
        return lax.dynamic_index_in_dim(array, index, axis, keepdims=False)

    def tie(*arrays):
        return lax.optimization_barrier(arrays)

    def launch(*messages):
        return [
            (order, segments, kept, swap(sent, order[0]))
            for order, segments, sent, kept in messages
        ]

    def land(products, flights, *routes):
        count = len(products)
        tied = tie(*products, *[flight[3] for flight in flights])
        landed = [flight[1:3] + (got,) for flight, got in zip(flights, tied[count:])]
        made = join(landed, [route[1:] for route in routes])
        return list(tied[:count]), [(route[0],) + new for route, new in zip(routes, made)]

    def follow(array, messages):
        array, *kept = tie(array, *[message[3] for message in messages])
        return [array] + [message[:3] + (own,) for message, own in zip(messages, kept)]

    def finish(grad):
        if fine > 1:
            groups = [[i * fine + j for j in range(fine)] for i in range(8)]
            grad = lax.psum_scatter(
                grad, "batch", scatter_dimension=0, axis_index_groups=groups, tiled=True
            )
        return grad

    own = pick(inputs, chip)
    far = over_seq(pick(inputs, 1 - chip), 2)
    near = over_seq(own, 1)
    across = over_seq(far, 1)
    quarters = (own, near, far, across)

    query, key, value, *parts, context, lse = attend_forward(
        info, quarters, qkv_weight, query_bias, value_bias, segment
    )
    parts = [parts[0]] + [over_seq(parts[j], j) for j in (1, 2, 3)]
    x_t = turn(info, quarters)
    parts[0], x_t = tie(parts[0], x_t)

    outputs, d_res, n1, r1, turned, act, slope, mine, send, vec_two = middle_forward(
        info, parts, inputs, cotangent, out_weight, out_bias, norm1_gain, norm1_shift,
        up_weight, up_bias, down_weight, down_bias, norm2_gain, norm2_shift,
    )
    pair = over_seq(turned, 1), over_seq(act, 1), over_seq(send, 1)
    back = middle_backward(
        info, d_res, slope, down_weight, up_weight, out_weight, n1, r1, norm1_gain
    )
    turned_pair, act_pair, theirs, *back = tie(*pair, *back)
    to_core, mine_pre, d_up_bias, d_summed, q0, to_chip, mine_d, vec_one = back
    mine, d_summed = tie(mine, d_summed)

    from_core, from_chip = over_seq(to_core, 1), over_seq(to_chip, 2)
    made = down_grad(info, mine, theirs, act, act_pair)
    from_core, from_chip, *made = tie(from_core, from_chip, *made)
    downs = launch(
        (DOWN_ORDERS[0], [8], made[0], made[1]), (DOWN_ORDERS[1], [8], made[2], made[3])
    )
    across = over_seq(from_chip[1], 1)
    made = up_grad(info, turned, turned_pair, mine_pre, from_core, mine_d)
    across, *made = tie(across, *made)
    ups = launch((UP_ORDERS[0], [8], made[0], made[1]), (UP_ORDERS[1], [8, 4], made[2], made[3]))
    d_parts = (q0, from_core, from_core, from_chip, across)

    def piece(n, query):
        made = attend_backward(
            info, n, query, key, value, d_parts, context, lse, segment, x_t
        )
        return made

    def opening(n, made):
        return QKV_ORDERS[n], [4], made[4], made[5]

    zero = piece(0, query)
    zero, downs = land(zero, downs, (DOWN_ORDERS[0][1:], (0, 0)), (DOWN_ORDERS[1][1:], (1, 0)))
    query, *downs = follow(query, downs)
    *downs, first = launch(*downs, opening(0, zero))

    one = piece(1, query)
    one, (up_a, up_b, down, first) = land(
        one,
        ups + downs + [first],
        (UP_ORDERS[0][1:], (0, 0)),
        (UP_ORDERS[1][1:], (1, 0), (1, 1)),
        ("yw", (2, 0), (3, 0)),
        (QKV_ORDERS[0][1:], (4, 0)),
    )
    query, up_a, up_b, down, first = follow(query, [up_a, up_b, down, first])
    flights = launch(up_a, up_b, down, opening(1, one), first)

    two = piece(2, query)
    two, (up, down, second, first) = land(
        two,
        flights,
        ("zw", (0, 0), (1, 0), (1, 1)),
        ("w", (2, 0), (2, 1)),
        (QKV_ORDERS[1][1:], (3, 0)),
        ("w", (4, 0)),
    )
    grads = [*zero[:3], *one[:3], *two[:3]]
    grads[0], up, down, second, first = follow(grads[0], [up, down, second, first])
    flights = launch(opening(2, two), up, down, second)
    bias_part = jnp.concatenate([zero[3], one[3], two[3]], axis=1)
    bias_zero = jnp.zeros_like(bias_part)
    bias_part = jnp.where(
        core == 0,
        jnp.concatenate([bias_part, bias_zero], axis=1),
        jnp.concatenate([bias_zero, bias_part], axis=1),
    )
    vectors = jnp.concatenate([vec_one[:3], vec_two[:3], d_up_bias.reshape(-1, width), bias_part])
    vectors_got = over_seq(vectors, 1)

    keep, send = input_part(info, grads, qkv_weight)
    (keep, send, vectors_got), (third, up, down, second) = land(
        [keep, send, vectors_got],
        flights,
        (QKV_ORDERS[2][1:], (0, 0)),
        ("w", (1, 0), (1, 1), (1, 2)),
        ("", (2, 0), (2, 1)),
        ("w", (3, 0)),
    )
    out_total, down_total = up[3][2], down[3]
    third, up, first = launch(third, up, first)
    vectors = vectors + vectors_got
    vectors_got = over_seq(vectors, 2)
    d_row_got = over_seq(send, 1)
    first_got, (d_row_got, vectors_got), (third, up) = first[3], *land(
        [d_row_got, vectors_got], [third, up], ("w", (0, 0)), ("", (1, 0), (1, 1))
    )
    up_total = up[3]
    vectors = vectors + vectors_got
    third, second = launch(third, second)
    vectors = vectors + swap(vectors, "y")
    vectors_got = swap(vectors, "z")
    d_row = keep + d_row_got
    d_far = over_seq(d_row[1].astype(LOW), 2)
    third_got, second_got, vectors_got, d_far = tie(third[3], second[3], vectors_got, d_far)
    own, *others = share(
        info, (first[2], second[2], third[2]), (first_got, second_got, third_got)
    )
    qkv_total = gather(info, own, *[over_seq(other, 1 + j) for j, other in enumerate(others)])
    qkv_total = finish(qkv_total)
    vectors = vectors + vectors_got
    wide = half // 2
    out_total = out_total[:, :wide] + swap(out_total[:, wide:].astype(LOW), "w").astype(F32)
    out_total = finish(out_total)
    down_total = finish(down_total.reshape(wide, half).T)
    up_total = finish(jnp.concatenate([up_total[0], up_total[1]], axis=1))

    vectors = vectors + swap(vectors, "w")
    flip = 1
    while flip < fine:
        vectors = vectors + over_batch(vectors, flip)
        flip *= 2
    d_near = d_summed[:quarter] + d_row[0]
    d_far = d_summed[quarter:] + d_far.astype(F32)
    d_inputs = jnp.stack([jnp.where(chip == 0, d_near, d_far), jnp.where(chip == 0, d_far, d_near)])
    return (
        outputs,
        d_inputs,
        qkv_total,
        vectors[-2],
        vectors[-1],
        out_total,
        vectors[0],
        vectors[1],
        vectors[2],
        up_total,
        vectors[6:-2].reshape(-1),
        down_total,
        vectors[3],
        vectors[4],
        vectors[5],
    )


def solution(mesh):
    whole, split = P(), P("batch", "seq")
    tokens = P("batch", "seq", None)
    return jax.shard_map(
        body,
        mesh=mesh,
        in_specs=(tokens, P("batch", None)) + (whole,) * 13 + (tokens,),
        out_specs=(tokens, tokens, split, whole, whole, split)
        + (whole,) * 3
        + (split, whole, split)
        + (whole,) * 3,
        check_vma=False,
    )
```

time: 351 us -> 242 us (0.69)
  waiting for transfers between devices: 126 us -> 26.6 us
  Pallas kernels: 127 us -> 144 us
  starting transfers between devices: 54.4 us -> 42.1 us
  other arithmetic: 17 us -> 6.36 us
  local copies, waits for them, and re-layouts: 23.7 us -> 19.8 us
    ppermute x36 -> x21, waiting for transfers between devices: 92.1 us -> 13.7 us  [over_batch(): lax.ppermute(array, 'batch', [(i, i ^ flip) for i in range(batch_size)])]
    ppermute x30 -> x23, waiting for transfers between devices: 34.1 us -> 12.8 us  [over_seq(): return lax.ppermute(array, 'seq', [(i, i ^ flip) for i in range(seq_size)])]
    pallas_call x3 -> x10, Pallas kernels: 39.6 us -> 52.9 us  [the longest x3 30.5 us: attend_backward(): pl.pallas_call(functools.partial(backward_kernel, QKV_ORDERS[n]), grid_sp...]
    ppermute x30 -> x23, starting transfers between devices: 21.4 us -> 12.8 us  [over_seq(): return lax.ppermute(array, 'seq', [(i, i ^ flip) for i in range(seq_size)])]
    pallas_call x1, Pallas kernels: 29.8 us -> 23.3 us  [attend_forward(): pl.pallas_call(forward_kernel, grid_spec=pltpu.PrefetchScalarGridSpec(num...]
    add x38 -> x7, other arithmetic: 8.88 us -> 2.47 us  [the longest x1 1.77 us: body(): d_row = keep + d_row_got]
    pallas_call x1, Pallas kernels: 7.48 us -> 11.1 us  [up_grad(): pl.pallas_call(up_kernel, grid_spec=pltpu.PrefetchScalarGridSpec(num_scal...]
    ppermute x36 -> x21, starting transfers between devices: 32.9 us -> 29.4 us  [over_batch(): lax.ppermute(array, 'batch', [(i, i ^ flip) for i in range(batch_size)])]
  transfers between devices with their start and end apart: 66 -> 44, of which waited for: 38 -> 10; matrix products, arithmetic and copies ran while one was open for 7% -> 6% of each run, Pallas kernels for 18% -> 40%
where the time goes in v1:
time: 242 us; the launch traced here: 241 us
  Pallas kernels  144 us (60%)
  starting transfers between devices  42.1 us (17%)
  waiting for transfers between devices  26.6 us (11%)
  local copies, waits for them, and re-layouts  19.8 us (8%)
  other arithmetic  6.36 us (3%)
    pallas_call x3, Pallas kernels, attend_backward(): pl.pallas_call(functools.partial(backward_kernel, QKV_ORDERS[n]), grid_sp...  30.5 us
    ppermute x21, starting transfers between devices, over_batch(): lax.ppermute(array, 'batch', [(i, i ^ flip) for i in range(batch_size)])  29.4 us
    pallas_call x1, Pallas kernels, attend_forward(): pl.pallas_call(forward_kernel, grid_spec=pltpu.PrefetchScalarGridSpec(num...  23.3 us
    pallas_call x1, Pallas kernels, middle_forward(): pl.pallas_call(middle_forward_kernel, grid_spec=pltpu.PrefetchScalarGridS...  18.2 us
    pallas_call x5, Pallas kernels, join(): pl.pallas_call(functools.partial(join_kernel, segments, routes), grid=(1,...  16.7 us
    pallas_call x1, Pallas kernels, middle_backward(): pl.pallas_call(middle_backward_kernel, grid_spec=pltpu.PrefetchScalarGrid...  16.7 us
    ppermute x21, waiting for transfers between devices, over_batch(): lax.ppermute(array, 'batch', [(i, i ^ flip) for i in range(batch_size)])  13.7 us
    ppermute x23, waiting for transfers between devices, over_seq(): return lax.ppermute(array, 'seq', [(i, i ^ flip) for i in range(seq_size)])  12.8 us
  transfers between devices with their start and end apart: 44, of which 10 were waited for; matrix products, arithmetic and copies ran while one was open for 6% of the time, Pallas kernels for 40%

profile of v1, /device:TPU:0, one launch (start us, length us, event | category | flops | bytes accessed | tf_op | source)
XLA Modules:
  0.0 240.6 jit_solution(9313304891862313531)
XLA Ops:
  0.7 1.2 dynamic-slice_bitcast_fusion
  1.9 3.0 %collective-permute-start.1 = (bf16[256,768]{1,0:T(8,128)(2,1)S(1)}, bf16[256,768]{1,0:T(8,128)(2,1)S(1)}, u32[]{:S(2)}, u32[]{:S(2)}) collective-permute-start(bf16[256,768]{1,0:T(8,128)(2,1)S(1)} %get-tuple-element.377), channel_id=1, source_target_pairs={{0,2},{1,3},{2,0},{3,1},{4,6},{5,7},{6,4},{7,5},{8,10},{9,11},{10,... | collective-permute-start | bytes 1179656 | tf_op jit(solution)/shard_map/ppermute | solution.py:882
  4.9 9.1 %collective-permute-done.1.x2 = bf16[256,768]{1,0:T(8,128)(2,1)S(1)} collective-permute-done((bf16[256,768]{1,0:T(8,128)(2,1)S(1)}, bf16[256,768]{1,0:T(8,128)(2,1)S(1)}, u32[]{:S(2)}, u32[]{:S(2)}) %collective-permute-start.1) | collective-permute-done | bytes 393248 | tf_op jit(solution)/shard_map/ppermute | solution.py:882
  17.9 23.3 %attend_forward.1 = (bf16[1024,384]{1,0:T(8,128)(2,1)}, bf16[1024,384]{1,0:T(8,128)(2,1)}, bf16[1024,384]{1,0:T(8,128)(2,1)}, bf16[256,384]{1,0:T(8,128)(2,1)}, ...) custom-call(s32[20]{0:T(128)} %concatenate.18.info, ...), custom_call_target="tpu_custom_call" | custom-call | flops 18400000000 | tf_op jit(solution)/shard_map/attend_forward/pallas_call | solution.py:237
  41.8 1.4 collective-permute-start.5
  47.3 3.7 %turn.1.x_t = bf16[768,1024]{1,0:T(8,128)(2,1)} custom-call(s32[20]{0:T(128)} %concatenate.18.info, bf16[256,768]{1,0:T(8,128)(2,1)} %copy-done.7, bf16[256,768]{1,0:T(8,128)(2,1)} %copy-done.35, bf16[256,768]{1,0:T(8,128)(2,1)} %copy-done.34, bf16[256,768]{1,0:T(8,128)(2,1)} %copy-done.36), custom_call_target="tpu_custom_call" | custom-call | flops 1150000000 | tf_op jit(solution)/shard_map/turn/pallas_call | solution.py:837
  51.0 1.2 collective-permute-done.5.p3
  52.9 18.2 %middle_forward.1 = (bf16[2,256,768]{2,1,0:T(8,128)(2,1)}, f32[512,768]{1,0:T(8,128)}, f32[512,768]{1,0:T(8,128)}, f32[512,1]{1,0:T(8,128)}, bf16[2,768,512]{2,1...) custom-call(s32[20]{0:T(128)} %concatenate.18.info, ...), custom_call_target="tpu_custom_call" | custom-call | flops 20700000256 | tf_op jit(solution)/shard_map/middle_forward/pallas_call | solution.py:451
  72.3 16.7 %middle_backward.1 = (bf16[1536,768]{1,0:T(8,128)(2,1)}, bf16[2,512,768]{2,1,0:T(8,128)(2,1)}, f32[1,3072]{1,0:T(1,128)}, f32[512,768]{1,0:T(8,128)}, bf16[256,3...) custom-call(s32[20]{0:T(128)} %concatenate.18.info, ...), custom_call_target="tpu_custom_call" | custom-call | flops 18400000000 | tf_op jit(solution)/shard_map/middle_backward/pallas_call | solution.py:561
  89.9 1.5 copy-done.31
  91.8 10.6 %down_grad.1 = (bf16[8,96,384]{2,1,0:T(8,128)(2,1)}, f32[8,96,384]{2,1,0:T(8,128)}, bf16[8,96,384]{2,1,0:T(8,128)(2,1)}, f32[8,96,384]{2,1,0:T(8,128)}) custom-call(s32[20]{0:T(128)} %concatenate.18.info, bf16[2,192,512]{2,1,0:T(8,128)(2,1)} %get-tuple-element.218.mine, bf16[384,512]{1,0:T(8,128)(2,1)} %copy-done.37, ...), custom_call_target="tpu_custom_call" | custom-call | flops 9200000000 | tf_op jit(solution)/shard_map/down_grad/pallas_call | solution.py:622
  103.8 3.2 %collective-permute-start.12 = (bf16[8,96,384]{2,1,0:T(8,128)(2,1)}, bf16[8,96,384]{2,1,0:T(8,128)(2,1)S(1)}, u32[]{:S(2)}, u32[]{:S(2)}) collective-permute-start(bf16[8,96,384]{2,1,0:T(8,128)(2,1)} %get-tuple-element.244), channel_id=1, source_target_pairs={{0,8},{4,12},{8,0},{12,4},{16,24},{20,28},{24,16},{28,20},{1,9},{5... | collective-permute-start | bytes 1769480 | tf_op jit(solution)/shard_map/ppermute | solution.py:885
  107.3 11.1 %up_grad.1 = (bf16[8,96,384]{2,1,0:T(8,128)(2,1)}, f32[8,96,384]{2,1,0:T(8,128)}, bf16[12,96,384]{2,1,0:T(8,128)(2,1)}, f32[12,96,384]{2,1,0:T(8,128)}) custom-call(s32[20]{0:T(128)} %concatenate.18.info, bf16[2,768,512]{2,1,0:T(8,128)(2,1)} %get-tuple-element.195.left, bf16[2,768,512]{2,1,0:T(8,128)(2,1)} %collective-permute-done.6.left_pair, ...), custom_call_target="tpu_custom_call" | custom-call | flops 11500000256 | tf_op jit(solution)/shard_map/up_grad/pallas_call | solution.py:685
  118.4 1.6 collective-permute-start.15
  119.9 1.7 collective-permute-start.14
  121.7 10.1 %attend_backward.3 = (bf16[1024,128]{1,0:T(8,128)(2,1)}, bf16[1024,128]{1,0:T(8,128)(2,1)}, bf16[1024,128]{1,0:T(8,128)(2,1)}, f32[2,128]{1,0:T(2,128)}, bf16[4,...) custom-call(s32[20]{0:T(128)} %concatenate.18.info, bf16[1024,384]{1,0:T(8,128)(2,1)} %get-tuple-element.280.q_in, ...), custom_call_target="tpu_custom_call" | custom-call | flops 9200000000 | tf_op jit(solution)/shard_map/attend_backward/pallas_call | solution.py:334
  132.8 3.3 %join.5 = (bf16[4,96,384]{2,1,0:T(8,128)(2,1)}, f32[4,96,384]{2,1,0:T(8,128)}, bf16[4,96,384]{2,1,0:T(8,128)(2,1)}, f32[4,96,384]{2,1,0:T(8,128)}) custom-call(f32[8,96,384]{2,1,0:T(8,128)} %get-tuple-element.247.refs_0_, bf16[8,96,384]{2,1,0:T(8,128)(2,1)} %copy-done.32, f32[8,96,384]{2,1,0:T(8,128)} %get-tuple-element.249.refs_2_, ...), custom_call_target="tpu_custom_call" | custom-call | flops 1150000000 | tf_op jit(solution)/shard_map/join/pallas_call | solution.py:115
  136.0 1.0 collective-permute-start.17
  137.3 10.3 %attend_backward.4 = (bf16[1024,128]{1,0:T(8,128)(2,1)}, bf16[1024,128]{1,0:T(8,128)(2,1)}, bf16[1024,128]{1,0:T(8,128)(2,1)}, f32[2,128]{1,0:T(2,128)}, bf16[4,...) custom-call(s32[20]{0:T(128)} %concatenate.18.info, bf16[1024,384]{1,0:T(8,128)(2,1)} %get-tuple-element.280.q_in, ...), custom_call_target="tpu_custom_call" | custom-call | flops 9200000000 | tf_op jit(solution)/shard_map/attend_backward/pallas_call | solution.py:334
  149.1 4.9 %join.6 = (bf16[4,96,384]{2,1,0:T(8,128)(2,1)}, f32[4,96,384]{2,1,0:T(8,128)}, bf16[6,96,384]{2,1,0:T(8,128)(2,1)}, f32[6,96,384]{2,1,0:T(8,128)}, bf16[4,96,384...) custom-call(f32[8,96,384]{2,1,0:T(8,128)} %get-tuple-element.254.refs_0_, ...), custom_call_target="tpu_custom_call" | custom-call | flops 1150000000 | tf_op jit(solution)/shard_map/join/pallas_call | solution.py:115
  154.7 1.7 collective-permute-start.19
  156.7 2.7 %collective-permute-start.23 = (bf16[2,96,384]{2,1,0:T(8,128)(2,1)}, bf16[2,96,384]{2,1,0:T(8,128)(2,1)S(1)}, u32[]{:S(2)}, u32[]{:S(2)}) collective-permute-start(bf16[2,96,384]{2,1,0:T(8,128)(2,1)} %get-tuple-element.291), channel_id=1, source_target_pairs={{0,8},{4,12},{8,0},{12,4},{16,24},{20,28},{24,16},{28,20},{1,9},{5... | collective-permute-start | bytes 442376 | tf_op jit(solution)/shard_map/ppermute | solution.py:885
  159.5 10.1 %attend_backward.5 = (bf16[1024,128]{1,0:T(8,128)(2,1)}, bf16[1024,128]{1,0:T(8,128)(2,1)}, bf16[1024,128]{1,0:T(8,128)(2,1)}, f32[2,128]{1,0:T(2,128)}, bf16[4,...) custom-call(s32[20]{0:T(128)} %concatenate.18.info, bf16[1024,384]{1,0:T(8,128)(2,1)} %get-tuple-element.280.q_in, ...), custom_call_target="tpu_custom_call" | custom-call | flops 9200000000 | tf_op jit(solution)/shard_map/attend_backward/pallas_call | solution.py:334
  170.7 3.6 %join.7 = (bf16[5,96,384]{2,1,0:T(8,128)(2,1)}, f32[5,96,384]{2,1,0:T(8,128)}, bf16[2,96,384]{2,1,0:T(8,128)(2,1)}, f32[2,96,384]{2,1,0:T(8,128)}, bf16[2,96,384...) custom-call(f32[4,96,384]{2,1,0:T(8,128)} %get-tuple-element.279.refs_0_, ...), custom_call_target="tpu_custom_call" | custom-call | flops 1150000000 | tf_op jit(solution)/shard_map/join/pallas_call | solution.py:115
  174.3 1.6 collective-permute-start.26
  175.9 3.1 %collective-permute-start.27 = (bf16[2,96,384]{2,1,0:T(8,128)(2,1)}, bf16[2,96,384]{2,1,0:T(8,128)(2,1)S(1)}, u32[]{:S(2)}, u32[]{:S(2)}) collective-permute-start(bf16[2,96,384]{2,1,0:T(8,128)(2,1)} %get-tuple-element.324), channel_id=1, source_target_pairs={{0,16},{4,20},{8,24},{12,28},{16,0},{20,4},{24,8},{28,12},{1,17},{... | collective-permute-start | bytes 442376 | tf_op jit(solution)/shard_map/ppermute | solution.py:885
  179.0 1.4 collective-permute-start.28
  181.0 7.8 %input_part.1 = (f32[2,256,768]{2,1,0:T(8,128)}, f32[2,256,768]{2,1,0:T(8,128)}) custom-call(s32[20]{0:T(128)} %concatenate.18.info, bf16[1024,128]{1,0:T(8,128)(2,1)} %get-tuple-element.305.refs_0_, bf16[1024,128]{1,0:T(8,128)(2,1)} %get-tuple-element.306.refs_1_, bf16[1024,128]{1,0:T(8,128)(2,1)} %get-tuple-element.307.refs_2_, ...), custom_call_target="tpu_custom_call" | custom-call | flops 6899999744 | tf_op jit(solution)/shard_map/input_part/pallas_call | solution.py:734
  188.9 2.3 collective-permute-done.25.refs_1_
  192.1 2.9 %join.8 = (bf16[2,96,384]{2,1,0:T(8,128)(2,1)}, f32[2,96,384]{2,1,0:T(8,128)}, bf16[2,96,384]{2,1,0:T(8,128)(2,1)}, f32[3,96,384]{2,1,0:T(8,128)}, f32[2,96,384]...) custom-call(f32[4,96,384]{2,1,0:T(8,128)} %get-tuple-element.329.refs_0_, ...), custom_call_target="tpu_custom_call" | custom-call | flops 1150000000 | tf_op jit(solution)/shard_map/join/pallas_call | solution.py:115
  196.0 2.3 collective-permute-start.43
  198.8 1.1 collective-permute-start.31
  200.0 1.8 collective-permute-done.43
  201.7 1.5 collective-permute-start.32
  203.9 1.4 collective-permute-start.34
  206.3 6.5 %collective-permute-done.32.refs_3_ = bf16[2,96,384]{2,1,0:T(8,128)(2,1)S(1)} collective-permute-done((bf16[2,96,384]{2,1,0:T(8,128)(2,1)}, bf16[2,96,384]{2,1,0:T(8,128)(2,1)S(1)}, u32[]{:S(2)}, u32[]{:S(2)}) %collective-permute-start.32) | collective-permute-done | bytes 147488 | tf_op jit(solution)/shard_map/ppermute | solution.py:885
  212.7 1.8 add.90
  216.3 2.0 join.9
  218.3 1.0 slice_bitcast_fusion.3
  219.4 2.9 %collective-permute-start.36 = (f32[12,768]{1,0:T(8,128)S(1)}, f32[12,768]{1,0:T(8,128)S(1)}, u32[]{:S(2)}, u32[]{:S(2)}) collective-permute-start(f32[12,768]{1,0:T(8,128)S(1)} %add.93), channel_id=1, source_target_pairs={{0,8},{4,12},{8,0},{12,4},{16,24},{20,28},{24,16},{28,20},{1,9},{5... | collective-permute-start | bytes 110600 | tf_op jit(solution)/shard_map/ppermute | solution.py:885
  223.1 2.1 collective-permute-done.36
  225.2 1.3 collective-permute-start.42
  227.1 3.2 %share.1 = (f32[2,96,192]{2,1,0:T(8,128)}, bf16[2,96,192]{2,1,0:T(8,128)(2,1)}, bf16[2,96,192]{2,1,0:T(8,128)(2,1)}, bf16[2,96,192]{2,1,0:T(8,128)(2,1)}) custom-call(s32[20]{0:T(128)} %concatenate.18.info, f32[1,96,384]{2,1,0:T(8,128)} %get-tuple-element.348.refs_0_, f32[1,96,384]{2,1,0:T(8,128)} %get-tuple-element.349.refs_1_, ...), custom_call_target="tpu_custom_call" | custom-call | flops 1150000000 | tf_op jit(solution)/shard_map/share/pallas_call | solution.py:776
  230.3 1.3 collective-permute-start.40
  232.3 1.2 pad_maximum_fusion
  234.9 1.3 collective-permute-done.40.two
  236.2 1.3 collective-permute-done.41.three
  238.0 2.6 %gather.1 = f32[96,576]{1,0:T(8,128)} custom-call(s32[20]{0:T(128)} %concatenate.18.info, f32[2,96,192]{2,1,0:T(8,128)} %get-tuple-element.354.own, bf16[2,96,192]{2,1,0:T(8,128)(2,1)} %copy-done.51, bf16[2,96,192]{2,1,0:T(8,128)(2,1)} %copy-done.52, bf16[2,96,192]{2,1,0:T(8,128)(2,1)} %copy-done.53), custom_call_target="tpu_custom_call" | custom-call | flops 1150000000 | tf_op jit(solution)/shard_map/gather/pallas_call | solution.py:813
  (214 shorter events, 28.5 us)
Async XLA Ops:
  1.9 12.1 %collective-permute-start.1 = (bf16[256,768]{1,0:T(8,128)(2,1)S(1)}, bf16[256,768]{1,0:T(8,128)(2,1)S(1)}, u32[]{:S(2)}, u32[]{:S(2)}) collective-permute-start(bf16[256,768]{1,0:T(8,128)(2,1)S(1)} %get-tuple-element.377), channel_id=1, source_target_pairs={{0,2},{1,3},{2,0},{3,1},{4,6},{5,7},{6,4},{7,5},{8,10},{9,11},{10,... | collective-permute-start | bytes 1179656 | tf_op jit(solution)/shard_map/ppermute | solution.py:882
  4.9 11.5 %collective-permute-start = (bf16[256,768]{1,0:T(8,128)(2,1)S(1)}, bf16[256,768]{1,0:T(8,128)(2,1)S(1)}, u32[]{:S(2)}, u32[]{:S(2)}) collective-permute-start(bf16[256,768]{1,0:T(8,128)(2,1)S(1)} %get-tuple-element.378.x0), channel_id=1, source_target_pairs={{0,1},{1,0},{2,3},{3,2},{4,5},{5,4},{6,7},{7,6},{8,9},{9,8},{10,11... | collective-permute-start | bytes 1179656 | tf_op jit(solution)/shard_map/ppermute | solution.py:882
  14.0 2.4 collective-permute-start.2
  16.3 28.7 %copy-start.25 = (bf16[768]{0:T(1024)(128)(2,1)S(1)}, bf16[768]{0:T(1024)(128)(2,1)}, u32[]{:S(2)}) copy-start(bf16[768]{0:T(1024)(128)(2,1)} %param.24) | copy-start | bytes 4612
  16.3 29.2 %copy-start.26 = (bf16[768]{0:T(1024)(128)(2,1)S(1)}, bf16[768]{0:T(1024)(128)(2,1)}, u32[]{:S(2)}) copy-start(bf16[768]{0:T(1024)(128)(2,1)} %param.28) | copy-start | bytes 4612
  16.3 29.8 %copy-start.27 = (bf16[768]{0:T(1024)(128)(2,1)S(1)}, bf16[768]{0:T(1024)(128)(2,1)}, u32[]{:S(2)}) copy-start(bf16[768]{0:T(1024)(128)(2,1)} %param.29) | copy-start | bytes 4612
  16.3 30.4 %copy-start.28 = (bf16[768]{0:T(1024)(128)(2,1)S(1)}, bf16[768]{0:T(1024)(128)(2,1)}, u32[]{:S(2)}) copy-start(bf16[768]{0:T(1024)(128)(2,1)} %param.30) | copy-start | bytes 4612
  41.2 9.8 %collective-permute-start.3 = (bf16[256,384]{1,0:T(8,128)(2,1)}, bf16[256,384]{1,0:T(8,128)(2,1)S(1)}, u32[]{:S(2)}, u32[]{:S(2)}) collective-permute-start(bf16[256,384]{1,0:T(8,128)(2,1)} %get-tuple-element.190), channel_id=1, source_target_pairs={{0,1},{1,0},{2,3},{3,2},{4,5},{5,4},{6,7},{7,6},{8,9},{9,8},{10,11... | collective-permute-start | bytes 589832 | tf_op jit(solution)/shard_map/ppermute | solution.py:882
  41.8 9.2 %collective-permute-start.4 = (bf16[256,384]{1,0:T(8,128)(2,1)}, bf16[256,384]{1,0:T(8,128)(2,1)S(1)}, u32[]{:S(2)}, u32[]{:S(2)}) collective-permute-start(bf16[256,384]{1,0:T(8,128)(2,1)} %get-tuple-element.191), channel_id=1, source_target_pairs={{0,2},{1,3},{2,0},{3,1},{4,6},{5,7},{6,4},{7,5},{8,10},{9,11},{10,... | collective-permute-start | bytes 589832 | tf_op jit(solution)/shard_map/ppermute | solution.py:882
  41.8 10.4 %collective-permute-start.5 = (bf16[256,384]{1,0:T(8,128)(2,1)}, bf16[256,384]{1,0:T(8,128)(2,1)S(1)}, u32[]{:S(2)}, u32[]{:S(2)}) collective-permute-start(bf16[256,384]{1,0:T(8,128)(2,1)} %get-tuple-element.192), channel_id=1, source_target_pairs={{0,3},{1,2},{2,1},{3,0},{4,7},{5,6},{6,5},{7,4},{8,11},{9,10},{10,... | collective-permute-start | bytes 589832 | tf_op jit(solution)/shard_map/ppermute | solution.py:882
  71.0 18.0 %collective-permute-start.7 = (bf16[512,3072]{1,0:T(8,128)(2,1)}, bf16[512,3072]{1,0:T(8,128)(2,1)S(1)}, u32[]{:S(2)}, u32[]{:S(2)}) collective-permute-start(bf16[512,3072]{1,0:T(8,128)(2,1)} %get-tuple-element.196.act), channel_id=1, source_target_pairs={{0,1},{1,0},{2,3},{3,2},{4,5},{5,4},{6,7},{7,6},{8,9},{9,8},{10,11... | collective-permute-start | bytes 9437192 | tf_op jit(solution)/shard_map/ppermute | solution.py:882
  71.8 17.2 %collective-permute-start.6 = (bf16[2,768,512]{2,1,0:T(8,128)(2,1)}, bf16[2,768,512]{2,1,0:T(8,128)(2,1)}, u32[]{:S(2)}, u32[]{:S(2)}) collective-permute-start(bf16[2,768,512]{2,1,0:T(8,128)(2,1)} %get-tuple-element.195.left), channel_id=1, source_target_pairs={{0,1},{1,0},{2,3},{3,2},{4,5},{5,4},{6,7},{7,6},{8,9},{9,8},{10,11... | collective-permute-start | bytes 4718600 | tf_op jit(solution)/shard_map/ppermute | solution.py:882
  71.9 17.1 %collective-permute-start.8 = (bf16[384,512]{1,0:T(8,128)(2,1)}, bf16[384,512]{1,0:T(8,128)(2,1)S(1)}, u32[]{:S(2)}, u32[]{:S(2)}) collective-permute-start(bf16[384,512]{1,0:T(8,128)(2,1)} %get-tuple-element.197), channel_id=1, source_target_pairs={{0,1},{1,0},{2,3},{3,2},{4,5},{5,4},{6,7},{7,6},{8,9},{9,8},{10,11... | collective-permute-start | bytes 1179656 | tf_op jit(solution)/shard_map/ppermute | solution.py:882
  89.8 13.9 %collective-permute-start.9 = (bf16[1536,768]{1,0:T(8,128)(2,1)}, bf16[1536,768]{1,0:T(8,128)(2,1)}, u32[]{:S(2)}, u32[]{:S(2)}) collective-permute-start(bf16[1536,768]{1,0:T(8,128)(2,1)} %get-tuple-element.216), channel_id=1, source_target_pairs={{0,1},{1,0},{2,3},{3,2},{4,5},{5,4},{6,7},{7,6},{8,9},{9,8},{10,11... | collective-permute-start | bytes 7077896 | tf_op jit(solution)/shard_map/ppermute | solution.py:882
  91.4 12.2 %collective-permute-start.10 = (bf16[2,256,384]{2,1,0:T(8,128)(2,1)}, bf16[2,256,384]{2,1,0:T(8,128)(2,1)S(1)}, u32[]{:S(2)}, u32[]{:S(2)}) collective-permute-start(bf16[2,256,384]{2,1,0:T(8,128)(2,1)} %get-tuple-element.217), channel_id=1, source_target_pairs={{0,2},{1,3},{2,0},{3,1},{4,6},{5,7},{6,4},{7,5},{8,10},{9,11},{10,... | collective-permute-start | bytes 1179656 | tf_op jit(solution)/shard_map/ppermute | solution.py:882
  103.7 14.6 %collective-permute-start.11 = (bf16[256,384]{1,0:T(8,128)(2,1)S(1)}, bf16[256,384]{1,0:T(8,128)(2,1)S(1)}, u32[]{:S(2)}, u32[]{:S(2)}) collective-permute-start(bf16[256,384]{1,0:T(8,128)(2,1)S(1)} %slice_bitcast_fusion.1), channel_id=1, source_target_pairs={{0,1},{1,0},{2,3},{3,2},{4,5},{5,4},{6,7},{7,6},{8,9},{9,8},{10,11... | collective-permute-start | bytes 589832 | tf_op jit(solution)/shard_map/ppermute | solution.py:882
  103.8 27.9 %collective-permute-start.12 = (bf16[8,96,384]{2,1,0:T(8,128)(2,1)}, bf16[8,96,384]{2,1,0:T(8,128)(2,1)S(1)}, u32[]{:S(2)}, u32[]{:S(2)}) collective-permute-start(bf16[8,96,384]{2,1,0:T(8,128)(2,1)} %get-tuple-element.244), channel_id=1, source_target_pairs={{0,8},{4,12},{8,0},{12,4},{16,24},{20,28},{24,16},{28,20},{1,9},{5... | collective-permute-start | bytes 1769480 | tf_op jit(solution)/shard_map/ppermute | solution.py:885
  107.0 24.8 %collective-permute-start.13 = (bf16[8,96,384]{2,1,0:T(8,128)(2,1)}, bf16[8,96,384]{2,1,0:T(8,128)(2,1)S(1)}, u32[]{:S(2)}, u32[]{:S(2)}) collective-permute-start(bf16[8,96,384]{2,1,0:T(8,128)(2,1)} %get-tuple-element.245), channel_id=1, source_target_pairs={{0,2},{1,3},{2,0},{3,1},{4,6},{5,7},{6,4},{7,5},{8,10},{9,11},{10,... | collective-permute-start | bytes 1769480 | tf_op jit(solution)/shard_map/ppermute | solution.py:882
  118.4 29.3 %collective-permute-start.15 = (bf16[12,96,384]{2,1,0:T(8,128)(2,1)}, bf16[12,96,384]{2,1,0:T(8,128)(2,1)S(1)}, u32[]{:S(2)}, u32[]{:S(2)}) collective-permute-start(bf16[12,96,384]{2,1,0:T(8,128)(2,1)} %get-tuple-element.262), channel_id=1, source_target_pairs={{0,4},{4,0},{8,12},{12,8},{16,20},{20,16},{24,28},{28,24},{1,5},{5... | collective-permute-start | bytes 2654216 | tf_op jit(solution)/shard_map/ppermute | solution.py:885
  119.9 27.7 %collective-permute-start.14 = (bf16[8,96,384]{2,1,0:T(8,128)(2,1)}, bf16[8,96,384]{2,1,0:T(8,128)(2,1)S(1)}, u32[]{:S(2)}, u32[]{:S(2)}) collective-permute-start(bf16[8,96,384]{2,1,0:T(8,128)(2,1)} %get-tuple-element.261), channel_id=1, source_target_pairs={{0,2},{1,3},{2,0},{3,1},{4,6},{5,7},{6,4},{7,5},{8,10},{9,11},{10,... | collective-permute-start | bytes 1769480 | tf_op jit(solution)/shard_map/ppermute | solution.py:882
  136.0 11.6 %collective-permute-start.16 = (bf16[4,96,384]{2,1,0:T(8,128)(2,1)}, bf16[4,96,384]{2,1,0:T(8,128)(2,1)S(1)}, u32[]{:S(2)}, u32[]{:S(2)}) collective-permute-start(bf16[4,96,384]{2,1,0:T(8,128)(2,1)} %get-tuple-element.263), channel_id=1, source_target_pairs={{0,2},{1,3},{2,0},{3,1},{4,6},{5,7},{6,4},{7,5},{8,10},{9,11},{10,... | collective-permute-start | bytes 884744 | tf_op jit(solution)/shard_map/ppermute | solution.py:882
  136.0 11.6 %collective-permute-start.17 = (bf16[4,96,384]{2,1,0:T(8,128)(2,1)}, bf16[4,96,384]{2,1,0:T(8,128)(2,1)S(1)}, u32[]{:S(2)}, u32[]{:S(2)}) collective-permute-start(bf16[4,96,384]{2,1,0:T(8,128)(2,1)} %get-tuple-element.264), channel_id=1, source_target_pairs={{0,8},{4,12},{8,0},{12,4},{16,24},{20,28},{24,16},{28,20},{1,9},{5... | collective-permute-start | bytes 884744 | tf_op jit(solution)/shard_map/ppermute | solution.py:885
  137.0 10.7 %collective-permute-start.18 = (bf16[4,96,384]{2,1,0:T(8,128)(2,1)S(1)}, bf16[4,96,384]{2,1,0:T(8,128)(2,1)S(1)}, u32[]{:S(2)}, u32[]{:S(2)}) collective-permute-start(bf16[4,96,384]{2,1,0:T(8,128)(2,1)S(1)} %copy-done.42), channel_id=1, source_target_pairs={{0,4},{4,0},{8,12},{12,8},{16,20},{20,16},{24,28},{28,24},{1,5},{5... | collective-permute-start | bytes 884744 | tf_op jit(solution)/shard_map/ppermute | solution.py:885
  154.0 15.6 %collective-permute-start.20 = (bf16[6,96,384]{2,1,0:T(8,128)(2,1)}, bf16[6,96,384]{2,1,0:T(8,128)(2,1)S(1)}, u32[]{:S(2)}, u32[]{:S(2)}) collective-permute-start(bf16[6,96,384]{2,1,0:T(8,128)(2,1)} %get-tuple-element.288), channel_id=1, source_target_pairs={{0,2},{1,3},{2,0},{3,1},{4,6},{5,7},{6,4},{7,5},{8,10},{9,11},{10,... | collective-permute-start | bytes 1327112 | tf_op jit(solution)/shard_map/ppermute | solution.py:882
  154.7 14.9 %collective-permute-start.19 = (bf16[4,96,384]{2,1,0:T(8,128)(2,1)}, bf16[4,96,384]{2,1,0:T(8,128)(2,1)S(1)}, u32[]{:S(2)}, u32[]{:S(2)}) collective-permute-start(bf16[4,96,384]{2,1,0:T(8,128)(2,1)} %get-tuple-element.287), channel_id=1, source_target_pairs={{0,4},{4,0},{8,12},{12,8},{16,20},{20,16},{24,28},{28,24},{1,5},{5... | collective-permute-start | bytes 884744 | tf_op jit(solution)/shard_map/ppermute | solution.py:885
  156.4 13.2 %collective-permute-start.21 = (bf16[4,96,384]{2,1,0:T(8,128)(2,1)}, bf16[4,96,384]{2,1,0:T(8,128)(2,1)S(1)}, u32[]{:S(2)}, u32[]{:S(2)}) collective-permute-start(bf16[4,96,384]{2,1,0:T(8,128)(2,1)} %get-tuple-element.289), channel_id=1, source_target_pairs={{0,4},{4,0},{8,12},{12,8},{16,20},{20,16},{24,28},{28,24},{1,5},{5... | collective-permute-start | bytes 884744 | tf_op jit(solution)/shard_map/ppermute | solution.py:885
  156.7 12.9 %collective-permute-start.23 = (bf16[2,96,384]{2,1,0:T(8,128)(2,1)}, bf16[2,96,384]{2,1,0:T(8,128)(2,1)S(1)}, u32[]{:S(2)}, u32[]{:S(2)}) collective-permute-start(bf16[2,96,384]{2,1,0:T(8,128)(2,1)} %get-tuple-element.291), channel_id=1, source_target_pairs={{0,8},{4,12},{8,0},{12,4},{16,24},{20,28},{24,16},{28,20},{1,9},{5... | collective-permute-start | bytes 442376 | tf_op jit(solution)/shard_map/ppermute | solution.py:885
  159.4 10.2 %collective-permute-start.22 = (bf16[4,96,384]{2,1,0:T(8,128)(2,1)S(1)}, bf16[4,96,384]{2,1,0:T(8,128)(2,1)S(1)}, u32[]{:S(2)}, u32[]{:S(2)}) collective-permute-start(bf16[4,96,384]{2,1,0:T(8,128)(2,1)S(1)} %copy-done.40), channel_id=1, source_target_pairs={{0,8},{4,12},{8,0},{12,4},{16,24},{20,28},{24,16},{28,20},{1,9},{5... | collective-permute-start | bytes 884744 | tf_op jit(solution)/shard_map/ppermute | solution.py:885
  170.6 18.3 %collective-permute-start.24 = (f32[12,768]{1,0:T(8,128)S(1)}, f32[12,768]{1,0:T(8,128)S(1)}, u32[]{:S(2)}, u32[]{:S(2)}) collective-permute-start(f32[12,768]{1,0:T(8,128)S(1)} %pad_maximum_fusion.2), channel_id=1, source_target_pairs={{0,1},{1,0},{2,3},{3,2},{4,5},{5,4},{6,7},{7,6},{8,9},{9,8},{10,11... | collective-permute-start | bytes 110600 | tf_op jit(solution)/shard_map/ppermute | solution.py:882
  174.3 16.9 %collective-permute-start.26 = (bf16[5,96,384]{2,1,0:T(8,128)(2,1)}, bf16[5,96,384]{2,1,0:T(8,128)(2,1)S(1)}, u32[]{:S(2)}, u32[]{:S(2)}) collective-permute-start(bf16[5,96,384]{2,1,0:T(8,128)(2,1)} %get-tuple-element.323), channel_id=1, source_target_pairs={{0,8},{4,12},{8,0},{12,4},{16,24},{20,28},{24,16},{28,20},{1,9},{5... | collective-permute-start | bytes 1105928 | tf_op jit(solution)/shard_map/ppermute | solution.py:885
  175.9 13.0 %collective-permute-start.27 = (bf16[2,96,384]{2,1,0:T(8,128)(2,1)}, bf16[2,96,384]{2,1,0:T(8,128)(2,1)S(1)}, u32[]{:S(2)}, u32[]{:S(2)}) collective-permute-start(bf16[2,96,384]{2,1,0:T(8,128)(2,1)} %get-tuple-element.324), channel_id=1, source_target_pairs={{0,16},{4,20},{8,24},{12,28},{16,0},{20,4},{24,8},{28,12},{1,17},{... | collective-permute-start | bytes 442376 | tf_op jit(solution)/shard_map/ppermute | solution.py:885
  179.0 9.9 %collective-permute-start.28 = (bf16[2,96,384]{2,1,0:T(8,128)(2,1)}, bf16[2,96,384]{2,1,0:T(8,128)(2,1)S(1)}, u32[]{:S(2)}, u32[]{:S(2)}) collective-permute-start(bf16[2,96,384]{2,1,0:T(8,128)(2,1)} %get-tuple-element.325), channel_id=1, source_target_pairs={{0,4},{4,0},{8,12},{12,8},{16,20},{20,16},{24,28},{28,24},{1,5},{5... | collective-permute-start | bytes 442376 | tf_op jit(solution)/shard_map/ppermute | solution.py:885
  180.4 10.8 %collective-permute-start.25 = (bf16[4,96,384]{2,1,0:T(8,128)(2,1)S(1)}, bf16[4,96,384]{2,1,0:T(8,128)(2,1)S(1)}, u32[]{:S(2)}, u32[]{:S(2)}) collective-permute-start(bf16[4,96,384]{2,1,0:T(8,128)(2,1)S(1)} %copy-done.39), channel_id=1, source_target_pairs={{0,4},{4,0},{8,12},{12,8},{16,20},{20,16},{24,28},{28,24},{1,5},{5... | collective-permute-start | bytes 884744 | tf_op jit(solution)/shard_map/ppermute | solution.py:885
  191.2 21.5 %collective-permute-start.29 = (f32[2,256,768]{2,1,0:T(8,128)}, f32[2,256,768]{2,1,0:T(8,128)}, u32[]{:S(2)}, u32[]{:S(2)}) collective-permute-start(f32[2,256,768]{2,1,0:T(8,128)} %get-tuple-element.327), channel_id=1, source_target_pairs={{0,1},{1,0},{2,3},{3,2},{4,5},{5,4},{6,7},{7,6},{8,9},{9,8},{10,11... | collective-permute-start | bytes 4718600 | tf_op jit(solution)/shard_map/ppermute | solution.py:882
  191.3 35.2 %collective-permute-start.38 = (bf16[1,96,384]{2,1,0:T(8,128)(2,1)S(1)}, bf16[1,96,384]{2,1,0:T(8,128)(2,1)S(1)}, u32[]{:S(2)}, u32[]{:S(2)}) collective-permute-start(bf16[1,96,384]{2,1,0:T(8,128)(2,1)S(1)} %copy-done.54), channel_id=1, source_target_pairs={{0,16},{4,20},{8,24},{12,28},{16,0},{20,4},{24,8},{28,12},{1,17},{... | collective-permute-start | bytes 221192 | tf_op jit(solution)/shard_map/ppermute | solution.py:885
  196.0 5.8 %collective-permute-start.43 = (bf16[96,192]{1,0:T(8,128)(2,1)S(1)}, bf16[96,192]{1,0:T(8,128)(2,1)S(1)}, u32[]{:S(2)}, u32[]{:S(2)}) collective-permute-start(bf16[96,192]{1,0:T(8,128)(2,1)S(1)} %slice.143), channel_id=1, source_target_pairs={{0,16},{4,20},{8,24},{12,28},{16,0},{20,4},{24,8},{28,12},{1,17},{... | collective-permute-start | bytes 110600 | tf_op jit(solution)/shard_map/ppermute | solution.py:885
  198.3 5.6 %collective-permute-start.30 = (f32[12,768]{1,0:T(8,128)S(1)}, f32[12,768]{1,0:T(8,128)S(1)}, u32[]{:S(2)}, u32[]{:S(2)}) collective-permute-start(f32[12,768]{1,0:T(8,128)S(1)} %fusion.14), channel_id=1, source_target_pairs={{0,2},{1,3},{2,0},{3,1},{4,6},{5,7},{6,4},{7,5},{8,10},{9,11},{10,... | collective-permute-start | bytes 110600 | tf_op jit(solution)/shard_map/ppermute | solution.py:882
  198.8 7.4 %collective-permute-start.31 = (bf16[2,96,384]{2,1,0:T(8,128)(2,1)}, bf16[2,96,384]{2,1,0:T(8,128)(2,1)S(1)}, u32[]{:S(2)}, u32[]{:S(2)}) collective-permute-start(bf16[2,96,384]{2,1,0:T(8,128)(2,1)} %get-tuple-element.337), channel_id=1, source_target_pairs={{0,8},{4,12},{8,0},{12,4},{16,24},{20,28},{24,16},{28,20},{1,9},{5... | collective-permute-start | bytes 442376 | tf_op jit(solution)/shard_map/ppermute | solution.py:885
  201.7 11.0 %collective-permute-start.32 = (bf16[2,96,384]{2,1,0:T(8,128)(2,1)}, bf16[2,96,384]{2,1,0:T(8,128)(2,1)S(1)}, u32[]{:S(2)}, u32[]{:S(2)}) collective-permute-start(bf16[2,96,384]{2,1,0:T(8,128)(2,1)} %get-tuple-element.338), channel_id=1, source_target_pairs={{0,16},{4,20},{8,24},{12,28},{16,0},{20,4},{24,8},{28,12},{1,17},{... | collective-permute-start | bytes 442376 | tf_op jit(solution)/shard_map/ppermute | solution.py:885
  203.9 19.1 %collective-permute-start.34 = (bf16[1,96,384]{2,1,0:T(8,128)(2,1)}, bf16[1,96,384]{2,1,0:T(8,128)(2,1)S(1)}, u32[]{:S(2)}, u32[]{:S(2)}) collective-permute-start(bf16[1,96,384]{2,1,0:T(8,128)(2,1)} %get-tuple-element.345), channel_id=1, source_target_pairs={{0,16},{4,20},{8,24},{12,28},{16,0},{20,4},{24,8},{28,12},{1,17},{... | collective-permute-start | bytes 221192 | tf_op jit(solution)/shard_map/ppermute | solution.py:885
  214.6 10.6 %collective-permute-start.37 = (bf16[256,768]{1,0:T(8,128)(2,1)S(1)}, bf16[256,768]{1,0:T(8,128)(2,1)S(1)}, u32[]{:S(2)}, u32[]{:S(2)}) collective-permute-start(bf16[256,768]{1,0:T(8,128)(2,1)S(1)} %fusion.1), channel_id=1, source_target_pairs={{0,2},{1,3},{2,0},{3,1},{4,6},{5,7},{6,4},{7,5},{8,10},{9,11},{10,... | collective-permute-start | bytes 1179656 | tf_op jit(solution)/shard_map/ppermute | solution.py:882
  215.4 4.1 %collective-permute-start.35 = (f32[12,768]{1,0:T(8,128)S(1)}, f32[12,768]{1,0:T(8,128)S(1)}, u32[]{:S(2)}, u32[]{:S(2)}) collective-permute-start(f32[12,768]{1,0:T(8,128)S(1)} %add.92), channel_id=1, source_target_pairs={{0,4},{4,0},{8,12},{12,8},{16,20},{20,16},{24,28},{28,24},{1,5},{5... | collective-permute-start | bytes 110600 | tf_op jit(solution)/shard_map/ppermute | solution.py:885
  219.3 5.9 %collective-permute-start.33 = (bf16[1,96,384]{2,1,0:T(8,128)(2,1)}, bf16[1,96,384]{2,1,0:T(8,128)(2,1)S(1)}, u32[]{:S(2)}, u32[]{:S(2)}) collective-permute-start(bf16[1,96,384]{2,1,0:T(8,128)(2,1)} %get-tuple-element.344), channel_id=1, source_target_pairs={{0,16},{4,20},{8,24},{12,28},{16,0},{20,4},{24,8},{28,12},{1,17},{... | collective-permute-start | bytes 221192 | tf_op jit(solution)/shard_map/ppermute | solution.py:885
  219.4 5.7 %collective-permute-start.36 = (f32[12,768]{1,0:T(8,128)S(1)}, f32[12,768]{1,0:T(8,128)S(1)}, u32[]{:S(2)}, u32[]{:S(2)}) collective-permute-start(f32[12,768]{1,0:T(8,128)S(1)} %add.93), channel_id=1, source_target_pairs={{0,8},{4,12},{8,0},{12,4},{16,24},{20,28},{24,16},{28,20},{1,9},{5... | collective-permute-start | bytes 110600 | tf_op jit(solution)/shard_map/ppermute | solution.py:885
  225.2 8.4 %collective-permute-start.42 = (f32[12,768]{1,0:T(8,128)S(1)}, f32[12,768]{1,0:T(8,128)S(1)}, u32[]{:S(2)}, u32[]{:S(2)}) collective-permute-start(f32[12,768]{1,0:T(8,128)S(1)} %add.95), channel_id=1, source_target_pairs={{0,16},{4,20},{8,24},{12,28},{16,0},{20,4},{24,8},{28,12},{1,17},{... | collective-permute-start | bytes 110600 | tf_op jit(solution)/shard_map/ppermute | solution.py:885
  230.3 4.6 %collective-permute-start.39 = (bf16[2,96,192]{2,1,0:T(8,128)(2,1)}, bf16[2,96,192]{2,1,0:T(8,128)(2,1)S(1)}, u32[]{:S(2)}, u32[]{:S(2)}) collective-permute-start(bf16[2,96,192]{2,1,0:T(8,128)(2,1)} %get-tuple-element.355), channel_id=1, source_target_pairs={{0,1},{1,0},{2,3},{3,2},{4,5},{5,4},{6,7},{7,6},{8,9},{9,8},{10,11... | collective-permute-start | bytes 221192 | tf_op jit(solution)/shard_map/ppermute | solution.py:882
  230.3 5.8 %collective-permute-start.40 = (bf16[2,96,192]{2,1,0:T(8,128)(2,1)}, bf16[2,96,192]{2,1,0:T(8,128)(2,1)S(1)}, u32[]{:S(2)}, u32[]{:S(2)}) collective-permute-start(bf16[2,96,192]{2,1,0:T(8,128)(2,1)} %get-tuple-element.356), channel_id=1, source_target_pairs={{0,2},{1,3},{2,0},{3,1},{4,6},{5,7},{6,4},{7,5},{8,10},{9,11},{10,... | collective-permute-start | bytes 221192 | tf_op jit(solution)/shard_map/ppermute | solution.py:882
  231.6 5.8 %collective-permute-start.41 = (bf16[2,96,192]{2,1,0:T(8,128)(2,1)}, bf16[2,96,192]{2,1,0:T(8,128)(2,1)S(1)}, u32[]{:S(2)}, u32[]{:S(2)}) collective-permute-start(bf16[2,96,192]{2,1,0:T(8,128)(2,1)} %get-tuple-element.357), channel_id=1, source_target_pairs={{0,3},{1,2},{2,1},{3,0},{4,7},{5,6},{6,5},{7,4},{8,11},{9,10},{10,... | collective-permute-start | bytes 221192 | tf_op jit(solution)/shard_map/ppermute | solution.py:882
  (54 other events, 342.0 us)

commit v2 on v1

--- a/solution.py
+++ b/solution.py
@@ -15,8 +15,8 @@
 PAIR = 2 * DH
 SCALE = DH**-0.5
 BLOCK = 128
-SIZES = (2, 3, 4, 5, 6, 8)
-VMEM = 60
+SIZES = (2, 3, 5, 6, 8)
+VMEM = 18
 ROOT_HALF = 0.5**0.5
 ROOT_TWO_PI = 0.3989422804014327
 
@@ -37,12 +37,20 @@
     return pltpu.CompilerParams(vmem_limit_bytes=mib << 20, dimension_semantics=("arbitrary",))
 
 
+def waiting(after):
+    return [pl.BlockSpec(memory_space=pl.ANY)] * len(after)
+
+
+def ordered(kernel, after):
+    return lambda info, *refs: kernel(info, *refs[len(after) :])
+
+
 def full(shape):
     return pl.BlockSpec(shape, lambda *_: (0,) * len(shape))
 
 
 def cost(micros):
-    return pl.CostEstimate(flops=int(micros * 1.15e9), transcendentals=0, bytes_accessed=0)
+    return pl.CostEstimate(flops=int(micros * 0.6e9), transcendentals=0, bytes_accessed=0)
 
 
 def column_sum(values):
@@ -82,8 +90,10 @@
             keep[index] = value
 
 
-def join_kernel(segments, routes, *refs):
-    ins, outs = refs[: 2 * len(segments)], list(refs[2 * len(segments) :])
+def join_kernel(skip, segments, routes, *refs):
+    refs = refs[skip:]
+    ins, outs = refs[: 2 * len(segments)], list(refs[2 * len(segments) : -1])
+    refs[-1][...] = jnp.zeros_like(refs[-1])
     for route in routes:
         send = outs.pop(0) if any(segments[m][n] > 1 for m, n in route) else None
         keep = outs.pop(0)
@@ -100,7 +110,7 @@
             filled += size
 
 
-def join(messages, routes):
+def join(messages, routes, after):
     segments = [list(message[0]) for message in messages]
     tail = messages[0][1].shape[1:]
     shapes, results = [], []
@@ -112,18 +122,18 @@
             shapes.append(shaped((sum(left),) + tail, LOW))
         shapes.append(shaped((sum(max(size // 2, 1) for size in sizes),) + tail, F32))
     operands = [array for message in messages for array in message[1:]]
-    arrays = pl.pallas_call(
-        functools.partial(join_kernel, segments, routes),
+    shapes.append(shaped((8, 128), F32))
+    *arrays, token = pl.pallas_call(
+        functools.partial(join_kernel, len(after), segments, routes),
         grid=(1,),
-        in_specs=[full(array.shape) for array in operands],
+        in_specs=waiting(after) + [full(array.shape) for array in operands],
         out_specs=[full(shape.shape) for shape in shapes],
         out_shape=shapes,
         compiler_params=params(VMEM),
         cost_estimate=cost(1),
         name="join",
-    )(*operands)
-    arrays = list(arrays)
-    return [(left, arrays.pop(0) if left else None, arrays.pop(0)) for left in results]
+    )(*after, *operands)
+    return [(left, arrays.pop(0) if left else None, arrays.pop(0)) for left in results], token
 
 
 def each_window(info, block, run):
@@ -318,7 +328,7 @@
     put_rows(grad, w_rows, me, 0, order, w_send, w_keep)
 
 
-def attend_backward(info, n, query, key, value, parts, context, lse, seg, x_t):
+def attend_backward(info, n, query, key, value, parts, context, lse, seg, x_t, after):
     tokens, half = query.shape
     quarter, blocks, width = tokens // 4, tokens // BLOCK, x_t.shape[0]
     col = pl.BlockSpec((tokens, PAIR), lambda p, i: (0, n))
@@ -332,11 +342,12 @@
     ]
     weight = (4, width // 8, 3 * PAIR)
     return pl.pallas_call(
-        functools.partial(backward_kernel, QKV_ORDERS[n]),
+        ordered(functools.partial(backward_kernel, QKV_ORDERS[n]), after),
         grid_spec=pltpu.PrefetchScalarGridSpec(
             num_scalar_prefetch=1,
             grid=(1,),
-            in_specs=[col] * 3
+            in_specs=waiting(after)
+            + [col] * 3
             + [part, low, high, first, part]
             + [pl.BlockSpec((PAIR, tokens), lambda p, i: (n, 0))]
             + [pl.BlockSpec((1, blocks, 2 * BLOCK), lambda p, i: (n, 0, 0))]
@@ -357,7 +368,7 @@
         compiler_params=params(VMEM),
         cost_estimate=cost(8),
         name="attend_backward",
-    )(info, query, key, value, *parts, context, lse, seg, x_t)
+    )(info, *after, query, key, value, *parts, context, lse, seg, x_t)
 
 
 def normalise(values):
@@ -440,7 +451,24 @@
         store_columns(place, back.astype(LOW).T, mine, send)
 
 
-def middle_forward(info, parts, inputs, cotangent, wo, bo, g1, s1, up, bup, down, bdown, g2, s2):
+def mark_kernel(*refs):
+    refs[-1][...] = jnp.zeros_like(refs[-1])
+
+
+def mark(*after):
+    return pl.pallas_call(
+        mark_kernel,
+        grid=(1,),
+        in_specs=waiting(after),
+        out_specs=full((8, 128)),
+        out_shape=shaped((8, 128), F32),
+        compiler_params=params(VMEM),
+        cost_estimate=cost(1),
+        name="mark",
+    )(*after)
+
+
+def middle_forward(after, info, parts, inputs, cotangent, wo, bo, g1, s1, up, bup, down, bdown, g2, s2):
     quarter, half = parts[0].shape
     width, inner = 2 * half, up.shape[1]
     count, steps = 2 * quarter, 4
@@ -449,11 +477,12 @@
     tokens = full((count, width))
     turned = full((2, width // 4, count))
     return pl.pallas_call(
-        middle_forward_kernel,
+        ordered(middle_forward_kernel, after),
         grid_spec=pltpu.PrefetchScalarGridSpec(
             num_scalar_prefetch=1,
             grid=(steps,),
-            in_specs=[full((quarter, half))] * 4
+            in_specs=waiting(after)
+            + [full((quarter, half))] * 4
             + [full((2, quarter, width))] * 2
             + [full((width, width)), vector, vector, vector]
             + [
@@ -488,7 +517,7 @@
         cost_estimate=cost(18),
         name="middle_forward",
     )(
-        info, *parts, inputs, cotangent, wo, bo[None], g1[None], s1[None],
+        info, *after, *parts, inputs, cotangent, wo, bo[None], g1[None], s1[None],
         up, bup[None], down, bdown[None], g2[None], s2[None],
     )
 
@@ -614,24 +643,24 @@
             put(grad[start : start + size], rel, flip, order, outs[2 * n], outs[2 * n + 1])
 
 
-def down_grad(info, mine, theirs, act, act_pair):
+def down_grad(info, mine, theirs, act, act_pair, after):
     _, size, count = mine.shape
     block = act.shape[1] // 8
     part = (8, size // 2, block)
     spec = pl.BlockSpec((count, block), lambda r, i: (0, r ^ i[3]))
     return pl.pallas_call(
-        down_kernel,
+        ordered(down_kernel, after),
         grid_spec=pltpu.PrefetchScalarGridSpec(
             num_scalar_prefetch=1,
             grid=(8,),
-            in_specs=[full(mine.shape), full(theirs.shape), spec, spec],
+            in_specs=waiting(after) + [full(mine.shape), full(theirs.shape), spec, spec],
             out_specs=[full(part)] * 4,
         ),
         out_shape=[shaped(part, LOW), shaped(part, F32)] * 2,
         compiler_params=params(VMEM),
         cost_estimate=cost(8),
         name="down_grad",
-    )(info, mine, theirs, act, act_pair)
+    )(info, *after, mine, theirs, act, act_pair)
 
 
 UP_ORDERS = ("xyzw", "yxzw")
@@ -672,7 +701,7 @@
                     keep_b[index] = value
 
 
-def up_grad(info, left, left_pair, mine, from_core, mine_d):
+def up_grad(info, left, left_pair, mine, from_core, mine_d, after):
     _, width, count = left.shape
     half = width // 2
 
@@ -683,11 +712,12 @@
         shaped((lead, width // 8, half), dtype) for lead in (8, 12) for dtype in (LOW, F32)
     ]
     return pl.pallas_call(
-        up_kernel,
+        ordered(up_kernel, after),
         grid_spec=pltpu.PrefetchScalarGridSpec(
             num_scalar_prefetch=1,
             grid=(5,),
-            in_specs=[full(left.shape)] * 2
+            in_specs=waiting(after)
+            + [full(left.shape)] * 2
             + [
                 pl.BlockSpec((1, count, half), lambda s, i: (at(s) // 2, 0, at(s) % 2)),
                 pl.BlockSpec((count, half), lambda s, i: (1 + at(s) // 2, at(s) % 2)),
@@ -701,7 +731,7 @@
         compiler_params=params(VMEM),
         cost_estimate=cost(10),
         name="up_grad",
-    )(info, left, left_pair, mine, from_core, mine_d, from_core)
+    )(info, *after, left, left_pair, mine, from_core, mine_d, from_core)
 
 
 def input_kernel(info, *refs):
@@ -721,7 +751,7 @@
         keep[0] = total
 
 
-def input_part(info, grads, qkv_weight):
+def input_part(info, grads, qkv_weight, after):
     tokens = grads[0].shape[0]
     width = qkv_weight.shape[0]
     quarter, half = tokens // 4, width // 2
@@ -732,11 +762,11 @@
         return pl.BlockSpec((width, half), lambda c, i: (0, 2 * t + i[1]))
 
     return pl.pallas_call(
-        input_kernel,
+        ordered(input_kernel, after),
         grid_spec=pltpu.PrefetchScalarGridSpec(
             num_scalar_prefetch=1,
             grid=(4,),
-            in_specs=[rows] * 9 + [weight(0), weight(1), weight(2)],
+            in_specs=waiting(after) + [rows] * 9 + [weight(0), weight(1), weight(2)],
             out_specs=[
                 pl.BlockSpec((1, quarter, width), lambda c, i: (jnp.maximum(c - 2, 0), 0, 0)),
                 pl.BlockSpec((1, quarter, width), lambda c, i: (jnp.minimum(c, 1), 0, 0)),
@@ -746,7 +776,7 @@
         compiler_params=params(VMEM),
         cost_estimate=cost(6),
         name="input_part",
-    )(info, *grads, qkv_weight, qkv_weight, qkv_weight)
+    )(info, *after, *grads, qkv_weight, qkv_weight, qkv_weight)
 
 
 UNITS = (((0, 1), (2, 3), (4,), (5,)), ((0,), (1,), (2, 3), (4, 5)))
@@ -901,16 +931,11 @@
             for order, segments, sent, kept in messages
         ]
 
-    def land(products, flights, *routes):
-        count = len(products)
-        tied = tie(*products, *[flight[3] for flight in flights])
-        landed = [flight[1:3] + (got,) for flight, got in zip(flights, tied[count:])]
-        made = join(landed, [route[1:] for route in routes])
-        return list(tied[:count]), [(route[0],) + new for route, new in zip(routes, made)]
-
-    def follow(array, messages):
-        array, *kept = tie(array, *[message[3] for message in messages])
-        return [array] + [message[:3] + (own,) for message, own in zip(messages, kept)]
+    def land(after, flights, *routes):
+        made, token = join(
+            [flight[1:] for flight in flights], [route[1:] for route in routes], after
+        )
+        return [(route[0],) + new for route, new in zip(routes, made)], token
 
     def finish(grad):
         if fine > 1:
@@ -931,61 +956,59 @@
     )
     parts = [parts[0]] + [over_seq(parts[j], j) for j in (1, 2, 3)]
     x_t = turn(info, quarters)
-    parts[0], x_t = tie(parts[0], x_t)
 
     outputs, d_res, n1, r1, turned, act, slope, mine, send, vec_two = middle_forward(
-        info, parts, inputs, cotangent, out_weight, out_bias, norm1_gain, norm1_shift,
+        [x_t], info, parts, inputs, cotangent, out_weight, out_bias, norm1_gain, norm1_shift,
         up_weight, up_bias, down_weight, down_bias, norm2_gain, norm2_shift,
     )
     pair = over_seq(turned, 1), over_seq(act, 1), over_seq(send, 1)
     back = middle_backward(
         info, d_res, slope, down_weight, up_weight, out_weight, n1, r1, norm1_gain
     )
-    turned_pair, act_pair, theirs, *back = tie(*pair, *back)
+    turned_pair, act_pair, theirs = pair
     to_core, mine_pre, d_up_bias, d_summed, q0, to_chip, mine_d, vec_one = back
-    mine, d_summed = tie(mine, d_summed)
-
+
+    token = mark(turned_pair, act_pair, theirs, vec_one)
+    to_core, to_chip, token = tie(to_core, to_chip, token)
     from_core, from_chip = over_seq(to_core, 1), over_seq(to_chip, 2)
-    made = down_grad(info, mine, theirs, act, act_pair)
-    from_core, from_chip, *made = tie(from_core, from_chip, *made)
+    made = down_grad(info, mine, theirs, act, act_pair, [token])
     downs = launch(
         (DOWN_ORDERS[0], [8], made[0], made[1]), (DOWN_ORDERS[1], [8], made[2], made[3])
     )
     across = over_seq(from_chip[1], 1)
-    made = up_grad(info, turned, turned_pair, mine_pre, from_core, mine_d)
-    across, *made = tie(across, *made)
+    made = up_grad(info, turned, turned_pair, mine_pre, from_core, mine_d, [made[1]])
     ups = launch((UP_ORDERS[0], [8], made[0], made[1]), (UP_ORDERS[1], [8, 4], made[2], made[3]))
     d_parts = (q0, from_core, from_core, from_chip, across)
 
-    def piece(n, query):
+    def piece(n, after):
         made = attend_backward(
-            info, n, query, key, value, d_parts, context, lse, segment, x_t
+            info, n, query, key, value, d_parts, context, lse, segment, x_t, after
         )
-        return made
-
-    def opening(n, made):
-        return QKV_ORDERS[n], [4], made[4], made[5]
-
-    zero = piece(0, query)
-    zero, downs = land(zero, downs, (DOWN_ORDERS[0][1:], (0, 0)), (DOWN_ORDERS[1][1:], (1, 0)))
-    query, *downs = follow(query, downs)
-    *downs, first = launch(*downs, opening(0, zero))
-
-    one = piece(1, query)
-    one, (up_a, up_b, down, first) = land(
-        one,
+        return list(made)
+
+    def opening(n, made, token):
+        return QKV_ORDERS[n], [4], tie(made[4], token)[0], made[5]
+
+    zero = piece(0, [made[1]])
+    downs, token = land(
+        zero[3:4], downs, (DOWN_ORDERS[0][1:], (0, 0)), (DOWN_ORDERS[1][1:], (1, 0))
+    )
+    *downs, first = launch(*downs, opening(0, zero, token))
+
+    one = piece(1, [token])
+    (up_a, up_b, down, first), token = land(
+        one[3:4],
         ups + downs + [first],
         (UP_ORDERS[0][1:], (0, 0)),
         (UP_ORDERS[1][1:], (1, 0), (1, 1)),
         ("yw", (2, 0), (3, 0)),
         (QKV_ORDERS[0][1:], (4, 0)),
     )
-    query, up_a, up_b, down, first = follow(query, [up_a, up_b, down, first])
-    flights = launch(up_a, up_b, down, opening(1, one), first)
-
-    two = piece(2, query)
-    two, (up, down, second, first) = land(
-        two,
+    flights = launch(up_a, up_b, down, opening(1, one, token), first)
+
+    two = piece(2, [token])
+    (up, down, second, first), token = land(
+        two[3:4],
         flights,
         ("zw", (0, 0), (1, 0), (1, 1)),
         ("w", (2, 0), (2, 1)),
@@ -993,9 +1016,8 @@
         ("w", (4, 0)),
     )
     grads = [*zero[:3], *one[:3], *two[:3]]
-    grads[0], up, down, second, first = follow(grads[0], [up, down, second, first])
-    flights = launch(opening(2, two), up, down, second)
-    bias_part = jnp.concatenate([zero[3], one[3], two[3]], axis=1)
+    flights = launch(opening(2, two, token), up, down, second)
+    bias_part = jnp.concatenate([zero[3], one[3], tie(two[3], token)[0]], axis=1)
     bias_zero = jnp.zeros_like(bias_part)
     bias_part = jnp.where(
         core == 0,
@@ -1005,9 +1027,9 @@
     vectors = jnp.concatenate([vec_one[:3], vec_two[:3], d_up_bias.reshape(-1, width), bias_part])
     vectors_got = over_seq(vectors, 1)
 
-    keep, send = input_part(info, grads, qkv_weight)
-    (keep, send, vectors_got), (third, up, down, second) = land(
-        [keep, send, vectors_got],
+    keep, send = input_part(info, grads, qkv_weight, [token])
+    (third, up, down, second), token = land(
+        [keep],
         flights,
         (QKV_ORDERS[2][1:], (0, 0)),
         ("w", (1, 0), (1, 1), (1, 2)),
@@ -1016,28 +1038,31 @@
     )
     out_total, down_total = up[3][2], down[3]
     third, up, first = launch(third, up, first)
+    send, vectors_got, token = tie(send, vectors_got, token)
     vectors = vectors + vectors_got
     vectors_got = over_seq(vectors, 2)
     d_row_got = over_seq(send, 1)
-    first_got, (d_row_got, vectors_got), (third, up) = first[3], *land(
-        [d_row_got, vectors_got], [third, up], ("w", (0, 0)), ("", (1, 0), (1, 1))
-    )
+    (third, up), token = land([token], [third, up], ("w", (0, 0)), ("", (1, 0), (1, 1)))
     up_total = up[3]
+    d_row_got, vectors_got, second_sent, out_total, token = tie(
+        d_row_got, vectors_got, second[2], out_total, token
+    )
+    third, second = launch(third, second[:2] + (second_sent, second[3]))
+    wide = half // 2
+    out_got = swap(out_total[:, wide:].astype(LOW), "w")
     vectors = vectors + vectors_got
-    third, second = launch(third, second)
     vectors = vectors + swap(vectors, "y")
     vectors_got = swap(vectors, "z")
     d_row = keep + d_row_got
     d_far = over_seq(d_row[1].astype(LOW), 2)
-    third_got, second_got, vectors_got, d_far = tie(third[3], second[3], vectors_got, d_far)
+    third_got, vectors_got, d_far, out_got = tie(third[3], vectors_got, d_far, out_got)
     own, *others = share(
-        info, (first[2], second[2], third[2]), (first_got, second_got, third_got)
+        info, (first[2], second[2], third[2]), (first[3], second[3], third_got)
     )
     qkv_total = gather(info, own, *[over_seq(other, 1 + j) for j, other in enumerate(others)])
     qkv_total = finish(qkv_total)
     vectors = vectors + vectors_got
-    wide = half // 2
-    out_total = out_total[:, :wide] + swap(out_total[:, wide:].astype(LOW), "w").astype(F32)
+    out_total = out_total[:, :wide] + out_got.astype(F32)
     out_total = finish(out_total)
     down_total = finish(down_total.reshape(wide, half).T)
     up_total = finish(jnp.concatenate([up_total[0], up_total[1]], axis=1))

time: 242 us -> 207 us (0.86)
  Pallas kernels: 144 us -> 95.7 us
  waiting for transfers between devices: 26.6 us -> 42 us
    pallas_call x12 -> x13, Pallas kernels: 94.9 us -> 59.1 us  [the longest x3 24.7 us: attend_backward(): pl.pallas_call(ordered(functools.partial(backward_kernel, QKV_ORDERS[n]),...]
    ppermute x23, waiting for transfers between devices: 12.8 us -> 23.7 us  [over_seq(): return lax.ppermute(array, 'seq', [(i, i ^ flip) for i in range(seq_size)])]
    pallas_call x1, Pallas kernels: 16.7 us -> 11.8 us  [middle_backward(): pl.pallas_call(middle_backward_kernel, grid_spec=pltpu.PrefetchScalarGrid...]
    ppermute x21, waiting for transfers between devices: 13.7 us -> 18.3 us  [over_batch(): lax.ppermute(array, 'batch', [(i, i ^ flip) for i in range(batch_size)])]
    unnamed x116 -> x108, local copies, waits for them, and re-layouts: 8.64 us -> 11.5 us
    pallas_call x1, Pallas kernels: 3.67 us -> 1.03 us  [turn(): pl.pallas_call(turn_kernel, grid_spec=pltpu.PrefetchScalarGridSpec(num_sc...]
  transfers between devices with their start and end apart: 44 -> 44, of which waited for: 10 -> 16; matrix products, arithmetic and copies ran while one was open for 6% -> 6% of each run, Pallas kernels for 40% -> 29%
where the time goes in v2:
time: 207 us
  Pallas kernels  95.7 us (46%)
  starting transfers between devices  42.2 us (20%)
  waiting for transfers between devices  42 us (20%)
  local copies, waits for them, and re-layouts  18.4 us (9%)
  other arithmetic  6.73 us (3%)
    ppermute x21, starting transfers between devices, over_batch(): lax.ppermute(array, 'batch', [(i, i ^ flip) for i in range(batch_size)])  29 us
    pallas_call x3, Pallas kernels, attend_backward(): pl.pallas_call(ordered(functools.partial(backward_kernel, QKV_ORDERS[n]),...  24.7 us
    ppermute x23, waiting for transfers between devices, over_seq(): return lax.ppermute(array, 'seq', [(i, i ^ flip) for i in range(seq_size)])  23.7 us
    pallas_call x1, Pallas kernels, attend_forward(): pl.pallas_call(forward_kernel, grid_spec=pltpu.PrefetchScalarGridSpec(num...  21.5 us
    ppermute x21, waiting for transfers between devices, over_batch(): lax.ppermute(array, 'batch', [(i, i ^ flip) for i in range(batch_size)])  18.3 us
    ppermute x23, starting transfers between devices, over_seq(): return lax.ppermute(array, 'seq', [(i, i ^ flip) for i in range(seq_size)])  13.2 us
    pallas_call x1, Pallas kernels, middle_forward(): pl.pallas_call(ordered(middle_forward_kernel, after), grid_spec=pltpu.Pre...  12.6 us
    pallas_call x1, Pallas kernels, middle_backward(): pl.pallas_call(middle_backward_kernel, grid_spec=pltpu.PrefetchScalarGrid...  11.8 us
  transfers between devices with their start and end apart: 44, of which 16 were waited for; matrix products, arithmetic and copies ran while one was open for 6% of the time, Pallas kernels for 29%

profile of v2, /device:TPU:0, one launch (start us, length us, event | category | flops | bytes accessed | tf_op | source)
XLA Modules:
  0.0 206.5 jit_solution(1026694234827346471)
XLA Ops:
  0.7 1.2 dynamic-slice_bitcast_fusion
  1.9 3.0 %collective-permute-start.1 = (bf16[256,768]{1,0:T(8,128)(2,1)S(1)}, bf16[256,768]{1,0:T(8,128)(2,1)S(1)}, u32[]{:S(2)}, u32[]{:S(2)}) collective-permute-start(bf16[256,768]{1,0:T(8,128)(2,1)S(1)} %get-tuple-element.253), channel_id=1, source_target_pairs={{0,2},{1,3},{2,0},{3,1},{4,6},{5,7},{6,4},{7,5},{8,10},{9,11},{10,... | collective-permute-start | bytes 1179656 | tf_op jit(solution)/shard_map/ppermute | solution.py:912
  4.9 9.1 %collective-permute-done.1.x2 = bf16[256,768]{1,0:T(8,128)(2,1)S(1)} collective-permute-done((bf16[256,768]{1,0:T(8,128)(2,1)S(1)}, bf16[256,768]{1,0:T(8,128)(2,1)S(1)}, u32[]{:S(2)}, u32[]{:S(2)}) %collective-permute-start.1) | collective-permute-done | bytes 393248 | tf_op jit(solution)/shard_map/ppermute | solution.py:912
  14.6 1.1 collective-permute-done.2.x3
  15.7 2.0 copy-done.14
  17.8 21.5 %attend_forward.1 = (bf16[1024,384]{1,0:T(8,128)(2,1)S(1)}, bf16[1024,384]{1,0:T(8,128)(2,1)S(1)}, bf16[1024,384]{1,0:T(8,128)(2,1)S(1)}, bf16[256,384]{1,0:T(8,...) custom-call(s32[20]{0:T(128)S(1)} %concatenate.18.info, ...), custom_call_target="tpu_custom_call" | custom-call | flops 9600000000 | tf_op jit(solution)/shard_map/attend_forward/pallas_call | solution.py:247
  39.3 1.1 copy-done.23
  42.5 1.3 collective-permute-start.5
  45.1 4.7 %collective-permute-done.4.refs_3_ = bf16[256,384]{1,0:T(8,128)(2,1)S(1)} collective-permute-done((bf16[256,384]{1,0:T(8,128)(2,1)S(1)}, bf16[256,384]{1,0:T(8,128)(2,1)S(1)}, u32[]{:S(2)}, u32[]{:S(2)}) %collective-permute-start.4) | collective-permute-done | bytes 196640 | tf_op jit(solution)/shard_map/ppermute | solution.py:912
  49.8 3.1 %collective-permute-done.5.refs_4_ = bf16[256,384]{1,0:T(8,128)(2,1)S(1)} collective-permute-done((bf16[256,384]{1,0:T(8,128)(2,1)S(1)}, bf16[256,384]{1,0:T(8,128)(2,1)S(1)}, u32[]{:S(2)}, u32[]{:S(2)}) %collective-permute-start.5) | collective-permute-done | bytes 196640 | tf_op jit(solution)/shard_map/ppermute | solution.py:912
  52.9 12.6 %middle_forward.1 = (bf16[2,256,768]{2,1,0:T(8,128)(2,1)}, f32[512,768]{1,0:T(8,128)S(1)}, f32[512,768]{1,0:T(8,128)S(1)}, f32[512,1]{1,0:T(8,128)S(1)}, bf16[2,...) custom-call(s32[20]{0:T(128)S(1)} %concatenate.18.info, ...), custom_call_target="tpu_custom_call" | custom-call | flops 10800000000 | tf_op jit(solution)/shard_map/middle_forward/pallas_call | solution.py:479
  67.2 11.8 %middle_backward.1 = (bf16[1536,768]{1,0:T(8,128)(2,1)}, bf16[2,512,768]{2,1,0:T(8,128)(2,1)S(1)}, f32[1,3072]{1,0:T(1,128)S(1)}, f32[512,768]{1,0:T(8,128)S(1)}...) custom-call(s32[20]{0:T(128)S(1)} %concatenate.18.info, ...), custom_call_target="tpu_custom_call" | custom-call | flops 9600000000 | tf_op jit(solution)/shard_map/middle_backward/pallas_call | solution.py:590
  79.0 1.1 copy-done.31
  80.3 1.1 copy-done.2
  82.3 1.3 slice.75
  84.2 2.0 reduce.23
  86.1 1.3 reshape.40
  88.6 1.9 copy-done.17
  91.5 6.2 %down_grad.1 = (bf16[8,96,384]{2,1,0:T(8,128)(2,1)S(1)}, f32[8,96,384]{2,1,0:T(8,128)S(1)}, bf16[8,96,384]{2,1,0:T(8,128)(2,1)S(1)}, f32[8,96,384]{2,1,0:T(8,128)S(1)}) custom-call(s32[20]{0:T(128)S(1)} %concatenate.18.info, f32[8,128]{1,0:T(8,128)S(1)} %mark.1.refs_0_, bf16[2,192,512]{2,1,0:T(8,128)(2,1)S(1)} %copy-done.36, ...), custom_call_target="tpu_custom_call" | custom-call | flops 4800000000 | tf_op jit(solution)/shard_map/down_grad/pallas_call | solution.py:651
  97.8 2.9 %collective-permute-start.12 = (bf16[8,96,384]{2,1,0:T(8,128)(2,1)S(1)}, bf16[8,96,384]{2,1,0:T(8,128)(2,1)S(1)}, u32[]{:S(2)}, u32[]{:S(2)}) collective-permute-start(bf16[8,96,384]{2,1,0:T(8,128)(2,1)S(1)} %get-tuple-element.157), channel_id=1, source_target_pairs={{0,8},{4,12},{8,0},{12,4},{16,24},{20,28},{24,16},{28,20},{1,9},{5... | collective-permute-start | bytes 1769480 | tf_op jit(solution)/shard_map/ppermute | solution.py:915
  101.5 8.1 %up_grad.1 = (bf16[8,96,384]{2,1,0:T(8,128)(2,1)S(1)}, f32[8,96,384]{2,1,0:T(8,128)S(1)}, bf16[12,96,384]{2,1,0:T(8,128)(2,1)S(1)}, f32[12,96,384]{2,1,0:T(8,128)S(1)}) custom-call(s32[20]{0:T(128)S(1)} %concatenate.18.info, f32[8,96,384]{2,1,0:T(8,128)S(1)} %get-tuple-element.144.refs_0_.refs_1_, bf16[2,768,512]{2,1,0:T(8,128)(2,1)S(1)} %copy-done.19, ...), custom_call_target="tpu_custom_call" | custom-call | flops 6000000000 | tf_op jit(solution)/shard_map/up_grad/pallas_call | solution.py:714
  109.6 1.8 collective-permute-start.15
  112.2 8.2 %attend_backward.3 = (bf16[1024,128]{1,0:T(8,128)(2,1)S(1)}, bf16[1024,128]{1,0:T(8,128)(2,1)S(1)}, bf16[1024,128]{1,0:T(8,128)(2,1)S(1)}, f32[2,128]{1,0:T(2,12...) custom-call(s32[20]{0:T(128)S(1)} %concatenate.18.info, ...), custom_call_target="tpu_custom_call" | custom-call | flops 4800000000 | tf_op jit(solution)/shard_map/attend_backward/pallas_call | solution.py:344
  122.3 8.4 %attend_backward.4 = (bf16[1024,128]{1,0:T(8,128)(2,1)S(1)}, bf16[1024,128]{1,0:T(8,128)(2,1)S(1)}, bf16[1024,128]{1,0:T(8,128)(2,1)S(1)}, f32[2,128]{1,0:T(2,12...) custom-call(s32[20]{0:T(128)S(1)} %concatenate.18.info, f32[8,128]{1,0:T(8,128)S(1)} %get-tuple-element.160.refs_0_, ...), custom_call_target="tpu_custom_call" | custom-call | flops 4800000000 | tf_op jit(solution)/shard_map/attend_backward/pallas_call | solution.py:344
  130.7 7.3 %collective-permute-done.18.refs_10_ = bf16[4,96,384]{2,1,0:T(8,128)(2,1)S(1)} collective-permute-done((bf16[4,96,384]{2,1,0:T(8,128)(2,1)S(1)}, bf16[4,96,384]{2,1,0:T(8,128)(2,1)S(1)}, u32[]{:S(2)}, u32[]{:S(2)}) %collective-permute-start.18) | collective-permute-done | bytes 294944 | tf_op jit(solution)/shard_map/ppermute | solution.py:915
  138.8 1.6 collective-permute-start.20
  142.4 1.7 collective-permute-start.23
  144.1 8.1 %attend_backward.5 = (bf16[1024,128]{1,0:T(8,128)(2,1)S(1)}, bf16[1024,128]{1,0:T(8,128)(2,1)S(1)}, bf16[1024,128]{1,0:T(8,128)(2,1)S(1)}, f32[2,128]{1,0:T(2,12...) custom-call(s32[20]{0:T(128)S(1)} %concatenate.18.info, f32[8,128]{1,0:T(8,128)S(1)} %get-tuple-element.172.refs_0_, ...), custom_call_target="tpu_custom_call" | custom-call | flops 4800000000 | tf_op jit(solution)/shard_map/attend_backward/pallas_call | solution.py:344
  152.3 2.5 %collective-permute-done.21.refs_6_ = bf16[4,96,384]{2,1,0:T(8,128)(2,1)S(1)} collective-permute-done((bf16[4,96,384]{2,1,0:T(8,128)(2,1)S(1)}, bf16[4,96,384]{2,1,0:T(8,128)(2,1)S(1)}, u32[]{:S(2)}, u32[]{:S(2)}) %collective-permute-start.21) | collective-permute-done | bytes 294944 | tf_op jit(solution)/shard_map/ppermute | solution.py:915
  155.0 1.1 collective-permute-start.25
  156.1 1.7 collective-permute-start.26
  157.8 3.1 %collective-permute-start.27 = (bf16[2,96,384]{2,1,0:T(8,128)(2,1)S(1)}, bf16[2,96,384]{2,1,0:T(8,128)(2,1)S(1)}, u32[]{:S(2)}, u32[]{:S(2)}) collective-permute-start(bf16[2,96,384]{2,1,0:T(8,128)(2,1)S(1)} %get-tuple-element.206), channel_id=1, source_target_pairs={{0,16},{4,20},{8,24},{12,28},{16,0},{20,4},{24,8},{28,12},{1,17},{... | collective-permute-start | bytes 442376 | tf_op jit(solution)/shard_map/ppermute | solution.py:915
  161.5 5.1 %input_part.1 = (f32[2,256,768]{2,1,0:T(8,128)S(1)}, f32[2,256,768]{2,1,0:T(8,128)}) custom-call(s32[20]{0:T(128)S(1)} %concatenate.18.info, f32[8,128]{1,0:T(8,128)S(1)} %get-tuple-element.185.refs_0_, bf16[1024,128]{1,0:T(8,128)(2,1)S(1)} %get-tuple-element.186.refs_1_, bf16[1024,128]{1,0:T(8,128)(2,1)S(1)} %get-tuple-element.187.refs_2_, ...), custom_call_target="tpu_custom_call" | custom-call | flops 3600000000 | tf_op jit(solution)/shard_map/input_part/pallas_call | solution.py:764
  168.5 2.6 %collective-permute-start.38 = (bf16[1,96,384]{2,1,0:T(8,128)(2,1)S(1)}, bf16[1,96,384]{2,1,0:T(8,128)(2,1)S(1)}, u32[]{:S(2)}, u32[]{:S(2)}) collective-permute-start(bf16[1,96,384]{2,1,0:T(8,128)(2,1)S(1)} %get-tuple-element.226), channel_id=1, source_target_pairs={{0,16},{4,20},{8,24},{12,28},{16,0},{20,4},{24,8},{28,12},{1,17},{... | collective-permute-start | bytes 221192 | tf_op jit(solution)/shard_map/ppermute | solution.py:915
  171.1 2.2 %collective-permute-start.31 = (bf16[2,96,384]{2,1,0:T(8,128)(2,1)S(1)}, bf16[2,96,384]{2,1,0:T(8,128)(2,1)S(1)}, u32[]{:S(2)}, u32[]{:S(2)}) collective-permute-start(bf16[2,96,384]{2,1,0:T(8,128)(2,1)S(1)} %get-tuple-element.217), channel_id=1, source_target_pairs={{0,8},{4,12},{8,0},{12,4},{16,24},{20,28},{24,16},{28,20},{1,9},{5... | collective-permute-start | bytes 442376 | tf_op jit(solution)/shard_map/ppermute | solution.py:915
  173.3 1.3 collective-permute-start.32
  175.5 3.3 %collective-permute-done.30 = f32[12,768]{1,0:T(8,128)S(1)} collective-permute-done((f32[12,768]{1,0:T(8,128)S(1)}, f32[12,768]{1,0:T(8,128)S(1)}, u32[]{:S(2)}, u32[]{:S(2)}) %collective-permute-start.30) | collective-permute-done | bytes 36896 | tf_op jit(solution)/shard_map/ppermute | solution.py:912
  178.8 1.6 add.82
  181.3 2.0 collective-permute-done.32.refs_4_
  185.0 2.6 %collective-permute-start.37 = (bf16[96,192]{1,0:T(8,128)(2,1)S(1)}, bf16[96,192]{1,0:T(8,128)(2,1)S(1)}, u32[]{:S(2)}, u32[]{:S(2)}) collective-permute-start(bf16[96,192]{1,0:T(8,128)(2,1)S(1)} %slice.143), channel_id=1, source_target_pairs={{0,16},{4,20},{8,24},{12,28},{16,0},{20,4},{24,8},{28,12},{1,17},{... | collective-permute-start | bytes 110600 | tf_op jit(solution)/shard_map/ppermute | solution.py:915
  189.2 1.3 collective-permute-done.33.refs_5_
  190.5 1.3 collective-permute-start.39
  193.2 1.2 collective-permute-start.43
  194.4 2.9 %collective-permute-done.39.refs_4_ = bf16[1,96,384]{2,1,0:T(8,128)(2,1)S(1)} collective-permute-done((bf16[1,96,384]{2,1,0:T(8,128)(2,1)S(1)}, bf16[1,96,384]{2,1,0:T(8,128)(2,1)S(1)}, u32[]{:S(2)}, u32[]{:S(2)}) %collective-permute-start.39) | collective-permute-done | bytes 73760 | tf_op jit(solution)/shard_map/ppermute | solution.py:915
  200.4 1.2 pad_maximum_fusion
  202.9 1.0 collective-permute-done.41.two
  204.0 1.2 collective-permute-done.42.three
  205.2 1.4 gather.1
  (207 shorter events, 29.0 us)
Async XLA Ops:
  1.9 12.1 %collective-permute-start.1 = (bf16[256,768]{1,0:T(8,128)(2,1)S(1)}, bf16[256,768]{1,0:T(8,128)(2,1)S(1)}, u32[]{:S(2)}, u32[]{:S(2)}) collective-permute-start(bf16[256,768]{1,0:T(8,128)(2,1)S(1)} %get-tuple-element.253), channel_id=1, source_target_pairs={{0,2},{1,3},{2,0},{3,1},{4,6},{5,7},{6,4},{7,5},{8,10},{9,11},{10,... | collective-permute-start | bytes 1179656 | tf_op jit(solution)/shard_map/ppermute | solution.py:912
  4.9 9.7 %collective-permute-start = (bf16[256,768]{1,0:T(8,128)(2,1)S(1)}, bf16[256,768]{1,0:T(8,128)(2,1)S(1)}, u32[]{:S(2)}, u32[]{:S(2)}) collective-permute-start(bf16[256,768]{1,0:T(8,128)(2,1)S(1)} %get-tuple-element.254.x0), channel_id=1, source_target_pairs={{0,1},{1,0},{2,3},{3,2},{4,5},{5,4},{6,7},{7,6},{8,9},{9,8},{10,11... | collective-permute-start | bytes 1179656 | tf_op jit(solution)/shard_map/ppermute | solution.py:912
  14.0 1.7 collective-permute-start.2
  14.5 29.3 %copy-start.48 = (bf16[768]{0:T(1024)(128)(2,1)S(1)}, bf16[768]{0:T(1024)(128)(2,1)}, u32[]{:S(2)}) copy-start(bf16[768]{0:T(1024)(128)(2,1)} %param.23) | copy-start | bytes 4612
  17.8 35.2 %copy-start.12 = (bf16[768,3072]{1,0:T(8,128)(2,1)S(1)}, bf16[768,3072]{1,0:T(8,128)(2,1)}, u32[]{:S(2)}) copy-start(bf16[768,3072]{1,0:T(8,128)(2,1)} %up.1) | copy-start | bytes 14155780
  17.8 35.1 %copy-start.13 = (bf16[3072,768]{1,0:T(8,128)(2,1)S(1)}, bf16[3072,768]{1,0:T(8,128)(2,1)}, u32[]{:S(2)}) copy-start(bf16[3072,768]{1,0:T(8,128)(2,1)} %down.1) | copy-start | bytes 14155780
  41.9 3.1 %collective-permute-start.3 = (bf16[256,384]{1,0:T(8,128)(2,1)S(1)}, bf16[256,384]{1,0:T(8,128)(2,1)S(1)}, u32[]{:S(2)}, u32[]{:S(2)}) collective-permute-start(bf16[256,384]{1,0:T(8,128)(2,1)S(1)} %get-tuple-element.127), channel_id=1, source_target_pairs={{0,1},{1,0},{2,3},{3,2},{4,5},{5,4},{6,7},{7,6},{8,9},{9,8},{10,11... | collective-permute-start | bytes 589832 | tf_op jit(solution)/shard_map/ppermute | solution.py:912
  42.1 7.7 %collective-permute-start.4 = (bf16[256,384]{1,0:T(8,128)(2,1)S(1)}, bf16[256,384]{1,0:T(8,128)(2,1)S(1)}, u32[]{:S(2)}, u32[]{:S(2)}) collective-permute-start(bf16[256,384]{1,0:T(8,128)(2,1)S(1)} %get-tuple-element.128), channel_id=1, source_target_pairs={{0,2},{1,3},{2,0},{3,1},{4,6},{5,7},{6,4},{7,5},{8,10},{9,11},{10,... | collective-permute-start | bytes 589832 | tf_op jit(solution)/shard_map/ppermute | solution.py:912
  42.5 10.4 %collective-permute-start.5 = (bf16[256,384]{1,0:T(8,128)(2,1)S(1)}, bf16[256,384]{1,0:T(8,128)(2,1)S(1)}, u32[]{:S(2)}, u32[]{:S(2)}) collective-permute-start(bf16[256,384]{1,0:T(8,128)(2,1)S(1)} %get-tuple-element.129), channel_id=1, source_target_pairs={{0,3},{1,2},{2,1},{3,0},{4,7},{5,6},{6,5},{7,4},{8,11},{9,10},{10,... | collective-permute-start | bytes 589832 | tf_op jit(solution)/shard_map/ppermute | solution.py:912
  66.3 13.9 %collective-permute-start.7 = (bf16[512,3072]{1,0:T(8,128)(2,1)S(1)}, bf16[512,3072]{1,0:T(8,128)(2,1)S(1)}, u32[]{:S(2)}, u32[]{:S(2)}) collective-permute-start(bf16[512,3072]{1,0:T(8,128)(2,1)S(1)} %get-tuple-element.139.refs_3_), channel_id=1, source_target_pairs={{0,1},{1,0},{2,3},{3,2},{4,5},{5,4},{6,7},{7,6},{8,9},{9,8},{10,11... | collective-permute-start | bytes 9437192 | tf_op jit(solution)/shard_map/ppermute | solution.py:912
  66.7 13.5 %collective-permute-start.6 = (bf16[2,768,512]{2,1,0:T(8,128)(2,1)S(1)}, bf16[2,768,512]{2,1,0:T(8,128)(2,1)S(1)}, u32[]{:S(2)}, u32[]{:S(2)}) collective-permute-start(bf16[2,768,512]{2,1,0:T(8,128)(2,1)S(1)} %get-tuple-element.138.refs_1_), channel_id=1, source_target_pairs={{0,1},{1,0},{2,3},{3,2},{4,5},{5,4},{6,7},{7,6},{8,9},{9,8},{10,11... | collective-permute-start | bytes 4718600 | tf_op jit(solution)/shard_map/ppermute | solution.py:912
  66.8 13.4 %collective-permute-start.8 = (bf16[384,512]{1,0:T(8,128)(2,1)S(1)}, bf16[384,512]{1,0:T(8,128)(2,1)S(1)}, u32[]{:S(2)}, u32[]{:S(2)}) collective-permute-start(bf16[384,512]{1,0:T(8,128)(2,1)S(1)} %get-tuple-element.140), channel_id=1, source_target_pairs={{0,1},{1,0},{2,3},{3,2},{4,5},{5,4},{6,7},{7,6},{8,9},{9,8},{10,11... | collective-permute-start | bytes 1179656 | tf_op jit(solution)/shard_map/ppermute | solution.py:912
  82.2 19.2 %collective-permute-start.9 = (bf16[1536,768]{1,0:T(8,128)(2,1)}, bf16[1536,768]{1,0:T(8,128)(2,1)}, u32[]{:S(2)}, u32[]{:S(2)}) collective-permute-start(bf16[1536,768]{1,0:T(8,128)(2,1)} %get-tuple-element.146), channel_id=1, source_target_pairs={{0,1},{1,0},{2,3},{3,2},{4,5},{5,4},{6,7},{7,6},{8,9},{9,8},{10,11... | collective-permute-start | bytes 7077896 | tf_op jit(solution)/shard_map/ppermute | solution.py:912
  88.2 73.1 %copy-start.43 = (f32[3,768]{1,0:T(4,128)}, f32[3,768]{1,0:T(4,128)S(1)}, u32[]{:S(2)}) copy-start(f32[3,768]{1,0:T(4,128)S(1)} %slice.76) | copy-start | bytes 27652
  88.2 13.1 %collective-permute-start.10 = (bf16[2,256,384]{2,1,0:T(8,128)(2,1)}, bf16[2,256,384]{2,1,0:T(8,128)(2,1)S(1)}, u32[]{:S(2)}, u32[]{:S(2)}) collective-permute-start(bf16[2,256,384]{2,1,0:T(8,128)(2,1)} %copy-done.22), channel_id=1, source_target_pairs={{0,2},{1,3},{2,0},{3,1},{4,6},{5,7},{6,4},{7,5},{8,10},{9,11},{10,... | collective-permute-start | bytes 1179656 | tf_op jit(solution)/shard_map/ppermute | solution.py:912
  97.8 22.6 %collective-permute-start.12 = (bf16[8,96,384]{2,1,0:T(8,128)(2,1)S(1)}, bf16[8,96,384]{2,1,0:T(8,128)(2,1)S(1)}, u32[]{:S(2)}, u32[]{:S(2)}) collective-permute-start(bf16[8,96,384]{2,1,0:T(8,128)(2,1)S(1)} %get-tuple-element.157), channel_id=1, source_target_pairs={{0,8},{4,12},{8,0},{12,4},{16,24},{20,28},{24,16},{28,20},{1,9},{5... | collective-permute-start | bytes 1769480 | tf_op jit(solution)/shard_map/ppermute | solution.py:915
  100.7 19.7 %collective-permute-start.13 = (bf16[8,96,384]{2,1,0:T(8,128)(2,1)S(1)}, bf16[8,96,384]{2,1,0:T(8,128)(2,1)S(1)}, u32[]{:S(2)}, u32[]{:S(2)}) collective-permute-start(bf16[8,96,384]{2,1,0:T(8,128)(2,1)S(1)} %get-tuple-element.159), channel_id=1, source_target_pairs={{0,2},{1,3},{2,0},{3,1},{4,6},{5,7},{6,4},{7,5},{8,10},{9,11},{10,... | collective-permute-start | bytes 1769480 | tf_op jit(solution)/shard_map/ppermute | solution.py:912
  101.3 10.9 %collective-permute-start.11 = (bf16[256,384]{1,0:T(8,128)(2,1)S(1)}, bf16[256,384]{1,0:T(8,128)(2,1)S(1)}, u32[]{:S(2)}, u32[]{:S(2)}) collective-permute-start(bf16[256,384]{1,0:T(8,128)(2,1)S(1)} %slice_bitcast_fusion.1), channel_id=1, source_target_pairs={{0,1},{1,0},{2,3},{3,2},{4,5},{5,4},{6,7},{7,6},{8,9},{9,8},{10,11... | collective-permute-start | bytes 589832 | tf_op jit(solution)/shard_map/ppermute | solution.py:912
  109.6 28.4 %collective-permute-start.15 = (bf16[12,96,384]{2,1,0:T(8,128)(2,1)S(1)}, bf16[12,96,384]{2,1,0:T(8,128)(2,1)S(1)}, u32[]{:S(2)}, u32[]{:S(2)}) collective-permute-start(bf16[12,96,384]{2,1,0:T(8,128)(2,1)S(1)} %get-tuple-element.164), channel_id=1, source_target_pairs={{0,4},{4,0},{8,12},{12,8},{16,20},{20,16},{24,28},{28,24},{1,5},{5... | collective-permute-start | bytes 2654216 | tf_op jit(solution)/shard_map/ppermute | solution.py:915
  111.4 26.7 %collective-permute-start.14 = (bf16[8,96,384]{2,1,0:T(8,128)(2,1)S(1)}, bf16[8,96,384]{2,1,0:T(8,128)(2,1)S(1)}, u32[]{:S(2)}, u32[]{:S(2)}) collective-permute-start(bf16[8,96,384]{2,1,0:T(8,128)(2,1)S(1)} %get-tuple-element.162), channel_id=1, source_target_pairs={{0,2},{1,3},{2,0},{3,1},{4,6},{5,7},{6,4},{7,5},{8,10},{9,11},{10,... | collective-permute-start | bytes 1769480 | tf_op jit(solution)/shard_map/ppermute | solution.py:912
  120.6 17.4 %collective-permute-start.18 = (bf16[4,96,384]{2,1,0:T(8,128)(2,1)S(1)}, bf16[4,96,384]{2,1,0:T(8,128)(2,1)S(1)}, u32[]{:S(2)}, u32[]{:S(2)}) collective-permute-start(bf16[4,96,384]{2,1,0:T(8,128)(2,1)S(1)} %get-tuple-element.171), channel_id=1, source_target_pairs={{0,4},{4,0},{8,12},{12,8},{16,20},{20,16},{24,28},{28,24},{1,5},{5... | collective-permute-start | bytes 884744 | tf_op jit(solution)/shard_map/ppermute | solution.py:915
  121.6 16.5 %collective-permute-start.16 = (bf16[4,96,384]{2,1,0:T(8,128)(2,1)S(1)}, bf16[4,96,384]{2,1,0:T(8,128)(2,1)S(1)}, u32[]{:S(2)}, u32[]{:S(2)}) collective-permute-start(bf16[4,96,384]{2,1,0:T(8,128)(2,1)S(1)} %get-tuple-element.166), channel_id=1, source_target_pairs={{0,2},{1,3},{2,0},{3,1},{4,6},{5,7},{6,4},{7,5},{8,10},{9,11},{10,... | collective-permute-start | bytes 884744 | tf_op jit(solution)/shard_map/ppermute | solution.py:912
  121.8 16.2 %collective-permute-start.17 = (bf16[4,96,384]{2,1,0:T(8,128)(2,1)S(1)}, bf16[4,96,384]{2,1,0:T(8,128)(2,1)S(1)}, u32[]{:S(2)}, u32[]{:S(2)}) collective-permute-start(bf16[4,96,384]{2,1,0:T(8,128)(2,1)S(1)} %get-tuple-element.168), channel_id=1, source_target_pairs={{0,8},{4,12},{8,0},{12,4},{16,24},{20,28},{24,16},{28,20},{1,9},{5... | collective-permute-start | bytes 884744 | tf_op jit(solution)/shard_map/ppermute | solution.py:915
  138.5 13.8 %collective-permute-start.22 = (bf16[4,96,384]{2,1,0:T(8,128)(2,1)S(1)}, bf16[4,96,384]{2,1,0:T(8,128)(2,1)S(1)}, u32[]{:S(2)}, u32[]{:S(2)}) collective-permute-start(bf16[4,96,384]{2,1,0:T(8,128)(2,1)S(1)} %get-tuple-element.182), channel_id=1, source_target_pairs={{0,8},{4,12},{8,0},{12,4},{16,24},{20,28},{24,16},{28,20},{1,9},{5... | collective-permute-start | bytes 884744 | tf_op jit(solution)/shard_map/ppermute | solution.py:915
  138.8 15.9 %collective-permute-start.20 = (bf16[6,96,384]{2,1,0:T(8,128)(2,1)S(1)}, bf16[6,96,384]{2,1,0:T(8,128)(2,1)S(1)}, u32[]{:S(2)}, u32[]{:S(2)}) collective-permute-start(bf16[6,96,384]{2,1,0:T(8,128)(2,1)S(1)} %get-tuple-element.177), channel_id=1, source_target_pairs={{0,2},{1,3},{2,0},{3,1},{4,6},{5,7},{6,4},{7,5},{8,10},{9,11},{10,... | collective-permute-start | bytes 1327112 | tf_op jit(solution)/shard_map/ppermute | solution.py:912
  140.4 11.9 %collective-permute-start.19 = (bf16[4,96,384]{2,1,0:T(8,128)(2,1)S(1)}, bf16[4,96,384]{2,1,0:T(8,128)(2,1)S(1)}, u32[]{:S(2)}, u32[]{:S(2)}) collective-permute-start(bf16[4,96,384]{2,1,0:T(8,128)(2,1)S(1)} %get-tuple-element.175), channel_id=1, source_target_pairs={{0,4},{4,0},{8,12},{12,8},{16,20},{20,16},{24,28},{28,24},{1,5},{5... | collective-permute-start | bytes 884744 | tf_op jit(solution)/shard_map/ppermute | solution.py:915
  141.4 13.4 %collective-permute-start.21 = (bf16[4,96,384]{2,1,0:T(8,128)(2,1)S(1)}, bf16[4,96,384]{2,1,0:T(8,128)(2,1)S(1)}, u32[]{:S(2)}, u32[]{:S(2)}) collective-permute-start(bf16[4,96,384]{2,1,0:T(8,128)(2,1)S(1)} %get-tuple-element.179), channel_id=1, source_target_pairs={{0,4},{4,0},{8,12},{12,8},{16,20},{20,16},{24,28},{28,24},{1,5},{5... | collective-permute-start | bytes 884744 | tf_op jit(solution)/shard_map/ppermute | solution.py:915
  142.4 9.8 %collective-permute-start.23 = (bf16[2,96,384]{2,1,0:T(8,128)(2,1)S(1)}, bf16[2,96,384]{2,1,0:T(8,128)(2,1)S(1)}, u32[]{:S(2)}, u32[]{:S(2)}) collective-permute-start(bf16[2,96,384]{2,1,0:T(8,128)(2,1)S(1)} %get-tuple-element.184), channel_id=1, source_target_pairs={{0,8},{4,12},{8,0},{12,4},{16,24},{20,28},{24,16},{28,20},{1,9},{5... | collective-permute-start | bytes 442376 | tf_op jit(solution)/shard_map/ppermute | solution.py:915
  155.0 11.8 %collective-permute-start.25 = (bf16[4,96,384]{2,1,0:T(8,128)(2,1)S(1)}, bf16[4,96,384]{2,1,0:T(8,128)(2,1)S(1)}, u32[]{:S(2)}, u32[]{:S(2)}) collective-permute-start(bf16[4,96,384]{2,1,0:T(8,128)(2,1)S(1)} %get-tuple-element.202), channel_id=1, source_target_pairs={{0,4},{4,0},{8,12},{12,8},{16,20},{20,16},{24,28},{28,24},{1,5},{5... | collective-permute-start | bytes 884744 | tf_op jit(solution)/shard_map/ppermute | solution.py:915
  156.1 11.6 %collective-permute-start.26 = (bf16[5,96,384]{2,1,0:T(8,128)(2,1)S(1)}, bf16[5,96,384]{2,1,0:T(8,128)(2,1)S(1)}, u32[]{:S(2)}, u32[]{:S(2)}) collective-permute-start(bf16[5,96,384]{2,1,0:T(8,128)(2,1)S(1)} %get-tuple-element.204), channel_id=1, source_target_pairs={{0,8},{4,12},{8,0},{12,4},{16,24},{20,28},{24,16},{28,20},{1,9},{5... | collective-permute-start | bytes 1105928 | tf_op jit(solution)/shard_map/ppermute | solution.py:915
  157.8 9.1 %collective-permute-start.27 = (bf16[2,96,384]{2,1,0:T(8,128)(2,1)S(1)}, bf16[2,96,384]{2,1,0:T(8,128)(2,1)S(1)}, u32[]{:S(2)}, u32[]{:S(2)}) collective-permute-start(bf16[2,96,384]{2,1,0:T(8,128)(2,1)S(1)} %get-tuple-element.206), channel_id=1, source_target_pairs={{0,16},{4,20},{8,24},{12,28},{16,0},{20,4},{24,8},{28,12},{1,17},{... | collective-permute-start | bytes 442376 | tf_op jit(solution)/shard_map/ppermute | solution.py:915
  160.9 6.0 %collective-permute-start.28 = (bf16[2,96,384]{2,1,0:T(8,128)(2,1)S(1)}, bf16[2,96,384]{2,1,0:T(8,128)(2,1)S(1)}, u32[]{:S(2)}, u32[]{:S(2)}) collective-permute-start(bf16[2,96,384]{2,1,0:T(8,128)(2,1)S(1)} %get-tuple-element.208), channel_id=1, source_target_pairs={{0,4},{4,0},{8,12},{12,8},{16,20},{20,16},{24,28},{28,24},{1,5},{5... | collective-permute-start | bytes 442376 | tf_op jit(solution)/shard_map/ppermute | solution.py:915
  161.4 7.2 %collective-permute-start.24 = (f32[12,768]{1,0:T(8,128)S(1)}, f32[12,768]{1,0:T(8,128)S(1)}, u32[]{:S(2)}, u32[]{:S(2)}) collective-permute-start(f32[12,768]{1,0:T(8,128)S(1)} %pad_maximum_fusion.2), channel_id=1, source_target_pairs={{0,1},{1,0},{2,3},{3,2},{4,5},{5,4},{6,7},{7,6},{8,9},{9,8},{10,11... | collective-permute-start | bytes 110600 | tf_op jit(solution)/shard_map/ppermute | solution.py:912
  168.5 10.3 %collective-permute-start.29 = (f32[2,256,768]{2,1,0:T(8,128)}, f32[2,256,768]{2,1,0:T(8,128)}, u32[]{:S(2)}, u32[]{:S(2)}) collective-permute-start(f32[2,256,768]{2,1,0:T(8,128)} %get-tuple-element.210), channel_id=1, source_target_pairs={{0,1},{1,0},{2,3},{3,2},{4,5},{5,4},{6,7},{7,6},{8,9},{9,8},{10,11... | collective-permute-start | bytes 4718600 | tf_op jit(solution)/shard_map/ppermute | solution.py:912
  168.5 25.8 %collective-permute-start.38 = (bf16[1,96,384]{2,1,0:T(8,128)(2,1)S(1)}, bf16[1,96,384]{2,1,0:T(8,128)(2,1)S(1)}, u32[]{:S(2)}, u32[]{:S(2)}) collective-permute-start(bf16[1,96,384]{2,1,0:T(8,128)(2,1)S(1)} %get-tuple-element.226), channel_id=1, source_target_pairs={{0,16},{4,20},{8,24},{12,28},{16,0},{20,4},{24,8},{28,12},{1,17},{... | collective-permute-start | bytes 221192 | tf_op jit(solution)/shard_map/ppermute | solution.py:915
  171.1 10.2 %collective-permute-start.31 = (bf16[2,96,384]{2,1,0:T(8,128)(2,1)S(1)}, bf16[2,96,384]{2,1,0:T(8,128)(2,1)S(1)}, u32[]{:S(2)}, u32[]{:S(2)}) collective-permute-start(bf16[2,96,384]{2,1,0:T(8,128)(2,1)S(1)} %get-tuple-element.217), channel_id=1, source_target_pairs={{0,8},{4,12},{8,0},{12,4},{16,24},{20,28},{24,16},{28,20},{1,9},{5... | collective-permute-start | bytes 442376 | tf_op jit(solution)/shard_map/ppermute | solution.py:915
  173.3 10.0 %collective-permute-start.32 = (bf16[2,96,384]{2,1,0:T(8,128)(2,1)S(1)}, bf16[2,96,384]{2,1,0:T(8,128)(2,1)S(1)}, u32[]{:S(2)}, u32[]{:S(2)}) collective-permute-start(bf16[2,96,384]{2,1,0:T(8,128)(2,1)S(1)} %get-tuple-element.218), channel_id=1, source_target_pairs={{0,16},{4,20},{8,24},{12,28},{16,0},{20,4},{24,8},{28,12},{1,17},{... | collective-permute-start | bytes 442376 | tf_op jit(solution)/shard_map/ppermute | solution.py:915
  174.7 4.2 %collective-permute-start.30 = (f32[12,768]{1,0:T(8,128)S(1)}, f32[12,768]{1,0:T(8,128)S(1)}, u32[]{:S(2)}, u32[]{:S(2)}) collective-permute-start(f32[12,768]{1,0:T(8,128)S(1)} %fusion.12), channel_id=1, source_target_pairs={{0,2},{1,3},{2,0},{3,1},{4,6},{5,7},{6,4},{7,5},{8,10},{9,11},{10,... | collective-permute-start | bytes 110600 | tf_op jit(solution)/shard_map/ppermute | solution.py:912
  180.5 12.1 %collective-permute-start.36 = (bf16[256,768]{1,0:T(8,128)(2,1)S(1)}, bf16[256,768]{1,0:T(8,128)(2,1)S(1)}, u32[]{:S(2)}, u32[]{:S(2)}) collective-permute-start(bf16[256,768]{1,0:T(8,128)(2,1)S(1)} %fusion.1), channel_id=1, source_target_pairs={{0,2},{1,3},{2,0},{3,1},{4,6},{5,7},{6,4},{7,5},{8,10},{9,11},{10,... | collective-permute-start | bytes 1179656 | tf_op jit(solution)/shard_map/ppermute | solution.py:912
  183.9 4.1 %collective-permute-start.34 = (f32[12,768]{1,0:T(8,128)S(1)}, f32[12,768]{1,0:T(8,128)S(1)}, u32[]{:S(2)}, u32[]{:S(2)}) collective-permute-start(f32[12,768]{1,0:T(8,128)S(1)} %add.84), channel_id=1, source_target_pairs={{0,4},{4,0},{8,12},{12,8},{16,20},{20,16},{24,28},{28,24},{1,5},{5... | collective-permute-start | bytes 110600 | tf_op jit(solution)/shard_map/ppermute | solution.py:915
  184.4 6.1 %collective-permute-start.33 = (bf16[1,96,384]{2,1,0:T(8,128)(2,1)S(1)}, bf16[1,96,384]{2,1,0:T(8,128)(2,1)S(1)}, u32[]{:S(2)}, u32[]{:S(2)}) collective-permute-start(bf16[1,96,384]{2,1,0:T(8,128)(2,1)S(1)} %get-tuple-element.219), channel_id=1, source_target_pairs={{0,16},{4,20},{8,24},{12,28},{16,0},{20,4},{24,8},{28,12},{1,17},{... | collective-permute-start | bytes 221192 | tf_op jit(solution)/shard_map/ppermute | solution.py:915
  185.0 6.8 %collective-permute-start.37 = (bf16[96,192]{1,0:T(8,128)(2,1)S(1)}, bf16[96,192]{1,0:T(8,128)(2,1)S(1)}, u32[]{:S(2)}, u32[]{:S(2)}) collective-permute-start(bf16[96,192]{1,0:T(8,128)(2,1)S(1)} %slice.143), channel_id=1, source_target_pairs={{0,16},{4,20},{8,24},{12,28},{16,0},{20,4},{24,8},{28,12},{1,17},{... | collective-permute-start | bytes 110600 | tf_op jit(solution)/shard_map/ppermute | solution.py:915
  188.0 4.5 %collective-permute-start.35 = (f32[12,768]{1,0:T(8,128)S(1)}, f32[12,768]{1,0:T(8,128)S(1)}, u32[]{:S(2)}, u32[]{:S(2)}) collective-permute-start(f32[12,768]{1,0:T(8,128)S(1)} %add.85), channel_id=1, source_target_pairs={{0,8},{4,12},{8,0},{12,4},{16,24},{20,28},{24,16},{28,20},{1,9},{5... | collective-permute-start | bytes 110600 | tf_op jit(solution)/shard_map/ppermute | solution.py:915
  190.5 6.7 %collective-permute-start.39 = (bf16[1,96,384]{2,1,0:T(8,128)(2,1)S(1)}, bf16[1,96,384]{2,1,0:T(8,128)(2,1)S(1)}, u32[]{:S(2)}, u32[]{:S(2)}) collective-permute-start(bf16[1,96,384]{2,1,0:T(8,128)(2,1)S(1)} %get-tuple-element.227), channel_id=1, source_target_pairs={{0,16},{4,20},{8,24},{12,28},{16,0},{20,4},{24,8},{28,12},{1,17},{... | collective-permute-start | bytes 221192 | tf_op jit(solution)/shard_map/ppermute | solution.py:915
  193.2 8.4 %collective-permute-start.43 = (f32[12,768]{1,0:T(8,128)S(1)}, f32[12,768]{1,0:T(8,128)S(1)}, u32[]{:S(2)}, u32[]{:S(2)}) collective-permute-start(f32[12,768]{1,0:T(8,128)S(1)} %add.87), channel_id=1, source_target_pairs={{0,16},{4,20},{8,24},{12,28},{16,0},{20,4},{24,8},{28,12},{1,17},{... | collective-permute-start | bytes 110600 | tf_op jit(solution)/shard_map/ppermute | solution.py:915
  198.2 4.7 %collective-permute-start.40 = (bf16[2,96,192]{2,1,0:T(8,128)(2,1)S(1)}, bf16[2,96,192]{2,1,0:T(8,128)(2,1)S(1)}, u32[]{:S(2)}, u32[]{:S(2)}) collective-permute-start(bf16[2,96,192]{2,1,0:T(8,128)(2,1)S(1)} %get-tuple-element.230), channel_id=1, source_target_pairs={{0,1},{1,0},{2,3},{3,2},{4,5},{5,4},{6,7},{7,6},{8,9},{9,8},{10,11... | collective-permute-start | bytes 221192 | tf_op jit(solution)/shard_map/ppermute | solution.py:912
  198.3 5.7 %collective-permute-start.41 = (bf16[2,96,192]{2,1,0:T(8,128)(2,1)S(1)}, bf16[2,96,192]{2,1,0:T(8,128)(2,1)S(1)}, u32[]{:S(2)}, u32[]{:S(2)}) collective-permute-start(bf16[2,96,192]{2,1,0:T(8,128)(2,1)S(1)} %get-tuple-element.231), channel_id=1, source_target_pairs={{0,2},{1,3},{2,0},{3,1},{4,6},{5,7},{6,4},{7,5},{8,10},{9,11},{10,... | collective-permute-start | bytes 221192 | tf_op jit(solution)/shard_map/ppermute | solution.py:912
  199.1 6.0 %collective-permute-start.42 = (bf16[2,96,192]{2,1,0:T(8,128)(2,1)S(1)}, bf16[2,96,192]{2,1,0:T(8,128)(2,1)S(1)}, u32[]{:S(2)}, u32[]{:S(2)}) collective-permute-start(bf16[2,96,192]{2,1,0:T(8,128)(2,1)S(1)} %get-tuple-element.232), channel_id=1, source_target_pairs={{0,3},{1,2},{2,1},{3,0},{4,7},{5,6},{6,5},{7,4},{8,11},{9,10},{10,... | collective-permute-start | bytes 221192 | tf_op jit(solution)/shard_map/ppermute | solution.py:912
  (50 other events, 458.2 us)

commit v3 on v2

--- a/solution.py
+++ b/solution.py
@@ -273,15 +273,15 @@
     )(info, *quarters, qkv_weight, qkv_weight, qkv_weight, query_bias[None], value_bias[None], seg)
 
 
-QKV_ORDERS = ("yzw", "zyw", "yzw")
+QKV_ORDERS = ("zyw", "zyw", "yzw")
 
 
 def backward_kernel(
-    order, info, q_in, k_in, v_in, o0, o1, o1b, o2, o3, o_in, lse, seg_row, x_t,
-    dq_out, dk_out, dv_out, bias_out, w_send, w_keep,
+    n, info, q_in, k_in, v_in, o0, o1, o1b, o2, o3, o_in, lse, seg_row, x_t, vec,
+    dq_out, dk_out, dv_out, vec_out, w_send, w_keep,
     seg_col, qs, do, kt, dk, dv, w_rows,
 ):
-    place, me = info[0], info[3]
+    place, core, me = info[0], info[1], info[3]
     tokens = q_in.shape[0]
     quarter = tokens // 4
     fill_segments(seg_row, seg_col)
@@ -321,14 +321,22 @@
     lax.fori_loop(0, tokens // BLOCK, step, 0)
     dk_out[...] = dk[...].astype(LOW)
     dv_out[...] = dv[...].astype(LOW)
-    bias_out[0:1, :] = column_sum(dq_out[...].astype(F32))
-    bias_out[1:2, :] = column_sum(dv_out[...].astype(F32))
+    vec_out[...] = vec[...]
+    half = vec.shape[1] // 2
+    for side in range(2):
+
+        @pl.when(core == side)
+        def _():
+            cut = slice(side * half + n * PAIR, side * half + (n + 1) * PAIR)
+            vec_out[10:11, cut] = column_sum(dq_out[...].astype(F32))
+            vec_out[11:12, cut] = column_sum(dv_out[...].astype(F32))
+
     grad = jnp.concatenate([dq_out[...], dk_out[...], dv_out[...]], axis=1)
     grad = dot_nn(x_t[...], grad)
-    put_rows(grad, w_rows, me, 0, order, w_send, w_keep)
-
-
-def attend_backward(info, n, query, key, value, parts, context, lse, seg, x_t, after):
+    put_rows(grad, w_rows, me, 0, QKV_ORDERS[n], w_send, w_keep)
+
+
+def attend_backward(info, n, query, key, value, parts, context, lse, seg, x_t, vectors, after):
     tokens, half = query.shape
     quarter, blocks, width = tokens // 4, tokens // BLOCK, x_t.shape[0]
     col = pl.BlockSpec((tokens, PAIR), lambda p, i: (0, n))
@@ -341,8 +349,9 @@
         for at in range(2)
     ]
     weight = (4, width // 8, 3 * PAIR)
+    dtypes = (LOW, F32)
     return pl.pallas_call(
-        ordered(functools.partial(backward_kernel, QKV_ORDERS[n]), after),
+        ordered(functools.partial(backward_kernel, n), after),
         grid_spec=pltpu.PrefetchScalarGridSpec(
             num_scalar_prefetch=1,
             grid=(1,),
@@ -351,8 +360,10 @@
             + [part, low, high, first, part]
             + [pl.BlockSpec((PAIR, tokens), lambda p, i: (n, 0))]
             + [pl.BlockSpec((1, blocks, 2 * BLOCK), lambda p, i: (n, 0, 0))]
-            + [full((1, tokens)), full((width, tokens))],
-            out_specs=[full((tokens, PAIR))] * 3 + [full((2, PAIR))] + [full(weight)] * 2,
+            + [full((1, tokens)), full((width, tokens)), full(vectors.shape)],
+            out_specs=[full((tokens, PAIR))] * 3
+            + [full(vectors.shape)]
+            + [full(weight)] * len(dtypes),
             scratch_shapes=[
                 pltpu.VMEM((tokens, BLOCK), F32),
                 pltpu.VMEM((tokens, PAIR), LOW),
@@ -364,11 +375,12 @@
             ],
         ),
         out_shape=[shaped((tokens, PAIR), LOW)] * 3
-        + [shaped((2, PAIR), F32), shaped(weight, LOW), shaped(weight, F32)],
+        + [shaped(vectors.shape, F32)]
+        + [shaped(weight, dtype) for dtype in dtypes],
         compiler_params=params(VMEM),
         cost_estimate=cost(8),
         name="attend_backward",
-    )(info, *after, query, key, value, *parts, context, lse, seg, x_t)
+    )(info, *after, query, key, value, *parts, context, lse, seg, x_t, vectors)
 
 
 def normalise(values):
@@ -523,8 +535,8 @@
 
 
 def middle_backward_kernel(
-    info, d_res, slope, down, up, wo, n1, r1, g1,
-    to_core, mine_pre, d_up_bias, d_summed, q0, to_chip, mine, vec,
+    info, d_res, slope, down, up, wo, n1, r1, g1, vec_two,
+    to_core, mine_pre, d_summed, q0, to_chip, mine, vec,
     d_branch, d_hidden,
 ):
     place, core = info[0], info[1]
@@ -539,7 +551,8 @@
         d_hidden[...] = d_res[...]
 
     d_pre = (dot_nt(d_branch[...], down[...]) * slope[...]).astype(LOW)
-    d_up_bias[...] = column_sum(d_pre.astype(F32))
+    block = place ^ (1 - step // 2 + 2 * (step % 2))
+    vec[pl.ds(6 + block, 1), :] = column_sum(d_pre.astype(F32))
     d_hidden[...] += dot_nt(d_pre, up[...])
 
     @pl.when(step < 2)
@@ -557,6 +570,8 @@
         normal = n1[...]
         back = norm_back(grad, g1[...].astype(F32), normal, r1[...])
         d_summed[...] = back
+        vec[3:6, :] = vec_two[0:3, :]
+        vec[10:16, :] = jnp.zeros_like(vec[10:16, :])
         vec[0:1, :] = column_sum(back)
         vec[1:2, :] = column_sum(grad * normal)
         vec[2:3, :] = column_sum(grad)
@@ -576,7 +591,7 @@
         to_chip[1] = other[quarter:]
 
 
-def middle_backward(info, d_res, slope, down, up, wo, n1, r1, g1):
+def middle_backward(info, d_res, slope, down, up, wo, n1, r1, g1, vec_two):
     count, width = d_res.shape
     inner, quarter, half = up.shape[1], count // 2, width // 2
     steps = 4
@@ -601,35 +616,34 @@
                 tokens,
                 full((count, 1)),
                 full((1, width)),
+                full(vec_two.shape),
             ],
             out_specs=[
                 full((3 * count, width)),
                 pl.BlockSpec((1, count, chunk), lambda c, i: (jnp.maximum(c - 2, 0), 0, 0)),
-                pl.BlockSpec((1, chunk), lambda c, i: (0, block(c, i))),
                 tokens,
             ]
-            + [full((quarter, half)), full((2, quarter, half)), turned, full((8, width))],
+            + [full((quarter, half)), full((2, quarter, half)), turned, full((16, width))],
             scratch_shapes=[pltpu.VMEM((count, width), LOW), pltpu.VMEM((count, width), F32)],
         ),
         out_shape=[
             shaped((3 * count, width), LOW),
             shaped((2, count, chunk), LOW),
-            shaped((1, inner), F32),
             shaped((count, width), F32),
         ]
         + [
             shaped((quarter, half), LOW),
             shaped((2, quarter, half), LOW),
             shaped((2, width // 4, count), LOW),
-            shaped((8, width), F32),
+            shaped((16, width), F32),
         ],
         compiler_params=params(VMEM),
         cost_estimate=cost(16),
         name="middle_backward",
-    )(info, d_res, slope, down, up, wo, n1, r1, g1[None])
-
-
-DOWN_ORDERS = ("zxyw", "xzyw")
+    )(info, d_res, slope, down, up, wo, n1, r1, g1[None], vec_two)
+
+
+DOWN_ORDERS = ("zxwy", "xzwy")
 
 
 def down_kernel(info, mine, theirs, act, act_pair, *outs):
@@ -782,10 +796,9 @@
 UNITS = (((0, 1), (2, 3), (4,), (5,)), ((0,), (1,), (2, 3), (4, 5)))
 
 
-def share_kernel(info, *refs):
+def share_kernel(info, zero, first, kept, got, own, one, two, three):
     place, core = info[0], info[1]
-    kept, got, (own, one, two, three) = refs[:3], refs[3:6], refs[6:]
-    total = [kept[n][0] + got[n][0].astype(F32) for n in range(3)]
+    total = [zero[zero.shape[0] - 1], first[first.shape[0] - 1], kept[0] + got[0].astype(F32)]
     units = []
     for t in range(3):
         part = jnp.concatenate([pair[:, t * PAIR : (t + 1) * PAIR] for pair in total], axis=1)
@@ -801,21 +814,22 @@
                         ref[n] = unit.astype(ref.dtype)
 
 
-def share(info, kept, got):
-    unit = (2, kept[0].shape[1], kept[0].shape[2] // 2)
+def share(info, zero, one, kept, got, after):
+    unit = (2, got.shape[1], got.shape[2] // 2)
     return pl.pallas_call(
-        share_kernel,
+        ordered(share_kernel, after),
         grid_spec=pltpu.PrefetchScalarGridSpec(
             num_scalar_prefetch=1,
             grid=(1,),
-            in_specs=[full(kept[0].shape)] * 6,
+            in_specs=waiting(after)
+            + [full(array.shape) for array in (zero, one, kept, got)],
             out_specs=[full(unit)] * 4,
         ),
         out_shape=[shaped(unit, F32)] + [shaped(unit, LOW)] * 3,
         compiler_params=params(VMEM),
         cost_estimate=cost(1),
         name="share",
-    )(info, *kept, *got)
+    )(info, *after, zero, one, kept, got)
 
 
 def gather_kernel(info, own, one, two, three, out):
@@ -963,12 +977,12 @@
     )
     pair = over_seq(turned, 1), over_seq(act, 1), over_seq(send, 1)
     back = middle_backward(
-        info, d_res, slope, down_weight, up_weight, out_weight, n1, r1, norm1_gain
+        info, d_res, slope, down_weight, up_weight, out_weight, n1, r1, norm1_gain, vec_two
     )
     turned_pair, act_pair, theirs = pair
-    to_core, mine_pre, d_up_bias, d_summed, q0, to_chip, mine_d, vec_one = back
-
-    token = mark(turned_pair, act_pair, theirs, vec_one)
+    to_core, mine_pre, d_summed, q0, to_chip, mine_d, vectors = back
+
+    token = mark(turned_pair, act_pair, theirs, vectors)
     to_core, to_chip, token = tie(to_core, to_chip, token)
     from_core, from_chip = over_seq(to_core, 1), over_seq(to_chip, 2)
     made = down_grad(info, mine, theirs, act, act_pair, [token])
@@ -980,91 +994,79 @@
     ups = launch((UP_ORDERS[0], [8], made[0], made[1]), (UP_ORDERS[1], [8, 4], made[2], made[3]))
     d_parts = (q0, from_core, from_core, from_chip, across)
 
-    def piece(n, after):
+    def piece(n, vectors, after):
         made = attend_backward(
-            info, n, query, key, value, d_parts, context, lse, segment, x_t, after
+            info, n, query, key, value, d_parts, context, lse, segment, x_t, vectors, after
         )
         return list(made)
 
     def opening(n, made, token):
-        return QKV_ORDERS[n], [4], tie(made[4], token)[0], made[5]
-
-    zero = piece(0, [made[1]])
+        sent, token = tie(made[4], token)
+        return (QKV_ORDERS[n], [4], sent, made[5]), token
+
+    zero = piece(0, vectors, [made[1]])
     downs, token = land(
         zero[3:4], downs, (DOWN_ORDERS[0][1:], (0, 0)), (DOWN_ORDERS[1][1:], (1, 0))
     )
-    *downs, first = launch(*downs, opening(0, zero, token))
-
-    one = piece(1, [token])
-    (up_a, up_b, down, first), token = land(
+    opened, token = opening(0, zero, token)
+    *downs, first = launch(*downs, opened)
+
+    one = piece(1, zero[3], [token])
+    (up_a, up_b, down), token = land(
         one[3:4],
         ups + downs + [first],
-        (UP_ORDERS[0][1:], (0, 0)),
+        (UP_ORDERS[0][1:], (0, 0), (4, 0)),
         (UP_ORDERS[1][1:], (1, 0), (1, 1)),
-        ("yw", (2, 0), (3, 0)),
-        (QKV_ORDERS[0][1:], (4, 0)),
-    )
-    flights = launch(up_a, up_b, down, opening(1, one, token), first)
-
-    two = piece(2, [token])
-    (up, down, second, first), token = land(
+        ("wy", (2, 0), (3, 0)),
+    )
+    opened, token = opening(1, one, token)
+    flights = launch(up_a, up_b, down, opened)
+
+    two = piece(2, one[3], [token])
+    (up, first, down), token = land(
         two[3:4],
         flights,
         ("zw", (0, 0), (1, 0), (1, 1)),
-        ("w", (2, 0), (2, 1)),
-        (QKV_ORDERS[1][1:], (3, 0)),
-        ("w", (4, 0)),
+        ("w", (0, 1)),
+        ("y", (2, 0), (2, 1), (3, 0)),
     )
     grads = [*zero[:3], *one[:3], *two[:3]]
-    flights = launch(opening(2, two, token), up, down, second)
-    bias_part = jnp.concatenate([zero[3], one[3], tie(two[3], token)[0]], axis=1)
-    bias_zero = jnp.zeros_like(bias_part)
-    bias_part = jnp.where(
-        core == 0,
-        jnp.concatenate([bias_part, bias_zero], axis=1),
-        jnp.concatenate([bias_zero, bias_part], axis=1),
-    )
-    vectors = jnp.concatenate([vec_one[:3], vec_two[:3], d_up_bias.reshape(-1, width), bias_part])
+    opened, token = opening(2, two, token)
+    vectors, token = tie(two[3], token)
+    flights = launch(opened, up, first, down)
     vectors_got = over_seq(vectors, 1)
 
     keep, send = input_part(info, grads, qkv_weight, [token])
-    (third, up, down, second), token = land(
+    (third, up, down), token = land(
         [keep],
         flights,
         (QKV_ORDERS[2][1:], (0, 0)),
-        ("w", (1, 0), (1, 1), (1, 2)),
-        ("", (2, 0), (2, 1)),
-        ("w", (3, 0)),
-    )
-    out_total, down_total = up[3][2], down[3]
-    third, up, first = launch(third, up, first)
+        ("w", (1, 0), (1, 1), (3, 2), (1, 2)),
+        ("", (3, 0), (3, 1), (2, 0)),
+    )
+    down_total, out_total = down[3], up[3][3]
+    third, up = launch(third, up)
     send, vectors_got, token = tie(send, vectors_got, token)
+    d_row = keep + over_seq(send, 1)
+    d_far = over_seq(d_row[1].astype(LOW), 2)
     vectors = vectors + vectors_got
-    vectors_got = over_seq(vectors, 2)
-    d_row_got = over_seq(send, 1)
-    (third, up), token = land([token], [third, up], ("w", (0, 0)), ("", (1, 0), (1, 1)))
+    vectors = vectors + over_seq(vectors, 2)
+    vectors = vectors + swap(vectors, "y")
+    (third, up), token = land([token, vectors], [third, up], ("w", (0, 0)), ("", (1, 0), (1, 1), (1, 2)))
     up_total = up[3]
-    d_row_got, vectors_got, second_sent, out_total, token = tie(
-        d_row_got, vectors_got, second[2], out_total, token
-    )
-    third, second = launch(third, second[:2] + (second_sent, second[3]))
+    vectors, out_total, token = tie(vectors, out_total, token)
+    (third,) = launch(third)
     wide = half // 2
     out_got = swap(out_total[:, wide:].astype(LOW), "w")
+    vectors_got = swap(vectors, "z")
+    own, *others = share(info, down[3], up[3], third[2], third[3], [token, vectors_got, d_far])
+    vectors_got, own = tie(vectors_got, own)
     vectors = vectors + vectors_got
-    vectors = vectors + swap(vectors, "y")
-    vectors_got = swap(vectors, "z")
-    d_row = keep + d_row_got
-    d_far = over_seq(d_row[1].astype(LOW), 2)
-    third_got, vectors_got, d_far, out_got = tie(third[3], vectors_got, d_far, out_got)
-    own, *others = share(
-        info, (first[2], second[2], third[2]), (first[3], second[3], third_got)
-    )
     qkv_total = gather(info, own, *[over_seq(other, 1 + j) for j, other in enumerate(others)])
     qkv_total = finish(qkv_total)
-    vectors = vectors + vectors_got
     out_total = out_total[:, :wide] + out_got.astype(F32)
     out_total = finish(out_total)
-    down_total = finish(down_total.reshape(wide, half).T)
+    down_total = finish(down_total[:2].reshape(wide, half).T)
     up_total = finish(jnp.concatenate([up_total[0], up_total[1]], axis=1))
 
     vectors = vectors + swap(vectors, "w")
@@ -1079,14 +1081,14 @@
         outputs,
         d_inputs,
         qkv_total,
-        vectors[-2],
-        vectors[-1],
+        vectors[10],
+        vectors[11],
         out_total,
         vectors[0],
         vectors[1],
         vectors[2],
         up_total,
-        vectors[6:-2].reshape(-1),
+        vectors[6:10].reshape(-1),
         down_total,
         vectors[3],
         vectors[4],

time: 207 us -> 193 us (0.932)
  local copies, waits for them, and re-layouts: 18.4 us -> 11.6 us
  Pallas kernels: 95.7 us -> 89.2 us
  starting transfers between devices: 42.2 us -> 37 us
  waiting for transfers between devices: 42 us -> 46.8 us
    ppermute x21 -> x18, starting transfers between devices: 29 us -> 22.8 us  [over_batch(): lax.ppermute(array, 'batch', [(i, i ^ flip) for i in range(batch_size)])]
    unnamed x108 -> x48, local copies, waits for them, and re-layouts: 11.5 us -> 6.05 us
    pallas_call x4, Pallas kernels: 25.6 us -> 22.3 us  [the longest x3 21.3 us: attend_backward(): pl.pallas_call(ordered(functools.partial(backward_kernel, n), after), gri...]
    ppermute x23, waiting for transfers between devices: 23.7 us -> 26.3 us  [over_seq(): return lax.ppermute(array, 'seq', [(i, i ^ flip) for i in range(seq_size)])]
    ppermute x21 -> x18, waiting for transfers between devices: 18.3 us -> 20.5 us  [over_batch(): lax.ppermute(array, 'batch', [(i, i ^ flip) for i in range(batch_size)])]
  transfers between devices with their start and end apart: 44 -> 41, of which waited for: 16 -> 19; matrix products, arithmetic and copies ran while one was open for 6% -> 4% of each run, Pallas kernels for 29% -> 28%
where the time goes in v3:
time: 193 us; the launch traced here: 191 us
  Pallas kernels  89.2 us (46%)
  waiting for transfers between devices  46.8 us (24%)
  starting transfers between devices  37 us (19%)
  local copies, waits for them, and re-layouts  11.6 us (6%)
  other arithmetic  4.92 us (3%)
    ppermute x23, waiting for transfers between devices, over_seq(): return lax.ppermute(array, 'seq', [(i, i ^ flip) for i in range(seq_size)])  26.3 us
    ppermute x18, starting transfers between devices, over_batch(): lax.ppermute(array, 'batch', [(i, i ^ flip) for i in range(batch_size)])  22.8 us
    pallas_call x3, Pallas kernels, attend_backward(): pl.pallas_call(ordered(functools.partial(backward_kernel, n), after), gri...  21.3 us
    ppermute x18, waiting for transfers between devices, over_batch(): lax.ppermute(array, 'batch', [(i, i ^ flip) for i in range(batch_size)])  20.5 us
    pallas_call x1, Pallas kernels, attend_forward(): pl.pallas_call(forward_kernel, grid_spec=pltpu.PrefetchScalarGridSpec(num...  20.3 us
    ppermute x23, starting transfers between devices, over_seq(): return lax.ppermute(array, 'seq', [(i, i ^ flip) for i in range(seq_size)])  14.3 us
    pallas_call x1, Pallas kernels, middle_forward(): pl.pallas_call(ordered(middle_forward_kernel, after), grid_spec=pltpu.Pre...  12.9 us
    pallas_call x1, Pallas kernels, middle_backward(): pl.pallas_call(middle_backward_kernel, grid_spec=pltpu.PrefetchScalarGrid...  10.4 us
  transfers between devices with their start and end apart: 41, of which 19 were waited for; matrix products, arithmetic and copies ran while one was open for 4% of the time, Pallas kernels for 28%

profile of v3, /device:TPU:0, one launch (start us, length us, event | category | flops | bytes accessed | tf_op | source)
XLA Modules:
  0.0 190.9 jit_solution(16215199897648746562)
XLA Ops:
  0.7 1.2 dynamic-slice_bitcast_fusion
  1.9 3.0 %collective-permute-start.1 = (bf16[256,768]{1,0:T(8,128)(2,1)S(1)}, bf16[256,768]{1,0:T(8,128)(2,1)S(1)}, u32[]{:S(2)}, u32[]{:S(2)}) collective-permute-start(bf16[256,768]{1,0:T(8,128)(2,1)S(1)} %get-tuple-element.243), channel_id=1, source_target_pairs={{0,2},{1,3},{2,0},{3,1},{4,6},{5,7},{6,4},{7,5},{8,10},{9,11},{10,... | collective-permute-start | bytes 1179656 | tf_op jit(solution)/shard_map/ppermute | solution.py:926
  4.9 9.1 %collective-permute-done.1.x2 = bf16[256,768]{1,0:T(8,128)(2,1)S(1)} collective-permute-done((bf16[256,768]{1,0:T(8,128)(2,1)S(1)}, bf16[256,768]{1,0:T(8,128)(2,1)S(1)}, u32[]{:S(2)}, u32[]{:S(2)}) %collective-permute-start.1) | collective-permute-done | bytes 393248 | tf_op jit(solution)/shard_map/ppermute | solution.py:926
  14.6 1.1 collective-permute-done.2.x3
  15.7 2.0 %copy-done.9 = bf16[768,2304]{1,0:T(8,128)(2,1)S(1)} copy-done((bf16[768,2304]{1,0:T(8,128)(2,1)S(1)}, bf16[768,2304]{1,0:T(8,128)(2,1)}, u32[]{:S(2)}) %copy-start.9) | copy-done | bytes 3538968
  17.8 20.3 %attend_forward.1 = (bf16[1024,384]{1,0:T(8,128)(2,1)S(1)}, bf16[1024,384]{1,0:T(8,128)(2,1)S(1)}, bf16[1024,384]{1,0:T(8,128)(2,1)S(1)}, bf16[256,384]{1,0:T(8,...) custom-call(s32[20]{0:T(128)S(1)} %concatenate.6.info, ...), custom_call_target="tpu_custom_call" | custom-call | flops 9600000000 | tf_op jit(solution)/shard_map/attend_forward/pallas_call | solution.py:247
  38.3 1.8 collective-permute-start.4
  40.3 1.0 turn.1.refs_0_.refs_12_
  41.3 4.7 %collective-permute-done.4.refs_3_ = bf16[256,384]{1,0:T(8,128)(2,1)S(1)} collective-permute-done((bf16[256,384]{1,0:T(8,128)(2,1)S(1)}, bf16[256,384]{1,0:T(8,128)(2,1)S(1)}, u32[]{:S(2)}, u32[]{:S(2)}) %collective-permute-start.4) | collective-permute-done | bytes 196640 | tf_op jit(solution)/shard_map/ppermute | solution.py:926
  46.0 3.1 %collective-permute-done.5.refs_4_ = bf16[256,384]{1,0:T(8,128)(2,1)S(1)} collective-permute-done((bf16[256,384]{1,0:T(8,128)(2,1)S(1)}, bf16[256,384]{1,0:T(8,128)(2,1)S(1)}, u32[]{:S(2)}, u32[]{:S(2)}) %collective-permute-start.5) | collective-permute-done | bytes 196640 | tf_op jit(solution)/shard_map/ppermute | solution.py:926
  49.2 12.9 %middle_forward.1 = (bf16[2,256,768]{2,1,0:T(8,128)(2,1)}, f32[512,768]{1,0:T(8,128)S(1)}, f32[512,768]{1,0:T(8,128)S(1)}, f32[512,1]{1,0:T(8,128)S(1)}, bf16[2,...) custom-call(s32[20]{0:T(128)S(1)} %concatenate.6.info, ...), custom_call_target="tpu_custom_call" | custom-call | flops 10800000000 | tf_op jit(solution)/shard_map/middle_forward/pallas_call | solution.py:491
  62.9 10.4 %middle_backward.1 = (bf16[1536,768]{1,0:T(8,128)(2,1)S(1)}, bf16[2,512,768]{2,1,0:T(8,128)(2,1)S(1)}, f32[512,768]{1,0:T(8,128)S(1)}, bf16[256,384]{1,0:T(8,128...) custom-call(s32[20]{0:T(128)S(1)} %concatenate.6.info, ...), custom_call_target="tpu_custom_call" | custom-call | flops 9600000000 | tf_op jit(solution)/shard_map/middle_backward/pallas_call | solution.py:605
  73.6 1.7 collective-permute-start.10
  75.3 7.8 %down_grad.1 = (bf16[8,96,384]{2,1,0:T(8,128)(2,1)S(1)}, f32[8,96,384]{2,1,0:T(8,128)S(1)}, bf16[8,96,384]{2,1,0:T(8,128)(2,1)S(1)}, f32[8,96,384]{2,1,0:T(8,128)S(1)}) custom-call(s32[20]{0:T(128)S(1)} %concatenate.6.info, f32[8,128]{1,0:T(8,128)S(1)} %mark.1.refs_0_, bf16[2,192,512]{2,1,0:T(8,128)(2,1)S(1)} %get-tuple-element.139.refs_1_, ...), custom_call_target="tpu_custom_call" | custom-call | flops 4800000000 | tf_op jit(solution)/shard_map/down_grad/pallas_call | solution.py:665
  83.1 2.4 %collective-permute-start.12 = (bf16[8,96,384]{2,1,0:T(8,128)(2,1)S(1)}, bf16[8,96,384]{2,1,0:T(8,128)(2,1)S(1)}, u32[]{:S(2)}, u32[]{:S(2)}) collective-permute-start(bf16[8,96,384]{2,1,0:T(8,128)(2,1)S(1)} %get-tuple-element.154), channel_id=1, source_target_pairs={{0,8},{4,12},{8,0},{12,4},{16,24},{20,28},{24,16},{28,20},{1,9},{5... | collective-permute-start | bytes 1769480 | tf_op jit(solution)/shard_map/ppermute | solution.py:929
  86.2 7.0 %up_grad.1 = (bf16[8,96,384]{2,1,0:T(8,128)(2,1)S(1)}, f32[8,96,384]{2,1,0:T(8,128)S(1)}, bf16[12,96,384]{2,1,0:T(8,128)(2,1)S(1)}, f32[12,96,384]{2,1,0:T(8,128)S(1)}) custom-call(s32[20]{0:T(128)S(1)} %concatenate.6.info, f32[8,96,384]{2,1,0:T(8,128)S(1)} %get-tuple-element.140.refs_0_.refs_1_, bf16[2,768,512]{2,1,0:T(8,128)(2,1)S(1)} %get-tuple-element.134.refs_1_, ...), custom_call_target="tpu_custom_call" | custom-call | flops 6000000000 | tf_op jit(solution)/shard_map/up_grad/pallas_call | solution.py:728
  93.1 2.3 %collective-permute-start.15 = (bf16[12,96,384]{2,1,0:T(8,128)(2,1)S(1)}, bf16[12,96,384]{2,1,0:T(8,128)(2,1)S(1)}, u32[]{:S(2)}, u32[]{:S(2)}) collective-permute-start(bf16[12,96,384]{2,1,0:T(8,128)(2,1)S(1)} %get-tuple-element.163), channel_id=1, source_target_pairs={{0,4},{4,0},{8,12},{12,8},{16,20},{20,16},{24,28},{28,24},{1,5},{5... | collective-permute-start | bytes 2654216 | tf_op jit(solution)/shard_map/ppermute | solution.py:929
  95.5 1.5 collective-permute-start.14
  97.0 7.0 %attend_backward.3 = (bf16[1024,128]{1,0:T(8,128)(2,1)S(1)}, bf16[1024,128]{1,0:T(8,128)(2,1)S(1)}, bf16[1024,128]{1,0:T(8,128)(2,1)S(1)}, f32[16,768]{1,0:T(8,1...) custom-call(s32[20]{0:T(128)S(1)} %concatenate.6.info, ...), custom_call_target="tpu_custom_call" | custom-call | flops 4800000000 | tf_op jit(solution)/shard_map/attend_backward/pallas_call | solution.py:353
  104.2 2.0 %collective-permute-start.18 = (bf16[4,96,384]{2,1,0:T(8,128)(2,1)S(1)}, bf16[4,96,384]{2,1,0:T(8,128)(2,1)S(1)}, u32[]{:S(2)}, u32[]{:S(2)}) collective-permute-start(bf16[4,96,384]{2,1,0:T(8,128)(2,1)S(1)} %get-tuple-element.169), channel_id=1, source_target_pairs={{0,8},{4,12},{8,0},{12,4},{16,24},{20,28},{24,16},{28,20},{1,9},{5... | collective-permute-start | bytes 884744 | tf_op jit(solution)/shard_map/ppermute | solution.py:929
  106.9 7.2 %attend_backward.4 = (bf16[1024,128]{1,0:T(8,128)(2,1)S(1)}, bf16[1024,128]{1,0:T(8,128)(2,1)S(1)}, bf16[1024,128]{1,0:T(8,128)(2,1)S(1)}, f32[16,768]{1,0:T(8,1...) custom-call(s32[20]{0:T(128)S(1)} %concatenate.6.info, f32[8,128]{1,0:T(8,128)S(1)} %get-tuple-element.158.refs_0_, ...), custom_call_target="tpu_custom_call" | custom-call | flops 4800000000 | tf_op jit(solution)/shard_map/attend_backward/pallas_call | solution.py:353
  114.2 5.3 %collective-permute-done.16.refs_6_ = bf16[4,96,384]{2,1,0:T(8,128)(2,1)S(1)} collective-permute-done((bf16[4,96,384]{2,1,0:T(8,128)(2,1)S(1)}, bf16[4,96,384]{2,1,0:T(8,128)(2,1)S(1)}, u32[]{:S(2)}, u32[]{:S(2)}) %collective-permute-start.16) | collective-permute-done | bytes 294944 | tf_op jit(solution)/shard_map/ppermute | solution.py:926
  120.1 2.1 %collective-permute-start.19 = (bf16[6,96,384]{2,1,0:T(8,128)(2,1)S(1)}, bf16[6,96,384]{2,1,0:T(8,128)(2,1)S(1)}, u32[]{:S(2)}, u32[]{:S(2)}) collective-permute-start(bf16[6,96,384]{2,1,0:T(8,128)(2,1)S(1)} %get-tuple-element.175), channel_id=1, source_target_pairs={{0,4},{4,0},{8,12},{12,8},{16,20},{20,16},{24,28},{28,24},{1,5},{5... | collective-permute-start | bytes 1327112 | tf_op jit(solution)/shard_map/ppermute | solution.py:929
  123.3 1.8 collective-permute-start.21
  125.1 7.0 %attend_backward.5 = (bf16[1024,128]{1,0:T(8,128)(2,1)S(1)}, bf16[1024,128]{1,0:T(8,128)(2,1)S(1)}, bf16[1024,128]{1,0:T(8,128)(2,1)S(1)}, f32[16,768]{1,0:T(8,1...) custom-call(s32[20]{0:T(128)S(1)} %concatenate.6.info, f32[8,128]{1,0:T(8,128)S(1)} %get-tuple-element.171.refs_0_, ...), custom_call_target="tpu_custom_call" | custom-call | flops 4800000000 | tf_op jit(solution)/shard_map/attend_backward/pallas_call | solution.py:353
  132.2 3.7 %collective-permute-done.22.refs_8_ = bf16[4,96,384]{2,1,0:T(8,128)(2,1)S(1)} collective-permute-done((bf16[4,96,384]{2,1,0:T(8,128)(2,1)S(1)}, bf16[4,96,384]{2,1,0:T(8,128)(2,1)S(1)}, u32[]{:S(2)}, u32[]{:S(2)}) %collective-permute-start.22) | collective-permute-done | bytes 294944 | tf_op jit(solution)/shard_map/ppermute | solution.py:929
  135.8 2.3 %collective-permute-done.21.refs_6_ = bf16[4,96,384]{2,1,0:T(8,128)(2,1)S(1)} collective-permute-done((bf16[4,96,384]{2,1,0:T(8,128)(2,1)S(1)}, bf16[4,96,384]{2,1,0:T(8,128)(2,1)S(1)}, u32[]{:S(2)}, u32[]{:S(2)}) %collective-permute-start.21) | collective-permute-done | bytes 294944 | tf_op jit(solution)/shard_map/ppermute | solution.py:929
  139.5 1.2 collective-permute-start.27
  140.7 2.7 %collective-permute-start.26 = (bf16[1,96,384]{2,1,0:T(8,128)(2,1)S(1)}, bf16[1,96,384]{2,1,0:T(8,128)(2,1)S(1)}, u32[]{:S(2)}, u32[]{:S(2)}) collective-permute-start(bf16[1,96,384]{2,1,0:T(8,128)(2,1)S(1)} %get-tuple-element.202), channel_id=1, source_target_pairs={{0,16},{4,20},{8,24},{12,28},{16,0},{20,4},{24,8},{28,12},{1,17},{... | collective-permute-start | bytes 221192 | tf_op jit(solution)/shard_map/ppermute | solution.py:929
  143.4 5.1 %input_part.1 = (f32[2,256,768]{2,1,0:T(8,128)S(1)}, f32[2,256,768]{2,1,0:T(8,128)}) custom-call(s32[20]{0:T(128)S(1)} %concatenate.6.info, f32[8,128]{1,0:T(8,128)S(1)} %get-tuple-element.184.refs_0_, bf16[1024,128]{1,0:T(8,128)(2,1)S(1)} %get-tuple-element.185.refs_1_, bf16[1024,128]{1,0:T(8,128)(2,1)S(1)} %get-tuple-element.186.refs_2_, ...), custom_call_target="tpu_custom_call" | custom-call | flops 3600000000 | tf_op jit(solution)/shard_map/input_part/pallas_call | solution.py:778
  148.5 2.5 %collective-permute-done.27.refs_8_ = bf16[4,96,384]{2,1,0:T(8,128)(2,1)S(1)} collective-permute-done((bf16[4,96,384]{2,1,0:T(8,128)(2,1)S(1)}, bf16[4,96,384]{2,1,0:T(8,128)(2,1)S(1)}, u32[]{:S(2)}, u32[]{:S(2)}) %collective-permute-start.27) | collective-permute-done | bytes 294944 | tf_op jit(solution)/shard_map/ppermute | solution.py:929
  154.1 1.4 collective-permute-start.30
  156.0 1.7 collective-permute-start.32
  159.7 1.7 slice.86
  161.4 1.0 collective-permute-done.31
  162.4 1.7 collective-permute-done.32.refs_3_
  164.0 4.3 %collective-permute-done.33.refs_5_ = bf16[3,96,384]{2,1,0:T(8,128)(2,1)S(1)} collective-permute-done((bf16[3,96,384]{2,1,0:T(8,128)(2,1)}, bf16[3,96,384]{2,1,0:T(8,128)(2,1)S(1)}, u32[]{:S(2)}, u32[]{:S(2)}) %collective-permute-start.33) | collective-permute-done | bytes 221216 | tf_op jit(solution)/shard_map/ppermute | solution.py:929
  168.4 1.1 copy-done.6
  169.5 1.7 add.81
  172.1 2.9 %collective-permute-start.35 = (bf16[1,96,384]{2,1,0:T(8,128)(2,1)S(1)}, bf16[1,96,384]{2,1,0:T(8,128)(2,1)S(1)}, u32[]{:S(2)}, u32[]{:S(2)}) collective-permute-start(bf16[1,96,384]{2,1,0:T(8,128)(2,1)S(1)} %get-tuple-element.219), channel_id=1, source_target_pairs={{0,16},{4,20},{8,24},{12,28},{16,0},{20,4},{24,8},{28,12},{1,17},{... | collective-permute-start | bytes 221192 | tf_op jit(solution)/shard_map/ppermute | solution.py:929
  175.8 2.4 %collective-permute-done.40 = bf16[96,192]{1,0:T(8,128)(2,1)S(1)} collective-permute-done((bf16[96,192]{1,0:T(8,128)(2,1)S(1)}, bf16[96,192]{1,0:T(8,128)(2,1)S(1)}, u32[]{:S(2)}, u32[]{:S(2)}) %collective-permute-start.40) | collective-permute-done | bytes 36896 | tf_op jit(solution)/shard_map/ppermute | solution.py:929
  179.8 1.7 collective-permute-done.29.refs_2_
  181.5 1.0 share.1
  182.6 0.9 collective-permute-start.37
  183.5 0.9 collective-permute-start.38
  184.7 1.3 pad_maximum_fusion
  186.0 1.5 collective-permute-done.39
  189.5 1.4 gather.1
  (134 shorter events, 17.7 us)
Async XLA Ops:
  1.9 12.1 %collective-permute-start.1 = (bf16[256,768]{1,0:T(8,128)(2,1)S(1)}, bf16[256,768]{1,0:T(8,128)(2,1)S(1)}, u32[]{:S(2)}, u32[]{:S(2)}) collective-permute-start(bf16[256,768]{1,0:T(8,128)(2,1)S(1)} %get-tuple-element.243), channel_id=1, source_target_pairs={{0,2},{1,3},{2,0},{3,1},{4,6},{5,7},{6,4},{7,5},{8,10},{9,11},{10,... | collective-permute-start | bytes 1179656 | tf_op jit(solution)/shard_map/ppermute | solution.py:926
  4.9 9.7 %collective-permute-start = (bf16[256,768]{1,0:T(8,128)(2,1)S(1)}, bf16[256,768]{1,0:T(8,128)(2,1)S(1)}, u32[]{:S(2)}, u32[]{:S(2)}) collective-permute-start(bf16[256,768]{1,0:T(8,128)(2,1)S(1)} %get-tuple-element.244.x0), channel_id=1, source_target_pairs={{0,1},{1,0},{2,3},{3,2},{4,5},{5,4},{6,7},{7,6},{8,9},{9,8},{10,11... | collective-permute-start | bytes 1179656 | tf_op jit(solution)/shard_map/ppermute | solution.py:926
  14.0 1.7 collective-permute-start.2
  14.5 25.6 %copy-start.18 = (bf16[768]{0:T(1024)(128)(2,1)S(1)}, bf16[768]{0:T(1024)(128)(2,1)}, u32[]{:S(2)}) copy-start(bf16[768]{0:T(1024)(128)(2,1)} %param.23) | copy-start | bytes 4612
  17.7 22.4 %copy-start.20 = (bf16[768]{0:T(1024)(128)(2,1)S(1)}, bf16[768]{0:T(1024)(128)(2,1)}, u32[]{:S(2)}) copy-start(bf16[768]{0:T(1024)(128)(2,1)} %param.24) | copy-start | bytes 4612
  17.7 22.4 %copy-start.21 = (bf16[768]{0:T(1024)(128)(2,1)S(1)}, bf16[768]{0:T(1024)(128)(2,1)}, u32[]{:S(2)}) copy-start(bf16[768]{0:T(1024)(128)(2,1)} %param.28) | copy-start | bytes 4612
  17.7 22.4 %copy-start.22 = (bf16[768]{0:T(1024)(128)(2,1)S(1)}, bf16[768]{0:T(1024)(128)(2,1)}, u32[]{:S(2)}) copy-start(bf16[768]{0:T(1024)(128)(2,1)} %param.29) | copy-start | bytes 4612
  17.8 22.5 %copy-start.23 = (bf16[768]{0:T(1024)(128)(2,1)S(1)}, bf16[768]{0:T(1024)(128)(2,1)}, u32[]{:S(2)}) copy-start(bf16[768]{0:T(1024)(128)(2,1)} %param.30) | copy-start | bytes 4612
  17.8 31.4 %copy-start.7 = (bf16[768,3072]{1,0:T(8,128)(2,1)S(1)}, bf16[768,3072]{1,0:T(8,128)(2,1)}, u32[]{:S(2)}) copy-start(bf16[768,3072]{1,0:T(8,128)(2,1)} %up.1) | copy-start | bytes 14155780
  17.8 31.4 %copy-start.8 = (bf16[3072,768]{1,0:T(8,128)(2,1)S(1)}, bf16[3072,768]{1,0:T(8,128)(2,1)}, u32[]{:S(2)}) copy-start(bf16[3072,768]{1,0:T(8,128)(2,1)} %down.1) | copy-start | bytes 14155780
  38.1 3.2 %collective-permute-start.3 = (bf16[256,384]{1,0:T(8,128)(2,1)S(1)}, bf16[256,384]{1,0:T(8,128)(2,1)S(1)}, u32[]{:S(2)}, u32[]{:S(2)}) collective-permute-start(bf16[256,384]{1,0:T(8,128)(2,1)S(1)} %get-tuple-element.122), channel_id=1, source_target_pairs={{0,1},{1,0},{2,3},{3,2},{4,5},{5,4},{6,7},{7,6},{8,9},{9,8},{10,11... | collective-permute-start | bytes 589832 | tf_op jit(solution)/shard_map/ppermute | solution.py:926
  38.3 7.7 %collective-permute-start.4 = (bf16[256,384]{1,0:T(8,128)(2,1)S(1)}, bf16[256,384]{1,0:T(8,128)(2,1)S(1)}, u32[]{:S(2)}, u32[]{:S(2)}) collective-permute-start(bf16[256,384]{1,0:T(8,128)(2,1)S(1)} %get-tuple-element.123), channel_id=1, source_target_pairs={{0,2},{1,3},{2,0},{3,1},{4,6},{5,7},{6,4},{7,5},{8,10},{9,11},{10,... | collective-permute-start | bytes 589832 | tf_op jit(solution)/shard_map/ppermute | solution.py:926
  40.1 9.1 %collective-permute-start.5 = (bf16[256,384]{1,0:T(8,128)(2,1)S(1)}, bf16[256,384]{1,0:T(8,128)(2,1)S(1)}, u32[]{:S(2)}, u32[]{:S(2)}) collective-permute-start(bf16[256,384]{1,0:T(8,128)(2,1)S(1)} %get-tuple-element.124), channel_id=1, source_target_pairs={{0,3},{1,2},{2,1},{3,0},{4,7},{5,6},{6,5},{7,4},{8,11},{9,10},{10,... | collective-permute-start | bytes 589832 | tf_op jit(solution)/shard_map/ppermute | solution.py:926
  62.0 11.3 %collective-permute-start.7 = (bf16[512,3072]{1,0:T(8,128)(2,1)}, bf16[512,3072]{1,0:T(8,128)(2,1)S(1)}, u32[]{:S(2)}, u32[]{:S(2)}) collective-permute-start(bf16[512,3072]{1,0:T(8,128)(2,1)} %get-tuple-element.135.refs_3_), channel_id=1, source_target_pairs={{0,1},{1,0},{2,3},{3,2},{4,5},{5,4},{6,7},{7,6},{8,9},{9,8},{10,11... | collective-permute-start | bytes 9437192 | tf_op jit(solution)/shard_map/ppermute | solution.py:926
  62.4 10.9 %collective-permute-start.6 = (bf16[2,768,512]{2,1,0:T(8,128)(2,1)S(1)}, bf16[2,768,512]{2,1,0:T(8,128)(2,1)S(1)}, u32[]{:S(2)}, u32[]{:S(2)}) collective-permute-start(bf16[2,768,512]{2,1,0:T(8,128)(2,1)S(1)} %get-tuple-element.134.refs_1_), channel_id=1, source_target_pairs={{0,1},{1,0},{2,3},{3,2},{4,5},{5,4},{6,7},{7,6},{8,9},{9,8},{10,11... | collective-permute-start | bytes 4718600 | tf_op jit(solution)/shard_map/ppermute | solution.py:926
  62.5 10.8 %collective-permute-start.8 = (bf16[384,512]{1,0:T(8,128)(2,1)S(1)}, bf16[384,512]{1,0:T(8,128)(2,1)S(1)}, u32[]{:S(2)}, u32[]{:S(2)}) collective-permute-start(bf16[384,512]{1,0:T(8,128)(2,1)S(1)} %get-tuple-element.136), channel_id=1, source_target_pairs={{0,1},{1,0},{2,3},{3,2},{4,5},{5,4},{6,7},{7,6},{8,9},{9,8},{10,11... | collective-permute-start | bytes 1179656 | tf_op jit(solution)/shard_map/ppermute | solution.py:926
  73.4 12.8 %collective-permute-start.9 = (bf16[1536,768]{1,0:T(8,128)(2,1)S(1)}, bf16[1536,768]{1,0:T(8,128)(2,1)S(1)}, u32[]{:S(2)}, u32[]{:S(2)}) collective-permute-start(bf16[1536,768]{1,0:T(8,128)(2,1)S(1)} %get-tuple-element.142), channel_id=1, source_target_pairs={{0,1},{1,0},{2,3},{3,2},{4,5},{5,4},{6,7},{7,6},{8,9},{9,8},{10,11... | collective-permute-start | bytes 7077896 | tf_op jit(solution)/shard_map/ppermute | solution.py:926
  73.6 12.5 %collective-permute-start.10 = (bf16[2,256,384]{2,1,0:T(8,128)(2,1)S(1)}, bf16[2,256,384]{2,1,0:T(8,128)(2,1)S(1)}, u32[]{:S(2)}, u32[]{:S(2)}) collective-permute-start(bf16[2,256,384]{2,1,0:T(8,128)(2,1)S(1)} %get-tuple-element.149), channel_id=1, source_target_pairs={{0,2},{1,3},{2,0},{3,1},{4,6},{5,7},{6,4},{7,5},{8,10},{9,11},{10,... | collective-permute-start | bytes 1179656 | tf_op jit(solution)/shard_map/ppermute | solution.py:926
  83.1 20.9 %collective-permute-start.12 = (bf16[8,96,384]{2,1,0:T(8,128)(2,1)S(1)}, bf16[8,96,384]{2,1,0:T(8,128)(2,1)S(1)}, u32[]{:S(2)}, u32[]{:S(2)}) collective-permute-start(bf16[8,96,384]{2,1,0:T(8,128)(2,1)S(1)} %get-tuple-element.154), channel_id=1, source_target_pairs={{0,8},{4,12},{8,0},{12,4},{16,24},{20,28},{24,16},{28,20},{1,9},{5... | collective-permute-start | bytes 1769480 | tf_op jit(solution)/shard_map/ppermute | solution.py:929
  85.5 18.5 %collective-permute-start.13 = (bf16[8,96,384]{2,1,0:T(8,128)(2,1)S(1)}, bf16[8,96,384]{2,1,0:T(8,128)(2,1)S(1)}, u32[]{:S(2)}, u32[]{:S(2)}) collective-permute-start(bf16[8,96,384]{2,1,0:T(8,128)(2,1)S(1)} %get-tuple-element.156), channel_id=1, source_target_pairs={{0,2},{1,3},{2,0},{3,1},{4,6},{5,7},{6,4},{7,5},{8,10},{9,11},{10,... | collective-permute-start | bytes 1769480 | tf_op jit(solution)/shard_map/ppermute | solution.py:926
  86.1 10.9 %collective-permute-start.11 = (bf16[256,384]{1,0:T(8,128)(2,1)S(1)}, bf16[256,384]{1,0:T(8,128)(2,1)S(1)}, u32[]{:S(2)}, u32[]{:S(2)}) collective-permute-start(bf16[256,384]{1,0:T(8,128)(2,1)S(1)} %slice_bitcast_fusion.1), channel_id=1, source_target_pairs={{0,1},{1,0},{2,3},{3,2},{4,5},{5,4},{6,7},{7,6},{8,9},{9,8},{10,11... | collective-permute-start | bytes 589832 | tf_op jit(solution)/shard_map/ppermute | solution.py:926
  93.1 26.6 %collective-permute-start.15 = (bf16[12,96,384]{2,1,0:T(8,128)(2,1)S(1)}, bf16[12,96,384]{2,1,0:T(8,128)(2,1)S(1)}, u32[]{:S(2)}, u32[]{:S(2)}) collective-permute-start(bf16[12,96,384]{2,1,0:T(8,128)(2,1)S(1)} %get-tuple-element.163), channel_id=1, source_target_pairs={{0,4},{4,0},{8,12},{12,8},{16,20},{20,16},{24,28},{28,24},{1,5},{5... | collective-permute-start | bytes 2654216 | tf_op jit(solution)/shard_map/ppermute | solution.py:929
  95.5 24.3 %collective-permute-start.14 = (bf16[8,96,384]{2,1,0:T(8,128)(2,1)S(1)}, bf16[8,96,384]{2,1,0:T(8,128)(2,1)S(1)}, u32[]{:S(2)}, u32[]{:S(2)}) collective-permute-start(bf16[8,96,384]{2,1,0:T(8,128)(2,1)S(1)} %get-tuple-element.161), channel_id=1, source_target_pairs={{0,2},{1,3},{2,0},{3,1},{4,6},{5,7},{6,4},{7,5},{8,10},{9,11},{10,... | collective-permute-start | bytes 1769480 | tf_op jit(solution)/shard_map/ppermute | solution.py:926
  104.2 9.9 %collective-permute-start.18 = (bf16[4,96,384]{2,1,0:T(8,128)(2,1)S(1)}, bf16[4,96,384]{2,1,0:T(8,128)(2,1)S(1)}, u32[]{:S(2)}, u32[]{:S(2)}) collective-permute-start(bf16[4,96,384]{2,1,0:T(8,128)(2,1)S(1)} %get-tuple-element.169), channel_id=1, source_target_pairs={{0,8},{4,12},{8,0},{12,4},{16,24},{20,28},{24,16},{28,20},{1,9},{5... | collective-permute-start | bytes 884744 | tf_op jit(solution)/shard_map/ppermute | solution.py:929
  106.3 13.2 %collective-permute-start.16 = (bf16[4,96,384]{2,1,0:T(8,128)(2,1)S(1)}, bf16[4,96,384]{2,1,0:T(8,128)(2,1)S(1)}, u32[]{:S(2)}, u32[]{:S(2)}) collective-permute-start(bf16[4,96,384]{2,1,0:T(8,128)(2,1)S(1)} %get-tuple-element.165), channel_id=1, source_target_pairs={{0,2},{1,3},{2,0},{3,1},{4,6},{5,7},{6,4},{7,5},{8,10},{9,11},{10,... | collective-permute-start | bytes 884744 | tf_op jit(solution)/shard_map/ppermute | solution.py:926
  106.3 13.4 %collective-permute-start.17 = (bf16[4,96,384]{2,1,0:T(8,128)(2,1)S(1)}, bf16[4,96,384]{2,1,0:T(8,128)(2,1)S(1)}, u32[]{:S(2)}, u32[]{:S(2)}) collective-permute-start(bf16[4,96,384]{2,1,0:T(8,128)(2,1)S(1)} %get-tuple-element.167), channel_id=1, source_target_pairs={{0,8},{4,12},{8,0},{12,4},{16,24},{20,28},{24,16},{28,20},{1,9},{5... | collective-permute-start | bytes 884744 | tf_op jit(solution)/shard_map/ppermute | solution.py:929
  120.1 18.0 %collective-permute-start.19 = (bf16[6,96,384]{2,1,0:T(8,128)(2,1)S(1)}, bf16[6,96,384]{2,1,0:T(8,128)(2,1)S(1)}, u32[]{:S(2)}, u32[]{:S(2)}) collective-permute-start(bf16[6,96,384]{2,1,0:T(8,128)(2,1)S(1)} %get-tuple-element.175), channel_id=1, source_target_pairs={{0,4},{4,0},{8,12},{12,8},{16,20},{20,16},{24,28},{28,24},{1,5},{5... | collective-permute-start | bytes 1327112 | tf_op jit(solution)/shard_map/ppermute | solution.py:929
  122.2 15.9 %collective-permute-start.20 = (bf16[6,96,384]{2,1,0:T(8,128)(2,1)S(1)}, bf16[6,96,384]{2,1,0:T(8,128)(2,1)S(1)}, u32[]{:S(2)}, u32[]{:S(2)}) collective-permute-start(bf16[6,96,384]{2,1,0:T(8,128)(2,1)S(1)} %get-tuple-element.177), channel_id=1, source_target_pairs={{0,2},{1,3},{2,0},{3,1},{4,6},{5,7},{6,4},{7,5},{8,10},{9,11},{10,... | collective-permute-start | bytes 1327112 | tf_op jit(solution)/shard_map/ppermute | solution.py:926
  122.5 13.3 %collective-permute-start.22 = (bf16[4,96,384]{2,1,0:T(8,128)(2,1)S(1)}, bf16[4,96,384]{2,1,0:T(8,128)(2,1)S(1)}, u32[]{:S(2)}, u32[]{:S(2)}) collective-permute-start(bf16[4,96,384]{2,1,0:T(8,128)(2,1)S(1)} %get-tuple-element.181), channel_id=1, source_target_pairs={{0,8},{4,12},{8,0},{12,4},{16,24},{20,28},{24,16},{28,20},{1,9},{5... | collective-permute-start | bytes 884744 | tf_op jit(solution)/shard_map/ppermute | solution.py:929
  123.3 14.8 %collective-permute-start.21 = (bf16[4,96,384]{2,1,0:T(8,128)(2,1)S(1)}, bf16[4,96,384]{2,1,0:T(8,128)(2,1)S(1)}, u32[]{:S(2)}, u32[]{:S(2)}) collective-permute-start(bf16[4,96,384]{2,1,0:T(8,128)(2,1)S(1)} %get-tuple-element.179), channel_id=1, source_target_pairs={{0,16},{4,20},{8,24},{12,28},{16,0},{20,4},{24,8},{28,12},{1,17},{... | collective-permute-start | bytes 884744 | tf_op jit(solution)/shard_map/ppermute | solution.py:929
  138.4 12.6 %collective-permute-start.25 = (bf16[5,96,384]{2,1,0:T(8,128)(2,1)S(1)}, bf16[5,96,384]{2,1,0:T(8,128)(2,1)S(1)}, u32[]{:S(2)}, u32[]{:S(2)}) collective-permute-start(bf16[5,96,384]{2,1,0:T(8,128)(2,1)S(1)} %get-tuple-element.200), channel_id=1, source_target_pairs={{0,8},{4,12},{8,0},{12,4},{16,24},{20,28},{24,16},{28,20},{1,9},{5... | collective-permute-start | bytes 1105928 | tf_op jit(solution)/shard_map/ppermute | solution.py:929
  138.6 9.8 %collective-permute-start.24 = (bf16[4,96,384]{2,1,0:T(8,128)(2,1)S(1)}, bf16[4,96,384]{2,1,0:T(8,128)(2,1)S(1)}, u32[]{:S(2)}, u32[]{:S(2)}) collective-permute-start(bf16[4,96,384]{2,1,0:T(8,128)(2,1)S(1)} %get-tuple-element.198), channel_id=1, source_target_pairs={{0,4},{4,0},{8,12},{12,8},{16,20},{20,16},{24,28},{28,24},{1,5},{5... | collective-permute-start | bytes 884744 | tf_op jit(solution)/shard_map/ppermute | solution.py:929
  139.5 11.5 %collective-permute-start.27 = (bf16[4,96,384]{2,1,0:T(8,128)(2,1)S(1)}, bf16[4,96,384]{2,1,0:T(8,128)(2,1)S(1)}, u32[]{:S(2)}, u32[]{:S(2)}) collective-permute-start(bf16[4,96,384]{2,1,0:T(8,128)(2,1)S(1)} %get-tuple-element.204), channel_id=1, source_target_pairs={{0,4},{4,0},{8,12},{12,8},{16,20},{20,16},{24,28},{28,24},{1,5},{5... | collective-permute-start | bytes 884744 | tf_op jit(solution)/shard_map/ppermute | solution.py:929
  140.7 7.8 %collective-permute-start.26 = (bf16[1,96,384]{2,1,0:T(8,128)(2,1)S(1)}, bf16[1,96,384]{2,1,0:T(8,128)(2,1)S(1)}, u32[]{:S(2)}, u32[]{:S(2)}) collective-permute-start(bf16[1,96,384]{2,1,0:T(8,128)(2,1)S(1)} %get-tuple-element.202), channel_id=1, source_target_pairs={{0,16},{4,20},{8,24},{12,28},{16,0},{20,4},{24,8},{28,12},{1,17},{... | collective-permute-start | bytes 221192 | tf_op jit(solution)/shard_map/ppermute | solution.py:929
  143.4 10.1 %collective-permute-start.23 = (f32[16,768]{1,0:T(8,128)S(1)}, f32[16,768]{1,0:T(8,128)S(1)}, u32[]{:S(2)}, u32[]{:S(2)}) collective-permute-start(f32[16,768]{1,0:T(8,128)S(1)} %get-tuple-element.196.refs_0_), channel_id=1, source_target_pairs={{0,1},{1,0},{2,3},{3,2},{4,5},{5,4},{6,7},{7,6},{8,9},{9,8},{10,11... | collective-permute-start | bytes 147464 | tf_op jit(solution)/shard_map/ppermute | solution.py:926
  153.5 16.0 %collective-permute-start.28 = (f32[2,256,768]{2,1,0:T(8,128)}, f32[2,256,768]{2,1,0:T(8,128)}, u32[]{:S(2)}, u32[]{:S(2)}) collective-permute-start(f32[2,256,768]{2,1,0:T(8,128)} %get-tuple-element.206), channel_id=1, source_target_pairs={{0,1},{1,0},{2,3},{3,2},{4,5},{5,4},{6,7},{7,6},{8,9},{9,8},{10,11... | collective-permute-start | bytes 4718600 | tf_op jit(solution)/shard_map/ppermute | solution.py:926
  154.1 4.1 %collective-permute-start.30 = (f32[16,768]{1,0:T(8,128)S(1)}, f32[16,768]{1,0:T(8,128)S(1)}, u32[]{:S(2)}, u32[]{:S(2)}) collective-permute-start(f32[16,768]{1,0:T(8,128)S(1)} %add.84), channel_id=1, source_target_pairs={{0,2},{1,3},{2,0},{3,1},{4,6},{5,7},{6,4},{7,5},{8,10},{9,11},{10,... | collective-permute-start | bytes 147464 | tf_op jit(solution)/shard_map/ppermute | solution.py:926
  155.5 12.8 %collective-permute-start.33 = (bf16[3,96,384]{2,1,0:T(8,128)(2,1)}, bf16[3,96,384]{2,1,0:T(8,128)(2,1)S(1)}, u32[]{:S(2)}, u32[]{:S(2)}) collective-permute-start(bf16[3,96,384]{2,1,0:T(8,128)(2,1)} %copy-done.13), channel_id=1, source_target_pairs={{0,16},{4,20},{8,24},{12,28},{16,0},{20,4},{24,8},{28,12},{1,17},{... | collective-permute-start | bytes 663560 | tf_op jit(solution)/shard_map/ppermute | solution.py:929
  156.0 8.0 %collective-permute-start.32 = (bf16[2,96,384]{2,1,0:T(8,128)(2,1)}, bf16[2,96,384]{2,1,0:T(8,128)(2,1)S(1)}, u32[]{:S(2)}, u32[]{:S(2)}) collective-permute-start(bf16[2,96,384]{2,1,0:T(8,128)(2,1)} %copy-done.14), channel_id=1, source_target_pairs={{0,8},{4,12},{8,0},{12,4},{16,24},{20,28},{24,16},{28,20},{1,9},{5... | collective-permute-start | bytes 442376 | tf_op jit(solution)/shard_map/ppermute | solution.py:929
  158.2 4.2 %collective-permute-start.31 = (f32[16,768]{1,0:T(8,128)S(1)}, f32[16,768]{1,0:T(8,128)S(1)}, u32[]{:S(2)}, u32[]{:S(2)}) collective-permute-start(f32[16,768]{1,0:T(8,128)S(1)} %add.85), channel_id=1, source_target_pairs={{0,4},{4,0},{8,12},{12,8},{16,20},{20,16},{24,28},{28,24},{1,5},{5... | collective-permute-start | bytes 147464 | tf_op jit(solution)/shard_map/ppermute | solution.py:929
  171.3 10.2 %collective-permute-start.29 = (bf16[256,768]{1,0:T(8,128)(2,1)S(1)}, bf16[256,768]{1,0:T(8,128)(2,1)S(1)}, u32[]{:S(2)}, u32[]{:S(2)}) collective-permute-start(bf16[256,768]{1,0:T(8,128)(2,1)S(1)} %fusion.1), channel_id=1, source_target_pairs={{0,2},{1,3},{2,0},{3,1},{4,6},{5,7},{6,4},{7,5},{8,10},{9,11},{10,... | collective-permute-start | bytes 1179656 | tf_op jit(solution)/shard_map/ppermute | solution.py:926
  172.1 6.1 %collective-permute-start.40 = (bf16[96,192]{1,0:T(8,128)(2,1)S(1)}, bf16[96,192]{1,0:T(8,128)(2,1)S(1)}, u32[]{:S(2)}, u32[]{:S(2)}) collective-permute-start(bf16[96,192]{1,0:T(8,128)(2,1)S(1)} %slice.139), channel_id=1, source_target_pairs={{0,16},{4,20},{8,24},{12,28},{16,0},{20,4},{24,8},{28,12},{1,17},{... | collective-permute-start | bytes 110600 | tf_op jit(solution)/shard_map/ppermute | solution.py:929
  172.1 7.6 %collective-permute-start.35 = (bf16[1,96,384]{2,1,0:T(8,128)(2,1)S(1)}, bf16[1,96,384]{2,1,0:T(8,128)(2,1)S(1)}, u32[]{:S(2)}, u32[]{:S(2)}) collective-permute-start(bf16[1,96,384]{2,1,0:T(8,128)(2,1)S(1)} %get-tuple-element.219), channel_id=1, source_target_pairs={{0,16},{4,20},{8,24},{12,28},{16,0},{20,4},{24,8},{28,12},{1,17},{... | collective-permute-start | bytes 221192 | tf_op jit(solution)/shard_map/ppermute | solution.py:929
  175.1 4.1 %collective-permute-start.34 = (f32[16,768]{1,0:T(8,128)S(1)}, f32[16,768]{1,0:T(8,128)S(1)}, u32[]{:S(2)}, u32[]{:S(2)}) collective-permute-start(f32[16,768]{1,0:T(8,128)S(1)} %add.86.refs_1_), channel_id=1, source_target_pairs={{0,8},{4,12},{8,0},{12,4},{16,24},{20,28},{24,16},{28,20},{1,9},{5... | collective-permute-start | bytes 147464 | tf_op jit(solution)/shard_map/ppermute | solution.py:929
  182.5 5.1 %collective-permute-start.39 = (f32[16,768]{1,0:T(8,128)S(1)}, f32[16,768]{1,0:T(8,128)S(1)}, u32[]{:S(2)}, u32[]{:S(2)}) collective-permute-start(f32[16,768]{1,0:T(8,128)S(1)} %add.87), channel_id=1, source_target_pairs={{0,16},{4,20},{8,24},{12,28},{16,0},{20,4},{24,8},{28,12},{1,17},{... | collective-permute-start | bytes 147464 | tf_op jit(solution)/shard_map/ppermute | solution.py:929
  182.5 6.3 %collective-permute-start.36 = (bf16[2,96,192]{2,1,0:T(8,128)(2,1)S(1)}, bf16[2,96,192]{2,1,0:T(8,128)(2,1)S(1)}, u32[]{:S(2)}, u32[]{:S(2)}) collective-permute-start(bf16[2,96,192]{2,1,0:T(8,128)(2,1)S(1)} %get-tuple-element.222), channel_id=1, source_target_pairs={{0,1},{1,0},{2,3},{3,2},{4,5},{5,4},{6,7},{7,6},{8,9},{9,8},{10,11... | collective-permute-start | bytes 221192 | tf_op jit(solution)/shard_map/ppermute | solution.py:926
  182.6 6.2 %collective-permute-start.37 = (bf16[2,96,192]{2,1,0:T(8,128)(2,1)S(1)}, bf16[2,96,192]{2,1,0:T(8,128)(2,1)S(1)}, u32[]{:S(2)}, u32[]{:S(2)}) collective-permute-start(bf16[2,96,192]{2,1,0:T(8,128)(2,1)S(1)} %get-tuple-element.223), channel_id=1, source_target_pairs={{0,2},{1,3},{2,0},{3,1},{4,6},{5,7},{6,4},{7,5},{8,10},{9,11},{10,... | collective-permute-start | bytes 221192 | tf_op jit(solution)/shard_map/ppermute | solution.py:926
  183.5 5.9 %collective-permute-start.38 = (bf16[2,96,192]{2,1,0:T(8,128)(2,1)S(1)}, bf16[2,96,192]{2,1,0:T(8,128)(2,1)S(1)}, u32[]{:S(2)}, u32[]{:S(2)}) collective-permute-start(bf16[2,96,192]{2,1,0:T(8,128)(2,1)S(1)} %get-tuple-element.224), channel_id=1, source_target_pairs={{0,3},{1,2},{2,1},{3,0},{4,7},{5,6},{6,5},{7,4},{8,11},{9,10},{10,... | collective-permute-start | bytes 221192 | tf_op jit(solution)/shard_map/ppermute | solution.py:926
  (17 other events, 130.4 us)

commit v4 on v3

--- a/solution.py
+++ b/solution.py
@@ -14,9 +14,11 @@
 LOW = jnp.bfloat16
 PAIR = 2 * DH
 SCALE = DH**-0.5
-BLOCK = 128
-SIZES = (2, 3, 5, 6, 8)
+BLOCK = 256
+UNIT = 128
+SIZES = (5, 8)
 VMEM = 18
+CHUNKS = 1
 ROOT_HALF = 0.5**0.5
 ROOT_TWO_PI = 0.3989422804014327
 
@@ -137,26 +139,24 @@
 
 
 def each_window(info, block, run):
-    start = pl.multiple_of(info[4 + block], BLOCK)
+    start = pl.multiple_of(info[4 + block], UNIT)
     kind = info[4 + (info.shape[0] - 4) // 2 + block]
     for n, size in enumerate(SIZES):
 
         @pl.when(kind == n)
         def _():
-            run(pl.ds(start, size * BLOCK), size * BLOCK)
+            run(pl.ds(start, size * UNIT), size * UNIT)
 
 
 def windows(segment):
     tokens = segment.shape[0]
     rows = segment.reshape(tokens // BLOCK, BLOCK)
-    first = jnp.sum((segment[None] < rows[:, :1]).astype(jnp.int32), axis=1) // BLOCK
-    last = (jnp.sum((segment[None] <= rows[:, -1:]).astype(jnp.int32), axis=1) - 1) // BLOCK
+    first = jnp.sum((segment[None] < rows[:, :1]).astype(jnp.int32), axis=1) // UNIT
+    last = (jnp.sum((segment[None] <= rows[:, -1:]).astype(jnp.int32), axis=1) - 1) // UNIT
     need = last - first + 1
-    kind = sum((need > size).astype(jnp.int32) for size in SIZES[:-1])
-    size = sum(
-        jnp.where(kind == n, size, 0).astype(jnp.int32) for n, size in enumerate(SIZES)
-    )
-    return [jnp.minimum(first, tokens // BLOCK - size) * BLOCK, kind]
+    kind = sum(((need > size).astype(jnp.int32) for size in SIZES[:-1]), jnp.zeros_like(need))
+    size = sum(jnp.where(kind == n, size, 0).astype(jnp.int32) for n, size in enumerate(SIZES))
+    return [jnp.minimum(first, tokens // UNIT - size) * UNIT, kind]
 
 
 def both_heads(array):
@@ -172,68 +172,81 @@
 
 
 def fill_segments(seg_row, seg_col):
-    seg_col[...] = jnp.broadcast_to(seg_row[...].astype(F32), (BLOCK, seg_row.shape[1])).T
+    seg_col[...] = jnp.broadcast_to(seg_row[...].astype(F32), (UNIT, seg_row.shape[1])).T
 
 
 def masked_scores(key, query, seg_col, seg_row):
-    same = seg_col == seg_row
-    return jnp.where(jnp.concatenate([same, same], axis=1), dot_nt(key, query), NEG)
+    parts = [seg_col == seg_row[:, n : n + UNIT] for n in range(0, BLOCK, UNIT)]
+    return jnp.where(jnp.concatenate(parts + parts, axis=1), dot_nt(key, query), NEG)
 
 
 def forward_kernel(
-    info, x0, x1, x2, x3, wq, wk, wv, bq, bv, seg_row,
-    q_out, k_out, v_out, c0, c1, c2, c3, o_out, lse_out,
-    xs, seg_col, qs, vt, ctx,
+    project, info, *refs,
 ):
+    if project:
+        x0, x1, x2, x3, wq, wk, wv, bq, bv, seg_row, *refs = refs
+        q_all, k_all, v_all, *outs = refs[:8]
+        o_out, lse_out = outs[3:]
+        parts, first = outs[:3], 1
+        xs, seg_col, qs, vt, ctx = refs[8:]
+    else:
+        q_all, k_all, v_all, seg_row, *refs = refs
+        parts, first = refs[:1], 0
+        o_out, lse_out, seg_col, qs, vt, ctx = refs[1:]
     place = info[0]
-    tokens = xs.shape[0]
+    tokens = q_all.shape[0]
     quarter = tokens // 4
+    each = quarter // BLOCK
 
     @pl.when(pl.program_id(0) == 0)
     def _():
-        for j, ref in enumerate((x0, x1, x2, x3)):
-            xs[pl.ds(pl.multiple_of((place ^ j) * quarter, quarter), quarter), :] = ref[...]
+        if project:
+            for j, ref in enumerate((x0, x1, x2, x3)):
+                xs[pl.ds(pl.multiple_of((place ^ j) * quarter, quarter), quarter), :] = ref[...]
         fill_segments(seg_row, seg_col)
 
-    weights = jnp.concatenate([wq[...], wk[...], wv[...]], axis=1)
-    projected = dot_nn(xs[...], weights)
-    query = (projected[:, :PAIR] + bq[...].astype(F32)).astype(LOW)
-    key = projected[:, PAIR : 2 * PAIR].astype(LOW)
-    value = (projected[:, 2 * PAIR :] + bv[...].astype(F32)).astype(LOW)
-    q_out[...] = query
-    k_out[...] = key
-    v_out[...] = value
+    if project:
+        weights = jnp.concatenate([wq[...], wk[...], wv[...]], axis=1)
+        projected = dot_nn(xs[...], weights)
+        query = (projected[:, :PAIR] + bq[...].astype(F32)).astype(LOW)
+        value = (projected[:, 2 * PAIR :] + bv[...].astype(F32)).astype(LOW)
+        q_all[...] = query
+        k_all[...] = projected[:, PAIR : 2 * PAIR].astype(LOW)
+        v_all[...] = value
+    else:
+        query, value = q_all[...], v_all[...]
     qs[...] = query * jnp.asarray(SCALE, LOW)
     vt[...] = value.T
 
-    def step(b, _):
-        start = pl.multiple_of(b * BLOCK, BLOCK)
-        rows = pl.ds(start, BLOCK)
+    def step(i, _):
+        b = (place ^ (first + i // each)) * each + i % each
+        rows = pl.ds(pl.multiple_of(b * BLOCK, BLOCK), BLOCK)
+        here = pl.ds(pl.multiple_of(i * BLOCK, BLOCK), BLOCK)
 
         def run(window, size):
             row = seg_row[:, rows].astype(F32)
-            scores = masked_scores(k_out[window, :], both_heads(qs[rows, :]), seg_col[window, :], row)
+            scores = masked_scores(k_all[window, :], both_heads(qs[rows, :]), seg_col[window, :], row)
             top = jnp.max(scores, axis=0, keepdims=True)
             expo = jnp.exp(scores - top)
             total = jnp.sum(expo, axis=0, keepdims=True)
             mixed = dot_nn(vt[:, window], expo.astype(LOW)) * (1.0 / total)
-            lse_out[0, pl.ds(b, 1), :] = top + jnp.log(total)
+            lse_out[0, pl.ds(i, 1), :] = top + jnp.log(total)
             mixed = own_heads(mixed)
-            o_out[:, rows] = mixed
-            ctx[rows, :] = mixed.T.astype(LOW)
+            o_out[:, here] = mixed
+            ctx[here, :] = mixed.T.astype(LOW)
 
         each_window(info, b, run)
         return 0
 
-    lax.fori_loop(0, tokens // BLOCK, step, 0)
-    for j, ref in enumerate((c0, c1, c2, c3)):
-        ref[...] = ctx[pl.ds(pl.multiple_of((place ^ j) * quarter, quarter), quarter), :]
+    lax.fori_loop(0, len(parts) * each, step, 0)
+    for n, ref in enumerate(parts):
+        ref[...] = ctx[n * quarter : (n + 1) * quarter, :]
 
 
 def attend_forward(info, quarters, qkv_weight, query_bias, value_bias, seg):
     quarter, width = quarters[0].shape
     tokens, half = 4 * quarter, width // 2
-    pairs = half // PAIR
+    pairs, each = half // PAIR, quarter // BLOCK
 
     def weight_spec(t):
         return pl.BlockSpec((width, PAIR), lambda p, i: (0, (2 * t + i[1]) * pairs + p))
@@ -243,48 +256,81 @@
 
     col = pl.BlockSpec((tokens, PAIR), lambda p, i: (0, p))
     part = pl.BlockSpec((quarter, PAIR), lambda p, i: (0, p))
-    blocks = tokens // BLOCK
-    return pl.pallas_call(
-        forward_kernel,
+
+    def results(count):
+        return (
+            [part] * count
+            + [
+                pl.BlockSpec((PAIR, count * quarter), lambda p, i: (p, 0)),
+                pl.BlockSpec((1, count * each, 2 * BLOCK), lambda p, i: (p, 0, 0)),
+            ],
+            [shaped((quarter, half), LOW)] * count
+            + [
+                shaped((half, count * quarter), F32),
+                shaped((pairs, count * each, 2 * BLOCK), F32),
+            ],
+        )
+
+    def scratch(count):
+        return [
+            pltpu.VMEM((tokens, UNIT), F32),
+            pltpu.VMEM((tokens, PAIR), LOW),
+            pltpu.VMEM((PAIR, tokens), LOW),
+            pltpu.VMEM((count * quarter, PAIR), LOW),
+        ]
+
+    specs, shapes = results(3)
+    query, key, value, *parts, context, lse = pl.pallas_call(
+        functools.partial(forward_kernel, True),
         grid_spec=pltpu.PrefetchScalarGridSpec(
             num_scalar_prefetch=1,
             grid=(pairs,),
             in_specs=[full((quarter, width))] * 4
             + [weight_spec(0), weight_spec(1), weight_spec(2), bias_spec(), bias_spec()]
             + [full((1, tokens))],
-            out_specs=[col] * 3
-            + [part] * 4
-            + [pl.BlockSpec((PAIR, tokens), lambda p, i: (p, 0))]
-            + [pl.BlockSpec((1, blocks, 2 * BLOCK), lambda p, i: (p, 0, 0))],
-            scratch_shapes=[
-                pltpu.VMEM((tokens, width), LOW),
-                pltpu.VMEM((tokens, BLOCK), F32),
-                pltpu.VMEM((tokens, PAIR), LOW),
-                pltpu.VMEM((PAIR, tokens), LOW),
-                pltpu.VMEM((tokens, PAIR), LOW),
-            ],
+            out_specs=[col] * 3 + specs,
+            scratch_shapes=[pltpu.VMEM((tokens, width), LOW)] + scratch(3),
         ),
-        out_shape=[shaped((tokens, half), LOW)] * 3
-        + [shaped((quarter, half), LOW)] * 4
-        + [shaped((half, tokens), F32), shaped((pairs, blocks, 2 * BLOCK), F32)],
+        out_shape=[shaped((tokens, half), LOW)] * 3 + shapes,
         compiler_params=params(VMEM),
         cost_estimate=cost(16),
         name="attend_forward",
     )(info, *quarters, qkv_weight, qkv_weight, qkv_weight, query_bias[None], value_bias[None], seg)
+    specs, shapes = results(1)
+    own, own_context, own_lse = pl.pallas_call(
+        functools.partial(forward_kernel, False),
+        grid_spec=pltpu.PrefetchScalarGridSpec(
+            num_scalar_prefetch=1,
+            grid=(pairs,),
+            in_specs=[col] * 3 + [full((1, tokens))],
+            out_specs=specs,
+            scratch_shapes=scratch(1),
+        ),
+        out_shape=shapes,
+        compiler_params=params(VMEM),
+        cost_estimate=cost(5),
+        name="attend_own",
+    )(info, query, key, value, seg)
+    return query, key, value, [own] + parts, (own_context, context), (own_lse, lse)
 
 
 QKV_ORDERS = ("zyw", "zyw", "yzw")
 
 
 def backward_kernel(
-    n, info, q_in, k_in, v_in, o0, o1, o1b, o2, o3, o_in, lse, seg_row, x_t, vec,
+    n, info, q_in, k_in, v_in, o0, o1, o1b, o2, o3, o_own, o_far, lse_own, lse_far, seg_row, x_t, vec,
     dq_out, dk_out, dv_out, vec_out, w_send, w_keep,
-    seg_col, qs, do, kt, dk, dv, w_rows,
+    seg_col, qs, do, kt, dk, dv, w_rows, o_all, lse,
 ):
     place, core, me = info[0], info[1], info[3]
     tokens = q_in.shape[0]
     quarter = tokens // 4
     fill_segments(seg_row, seg_col)
+    each = quarter // BLOCK
+    o_all[:, :quarter] = o_own[...]
+    o_all[:, quarter:] = o_far[...]
+    lse[:each] = lse_own[0]
+    lse[each:] = lse_far[0]
     for j, ref in enumerate((o0, None, o2, o3)):
         if ref is None:
             at = pl.multiple_of((place ^ 1) * quarter, quarter)
@@ -305,10 +351,12 @@
             row = seg_row[:, rows].astype(F32)
             o_block = do[rows, :]
             query, grad = both_heads(qs[rows, :]), both_heads(o_block)
-            along = o_block.T.astype(F32) * o_in[:, rows]
+            i = (place ^ (b // each)) * each + b % each
+            here = pl.ds(pl.multiple_of(i * BLOCK, BLOCK), BLOCK)
+            along = o_block.T.astype(F32) * o_all[:, here]
             delta = jnp.concatenate([column_sum(along[:DH]), column_sum(along[DH:])], axis=1)
             scores = masked_scores(k_in[window, :], query, seg_col[window, :], row)
-            probs = jnp.exp(scores - lse[0, pl.ds(b, 1), :])
+            probs = jnp.exp(scores - lse[pl.ds(i, 1), :])
             d_scores = (probs * (dot_nt(v_in[window, :], grad) - delta)).astype(LOW)
             dv[window, :] += dot_nn(probs.astype(LOW), grad)
             dk[window, :] += dot_nn(d_scores, query)
@@ -358,20 +406,22 @@
             in_specs=waiting(after)
             + [col] * 3
             + [part, low, high, first, part]
-            + [pl.BlockSpec((PAIR, tokens), lambda p, i: (n, 0))]
-            + [pl.BlockSpec((1, blocks, 2 * BLOCK), lambda p, i: (n, 0, 0))]
+            + [pl.BlockSpec((PAIR, array.shape[1]), lambda p, i: (n, 0)) for array in context]
+            + [pl.BlockSpec((1,) + array.shape[1:], lambda p, i: (n, 0, 0)) for array in lse]
             + [full((1, tokens)), full((width, tokens)), full(vectors.shape)],
             out_specs=[full((tokens, PAIR))] * 3
             + [full(vectors.shape)]
             + [full(weight)] * len(dtypes),
             scratch_shapes=[
-                pltpu.VMEM((tokens, BLOCK), F32),
+                pltpu.VMEM((tokens, UNIT), F32),
                 pltpu.VMEM((tokens, PAIR), LOW),
                 pltpu.VMEM((tokens, PAIR), LOW),
                 pltpu.VMEM((PAIR, tokens), LOW),
                 pltpu.VMEM((tokens, PAIR), F32),
                 pltpu.VMEM((tokens, PAIR), F32),
                 pltpu.VMEM((8, width // 8, 3 * PAIR), F32),
+                pltpu.VMEM((PAIR, tokens), F32),
+                pltpu.VMEM((blocks, 2 * BLOCK), F32),
             ],
         ),
         out_shape=[shaped((tokens, PAIR), LOW)] * 3
@@ -380,7 +430,7 @@
         compiler_params=params(VMEM),
         cost_estimate=cost(8),
         name="attend_backward",
-    )(info, *after, query, key, value, *parts, context, lse, seg, x_t, vectors)
+    )(info, *after, query, key, value, *parts, *context, *lse, seg, x_t, vectors)
 
 
 def normalise(values):
@@ -441,12 +491,15 @@
         turned[0] = low.T
         branch[...] = jnp.zeros_like(branch)
 
-    pre = dot_nn(hid_low[...], up[...]) + bup[...].astype(F32)
-    phi = 0.5 + 0.5 * lax.erf(pre * ROOT_HALF)
-    low = (pre * phi).astype(LOW)
-    act[...] = low
-    slope[...] = phi + pre * (jnp.exp(-0.5 * pre * pre) * ROOT_TWO_PI)
-    branch[...] += dot_nn(low, down[...])
+    size = hid.shape[0] // CHUNKS
+    chunks = [slice(n * size, (n + 1) * size) for n in range(CHUNKS)]
+    pres = [dot_nn(hid_low[rows, :], up[...]) + bup[...].astype(F32) for rows in chunks]
+    for rows, pre in zip(chunks, pres):
+        phi = 0.5 + 0.5 * lax.erf(pre * ROOT_HALF)
+        low = (pre * phi).astype(LOW)
+        act[rows, :] = low
+        slope[rows, :] = phi + pre * (jnp.exp(-0.5 * pre * pre) * ROOT_TWO_PI)
+        branch[rows, :] += dot_nn(low, down[...])
 
     @pl.when(step == pl.num_programs(0) - 1)
     def _():
@@ -965,7 +1018,7 @@
     across = over_seq(far, 1)
     quarters = (own, near, far, across)
 
-    query, key, value, *parts, context, lse = attend_forward(
+    query, key, value, parts, context, lse = attend_forward(
         info, quarters, qkv_weight, query_bias, value_bias, segment
     )
     parts = [parts[0]] + [over_seq(parts[j], j) for j in (1, 2, 3)]

time: 193 us -> 185 us (0.959)
  waiting for transfers between devices: 46.8 us -> 36.8 us
  starting transfers between devices: 37 us -> 39.8 us
    ppermute x23, waiting for transfers between devices: 26.3 us -> 20.3 us  [over_seq(): return lax.ppermute(array, 'seq', [(i, i ^ flip) for i in range(seq_size)])]
    ppermute x18, waiting for transfers between devices: 20.5 us -> 16.5 us  [over_batch(): lax.ppermute(array, 'batch', [(i, i ^ flip) for i in range(batch_size)])]
    ppermute x18, starting transfers between devices: 22.8 us -> 25 us  [over_batch(): lax.ppermute(array, 'batch', [(i, i ^ flip) for i in range(batch_size)])]
    pallas_call x1 -> x2, Pallas kernels: 20.3 us -> 18.9 us  [the longest x1 13.7 us: attend_forward(): pl.pallas_call(functools.partial(forward_kernel, True), grid_spec=pltpu.P...]
    unnamed x48 -> x50, local copies, waits for them, and re-layouts: 6.05 us -> 6.06 us
  transfers between devices with their start and end apart: 41 -> 41, of which waited for: 19 -> 16; matrix products, arithmetic and copies ran while one was open for 4% -> 5% of each run, Pallas kernels for 28% -> 32%
where the time goes in v4:
time: 185 us
  Pallas kernels  89.2 us (48%)
  starting transfers between devices  39.8 us (22%)
  waiting for transfers between devices  36.8 us (20%)
  local copies, waits for them, and re-layouts  12.8 us (7%)
  other arithmetic  4.75 us (3%)
    ppermute x18, starting transfers between devices, over_batch(): lax.ppermute(array, 'batch', [(i, i ^ flip) for i in range(batch_size)])  25 us
    pallas_call x3, Pallas kernels, attend_backward(): pl.pallas_call(ordered(functools.partial(backward_kernel, n), after), gri...  22.8 us
    ppermute x23, waiting for transfers between devices, over_seq(): return lax.ppermute(array, 'seq', [(i, i ^ flip) for i in range(seq_size)])  20.3 us
    ppermute x18, waiting for transfers between devices, over_batch(): lax.ppermute(array, 'batch', [(i, i ^ flip) for i in range(batch_size)])  16.5 us
    ppermute x23, starting transfers between devices, over_seq(): return lax.ppermute(array, 'seq', [(i, i ^ flip) for i in range(seq_size)])  14.8 us
    pallas_call x1, Pallas kernels, attend_forward(): pl.pallas_call(functools.partial(forward_kernel, True), grid_spec=pltpu.P...  13.7 us
    pallas_call x1, Pallas kernels, middle_forward(): pl.pallas_call(ordered(middle_forward_kernel, after), grid_spec=pltpu.Pre...  12.8 us
    pallas_call x1, Pallas kernels, middle_backward(): pl.pallas_call(middle_backward_kernel, grid_spec=pltpu.PrefetchScalarGrid...  10.3 us
  transfers between devices with their start and end apart: 41, of which 16 were waited for; matrix products, arithmetic and copies ran while one was open for 5% of the time, Pallas kernels for 32%

profile of v4, /device:TPU:0, one launch (start us, length us, event | category | flops | bytes accessed | tf_op | source)
XLA Modules:
  0.0 184.8 jit_solution(1087260288949865771)
XLA Ops:
  0.8 1.2 dynamic-slice_bitcast_fusion
  2.0 3.0 %collective-permute-start.1 = (bf16[256,768]{1,0:T(8,128)(2,1)S(1)}, bf16[256,768]{1,0:T(8,128)(2,1)S(1)}, u32[]{:S(2)}, u32[]{:S(2)}) collective-permute-start(bf16[256,768]{1,0:T(8,128)(2,1)S(1)} %get-tuple-element.249), channel_id=1, source_target_pairs={{0,2},{1,3},{2,0},{3,1},{4,6},{5,7},{6,4},{7,5},{8,10},{9,11},{10,... | collective-permute-start | bytes 1179656 | tf_op jit(solution)/shard_map/ppermute | solution.py:979
  6.2 7.9 %collective-permute-done.1.x2.refs_2_ = bf16[256,768]{1,0:T(8,128)(2,1)S(1)} collective-permute-done((bf16[256,768]{1,0:T(8,128)(2,1)S(1)}, bf16[256,768]{1,0:T(8,128)(2,1)S(1)}, u32[]{:S(2)}, u32[]{:S(2)}) %collective-permute-start.1) | collective-permute-done | bytes 393248 | tf_op jit(solution)/shard_map/ppermute | solution.py:979
  14.8 1.0 collective-permute-done.2.x3.refs_3_
  15.8 2.0 %copy-done.5 = bf16[768,2304]{1,0:T(8,128)(2,1)S(1)} copy-done((bf16[768,2304]{1,0:T(8,128)(2,1)S(1)}, bf16[768,2304]{1,0:T(8,128)(2,1)}, u32[]{:S(2)}) %copy-start.5) | copy-done | bytes 3538968
  17.8 13.7 %attend_forward.1 = (bf16[1024,384]{1,0:T(8,128)(2,1)S(1)}, bf16[1024,384]{1,0:T(8,128)(2,1)S(1)}, bf16[1024,384]{1,0:T(8,128)(2,1)S(1)}, bf16[256,384]{1,0:T(8,...) custom-call(s32[12]{0:T(128)S(1)} %concatenate.6.info, ...), custom_call_target="tpu_custom_call" | custom-call | flops 9600000000 | tf_op jit(solution)/shard_map/attend_forward/pallas_call | solution.py:283
  31.6 1.1 collective-permute-start.3
  32.6 1.4 collective-permute-start.5
  34.1 1.0 turn.1.refs_0_.refs_14_
  35.2 5.1 %attend_own.1 = (bf16[256,384]{1,0:T(8,128)(2,1)S(1)}, f32[384,256]{1,0:T(8,128)S(1)}, f32[3,1,512]{2,1,0:T(1,128)S(1)}) custom-call(s32[12]{0:T(128)S(1)} %concatenate.6.info, bf16[1024,384]{1,0:T(8,128)(2,1)S(1)} %get-tuple-element.123.refs_0_.refs_1_, bf16[1024,384]{1,0:T(8,128)(2,1)S(1)} %get-tuple-element.124.refs_1_.refs_2_, ...), custom_call_target="tpu_custom_call" | custom-call | flops 3000000000 | tf_op jit(solution)/shard_map/attend_own/pallas_call | solution.py:300
  40.4 2.5 %collective-permute-done.5.refs_4_ = bf16[256,384]{1,0:T(8,128)(2,1)S(1)} collective-permute-done((bf16[256,384]{1,0:T(8,128)(2,1)S(1)}, bf16[256,384]{1,0:T(8,128)(2,1)S(1)}, u32[]{:S(2)}, u32[]{:S(2)}) %collective-permute-start.5) | collective-permute-done | bytes 196640 | tf_op jit(solution)/shard_map/ppermute | solution.py:979
  42.9 12.8 %middle_forward.1 = (bf16[2,256,768]{2,1,0:T(8,128)(2,1)}, f32[512,768]{1,0:T(8,128)S(1)}, f32[512,768]{1,0:T(8,128)S(1)}, f32[512,1]{1,0:T(8,128)S(1)}, bf16[2,...) custom-call(s32[12]{0:T(128)S(1)} %concatenate.6.info, ...), custom_call_target="tpu_custom_call" | custom-call | flops 10800000000 | tf_op jit(solution)/shard_map/middle_forward/pallas_call | solution.py:544
  56.9 10.3 %middle_backward.1 = (bf16[1536,768]{1,0:T(8,128)(2,1)S(1)}, bf16[2,512,768]{2,1,0:T(8,128)(2,1)S(1)}, f32[512,768]{1,0:T(8,128)S(1)}, bf16[256,384]{1,0:T(8,128...) custom-call(s32[12]{0:T(128)S(1)} %concatenate.6.info, ...), custom_call_target="tpu_custom_call" | custom-call | flops 9600000000 | tf_op jit(solution)/shard_map/middle_backward/pallas_call | solution.py:658
  67.8 7.8 %down_grad.1 = (bf16[8,96,384]{2,1,0:T(8,128)(2,1)S(1)}, f32[8,96,384]{2,1,0:T(8,128)S(1)}, bf16[8,96,384]{2,1,0:T(8,128)(2,1)S(1)}, f32[8,96,384]{2,1,0:T(8,128)S(1)}) custom-call(s32[12]{0:T(128)S(1)} %concatenate.6.info, f32[8,128]{1,0:T(8,128)S(1)} %mark.1.refs_0_, bf16[2,192,512]{2,1,0:T(8,128)(2,1)S(1)} %get-tuple-element.144.refs_1_, ...), custom_call_target="tpu_custom_call" | custom-call | flops 4800000000 | tf_op jit(solution)/shard_map/down_grad/pallas_call | solution.py:718
  75.6 2.6 %collective-permute-start.12 = (bf16[8,96,384]{2,1,0:T(8,128)(2,1)S(1)}, bf16[8,96,384]{2,1,0:T(8,128)(2,1)S(1)}, u32[]{:S(2)}, u32[]{:S(2)}) collective-permute-start(bf16[8,96,384]{2,1,0:T(8,128)(2,1)S(1)} %get-tuple-element.158), channel_id=1, source_target_pairs={{0,8},{4,12},{8,0},{12,4},{16,24},{20,28},{24,16},{28,20},{1,9},{5... | collective-permute-start | bytes 1769480 | tf_op jit(solution)/shard_map/ppermute | solution.py:982
  79.0 7.0 %up_grad.1 = (bf16[8,96,384]{2,1,0:T(8,128)(2,1)S(1)}, f32[8,96,384]{2,1,0:T(8,128)S(1)}, bf16[12,96,384]{2,1,0:T(8,128)(2,1)S(1)}, f32[12,96,384]{2,1,0:T(8,128)S(1)}) custom-call(s32[12]{0:T(128)S(1)} %concatenate.6.info, f32[8,96,384]{2,1,0:T(8,128)S(1)} %get-tuple-element.145.refs_0_.refs_1_, bf16[2,768,512]{2,1,0:T(8,128)(2,1)S(1)} %get-tuple-element.139.refs_1_, ...), custom_call_target="tpu_custom_call" | custom-call | flops 6000000000 | tf_op jit(solution)/shard_map/up_grad/pallas_call | solution.py:781
  86.0 2.1 %collective-permute-start.15 = (bf16[12,96,384]{2,1,0:T(8,128)(2,1)S(1)}, bf16[12,96,384]{2,1,0:T(8,128)(2,1)S(1)}, u32[]{:S(2)}, u32[]{:S(2)}) collective-permute-start(bf16[12,96,384]{2,1,0:T(8,128)(2,1)S(1)} %get-tuple-element.167), channel_id=1, source_target_pairs={{0,4},{4,0},{8,12},{12,8},{16,20},{20,16},{24,28},{28,24},{1,5},{5... | collective-permute-start | bytes 2654216 | tf_op jit(solution)/shard_map/ppermute | solution.py:982
  88.4 7.5 %attend_backward.3 = (bf16[1024,128]{1,0:T(8,128)(2,1)S(1)}, bf16[1024,128]{1,0:T(8,128)(2,1)S(1)}, bf16[1024,128]{1,0:T(8,128)(2,1)S(1)}, f32[16,768]{1,0:T(8,1...) custom-call(s32[12]{0:T(128)S(1)} %concatenate.6.info, ...), custom_call_target="tpu_custom_call" | custom-call | flops 4800000000 | tf_op jit(solution)/shard_map/attend_backward/pallas_call | solution.py:401
  96.4 1.8 collective-permute-start.16
  98.2 0.9 collective-permute-start.17
  99.1 7.8 %attend_backward.4 = (bf16[1024,128]{1,0:T(8,128)(2,1)S(1)}, bf16[1024,128]{1,0:T(8,128)(2,1)S(1)}, bf16[1024,128]{1,0:T(8,128)(2,1)S(1)}, f32[16,768]{1,0:T(8,1...) custom-call(s32[12]{0:T(128)S(1)} %concatenate.6.info, f32[8,128]{1,0:T(8,128)S(1)} %get-tuple-element.162.refs_0_, ...), custom_call_target="tpu_custom_call" | custom-call | flops 4800000000 | tf_op jit(solution)/shard_map/attend_backward/pallas_call | solution.py:401
  106.9 5.2 %collective-permute-done.16.refs_6_ = bf16[4,96,384]{2,1,0:T(8,128)(2,1)S(1)} collective-permute-done((bf16[4,96,384]{2,1,0:T(8,128)(2,1)S(1)}, bf16[4,96,384]{2,1,0:T(8,128)(2,1)S(1)}, u32[]{:S(2)}, u32[]{:S(2)}) %collective-permute-start.16) | collective-permute-done | bytes 294944 | tf_op jit(solution)/shard_map/ppermute | solution.py:979
  113.2 1.1 collective-permute-start.20
  114.3 1.7 collective-permute-start.22
  116.0 1.7 collective-permute-start.21
  117.7 7.5 %attend_backward.5 = (bf16[1024,128]{1,0:T(8,128)(2,1)S(1)}, bf16[1024,128]{1,0:T(8,128)(2,1)S(1)}, bf16[1024,128]{1,0:T(8,128)(2,1)S(1)}, f32[16,768]{1,0:T(8,1...) custom-call(s32[12]{0:T(128)S(1)} %concatenate.6.info, f32[8,128]{1,0:T(8,128)S(1)} %get-tuple-element.175.refs_0_, ...), custom_call_target="tpu_custom_call" | custom-call | flops 4800000000 | tf_op jit(solution)/shard_map/attend_backward/pallas_call | solution.py:401
  125.3 2.9 %collective-permute-done.22.refs_8_ = bf16[4,96,384]{2,1,0:T(8,128)(2,1)S(1)} collective-permute-done((bf16[4,96,384]{2,1,0:T(8,128)(2,1)S(1)}, bf16[4,96,384]{2,1,0:T(8,128)(2,1)S(1)}, u32[]{:S(2)}, u32[]{:S(2)}) %collective-permute-start.22) | collective-permute-done | bytes 294944 | tf_op jit(solution)/shard_map/ppermute | solution.py:982
  128.5 2.7 %collective-permute-start.25 = (bf16[5,96,384]{2,1,0:T(8,128)(2,1)S(1)}, bf16[5,96,384]{2,1,0:T(8,128)(2,1)S(1)}, u32[]{:S(2)}, u32[]{:S(2)}) collective-permute-start(bf16[5,96,384]{2,1,0:T(8,128)(2,1)S(1)} %get-tuple-element.204), channel_id=1, source_target_pairs={{0,8},{4,12},{8,0},{12,4},{16,24},{20,28},{24,16},{28,20},{1,9},{5... | collective-permute-start | bytes 1105928 | tf_op jit(solution)/shard_map/ppermute | solution.py:982
  131.8 1.5 collective-permute-start.27
  133.2 2.8 %collective-permute-start.26 = (bf16[1,96,384]{2,1,0:T(8,128)(2,1)S(1)}, bf16[1,96,384]{2,1,0:T(8,128)(2,1)S(1)}, u32[]{:S(2)}, u32[]{:S(2)}) collective-permute-start(bf16[1,96,384]{2,1,0:T(8,128)(2,1)S(1)} %get-tuple-element.206), channel_id=1, source_target_pairs={{0,16},{4,20},{8,24},{12,28},{16,0},{20,4},{24,8},{28,12},{1,17},{... | collective-permute-start | bytes 221192 | tf_op jit(solution)/shard_map/ppermute | solution.py:982
  136.0 5.1 %input_part.1 = (f32[2,256,768]{2,1,0:T(8,128)S(1)}, f32[2,256,768]{2,1,0:T(8,128)}) custom-call(s32[12]{0:T(128)S(1)} %concatenate.6.info, f32[8,128]{1,0:T(8,128)S(1)} %get-tuple-element.188.refs_0_, bf16[1024,128]{1,0:T(8,128)(2,1)S(1)} %get-tuple-element.189.refs_1_, bf16[1024,128]{1,0:T(8,128)(2,1)S(1)} %get-tuple-element.190.refs_2_, ...), custom_call_target="tpu_custom_call" | custom-call | flops 3600000000 | tf_op jit(solution)/shard_map/input_part/pallas_call | solution.py:831
  141.1 2.4 %collective-permute-done.27.refs_8_ = bf16[4,96,384]{2,1,0:T(8,128)(2,1)S(1)} collective-permute-done((bf16[4,96,384]{2,1,0:T(8,128)(2,1)S(1)}, bf16[4,96,384]{2,1,0:T(8,128)(2,1)S(1)}, u32[]{:S(2)}, u32[]{:S(2)}) %collective-permute-start.27) | collective-permute-done | bytes 294944 | tf_op jit(solution)/shard_map/ppermute | solution.py:982
  146.6 1.5 collective-permute-start.30
  148.2 3.3 %collective-permute-start.33 = (bf16[3,96,384]{2,1,0:T(8,128)(2,1)}, bf16[3,96,384]{2,1,0:T(8,128)(2,1)S(1)}, u32[]{:S(2)}, u32[]{:S(2)}) collective-permute-start(bf16[3,96,384]{2,1,0:T(8,128)(2,1)} %copy-done.9), channel_id=1, source_target_pairs={{0,16},{4,20},{8,24},{12,28},{16,0},{20,4},{24,8},{28,12},{1,17},{... | collective-permute-start | bytes 663560 | tf_op jit(solution)/shard_map/ppermute | solution.py:982
  153.1 1.7 slice.86
  154.8 1.2 collective-permute-done.31
  156.0 3.5 %collective-permute-done.32.refs_3_ = bf16[2,96,384]{2,1,0:T(8,128)(2,1)S(1)} collective-permute-done((bf16[2,96,384]{2,1,0:T(8,128)(2,1)}, bf16[2,96,384]{2,1,0:T(8,128)(2,1)S(1)}, u32[]{:S(2)}, u32[]{:S(2)}) %collective-permute-start.32) | collective-permute-done | bytes 147488 | tf_op jit(solution)/shard_map/ppermute | solution.py:982
  159.5 2.0 %collective-permute-done.33.refs_5_ = bf16[3,96,384]{2,1,0:T(8,128)(2,1)S(1)} collective-permute-done((bf16[3,96,384]{2,1,0:T(8,128)(2,1)}, bf16[3,96,384]{2,1,0:T(8,128)(2,1)S(1)}, u32[]{:S(2)}, u32[]{:S(2)}) %collective-permute-start.33) | collective-permute-done | bytes 221216 | tf_op jit(solution)/shard_map/ppermute | solution.py:982
  161.5 1.1 copy-done.4
  162.6 1.6 add.57
  164.9 2.9 %collective-permute-start.35 = (bf16[1,96,384]{2,1,0:T(8,128)(2,1)S(1)}, bf16[1,96,384]{2,1,0:T(8,128)(2,1)S(1)}, u32[]{:S(2)}, u32[]{:S(2)}) collective-permute-start(bf16[1,96,384]{2,1,0:T(8,128)(2,1)S(1)} %get-tuple-element.223), channel_id=1, source_target_pairs={{0,16},{4,20},{8,24},{12,28},{16,0},{20,4},{24,8},{28,12},{1,17},{... | collective-permute-start | bytes 221192 | tf_op jit(solution)/shard_map/ppermute | solution.py:982
  169.0 2.3 %collective-permute-done.40 = bf16[96,192]{1,0:T(8,128)(2,1)S(1)} collective-permute-done((bf16[96,192]{1,0:T(8,128)(2,1)S(1)}, bf16[96,192]{1,0:T(8,128)(2,1)S(1)}, u32[]{:S(2)}, u32[]{:S(2)}) %collective-permute-start.40) | collective-permute-done | bytes 36896 | tf_op jit(solution)/shard_map/ppermute | solution.py:982
  172.6 2.8 %collective-permute-done.29.refs_2_ = bf16[256,768]{1,0:T(8,128)(2,1)S(1)} collective-permute-done((bf16[256,768]{1,0:T(8,128)(2,1)S(1)}, bf16[256,768]{1,0:T(8,128)(2,1)S(1)}, u32[]{:S(2)}, u32[]{:S(2)}) %collective-permute-start.29) | collective-permute-done | bytes 393248 | tf_op jit(solution)/shard_map/ppermute | solution.py:979
  175.4 1.0 share.1
  177.0 1.4 collective-permute-start.38
  178.6 1.2 pad_maximum_fusion
  179.9 1.6 collective-permute-done.39
  183.4 1.4 gather.1
  (141 shorter events, 17.8 us)
Async XLA Ops:
  0.7 13.7 %copy-start.15 = (bf16[768]{0:T(1024)(128)(2,1)S(1)}, bf16[768]{0:T(1024)(128)(2,1)}, u32[]{:S(2)}) copy-start(bf16[768]{0:T(1024)(128)(2,1)} %param.23) | copy-start | bytes 4612
  0.7 13.7 %copy-start.11 = (bf16[3072]{0:T(1024)(128)(2,1)S(1)}, bf16[3072]{0:T(1024)(128)(2,1)}, u32[]{:S(2)}) copy-start(bf16[3072]{0:T(1024)(128)(2,1)} %param.26) | copy-start | bytes 18436
  0.7 13.7 %copy-start.16 = (bf16[768]{0:T(1024)(128)(2,1)S(1)}, bf16[768]{0:T(1024)(128)(2,1)}, u32[]{:S(2)}) copy-start(bf16[768]{0:T(1024)(128)(2,1)} %param.22) | copy-start | bytes 4612
  0.7 13.7 %copy-start.17 = (bf16[768]{0:T(1024)(128)(2,1)S(1)}, bf16[768]{0:T(1024)(128)(2,1)}, u32[]{:S(2)}) copy-start(bf16[768]{0:T(1024)(128)(2,1)} %param.24) | copy-start | bytes 4612
  0.7 13.7 %copy-start.18 = (bf16[768]{0:T(1024)(128)(2,1)S(1)}, bf16[768]{0:T(1024)(128)(2,1)}, u32[]{:S(2)}) copy-start(bf16[768]{0:T(1024)(128)(2,1)} %param.28) | copy-start | bytes 4612
  0.7 13.7 %copy-start.19 = (bf16[768]{0:T(1024)(128)(2,1)S(1)}, bf16[768]{0:T(1024)(128)(2,1)}, u32[]{:S(2)}) copy-start(bf16[768]{0:T(1024)(128)(2,1)} %param.29) | copy-start | bytes 4612
  0.7 13.7 %copy-start.20 = (bf16[768]{0:T(1024)(128)(2,1)S(1)}, bf16[768]{0:T(1024)(128)(2,1)}, u32[]{:S(2)}) copy-start(bf16[768]{0:T(1024)(128)(2,1)} %param.30) | copy-start | bytes 4612
  2.0 12.1 %collective-permute-start.1 = (bf16[256,768]{1,0:T(8,128)(2,1)S(1)}, bf16[256,768]{1,0:T(8,128)(2,1)S(1)}, u32[]{:S(2)}, u32[]{:S(2)}) collective-permute-start(bf16[256,768]{1,0:T(8,128)(2,1)S(1)} %get-tuple-element.249), channel_id=1, source_target_pairs={{0,2},{1,3},{2,0},{3,1},{4,6},{5,7},{6,4},{7,5},{8,10},{9,11},{10,... | collective-permute-start | bytes 1179656 | tf_op jit(solution)/shard_map/ppermute | solution.py:979
  5.0 9.9 %collective-permute-start = (bf16[256,768]{1,0:T(8,128)(2,1)S(1)}, bf16[256,768]{1,0:T(8,128)(2,1)S(1)}, u32[]{:S(2)}, u32[]{:S(2)}) collective-permute-start(bf16[256,768]{1,0:T(8,128)(2,1)S(1)} %get-tuple-element.250.x0.refs_0_), channel_id=1, source_target_pairs={{0,1},{1,0},{2,3},{3,2},{4,5},{5,4},{6,7},{7,6},{8,9},{9,8},{10,11... | collective-permute-start | bytes 1179656 | tf_op jit(solution)/shard_map/ppermute | solution.py:979
  14.1 1.7 collective-permute-start.2
  31.6 8.7 %collective-permute-start.3 = (bf16[256,384]{1,0:T(8,128)(2,1)S(1)}, bf16[256,384]{1,0:T(8,128)(2,1)S(1)}, u32[]{:S(2)}, u32[]{:S(2)}) collective-permute-start(bf16[256,384]{1,0:T(8,128)(2,1)S(1)} %get-tuple-element.127), channel_id=1, source_target_pairs={{0,1},{1,0},{2,3},{3,2},{4,5},{5,4},{6,7},{7,6},{8,9},{9,8},{10,11... | collective-permute-start | bytes 589832 | tf_op jit(solution)/shard_map/ppermute | solution.py:979
  32.6 7.8 %collective-permute-start.4 = (bf16[256,384]{1,0:T(8,128)(2,1)S(1)}, bf16[256,384]{1,0:T(8,128)(2,1)S(1)}, u32[]{:S(2)}, u32[]{:S(2)}) collective-permute-start(bf16[256,384]{1,0:T(8,128)(2,1)S(1)} %get-tuple-element.128), channel_id=1, source_target_pairs={{0,2},{1,3},{2,0},{3,1},{4,6},{5,7},{6,4},{7,5},{8,10},{9,11},{10,... | collective-permute-start | bytes 589832 | tf_op jit(solution)/shard_map/ppermute | solution.py:979
  32.6 10.2 %collective-permute-start.5 = (bf16[256,384]{1,0:T(8,128)(2,1)S(1)}, bf16[256,384]{1,0:T(8,128)(2,1)S(1)}, u32[]{:S(2)}, u32[]{:S(2)}) collective-permute-start(bf16[256,384]{1,0:T(8,128)(2,1)S(1)} %get-tuple-element.129), channel_id=1, source_target_pairs={{0,3},{1,2},{2,1},{3,0},{4,7},{5,6},{6,5},{7,4},{8,11},{9,10},{10,... | collective-permute-start | bytes 589832 | tf_op jit(solution)/shard_map/ppermute | solution.py:979
  55.7 11.6 %collective-permute-start.7 = (bf16[512,3072]{1,0:T(8,128)(2,1)}, bf16[512,3072]{1,0:T(8,128)(2,1)S(1)}, u32[]{:S(2)}, u32[]{:S(2)}) collective-permute-start(bf16[512,3072]{1,0:T(8,128)(2,1)} %get-tuple-element.140.refs_3_), channel_id=1, source_target_pairs={{0,1},{1,0},{2,3},{3,2},{4,5},{5,4},{6,7},{7,6},{8,9},{9,8},{10,11... | collective-permute-start | bytes 9437192 | tf_op jit(solution)/shard_map/ppermute | solution.py:979
  56.4 10.9 %collective-permute-start.6 = (bf16[2,768,512]{2,1,0:T(8,128)(2,1)S(1)}, bf16[2,768,512]{2,1,0:T(8,128)(2,1)S(1)}, u32[]{:S(2)}, u32[]{:S(2)}) collective-permute-start(bf16[2,768,512]{2,1,0:T(8,128)(2,1)S(1)} %get-tuple-element.139.refs_1_), channel_id=1, source_target_pairs={{0,1},{1,0},{2,3},{3,2},{4,5},{5,4},{6,7},{7,6},{8,9},{9,8},{10,11... | collective-permute-start | bytes 4718600 | tf_op jit(solution)/shard_map/ppermute | solution.py:979
  56.4 10.8 %collective-permute-start.8 = (bf16[384,512]{1,0:T(8,128)(2,1)S(1)}, bf16[384,512]{1,0:T(8,128)(2,1)S(1)}, u32[]{:S(2)}, u32[]{:S(2)}) collective-permute-start(bf16[384,512]{1,0:T(8,128)(2,1)S(1)} %get-tuple-element.141), channel_id=1, source_target_pairs={{0,1},{1,0},{2,3},{3,2},{4,5},{5,4},{6,7},{7,6},{8,9},{9,8},{10,11... | collective-permute-start | bytes 1179656 | tf_op jit(solution)/shard_map/ppermute | solution.py:979
  67.3 11.7 %collective-permute-start.9 = (bf16[1536,768]{1,0:T(8,128)(2,1)S(1)}, bf16[1536,768]{1,0:T(8,128)(2,1)S(1)}, u32[]{:S(2)}, u32[]{:S(2)}) collective-permute-start(bf16[1536,768]{1,0:T(8,128)(2,1)S(1)} %get-tuple-element.147), channel_id=1, source_target_pairs={{0,1},{1,0},{2,3},{3,2},{4,5},{5,4},{6,7},{7,6},{8,9},{9,8},{10,11... | collective-permute-start | bytes 7077896 | tf_op jit(solution)/shard_map/ppermute | solution.py:979
  67.4 11.5 %collective-permute-start.10 = (bf16[2,256,384]{2,1,0:T(8,128)(2,1)S(1)}, bf16[2,256,384]{2,1,0:T(8,128)(2,1)S(1)}, u32[]{:S(2)}, u32[]{:S(2)}) collective-permute-start(bf16[2,256,384]{2,1,0:T(8,128)(2,1)S(1)} %get-tuple-element.151), channel_id=1, source_target_pairs={{0,2},{1,3},{2,0},{3,1},{4,6},{5,7},{6,4},{7,5},{8,10},{9,11},{10,... | collective-permute-start | bytes 1179656 | tf_op jit(solution)/shard_map/ppermute | solution.py:979
  75.6 20.3 %collective-permute-start.12 = (bf16[8,96,384]{2,1,0:T(8,128)(2,1)S(1)}, bf16[8,96,384]{2,1,0:T(8,128)(2,1)S(1)}, u32[]{:S(2)}, u32[]{:S(2)}) collective-permute-start(bf16[8,96,384]{2,1,0:T(8,128)(2,1)S(1)} %get-tuple-element.158), channel_id=1, source_target_pairs={{0,8},{4,12},{8,0},{12,4},{16,24},{20,28},{24,16},{28,20},{1,9},{5... | collective-permute-start | bytes 1769480 | tf_op jit(solution)/shard_map/ppermute | solution.py:982
  78.2 17.7 %collective-permute-start.13 = (bf16[8,96,384]{2,1,0:T(8,128)(2,1)S(1)}, bf16[8,96,384]{2,1,0:T(8,128)(2,1)S(1)}, u32[]{:S(2)}, u32[]{:S(2)}) collective-permute-start(bf16[8,96,384]{2,1,0:T(8,128)(2,1)S(1)} %get-tuple-element.160), channel_id=1, source_target_pairs={{0,2},{1,3},{2,0},{3,1},{4,6},{5,7},{6,4},{7,5},{8,10},{9,11},{10,... | collective-permute-start | bytes 1769480 | tf_op jit(solution)/shard_map/ppermute | solution.py:979
  78.9 9.5 %collective-permute-start.11 = (bf16[256,384]{1,0:T(8,128)(2,1)S(1)}, bf16[256,384]{1,0:T(8,128)(2,1)S(1)}, u32[]{:S(2)}, u32[]{:S(2)}) collective-permute-start(bf16[256,384]{1,0:T(8,128)(2,1)S(1)} %slice_bitcast_fusion.1), channel_id=1, source_target_pairs={{0,1},{1,0},{2,3},{3,2},{4,5},{5,4},{6,7},{7,6},{8,9},{9,8},{10,11... | collective-permute-start | bytes 589832 | tf_op jit(solution)/shard_map/ppermute | solution.py:979
  86.0 26.2 %collective-permute-start.15 = (bf16[12,96,384]{2,1,0:T(8,128)(2,1)S(1)}, bf16[12,96,384]{2,1,0:T(8,128)(2,1)S(1)}, u32[]{:S(2)}, u32[]{:S(2)}) collective-permute-start(bf16[12,96,384]{2,1,0:T(8,128)(2,1)S(1)} %get-tuple-element.167), channel_id=1, source_target_pairs={{0,4},{4,0},{8,12},{12,8},{16,20},{20,16},{24,28},{28,24},{1,5},{5... | collective-permute-start | bytes 2654216 | tf_op jit(solution)/shard_map/ppermute | solution.py:982
  88.1 24.1 %collective-permute-start.14 = (bf16[8,96,384]{2,1,0:T(8,128)(2,1)S(1)}, bf16[8,96,384]{2,1,0:T(8,128)(2,1)S(1)}, u32[]{:S(2)}, u32[]{:S(2)}) collective-permute-start(bf16[8,96,384]{2,1,0:T(8,128)(2,1)S(1)} %get-tuple-element.165), channel_id=1, source_target_pairs={{0,2},{1,3},{2,0},{3,1},{4,6},{5,7},{6,4},{7,5},{8,10},{9,11},{10,... | collective-permute-start | bytes 1769480 | tf_op jit(solution)/shard_map/ppermute | solution.py:979
  96.2 10.8 %collective-permute-start.18 = (bf16[4,96,384]{2,1,0:T(8,128)(2,1)S(1)}, bf16[4,96,384]{2,1,0:T(8,128)(2,1)S(1)}, u32[]{:S(2)}, u32[]{:S(2)}) collective-permute-start(bf16[4,96,384]{2,1,0:T(8,128)(2,1)S(1)} %get-tuple-element.173), channel_id=1, source_target_pairs={{0,8},{4,12},{8,0},{12,4},{16,24},{20,28},{24,16},{28,20},{1,9},{5... | collective-permute-start | bytes 884744 | tf_op jit(solution)/shard_map/ppermute | solution.py:982
  96.4 15.8 %collective-permute-start.16 = (bf16[4,96,384]{2,1,0:T(8,128)(2,1)S(1)}, bf16[4,96,384]{2,1,0:T(8,128)(2,1)S(1)}, u32[]{:S(2)}, u32[]{:S(2)}) collective-permute-start(bf16[4,96,384]{2,1,0:T(8,128)(2,1)S(1)} %get-tuple-element.169), channel_id=1, source_target_pairs={{0,2},{1,3},{2,0},{3,1},{4,6},{5,7},{6,4},{7,5},{8,10},{9,11},{10,... | collective-permute-start | bytes 884744 | tf_op jit(solution)/shard_map/ppermute | solution.py:979
  98.2 13.9 %collective-permute-start.17 = (bf16[4,96,384]{2,1,0:T(8,128)(2,1)S(1)}, bf16[4,96,384]{2,1,0:T(8,128)(2,1)S(1)}, u32[]{:S(2)}, u32[]{:S(2)}) collective-permute-start(bf16[4,96,384]{2,1,0:T(8,128)(2,1)S(1)} %get-tuple-element.171), channel_id=1, source_target_pairs={{0,8},{4,12},{8,0},{12,4},{16,24},{20,28},{24,16},{28,20},{1,9},{5... | collective-permute-start | bytes 884744 | tf_op jit(solution)/shard_map/ppermute | solution.py:982
  112.6 15.6 %collective-permute-start.19 = (bf16[6,96,384]{2,1,0:T(8,128)(2,1)S(1)}, bf16[6,96,384]{2,1,0:T(8,128)(2,1)S(1)}, u32[]{:S(2)}, u32[]{:S(2)}) collective-permute-start(bf16[6,96,384]{2,1,0:T(8,128)(2,1)S(1)} %get-tuple-element.179), channel_id=1, source_target_pairs={{0,4},{4,0},{8,12},{12,8},{16,20},{20,16},{24,28},{28,24},{1,5},{5... | collective-permute-start | bytes 1327112 | tf_op jit(solution)/shard_map/ppermute | solution.py:982
  113.2 14.9 %collective-permute-start.20 = (bf16[6,96,384]{2,1,0:T(8,128)(2,1)S(1)}, bf16[6,96,384]{2,1,0:T(8,128)(2,1)S(1)}, u32[]{:S(2)}, u32[]{:S(2)}) collective-permute-start(bf16[6,96,384]{2,1,0:T(8,128)(2,1)S(1)} %get-tuple-element.181), channel_id=1, source_target_pairs={{0,2},{1,3},{2,0},{3,1},{4,6},{5,7},{6,4},{7,5},{8,10},{9,11},{10,... | collective-permute-start | bytes 1327112 | tf_op jit(solution)/shard_map/ppermute | solution.py:979
  114.3 13.8 %collective-permute-start.22 = (bf16[4,96,384]{2,1,0:T(8,128)(2,1)S(1)}, bf16[4,96,384]{2,1,0:T(8,128)(2,1)S(1)}, u32[]{:S(2)}, u32[]{:S(2)}) collective-permute-start(bf16[4,96,384]{2,1,0:T(8,128)(2,1)S(1)} %get-tuple-element.185), channel_id=1, source_target_pairs={{0,8},{4,12},{8,0},{12,4},{16,24},{20,28},{24,16},{28,20},{1,9},{5... | collective-permute-start | bytes 884744 | tf_op jit(solution)/shard_map/ppermute | solution.py:982
  116.0 12.1 %collective-permute-start.21 = (bf16[4,96,384]{2,1,0:T(8,128)(2,1)S(1)}, bf16[4,96,384]{2,1,0:T(8,128)(2,1)S(1)}, u32[]{:S(2)}, u32[]{:S(2)}) collective-permute-start(bf16[4,96,384]{2,1,0:T(8,128)(2,1)S(1)} %get-tuple-element.183), channel_id=1, source_target_pairs={{0,16},{4,20},{8,24},{12,28},{16,0},{20,4},{24,8},{28,12},{1,17},{... | collective-permute-start | bytes 884744 | tf_op jit(solution)/shard_map/ppermute | solution.py:982
  128.5 15.0 %collective-permute-start.25 = (bf16[5,96,384]{2,1,0:T(8,128)(2,1)S(1)}, bf16[5,96,384]{2,1,0:T(8,128)(2,1)S(1)}, u32[]{:S(2)}, u32[]{:S(2)}) collective-permute-start(bf16[5,96,384]{2,1,0:T(8,128)(2,1)S(1)} %get-tuple-element.204), channel_id=1, source_target_pairs={{0,8},{4,12},{8,0},{12,4},{16,24},{20,28},{24,16},{28,20},{1,9},{5... | collective-permute-start | bytes 1105928 | tf_op jit(solution)/shard_map/ppermute | solution.py:982
  131.2 9.9 %collective-permute-start.24 = (bf16[4,96,384]{2,1,0:T(8,128)(2,1)S(1)}, bf16[4,96,384]{2,1,0:T(8,128)(2,1)S(1)}, u32[]{:S(2)}, u32[]{:S(2)}) collective-permute-start(bf16[4,96,384]{2,1,0:T(8,128)(2,1)S(1)} %get-tuple-element.202), channel_id=1, source_target_pairs={{0,4},{4,0},{8,12},{12,8},{16,20},{20,16},{24,28},{28,24},{1,5},{5... | collective-permute-start | bytes 884744 | tf_op jit(solution)/shard_map/ppermute | solution.py:982
  131.8 11.7 %collective-permute-start.27 = (bf16[4,96,384]{2,1,0:T(8,128)(2,1)S(1)}, bf16[4,96,384]{2,1,0:T(8,128)(2,1)S(1)}, u32[]{:S(2)}, u32[]{:S(2)}) collective-permute-start(bf16[4,96,384]{2,1,0:T(8,128)(2,1)S(1)} %get-tuple-element.208), channel_id=1, source_target_pairs={{0,4},{4,0},{8,12},{12,8},{16,20},{20,16},{24,28},{28,24},{1,5},{5... | collective-permute-start | bytes 884744 | tf_op jit(solution)/shard_map/ppermute | solution.py:982
  133.2 7.9 %collective-permute-start.26 = (bf16[1,96,384]{2,1,0:T(8,128)(2,1)S(1)}, bf16[1,96,384]{2,1,0:T(8,128)(2,1)S(1)}, u32[]{:S(2)}, u32[]{:S(2)}) collective-permute-start(bf16[1,96,384]{2,1,0:T(8,128)(2,1)S(1)} %get-tuple-element.206), channel_id=1, source_target_pairs={{0,16},{4,20},{8,24},{12,28},{16,0},{20,4},{24,8},{28,12},{1,17},{... | collective-permute-start | bytes 221192 | tf_op jit(solution)/shard_map/ppermute | solution.py:982
  136.0 10.0 %collective-permute-start.23 = (f32[16,768]{1,0:T(8,128)S(1)}, f32[16,768]{1,0:T(8,128)S(1)}, u32[]{:S(2)}, u32[]{:S(2)}) collective-permute-start(f32[16,768]{1,0:T(8,128)S(1)} %get-tuple-element.200.refs_0_), channel_id=1, source_target_pairs={{0,1},{1,0},{2,3},{3,2},{4,5},{5,4},{6,7},{7,6},{8,9},{9,8},{10,11... | collective-permute-start | bytes 147464 | tf_op jit(solution)/shard_map/ppermute | solution.py:979
  146.0 16.6 %collective-permute-start.28 = (f32[2,256,768]{2,1,0:T(8,128)}, f32[2,256,768]{2,1,0:T(8,128)}, u32[]{:S(2)}, u32[]{:S(2)}) collective-permute-start(f32[2,256,768]{2,1,0:T(8,128)} %get-tuple-element.210), channel_id=1, source_target_pairs={{0,1},{1,0},{2,3},{3,2},{4,5},{5,4},{6,7},{7,6},{8,9},{9,8},{10,11... | collective-permute-start | bytes 4718600 | tf_op jit(solution)/shard_map/ppermute | solution.py:979
  146.6 5.2 %collective-permute-start.30 = (f32[16,768]{1,0:T(8,128)S(1)}, f32[16,768]{1,0:T(8,128)S(1)}, u32[]{:S(2)}, u32[]{:S(2)}) collective-permute-start(f32[16,768]{1,0:T(8,128)S(1)} %add.60), channel_id=1, source_target_pairs={{0,2},{1,3},{2,0},{3,1},{4,6},{5,7},{6,4},{7,5},{8,10},{9,11},{10,... | collective-permute-start | bytes 147464 | tf_op jit(solution)/shard_map/ppermute | solution.py:979
  148.2 13.3 %collective-permute-start.33 = (bf16[3,96,384]{2,1,0:T(8,128)(2,1)}, bf16[3,96,384]{2,1,0:T(8,128)(2,1)S(1)}, u32[]{:S(2)}, u32[]{:S(2)}) collective-permute-start(bf16[3,96,384]{2,1,0:T(8,128)(2,1)} %copy-done.9), channel_id=1, source_target_pairs={{0,16},{4,20},{8,24},{12,28},{16,0},{20,4},{24,8},{28,12},{1,17},{... | collective-permute-start | bytes 663560 | tf_op jit(solution)/shard_map/ppermute | solution.py:982
  151.5 8.0 %collective-permute-start.32 = (bf16[2,96,384]{2,1,0:T(8,128)(2,1)}, bf16[2,96,384]{2,1,0:T(8,128)(2,1)S(1)}, u32[]{:S(2)}, u32[]{:S(2)}) collective-permute-start(bf16[2,96,384]{2,1,0:T(8,128)(2,1)} %copy-done.10), channel_id=1, source_target_pairs={{0,8},{4,12},{8,0},{12,4},{16,24},{20,28},{24,16},{28,20},{1,9},{5... | collective-permute-start | bytes 442376 | tf_op jit(solution)/shard_map/ppermute | solution.py:982
  151.8 4.2 %collective-permute-start.31 = (f32[16,768]{1,0:T(8,128)S(1)}, f32[16,768]{1,0:T(8,128)S(1)}, u32[]{:S(2)}, u32[]{:S(2)}) collective-permute-start(f32[16,768]{1,0:T(8,128)S(1)} %add.61), channel_id=1, source_target_pairs={{0,4},{4,0},{8,12},{12,8},{16,20},{20,16},{24,28},{28,24},{1,5},{5... | collective-permute-start | bytes 147464 | tf_op jit(solution)/shard_map/ppermute | solution.py:982
  164.3 11.1 %collective-permute-start.29 = (bf16[256,768]{1,0:T(8,128)(2,1)S(1)}, bf16[256,768]{1,0:T(8,128)(2,1)S(1)}, u32[]{:S(2)}, u32[]{:S(2)}) collective-permute-start(bf16[256,768]{1,0:T(8,128)(2,1)S(1)} %fusion.1), channel_id=1, source_target_pairs={{0,2},{1,3},{2,0},{3,1},{4,6},{5,7},{6,4},{7,5},{8,10},{9,11},{10,... | collective-permute-start | bytes 1179656 | tf_op jit(solution)/shard_map/ppermute | solution.py:979
  164.8 6.5 %collective-permute-start.40 = (bf16[96,192]{1,0:T(8,128)(2,1)S(1)}, bf16[96,192]{1,0:T(8,128)(2,1)S(1)}, u32[]{:S(2)}, u32[]{:S(2)}) collective-permute-start(bf16[96,192]{1,0:T(8,128)(2,1)S(1)} %slice.141), channel_id=1, source_target_pairs={{0,16},{4,20},{8,24},{12,28},{16,0},{20,4},{24,8},{28,12},{1,17},{... | collective-permute-start | bytes 110600 | tf_op jit(solution)/shard_map/ppermute | solution.py:982
  164.9 7.7 %collective-permute-start.35 = (bf16[1,96,384]{2,1,0:T(8,128)(2,1)S(1)}, bf16[1,96,384]{2,1,0:T(8,128)(2,1)S(1)}, u32[]{:S(2)}, u32[]{:S(2)}) collective-permute-start(bf16[1,96,384]{2,1,0:T(8,128)(2,1)S(1)} %get-tuple-element.223), channel_id=1, source_target_pairs={{0,16},{4,20},{8,24},{12,28},{16,0},{20,4},{24,8},{28,12},{1,17},{... | collective-permute-start | bytes 221192 | tf_op jit(solution)/shard_map/ppermute | solution.py:982
  167.8 4.8 %collective-permute-start.34 = (f32[16,768]{1,0:T(8,128)S(1)}, f32[16,768]{1,0:T(8,128)S(1)}, u32[]{:S(2)}, u32[]{:S(2)}) collective-permute-start(f32[16,768]{1,0:T(8,128)S(1)} %add.62.refs_1_), channel_id=1, source_target_pairs={{0,8},{4,12},{8,0},{12,4},{16,24},{20,28},{24,16},{28,20},{1,9},{5... | collective-permute-start | bytes 147464 | tf_op jit(solution)/shard_map/ppermute | solution.py:982
  176.4 5.1 %collective-permute-start.39 = (f32[16,768]{1,0:T(8,128)S(1)}, f32[16,768]{1,0:T(8,128)S(1)}, u32[]{:S(2)}, u32[]{:S(2)}) collective-permute-start(f32[16,768]{1,0:T(8,128)S(1)} %add.63), channel_id=1, source_target_pairs={{0,16},{4,20},{8,24},{12,28},{16,0},{20,4},{24,8},{28,12},{1,17},{... | collective-permute-start | bytes 147464 | tf_op jit(solution)/shard_map/ppermute | solution.py:982
  176.5 6.3 %collective-permute-start.36 = (bf16[2,96,192]{2,1,0:T(8,128)(2,1)S(1)}, bf16[2,96,192]{2,1,0:T(8,128)(2,1)S(1)}, u32[]{:S(2)}, u32[]{:S(2)}) collective-permute-start(bf16[2,96,192]{2,1,0:T(8,128)(2,1)S(1)} %get-tuple-element.226), channel_id=1, source_target_pairs={{0,1},{1,0},{2,3},{3,2},{4,5},{5,4},{6,7},{7,6},{8,9},{9,8},{10,11... | collective-permute-start | bytes 221192 | tf_op jit(solution)/shard_map/ppermute | solution.py:979
  176.5 6.2 %collective-permute-start.37 = (bf16[2,96,192]{2,1,0:T(8,128)(2,1)S(1)}, bf16[2,96,192]{2,1,0:T(8,128)(2,1)S(1)}, u32[]{:S(2)}, u32[]{:S(2)}) collective-permute-start(bf16[2,96,192]{2,1,0:T(8,128)(2,1)S(1)} %get-tuple-element.227), channel_id=1, source_target_pairs={{0,2},{1,3},{2,0},{3,1},{4,6},{5,7},{6,4},{7,5},{8,10},{9,11},{10,... | collective-permute-start | bytes 221192 | tf_op jit(solution)/shard_map/ppermute | solution.py:979
  177.0 6.4 %collective-permute-start.38 = (bf16[2,96,192]{2,1,0:T(8,128)(2,1)S(1)}, bf16[2,96,192]{2,1,0:T(8,128)(2,1)S(1)}, u32[]{:S(2)}, u32[]{:S(2)}) collective-permute-start(bf16[2,96,192]{2,1,0:T(8,128)(2,1)S(1)} %get-tuple-element.228), channel_id=1, source_target_pairs={{0,3},{1,2},{2,1},{3,0},{4,7},{5,6},{6,5},{7,4},{8,11},{9,10},{10,... | collective-permute-start | bytes 221192 | tf_op jit(solution)/shard_map/ppermute | solution.py:979
  (18 other events, 113.5 us)

commit v5 on v4

--- a/solution.py
+++ b/solution.py
@@ -92,15 +92,30 @@
             keep[index] = value
 
 
-def join_kernel(skip, segments, routes, *refs):
+def leaves(segments, route):
+    return any(m >= len(segments) or segments[m][n] > 1 for m, n in route)
+
+
+def join_kernel(skip, segments, fresh, routes, *refs):
     refs = refs[skip:]
-    ins, outs = refs[: 2 * len(segments)], list(refs[2 * len(segments) : -1])
+    count = 2 * len(segments)
+    ins, new = refs[:count], refs[count : count + 2 * fresh]
+    outs = list(refs[count + 2 * fresh : -1])
     refs[-1][...] = jnp.zeros_like(refs[-1])
     for route in routes:
-        send = outs.pop(0) if any(segments[m][n] > 1 for m, n in route) else None
+        more = leaves(segments, route)
+        send = outs.pop(0) if more else None
         keep = outs.pop(0)
         sent = filled = 0
         for m, n in route:
+            if m >= len(segments):
+                at = 2 * (m - len(segments))
+                size = new[at].shape[0]
+                send[sent : sent + size] = new[at][...]
+                keep[filled : filled + size] = new[at + 1][...]
+                sent += size
+                filled += size
+                continue
             start, size = sum(segments[m][:n]), segments[m][n]
             total = ins[2 * m][start : start + size]
             total = total + ins[2 * m + 1][start : start + size].astype(F32)
@@ -108,25 +123,36 @@
                 size //= 2
                 send[sent : sent + size] = total[size:].astype(LOW)
                 sent += size
+            elif more:
+                wide = total.shape[2] // 2
+                turned = jnp.concatenate([total[0, :, wide:], total[0, :, :wide]], axis=1)
+                send[sent] = turned.astype(LOW)
+                sent += 1
             keep[filled : filled + size] = total[:size]
             filled += size
 
 
-def join(messages, routes, after):
+def join(messages, routes, after, fresh):
     segments = [list(message[0]) for message in messages]
     tail = messages[0][1].shape[1:]
     shapes, results = [], []
     for route in routes:
-        sizes = [segments[m][n] for m, n in route]
-        left = [size // 2 for size in sizes if size > 1]
-        results.append(left)
-        if left:
+        left = [
+            fresh[m - len(segments)][0].shape[0]
+            if m >= len(segments)
+            else max(segments[m][n] // 2, 1)
+            for m, n in route
+        ]
+        more = leaves(segments, route)
+        results.append(left if more else [])
+        if more:
             shapes.append(shaped((sum(left),) + tail, LOW))
-        shapes.append(shaped((sum(max(size // 2, 1) for size in sizes),) + tail, F32))
+        shapes.append(shaped((sum(left),) + tail, F32))
     operands = [array for message in messages for array in message[1:]]
+    operands += [array for pair in fresh for array in pair]
     shapes.append(shaped((8, 128), F32))
     *arrays, token = pl.pallas_call(
-        functools.partial(join_kernel, len(after), segments, routes),
+        functools.partial(join_kernel, len(after), segments, len(fresh), routes),
         grid=(1,),
         in_specs=waiting(after) + [full(array.shape) for array in operands],
         out_specs=[full(shape.shape) for shape in shapes],
@@ -730,7 +756,7 @@
     )(info, *after, mine, theirs, act, act_pair)
 
 
-UP_ORDERS = ("xyzw", "yxzw")
+UP_ORDERS = ("xyzw", "yxwz")
 
 
 def up_kernel(
@@ -802,7 +828,7 @@
 
 
 def input_kernel(info, *refs):
-    grads, weights, (keep, send) = refs[:9], refs[9:12], refs[12:]
+    grads, weights, (near, far, send) = refs[:9], refs[9:12], refs[12:]
     rel = pl.program_id(0)
     total = sum(
         dot_nt(jnp.concatenate([ref[...] for ref in grads[t::3]], axis=1), weights[t][...])
@@ -813,9 +839,13 @@
     def _():
         send[0] = total
 
-    @pl.when(rel >= 2)
-    def _():
-        keep[0] = total
+    @pl.when(rel == 2)
+    def _():
+        near[...] = total
+
+    @pl.when(rel == 3)
+    def _():
+        far[...] = total
 
 
 def input_part(info, grads, qkv_weight, after):
@@ -835,11 +865,12 @@
             grid=(4,),
             in_specs=waiting(after) + [rows] * 9 + [weight(0), weight(1), weight(2)],
             out_specs=[
-                pl.BlockSpec((1, quarter, width), lambda c, i: (jnp.maximum(c - 2, 0), 0, 0)),
+                full((quarter, width)),
+                full((quarter, width)),
                 pl.BlockSpec((1, quarter, width), lambda c, i: (jnp.minimum(c, 1), 0, 0)),
             ],
         ),
-        out_shape=[shaped((2, quarter, width), F32)] * 2,
+        out_shape=[shaped((quarter, width), F32)] * 2 + [shaped((2, quarter, width), F32)],
         compiler_params=params(VMEM),
         cost_estimate=cost(6),
         name="input_part",
@@ -998,9 +1029,9 @@
             for order, segments, sent, kept in messages
         ]
 
-    def land(after, flights, *routes):
+    def land(after, flights, *routes, fresh=()):
         made, token = join(
-            [flight[1:] for flight in flights], [route[1:] for route in routes], after
+            [flight[1:] for flight in flights], [route[1:] for route in routes], after, fresh
         )
         return [(route[0],) + new for route, new in zip(routes, made)], token
 
@@ -1059,7 +1090,10 @@
 
     zero = piece(0, vectors, [made[1]])
     downs, token = land(
-        zero[3:4], downs, (DOWN_ORDERS[0][1:], (0, 0)), (DOWN_ORDERS[1][1:], (1, 0))
+        zero[3:4],
+        downs,
+        (DOWN_ORDERS[0][1:], (0, 0)),
+        (DOWN_ORDERS[1][1:], (1, 0)),
     )
     opened, token = opening(0, zero, token)
     *downs, first = launch(*downs, opened)
@@ -1076,49 +1110,53 @@
     flights = launch(up_a, up_b, down, opened)
 
     two = piece(2, one[3], [token])
-    (up, first, down), token = land(
+    (up_a, up_b, others), token = land(
         two[3:4],
         flights,
-        ("zw", (0, 0), (1, 0), (1, 1)),
-        ("w", (0, 1)),
-        ("y", (2, 0), (2, 1), (3, 0)),
+        ("zw", (0, 0), (1, 1)),
+        ("wz", (1, 0), (0, 1)),
+        ("y", (2, 0), (2, 1), (3, 0), (4, 0)),
+        fresh=[two[4:6]],
     )
     grads = [*zero[:3], *one[:3], *two[:3]]
-    opened, token = opening(2, two, token)
     vectors, token = tie(two[3], token)
-    flights = launch(opened, up, first, down)
+    flights = launch(others, up_a, up_b)
     vectors_got = over_seq(vectors, 1)
 
-    keep, send = input_part(info, grads, qkv_weight, [token])
-    (third, up, down), token = land(
-        [keep],
+    near, far, send = input_part(info, grads, qkv_weight, [token])
+    (up_a, up_b, down), token = land(
+        [near],
         flights,
-        (QKV_ORDERS[2][1:], (0, 0)),
-        ("w", (1, 0), (1, 1), (3, 2), (1, 2)),
-        ("", (3, 0), (3, 1), (2, 0)),
-    )
-    down_total, out_total = down[3], up[3][3]
-    third, up = launch(third, up)
+        ("w", (1, 0), (0, 2), (1, 1)),
+        ("z", (2, 0), (0, 3)),
+        ("", (0, 0), (0, 1), (2, 1)),
+    )
+    down_total = down[3]
+    up_a, up_b = launch(up_a, up_b)
     send, vectors_got, token = tie(send, vectors_got, token)
-    d_row = keep + over_seq(send, 1)
-    d_far = over_seq(d_row[1].astype(LOW), 2)
+    d_row_got = over_seq(send, 1)
+    far = (far + d_row_got[1]).astype(LOW)
+    d_far = over_seq(far, 2)
     vectors = vectors + vectors_got
     vectors = vectors + over_seq(vectors, 2)
     vectors = vectors + swap(vectors, "y")
-    (third, up), token = land([token, vectors], [third, up], ("w", (0, 0)), ("", (1, 0), (1, 1), (1, 2)))
+    (up, third), token = land(
+        [token, vectors, far],
+        [up_a, up_b],
+        ("", (0, 0), (1, 0), (0, 2), (0, 1)),
+        ("w", (1, 1)),
+    )
     up_total = up[3]
-    vectors, out_total, token = tie(vectors, out_total, token)
+    wide = half // 2
+    vectors, token = tie(vectors, token)
     (third,) = launch(third)
-    wide = half // 2
-    out_got = swap(out_total[:, wide:].astype(LOW), "w")
     vectors_got = swap(vectors, "z")
     own, *others = share(info, down[3], up[3], third[2], third[3], [token, vectors_got, d_far])
     vectors_got, own = tie(vectors_got, own)
     vectors = vectors + vectors_got
     qkv_total = gather(info, own, *[over_seq(other, 1 + j) for j, other in enumerate(others)])
     qkv_total = finish(qkv_total)
-    out_total = out_total[:, :wide] + out_got.astype(F32)
-    out_total = finish(out_total)
+    out_total = finish(up_total[2, :, :wide])
     down_total = finish(down_total[:2].reshape(wide, half).T)
     up_total = finish(jnp.concatenate([up_total[0], up_total[1]], axis=1))
 
@@ -1127,7 +1165,7 @@
     while flip < fine:
         vectors = vectors + over_batch(vectors, flip)
         flip *= 2
-    d_near = d_summed[:quarter] + d_row[0]
+    d_near = d_summed[:quarter] + (near + d_row_got[0])
     d_far = d_summed[quarter:] + d_far.astype(F32)
     d_inputs = jnp.stack([jnp.where(chip == 0, d_near, d_far), jnp.where(chip == 0, d_far, d_near)])
     return (

time: 185 us -> 181 us (0.978)
  waiting for transfers between devices: 36.8 us -> 31.8 us
    ppermute x18 -> x16, waiting for transfers between devices: 16.5 us -> 10.1 us  [over_batch(): lax.ppermute(array, 'batch', [(i, i ^ flip) for i in range(batch_size)])]
    add x2 -> x0, other arithmetic: 2.27 us -> none  [the longest x1 1.62 us: body(): d_row = keep + over_seq(send, 1)]
    unnamed x50 -> x52, local copies, waits for them, and re-layouts: 6.06 us -> 5.11 us
    ppermute x18 -> x16, starting transfers between devices: 25 us -> 25.2 us  [over_batch(): lax.ppermute(array, 'batch', [(i, i ^ flip) for i in range(batch_size)])]
  transfers between devices with their start and end apart: 41 -> 39, of which waited for: 16 -> 14; matrix products, arithmetic and copies ran while one was open for 5% -> 6% of each run, Pallas kernels for 32% -> 33%
where the time goes in v5:
time: 181 us; the launch traced here: 180 us
  Pallas kernels  89.3 us (49%)
  starting transfers between devices  41.4 us (23%)
  waiting for transfers between devices  31.8 us (18%)
  local copies, waits for them, and re-layouts  11.5 us (6%)
  other arithmetic  4.9 us (3%)
    ppermute x16, starting transfers between devices, over_batch(): lax.ppermute(array, 'batch', [(i, i ^ flip) for i in range(batch_size)])  25.2 us
    pallas_call x3, Pallas kernels, attend_backward(): pl.pallas_call(ordered(functools.partial(backward_kernel, n), after), gri...  22.8 us
    ppermute x23, waiting for transfers between devices, over_seq(): return lax.ppermute(array, 'seq', [(i, i ^ flip) for i in range(seq_size)])  21.6 us
    ppermute x23, starting transfers between devices, over_seq(): return lax.ppermute(array, 'seq', [(i, i ^ flip) for i in range(seq_size)])  16.2 us
    pallas_call x1, Pallas kernels, attend_forward(): pl.pallas_call(functools.partial(forward_kernel, True), grid_spec=pltpu.P...  14.6 us
    pallas_call x1, Pallas kernels, middle_forward(): pl.pallas_call(ordered(middle_forward_kernel, after), grid_spec=pltpu.Pre...  12.8 us
    pallas_call x1, Pallas kernels, middle_backward(): pl.pallas_call(middle_backward_kernel, grid_spec=pltpu.PrefetchScalarGrid...  10.3 us
    ppermute x16, waiting for transfers between devices, over_batch(): lax.ppermute(array, 'batch', [(i, i ^ flip) for i in range(batch_size)])  10.1 us
  transfers between devices with their start and end apart: 39, of which 14 were waited for; matrix products, arithmetic and copies ran while one was open for 6% of the time, Pallas kernels for 33%

profile of v5, /device:TPU:0, one launch (start us, length us, event | category | flops | bytes accessed | tf_op | source)
XLA Modules:
  0.0 180.1 jit_solution(12915432059635978409)
XLA Ops:
  0.8 1.2 dynamic-slice_bitcast_fusion
  2.0 3.0 %collective-permute-start.1 = (bf16[256,768]{1,0:T(8,128)(2,1)S(1)}, bf16[256,768]{1,0:T(8,128)(2,1)S(1)}, u32[]{:S(2)}, u32[]{:S(2)}) collective-permute-start(bf16[256,768]{1,0:T(8,128)(2,1)S(1)} %get-tuple-element.245), channel_id=1, source_target_pairs={{0,2},{1,3},{2,0},{3,1},{4,6},{5,7},{6,4},{7,5},{8,10},{9,11},{10,... | collective-permute-start | bytes 1179656 | tf_op jit(solution)/shard_map/ppermute | solution.py:1010
  6.2 7.9 %collective-permute-done.1.x2.refs_2_ = bf16[256,768]{1,0:T(8,128)(2,1)S(1)} collective-permute-done((bf16[256,768]{1,0:T(8,128)(2,1)S(1)}, bf16[256,768]{1,0:T(8,128)(2,1)S(1)}, u32[]{:S(2)}, u32[]{:S(2)}) %collective-permute-start.1) | collective-permute-done | bytes 393248 | tf_op jit(solution)/shard_map/ppermute | solution.py:1010
  14.8 1.0 collective-permute-done.2.x3.refs_3_
  15.8 2.0 %copy-done.3 = bf16[768,2304]{1,0:T(8,128)(2,1)S(1)} copy-done((bf16[768,2304]{1,0:T(8,128)(2,1)S(1)}, bf16[768,2304]{1,0:T(8,128)(2,1)}, u32[]{:S(2)}) %copy-start.3) | copy-done | bytes 3538968
  17.8 14.6 %attend_forward.1 = (bf16[1024,384]{1,0:T(8,128)(2,1)S(1)}, bf16[1024,384]{1,0:T(8,128)(2,1)S(1)}, bf16[1024,384]{1,0:T(8,128)(2,1)S(1)}, bf16[256,384]{1,0:T(8,...) custom-call(s32[12]{0:T(128)S(1)} %concatenate.6.info, ...), custom_call_target="tpu_custom_call" | custom-call | flops 9600000000 | tf_op jit(solution)/shard_map/attend_forward/pallas_call | solution.py:309
  32.5 1.0 collective-permute-start.4
  33.5 0.9 collective-permute-start.5
  34.4 1.0 turn.1.refs_0_.refs_14_
  35.5 4.3 %attend_own.1 = (bf16[256,384]{1,0:T(8,128)(2,1)S(1)}, f32[384,256]{1,0:T(8,128)S(1)}, f32[3,1,512]{2,1,0:T(1,128)S(1)}) custom-call(s32[12]{0:T(128)S(1)} %concatenate.6.info, bf16[1024,384]{1,0:T(8,128)(2,1)S(1)} %get-tuple-element.121.refs_0_.refs_1_, bf16[1024,384]{1,0:T(8,128)(2,1)S(1)} %get-tuple-element.122.refs_1_.refs_2_, ...), custom_call_target="tpu_custom_call" | custom-call | flops 3000000000 | tf_op jit(solution)/shard_map/attend_own/pallas_call | solution.py:326
  40.3 3.3 %collective-permute-done.5.refs_4_ = bf16[256,384]{1,0:T(8,128)(2,1)S(1)} collective-permute-done((bf16[256,384]{1,0:T(8,128)(2,1)S(1)}, bf16[256,384]{1,0:T(8,128)(2,1)S(1)}, u32[]{:S(2)}, u32[]{:S(2)}) %collective-permute-start.5) | collective-permute-done | bytes 196640 | tf_op jit(solution)/shard_map/ppermute | solution.py:1010
  43.6 12.8 %middle_forward.1 = (bf16[2,256,768]{2,1,0:T(8,128)(2,1)}, f32[512,768]{1,0:T(8,128)S(1)}, f32[512,768]{1,0:T(8,128)S(1)}, f32[512,1]{1,0:T(8,128)S(1)}, bf16[2,...) custom-call(s32[12]{0:T(128)S(1)} %concatenate.6.info, ...), custom_call_target="tpu_custom_call" | custom-call | flops 10800000000 | tf_op jit(solution)/shard_map/middle_forward/pallas_call | solution.py:570
  57.2 10.3 %middle_backward.1 = (bf16[1536,768]{1,0:T(8,128)(2,1)S(1)}, bf16[2,512,768]{2,1,0:T(8,128)(2,1)S(1)}, f32[512,768]{1,0:T(8,128)S(1)}, bf16[256,384]{1,0:T(8,128...) custom-call(s32[12]{0:T(128)S(1)} %concatenate.6.info, ...), custom_call_target="tpu_custom_call" | custom-call | flops 9600000000 | tf_op jit(solution)/shard_map/middle_backward/pallas_call | solution.py:684
  68.3 7.8 %down_grad.1 = (bf16[8,96,384]{2,1,0:T(8,128)(2,1)S(1)}, f32[8,96,384]{2,1,0:T(8,128)S(1)}, bf16[8,96,384]{2,1,0:T(8,128)(2,1)S(1)}, f32[8,96,384]{2,1,0:T(8,128)S(1)}) custom-call(s32[12]{0:T(128)S(1)} %concatenate.6.info, f32[8,128]{1,0:T(8,128)S(1)} %mark.1.refs_0_, bf16[2,192,512]{2,1,0:T(8,128)(2,1)S(1)} %get-tuple-element.142.refs_1_, ...), custom_call_target="tpu_custom_call" | custom-call | flops 4800000000 | tf_op jit(solution)/shard_map/down_grad/pallas_call | solution.py:744
  76.1 1.6 collective-permute-start.12
  77.7 0.9 collective-permute-start.13
  79.3 7.0 %up_grad.1 = (bf16[8,96,384]{2,1,0:T(8,128)(2,1)S(1)}, f32[8,96,384]{2,1,0:T(8,128)S(1)}, bf16[12,96,384]{2,1,0:T(8,128)(2,1)S(1)}, f32[12,96,384]{2,1,0:T(8,128)S(1)}) custom-call(s32[12]{0:T(128)S(1)} %concatenate.6.info, f32[8,96,384]{2,1,0:T(8,128)S(1)} %get-tuple-element.143.refs_0_.refs_1_, bf16[2,768,512]{2,1,0:T(8,128)(2,1)S(1)} %get-tuple-element.137.refs_1_, ...), custom_call_target="tpu_custom_call" | custom-call | flops 6000000000 | tf_op jit(solution)/shard_map/up_grad/pallas_call | solution.py:807
  86.3 1.3 collective-permute-start.15
  87.5 1.8 collective-permute-start.14
  89.3 7.5 %attend_backward.3 = (bf16[1024,128]{1,0:T(8,128)(2,1)S(1)}, bf16[1024,128]{1,0:T(8,128)(2,1)S(1)}, bf16[1024,128]{1,0:T(8,128)(2,1)S(1)}, f32[16,768]{1,0:T(8,1...) custom-call(s32[12]{0:T(128)S(1)} %concatenate.6.info, ...), custom_call_target="tpu_custom_call" | custom-call | flops 4800000000 | tf_op jit(solution)/shard_map/attend_backward/pallas_call | solution.py:427
  97.4 0.9 collective-permute-start.16
  99.1 7.8 %attend_backward.4 = (bf16[1024,128]{1,0:T(8,128)(2,1)S(1)}, bf16[1024,128]{1,0:T(8,128)(2,1)S(1)}, bf16[1024,128]{1,0:T(8,128)(2,1)S(1)}, f32[16,768]{1,0:T(8,1...) custom-call(s32[12]{0:T(128)S(1)} %concatenate.6.info, f32[8,128]{1,0:T(8,128)S(1)} %get-tuple-element.160.refs_0_, ...), custom_call_target="tpu_custom_call" | custom-call | flops 4800000000 | tf_op jit(solution)/shard_map/attend_backward/pallas_call | solution.py:427
  107.0 4.8 %collective-permute-done.16.refs_6_ = bf16[4,96,384]{2,1,0:T(8,128)(2,1)S(1)} collective-permute-done((bf16[4,96,384]{2,1,0:T(8,128)(2,1)S(1)}, bf16[4,96,384]{2,1,0:T(8,128)(2,1)S(1)}, u32[]{:S(2)}, u32[]{:S(2)}) %collective-permute-start.16) | collective-permute-done | bytes 294944 | tf_op jit(solution)/shard_map/ppermute | solution.py:1010
  112.7 1.2 collective-permute-start.19
  115.4 2.3 %collective-permute-start.21 = (bf16[4,96,384]{2,1,0:T(8,128)(2,1)S(1)}, bf16[4,96,384]{2,1,0:T(8,128)(2,1)S(1)}, u32[]{:S(2)}, u32[]{:S(2)}) collective-permute-start(bf16[4,96,384]{2,1,0:T(8,128)(2,1)S(1)} %get-tuple-element.180), channel_id=1, source_target_pairs={{0,16},{4,20},{8,24},{12,28},{16,0},{20,4},{24,8},{28,12},{1,17},{... | collective-permute-start | bytes 884744 | tf_op jit(solution)/shard_map/ppermute | solution.py:1013
  117.7 7.5 %attend_backward.5 = (bf16[1024,128]{1,0:T(8,128)(2,1)S(1)}, bf16[1024,128]{1,0:T(8,128)(2,1)S(1)}, bf16[1024,128]{1,0:T(8,128)(2,1)S(1)}, f32[16,768]{1,0:T(8,1...) custom-call(s32[12]{0:T(128)S(1)} %concatenate.6.info, f32[8,128]{1,0:T(8,128)S(1)} %get-tuple-element.173.refs_0_, ...), custom_call_target="tpu_custom_call" | custom-call | flops 4800000000 | tf_op jit(solution)/shard_map/attend_backward/pallas_call | solution.py:427
  125.3 2.9 %collective-permute-done.22.refs_8_ = bf16[4,96,384]{2,1,0:T(8,128)(2,1)S(1)} collective-permute-done((bf16[4,96,384]{2,1,0:T(8,128)(2,1)S(1)}, bf16[4,96,384]{2,1,0:T(8,128)(2,1)S(1)}, u32[]{:S(2)}, u32[]{:S(2)}) %collective-permute-start.22) | collective-permute-done | bytes 294944 | tf_op jit(solution)/shard_map/ppermute | solution.py:1013
  129.2 3.1 %collective-permute-start.25 = (bf16[3,96,384]{2,1,0:T(8,128)(2,1)S(1)}, bf16[3,96,384]{2,1,0:T(8,128)(2,1)S(1)}, u32[]{:S(2)}, u32[]{:S(2)}) collective-permute-start(bf16[3,96,384]{2,1,0:T(8,128)(2,1)S(1)} %get-tuple-element.202), channel_id=1, source_target_pairs={{0,8},{4,12},{8,0},{12,4},{16,24},{20,28},{24,16},{28,20},{1,9},{5... | collective-permute-start | bytes 663560 | tf_op jit(solution)/shard_map/ppermute | solution.py:1013
  132.2 2.7 %collective-permute-start.26 = (bf16[3,96,384]{2,1,0:T(8,128)(2,1)S(1)}, bf16[3,96,384]{2,1,0:T(8,128)(2,1)S(1)}, u32[]{:S(2)}, u32[]{:S(2)}) collective-permute-start(bf16[3,96,384]{2,1,0:T(8,128)(2,1)S(1)} %get-tuple-element.204), channel_id=1, source_target_pairs={{0,16},{4,20},{8,24},{12,28},{16,0},{20,4},{24,8},{28,12},{1,17},{... | collective-permute-start | bytes 663560 | tf_op jit(solution)/shard_map/ppermute | solution.py:1013
  134.9 5.1 %input_part.1 = (f32[256,768]{1,0:T(8,128)S(1)}, f32[256,768]{1,0:T(8,128)S(1)}, f32[2,256,768]{2,1,0:T(8,128)}) custom-call(s32[12]{0:T(128)S(1)} %concatenate.6.info, f32[8,128]{1,0:T(8,128)S(1)} %get-tuple-element.186.refs_0_, bf16[1024,128]{1,0:T(8,128)(2,1)S(1)} %get-tuple-element.187.refs_1_, bf16[1024,128]{1,0:T(8,128)(2,1)S(1)} %get-tuple-element.188.refs_2_, ...), custom_call_target="tpu_custom_call" | custom-call | flops 3600000000 | tf_op jit(solution)/shard_map/input_part/pallas_call | solution.py:861
  140.0 2.8 %collective-permute-done.26.refs_6_ = bf16[3,96,384]{2,1,0:T(8,128)(2,1)S(1)} collective-permute-done((bf16[3,96,384]{2,1,0:T(8,128)(2,1)S(1)}, bf16[3,96,384]{2,1,0:T(8,128)(2,1)S(1)}, u32[]{:S(2)}, u32[]{:S(2)}) %collective-permute-start.26) | collective-permute-done | bytes 221216 | tf_op jit(solution)/shard_map/ppermute | solution.py:1013
  146.1 1.7 collective-permute-start.29
  147.8 2.4 %collective-permute-done.29 = f32[16,768]{1,0:T(8,128)S(1)} collective-permute-done((f32[16,768]{1,0:T(8,128)S(1)}, f32[16,768]{1,0:T(8,128)S(1)}, u32[]{:S(2)}, u32[]{:S(2)}) %collective-permute-start.29) | collective-permute-done | bytes 49184 | tf_op jit(solution)/shard_map/ppermute | solution.py:1010
  151.4 4.3 %collective-permute-start.32 = (bf16[3,96,384]{2,1,0:T(8,128)(2,1)S(1)}, bf16[3,96,384]{2,1,0:T(8,128)(2,1)S(1)}, u32[]{:S(2)}, u32[]{:S(2)}) collective-permute-start(bf16[3,96,384]{2,1,0:T(8,128)(2,1)S(1)} %get-tuple-element.213), channel_id=1, source_target_pairs={{0,8},{4,12},{8,0},{12,4},{16,24},{20,28},{24,16},{28,20},{1,9},{5... | collective-permute-start | bytes 663560 | tf_op jit(solution)/shard_map/ppermute | solution.py:1013
  155.7 1.7 slice.76
  157.4 1.2 fusion.1.refs_2_
  158.6 1.7 collective-permute-start.28
  160.3 2.6 %collective-permute-done.31.refs_4_ = bf16[3,96,384]{2,1,0:T(8,128)(2,1)S(1)} collective-permute-done((bf16[3,96,384]{2,1,0:T(8,128)(2,1)}, bf16[3,96,384]{2,1,0:T(8,128)(2,1)S(1)}, u32[]{:S(2)}, u32[]{:S(2)}) %collective-permute-start.31) | collective-permute-done | bytes 221216 | tf_op jit(solution)/shard_map/ppermute | solution.py:1013
  163.0 2.4 %collective-permute-start.34 = (bf16[1,96,384]{2,1,0:T(8,128)(2,1)S(1)}, bf16[1,96,384]{2,1,0:T(8,128)(2,1)S(1)}, u32[]{:S(2)}, u32[]{:S(2)}) collective-permute-start(bf16[1,96,384]{2,1,0:T(8,128)(2,1)S(1)} %get-tuple-element.220), channel_id=1, source_target_pairs={{0,16},{4,20},{8,24},{12,28},{16,0},{20,4},{24,8},{28,12},{1,17},{... | collective-permute-start | bytes 221192 | tf_op jit(solution)/shard_map/ppermute | solution.py:1013
  165.4 1.5 collective-permute-start.33
  168.3 1.3 collective-permute-done.33.refs_1_
  169.7 1.0 share.1
  170.7 1.2 collective-permute-start.38
  171.8 1.6 collective-permute-start.36
  173.7 1.4 select_bitcast_fusion.1
  175.1 1.2 pad_maximum_fusion
  177.6 1.1 collective-permute-done.37.three
  178.8 1.4 gather.1
  (136 shorter events, 16.8 us)
Async XLA Ops:
  0.7 13.6 %copy-start.14 = (bf16[768]{0:T(1024)(128)(2,1)S(1)}, bf16[768]{0:T(1024)(128)(2,1)}, u32[]{:S(2)}) copy-start(bf16[768]{0:T(1024)(128)(2,1)} %param.19) | copy-start | bytes 4612
  0.7 13.6 %copy-start.15 = (bf16[768]{0:T(1024)(128)(2,1)S(1)}, bf16[768]{0:T(1024)(128)(2,1)}, u32[]{:S(2)}) copy-start(bf16[768]{0:T(1024)(128)(2,1)} %param.20) | copy-start | bytes 4612
  0.7 13.7 %copy-start.16 = (bf16[768]{0:T(1024)(128)(2,1)S(1)}, bf16[768]{0:T(1024)(128)(2,1)}, u32[]{:S(2)}) copy-start(bf16[768]{0:T(1024)(128)(2,1)} %param.23) | copy-start | bytes 4612
  0.7 13.7 %copy-start.12 = (bf16[3072]{0:T(1024)(128)(2,1)S(1)}, bf16[3072]{0:T(1024)(128)(2,1)}, u32[]{:S(2)}) copy-start(bf16[3072]{0:T(1024)(128)(2,1)} %param.26) | copy-start | bytes 18436
  0.7 13.7 %copy-start.17 = (bf16[768]{0:T(1024)(128)(2,1)S(1)}, bf16[768]{0:T(1024)(128)(2,1)}, u32[]{:S(2)}) copy-start(bf16[768]{0:T(1024)(128)(2,1)} %param.22) | copy-start | bytes 4612
  0.7 13.7 %copy-start.18 = (bf16[768]{0:T(1024)(128)(2,1)S(1)}, bf16[768]{0:T(1024)(128)(2,1)}, u32[]{:S(2)}) copy-start(bf16[768]{0:T(1024)(128)(2,1)} %param.24) | copy-start | bytes 4612
  0.7 13.7 %copy-start.19 = (bf16[768]{0:T(1024)(128)(2,1)S(1)}, bf16[768]{0:T(1024)(128)(2,1)}, u32[]{:S(2)}) copy-start(bf16[768]{0:T(1024)(128)(2,1)} %param.28) | copy-start | bytes 4612
  0.7 13.7 %copy-start.20 = (bf16[768]{0:T(1024)(128)(2,1)S(1)}, bf16[768]{0:T(1024)(128)(2,1)}, u32[]{:S(2)}) copy-start(bf16[768]{0:T(1024)(128)(2,1)} %param.29) | copy-start | bytes 4612
  0.7 13.7 %copy-start.21 = (bf16[768]{0:T(1024)(128)(2,1)S(1)}, bf16[768]{0:T(1024)(128)(2,1)}, u32[]{:S(2)}) copy-start(bf16[768]{0:T(1024)(128)(2,1)} %param.30) | copy-start | bytes 4612
  2.0 12.1 %collective-permute-start.1 = (bf16[256,768]{1,0:T(8,128)(2,1)S(1)}, bf16[256,768]{1,0:T(8,128)(2,1)S(1)}, u32[]{:S(2)}, u32[]{:S(2)}) collective-permute-start(bf16[256,768]{1,0:T(8,128)(2,1)S(1)} %get-tuple-element.245), channel_id=1, source_target_pairs={{0,2},{1,3},{2,0},{3,1},{4,6},{5,7},{6,4},{7,5},{8,10},{9,11},{10,... | collective-permute-start | bytes 1179656 | tf_op jit(solution)/shard_map/ppermute | solution.py:1010
  5.0 9.9 %collective-permute-start = (bf16[256,768]{1,0:T(8,128)(2,1)S(1)}, bf16[256,768]{1,0:T(8,128)(2,1)S(1)}, u32[]{:S(2)}, u32[]{:S(2)}) collective-permute-start(bf16[256,768]{1,0:T(8,128)(2,1)S(1)} %get-tuple-element.246.x0.refs_0_), channel_id=1, source_target_pairs={{0,1},{1,0},{2,3},{3,2},{4,5},{5,4},{6,7},{7,6},{8,9},{9,8},{10,11... | collective-permute-start | bytes 1179656 | tf_op jit(solution)/shard_map/ppermute | solution.py:1010
  14.1 1.7 collective-permute-start.2
  32.4 7.4 %collective-permute-start.3 = (bf16[256,384]{1,0:T(8,128)(2,1)S(1)}, bf16[256,384]{1,0:T(8,128)(2,1)S(1)}, u32[]{:S(2)}, u32[]{:S(2)}) collective-permute-start(bf16[256,384]{1,0:T(8,128)(2,1)S(1)} %get-tuple-element.125), channel_id=1, source_target_pairs={{0,1},{1,0},{2,3},{3,2},{4,5},{5,4},{6,7},{7,6},{8,9},{9,8},{10,11... | collective-permute-start | bytes 589832 | tf_op jit(solution)/shard_map/ppermute | solution.py:1010
  32.5 7.8 %collective-permute-start.4 = (bf16[256,384]{1,0:T(8,128)(2,1)S(1)}, bf16[256,384]{1,0:T(8,128)(2,1)S(1)}, u32[]{:S(2)}, u32[]{:S(2)}) collective-permute-start(bf16[256,384]{1,0:T(8,128)(2,1)S(1)} %get-tuple-element.126), channel_id=1, source_target_pairs={{0,2},{1,3},{2,0},{3,1},{4,6},{5,7},{6,4},{7,5},{8,10},{9,11},{10,... | collective-permute-start | bytes 589832 | tf_op jit(solution)/shard_map/ppermute | solution.py:1010
  33.5 10.1 %collective-permute-start.5 = (bf16[256,384]{1,0:T(8,128)(2,1)S(1)}, bf16[256,384]{1,0:T(8,128)(2,1)S(1)}, u32[]{:S(2)}, u32[]{:S(2)}) collective-permute-start(bf16[256,384]{1,0:T(8,128)(2,1)S(1)} %get-tuple-element.127), channel_id=1, source_target_pairs={{0,3},{1,2},{2,1},{3,0},{4,7},{5,6},{6,5},{7,4},{8,11},{9,10},{10,... | collective-permute-start | bytes 589832 | tf_op jit(solution)/shard_map/ppermute | solution.py:1010
  56.4 11.1 %collective-permute-start.7 = (bf16[512,3072]{1,0:T(8,128)(2,1)}, bf16[512,3072]{1,0:T(8,128)(2,1)S(1)}, u32[]{:S(2)}, u32[]{:S(2)}) collective-permute-start(bf16[512,3072]{1,0:T(8,128)(2,1)} %get-tuple-element.138.refs_3_), channel_id=1, source_target_pairs={{0,1},{1,0},{2,3},{3,2},{4,5},{5,4},{6,7},{7,6},{8,9},{9,8},{10,11... | collective-permute-start | bytes 9437192 | tf_op jit(solution)/shard_map/ppermute | solution.py:1010
  56.7 10.9 %collective-permute-start.6 = (bf16[2,768,512]{2,1,0:T(8,128)(2,1)S(1)}, bf16[2,768,512]{2,1,0:T(8,128)(2,1)S(1)}, u32[]{:S(2)}, u32[]{:S(2)}) collective-permute-start(bf16[2,768,512]{2,1,0:T(8,128)(2,1)S(1)} %get-tuple-element.137.refs_1_), channel_id=1, source_target_pairs={{0,1},{1,0},{2,3},{3,2},{4,5},{5,4},{6,7},{7,6},{8,9},{9,8},{10,11... | collective-permute-start | bytes 4718600 | tf_op jit(solution)/shard_map/ppermute | solution.py:1010
  56.9 10.6 %collective-permute-start.8 = (bf16[384,512]{1,0:T(8,128)(2,1)S(1)}, bf16[384,512]{1,0:T(8,128)(2,1)S(1)}, u32[]{:S(2)}, u32[]{:S(2)}) collective-permute-start(bf16[384,512]{1,0:T(8,128)(2,1)S(1)} %get-tuple-element.139), channel_id=1, source_target_pairs={{0,1},{1,0},{2,3},{3,2},{4,5},{5,4},{6,7},{7,6},{8,9},{9,8},{10,11... | collective-permute-start | bytes 1179656 | tf_op jit(solution)/shard_map/ppermute | solution.py:1010
  67.6 11.7 %collective-permute-start.9 = (bf16[1536,768]{1,0:T(8,128)(2,1)S(1)}, bf16[1536,768]{1,0:T(8,128)(2,1)S(1)}, u32[]{:S(2)}, u32[]{:S(2)}) collective-permute-start(bf16[1536,768]{1,0:T(8,128)(2,1)S(1)} %get-tuple-element.145), channel_id=1, source_target_pairs={{0,1},{1,0},{2,3},{3,2},{4,5},{5,4},{6,7},{7,6},{8,9},{9,8},{10,11... | collective-permute-start | bytes 7077896 | tf_op jit(solution)/shard_map/ppermute | solution.py:1010
  67.9 11.3 %collective-permute-start.10 = (bf16[2,256,384]{2,1,0:T(8,128)(2,1)S(1)}, bf16[2,256,384]{2,1,0:T(8,128)(2,1)S(1)}, u32[]{:S(2)}, u32[]{:S(2)}) collective-permute-start(bf16[2,256,384]{2,1,0:T(8,128)(2,1)S(1)} %get-tuple-element.149), channel_id=1, source_target_pairs={{0,2},{1,3},{2,0},{3,1},{4,6},{5,7},{6,4},{7,5},{8,10},{9,11},{10,... | collective-permute-start | bytes 1179656 | tf_op jit(solution)/shard_map/ppermute | solution.py:1010
  76.1 20.7 %collective-permute-start.12 = (bf16[8,96,384]{2,1,0:T(8,128)(2,1)S(1)}, bf16[8,96,384]{2,1,0:T(8,128)(2,1)S(1)}, u32[]{:S(2)}, u32[]{:S(2)}) collective-permute-start(bf16[8,96,384]{2,1,0:T(8,128)(2,1)S(1)} %get-tuple-element.156), channel_id=1, source_target_pairs={{0,8},{4,12},{8,0},{12,4},{16,24},{20,28},{24,16},{28,20},{1,9},{5... | collective-permute-start | bytes 1769480 | tf_op jit(solution)/shard_map/ppermute | solution.py:1013
  77.7 19.1 %collective-permute-start.13 = (bf16[8,96,384]{2,1,0:T(8,128)(2,1)S(1)}, bf16[8,96,384]{2,1,0:T(8,128)(2,1)S(1)}, u32[]{:S(2)}, u32[]{:S(2)}) collective-permute-start(bf16[8,96,384]{2,1,0:T(8,128)(2,1)S(1)} %get-tuple-element.158), channel_id=1, source_target_pairs={{0,2},{1,3},{2,0},{3,1},{4,6},{5,7},{6,4},{7,5},{8,10},{9,11},{10,... | collective-permute-start | bytes 1769480 | tf_op jit(solution)/shard_map/ppermute | solution.py:1010
  79.2 10.1 %collective-permute-start.11 = (bf16[256,384]{1,0:T(8,128)(2,1)S(1)}, bf16[256,384]{1,0:T(8,128)(2,1)S(1)}, u32[]{:S(2)}, u32[]{:S(2)}) collective-permute-start(bf16[256,384]{1,0:T(8,128)(2,1)S(1)} %slice_bitcast_fusion.2), channel_id=1, source_target_pairs={{0,1},{1,0},{2,3},{3,2},{4,5},{5,4},{6,7},{7,6},{8,9},{9,8},{10,11... | collective-permute-start | bytes 589832 | tf_op jit(solution)/shard_map/ppermute | solution.py:1010
  86.3 26.0 %collective-permute-start.15 = (bf16[12,96,384]{2,1,0:T(8,128)(2,1)S(1)}, bf16[12,96,384]{2,1,0:T(8,128)(2,1)S(1)}, u32[]{:S(2)}, u32[]{:S(2)}) collective-permute-start(bf16[12,96,384]{2,1,0:T(8,128)(2,1)S(1)} %get-tuple-element.165), channel_id=1, source_target_pairs={{0,4},{4,0},{8,12},{12,8},{16,20},{20,16},{24,28},{28,24},{1,5},{5... | collective-permute-start | bytes 2654216 | tf_op jit(solution)/shard_map/ppermute | solution.py:1013
  87.5 24.8 %collective-permute-start.14 = (bf16[8,96,384]{2,1,0:T(8,128)(2,1)S(1)}, bf16[8,96,384]{2,1,0:T(8,128)(2,1)S(1)}, u32[]{:S(2)}, u32[]{:S(2)}) collective-permute-start(bf16[8,96,384]{2,1,0:T(8,128)(2,1)S(1)} %get-tuple-element.163), channel_id=1, source_target_pairs={{0,2},{1,3},{2,0},{3,1},{4,6},{5,7},{6,4},{7,5},{8,10},{9,11},{10,... | collective-permute-start | bytes 1769480 | tf_op jit(solution)/shard_map/ppermute | solution.py:1010
  97.0 10.0 %collective-permute-start.18 = (bf16[4,96,384]{2,1,0:T(8,128)(2,1)S(1)}, bf16[4,96,384]{2,1,0:T(8,128)(2,1)S(1)}, u32[]{:S(2)}, u32[]{:S(2)}) collective-permute-start(bf16[4,96,384]{2,1,0:T(8,128)(2,1)S(1)} %get-tuple-element.171), channel_id=1, source_target_pairs={{0,8},{4,12},{8,0},{12,4},{16,24},{20,28},{24,16},{28,20},{1,9},{5... | collective-permute-start | bytes 884744 | tf_op jit(solution)/shard_map/ppermute | solution.py:1013
  97.4 14.4 %collective-permute-start.16 = (bf16[4,96,384]{2,1,0:T(8,128)(2,1)S(1)}, bf16[4,96,384]{2,1,0:T(8,128)(2,1)S(1)}, u32[]{:S(2)}, u32[]{:S(2)}) collective-permute-start(bf16[4,96,384]{2,1,0:T(8,128)(2,1)S(1)} %get-tuple-element.167), channel_id=1, source_target_pairs={{0,2},{1,3},{2,0},{3,1},{4,6},{5,7},{6,4},{7,5},{8,10},{9,11},{10,... | collective-permute-start | bytes 884744 | tf_op jit(solution)/shard_map/ppermute | solution.py:1010
  98.3 14.0 %collective-permute-start.17 = (bf16[4,96,384]{2,1,0:T(8,128)(2,1)S(1)}, bf16[4,96,384]{2,1,0:T(8,128)(2,1)S(1)}, u32[]{:S(2)}, u32[]{:S(2)}) collective-permute-start(bf16[4,96,384]{2,1,0:T(8,128)(2,1)S(1)} %get-tuple-element.169), channel_id=1, source_target_pairs={{0,8},{4,12},{8,0},{12,4},{16,24},{20,28},{24,16},{28,20},{1,9},{5... | collective-permute-start | bytes 884744 | tf_op jit(solution)/shard_map/ppermute | solution.py:1013
  112.7 15.5 %collective-permute-start.19 = (bf16[6,96,384]{2,1,0:T(8,128)(2,1)S(1)}, bf16[6,96,384]{2,1,0:T(8,128)(2,1)S(1)}, u32[]{:S(2)}, u32[]{:S(2)}) collective-permute-start(bf16[6,96,384]{2,1,0:T(8,128)(2,1)S(1)} %get-tuple-element.176), channel_id=1, source_target_pairs={{0,4},{4,0},{8,12},{12,8},{16,20},{20,16},{24,28},{28,24},{1,5},{5... | collective-permute-start | bytes 1327112 | tf_op jit(solution)/shard_map/ppermute | solution.py:1013
  113.8 14.4 %collective-permute-start.20 = (bf16[6,96,384]{2,1,0:T(8,128)(2,1)S(1)}, bf16[6,96,384]{2,1,0:T(8,128)(2,1)S(1)}, u32[]{:S(2)}, u32[]{:S(2)}) collective-permute-start(bf16[6,96,384]{2,1,0:T(8,128)(2,1)S(1)} %get-tuple-element.178), channel_id=1, source_target_pairs={{0,2},{1,3},{2,0},{3,1},{4,6},{5,7},{6,4},{7,5},{8,10},{9,11},{10,... | collective-permute-start | bytes 1327112 | tf_op jit(solution)/shard_map/ppermute | solution.py:1010
  114.7 13.5 %collective-permute-start.22 = (bf16[4,96,384]{2,1,0:T(8,128)(2,1)S(1)}, bf16[4,96,384]{2,1,0:T(8,128)(2,1)S(1)}, u32[]{:S(2)}, u32[]{:S(2)}) collective-permute-start(bf16[4,96,384]{2,1,0:T(8,128)(2,1)S(1)} %get-tuple-element.182), channel_id=1, source_target_pairs={{0,8},{4,12},{8,0},{12,4},{16,24},{20,28},{24,16},{28,20},{1,9},{5... | collective-permute-start | bytes 884744 | tf_op jit(solution)/shard_map/ppermute | solution.py:1013
  115.4 12.8 %collective-permute-start.21 = (bf16[4,96,384]{2,1,0:T(8,128)(2,1)S(1)}, bf16[4,96,384]{2,1,0:T(8,128)(2,1)S(1)}, u32[]{:S(2)}, u32[]{:S(2)}) collective-permute-start(bf16[4,96,384]{2,1,0:T(8,128)(2,1)S(1)} %get-tuple-element.180), channel_id=1, source_target_pairs={{0,16},{4,20},{8,24},{12,28},{16,0},{20,4},{24,8},{28,12},{1,17},{... | collective-permute-start | bytes 884744 | tf_op jit(solution)/shard_map/ppermute | solution.py:1013
  128.5 14.3 %collective-permute-start.24 = (bf16[8,96,384]{2,1,0:T(8,128)(2,1)S(1)}, bf16[8,96,384]{2,1,0:T(8,128)(2,1)S(1)}, u32[]{:S(2)}, u32[]{:S(2)}) collective-permute-start(bf16[8,96,384]{2,1,0:T(8,128)(2,1)S(1)} %get-tuple-element.200), channel_id=1, source_target_pairs={{0,4},{4,0},{8,12},{12,8},{16,20},{20,16},{24,28},{28,24},{1,5},{5... | collective-permute-start | bytes 1769480 | tf_op jit(solution)/shard_map/ppermute | solution.py:1013
  129.2 10.8 %collective-permute-start.25 = (bf16[3,96,384]{2,1,0:T(8,128)(2,1)S(1)}, bf16[3,96,384]{2,1,0:T(8,128)(2,1)S(1)}, u32[]{:S(2)}, u32[]{:S(2)}) collective-permute-start(bf16[3,96,384]{2,1,0:T(8,128)(2,1)S(1)} %get-tuple-element.202), channel_id=1, source_target_pairs={{0,8},{4,12},{8,0},{12,4},{16,24},{20,28},{24,16},{28,20},{1,9},{5... | collective-permute-start | bytes 663560 | tf_op jit(solution)/shard_map/ppermute | solution.py:1013
  132.2 10.6 %collective-permute-start.26 = (bf16[3,96,384]{2,1,0:T(8,128)(2,1)S(1)}, bf16[3,96,384]{2,1,0:T(8,128)(2,1)S(1)}, u32[]{:S(2)}, u32[]{:S(2)}) collective-permute-start(bf16[3,96,384]{2,1,0:T(8,128)(2,1)S(1)} %get-tuple-element.204), channel_id=1, source_target_pairs={{0,16},{4,20},{8,24},{12,28},{16,0},{20,4},{24,8},{28,12},{1,17},{... | collective-permute-start | bytes 663560 | tf_op jit(solution)/shard_map/ppermute | solution.py:1013
  134.9 11.1 %collective-permute-start.23 = (f32[16,768]{1,0:T(8,128)S(1)}, f32[16,768]{1,0:T(8,128)S(1)}, u32[]{:S(2)}, u32[]{:S(2)}) collective-permute-start(f32[16,768]{1,0:T(8,128)S(1)} %get-tuple-element.198.refs_0_), channel_id=1, source_target_pairs={{0,1},{1,0},{2,3},{3,2},{4,5},{5,4},{6,7},{7,6},{8,9},{9,8},{10,11... | collective-permute-start | bytes 147464 | tf_op jit(solution)/shard_map/ppermute | solution.py:1010
  146.1 11.3 %collective-permute-start.27 = (f32[2,256,768]{2,1,0:T(8,128)}, f32[2,256,768]{2,1,0:T(8,128)}, u32[]{:S(2)}, u32[]{:S(2)}) collective-permute-start(f32[2,256,768]{2,1,0:T(8,128)} %get-tuple-element.206), channel_id=1, source_target_pairs={{0,1},{1,0},{2,3},{3,2},{4,5},{5,4},{6,7},{7,6},{8,9},{9,8},{10,11... | collective-permute-start | bytes 4718600 | tf_op jit(solution)/shard_map/ppermute | solution.py:1010
  146.1 4.2 %collective-permute-start.29 = (f32[16,768]{1,0:T(8,128)S(1)}, f32[16,768]{1,0:T(8,128)S(1)}, u32[]{:S(2)}, u32[]{:S(2)}) collective-permute-start(f32[16,768]{1,0:T(8,128)S(1)} %add.61), channel_id=1, source_target_pairs={{0,2},{1,3},{2,0},{3,1},{4,6},{5,7},{6,4},{7,5},{8,10},{9,11},{10,... | collective-permute-start | bytes 147464 | tf_op jit(solution)/shard_map/ppermute | solution.py:1010
  150.2 7.1 %collective-permute-start.30 = (f32[16,768]{1,0:T(8,128)S(1)}, f32[16,768]{1,0:T(8,128)S(1)}, u32[]{:S(2)}, u32[]{:S(2)}) collective-permute-start(f32[16,768]{1,0:T(8,128)S(1)} %add.62), channel_id=1, source_target_pairs={{0,4},{4,0},{8,12},{12,8},{16,20},{20,16},{24,28},{28,24},{1,5},{5... | collective-permute-start | bytes 147464 | tf_op jit(solution)/shard_map/ppermute | solution.py:1013
  150.7 12.2 %collective-permute-start.31 = (bf16[3,96,384]{2,1,0:T(8,128)(2,1)}, bf16[3,96,384]{2,1,0:T(8,128)(2,1)S(1)}, u32[]{:S(2)}, u32[]{:S(2)}) collective-permute-start(bf16[3,96,384]{2,1,0:T(8,128)(2,1)} %copy-done.11), channel_id=1, source_target_pairs={{0,16},{4,20},{8,24},{12,28},{16,0},{20,4},{24,8},{28,12},{1,17},{... | collective-permute-start | bytes 663560 | tf_op jit(solution)/shard_map/ppermute | solution.py:1013
  151.4 11.6 %collective-permute-start.32 = (bf16[3,96,384]{2,1,0:T(8,128)(2,1)S(1)}, bf16[3,96,384]{2,1,0:T(8,128)(2,1)S(1)}, u32[]{:S(2)}, u32[]{:S(2)}) collective-permute-start(bf16[3,96,384]{2,1,0:T(8,128)(2,1)S(1)} %get-tuple-element.213), channel_id=1, source_target_pairs={{0,8},{4,12},{8,0},{12,4},{16,24},{20,28},{24,16},{28,20},{1,9},{5... | collective-permute-start | bytes 663560 | tf_op jit(solution)/shard_map/ppermute | solution.py:1013
  158.6 11.0 %collective-permute-start.28 = (bf16[256,768]{1,0:T(8,128)(2,1)S(1)}, bf16[256,768]{1,0:T(8,128)(2,1)S(1)}, u32[]{:S(2)}, u32[]{:S(2)}) collective-permute-start(bf16[256,768]{1,0:T(8,128)(2,1)S(1)} %fusion.1.refs_2_), channel_id=1, source_target_pairs={{0,2},{1,3},{2,0},{3,1},{4,6},{5,7},{6,4},{7,5},{8,10},{9,11},{10,... | collective-permute-start | bytes 1179656 | tf_op jit(solution)/shard_map/ppermute | solution.py:1010
  163.0 6.6 %collective-permute-start.34 = (bf16[1,96,384]{2,1,0:T(8,128)(2,1)S(1)}, bf16[1,96,384]{2,1,0:T(8,128)(2,1)S(1)}, u32[]{:S(2)}, u32[]{:S(2)}) collective-permute-start(bf16[1,96,384]{2,1,0:T(8,128)(2,1)S(1)} %get-tuple-element.220), channel_id=1, source_target_pairs={{0,16},{4,20},{8,24},{12,28},{16,0},{20,4},{24,8},{28,12},{1,17},{... | collective-permute-start | bytes 221192 | tf_op jit(solution)/shard_map/ppermute | solution.py:1013
  165.4 4.2 %collective-permute-start.33 = (f32[16,768]{1,0:T(8,128)S(1)}, f32[16,768]{1,0:T(8,128)S(1)}, u32[]{:S(2)}, u32[]{:S(2)}) collective-permute-start(f32[16,768]{1,0:T(8,128)S(1)} %add.63.refs_1_), channel_id=1, source_target_pairs={{0,8},{4,12},{8,0},{12,4},{16,24},{20,28},{24,16},{28,20},{1,9},{5... | collective-permute-start | bytes 147464 | tf_op jit(solution)/shard_map/ppermute | solution.py:1013
  170.7 5.7 %collective-permute-start.38 = (f32[16,768]{1,0:T(8,128)S(1)}, f32[16,768]{1,0:T(8,128)S(1)}, u32[]{:S(2)}, u32[]{:S(2)}) collective-permute-start(f32[16,768]{1,0:T(8,128)S(1)} %add.64), channel_id=1, source_target_pairs={{0,16},{4,20},{8,24},{12,28},{16,0},{20,4},{24,8},{28,12},{1,17},{... | collective-permute-start | bytes 147464 | tf_op jit(solution)/shard_map/ppermute | solution.py:1013
  171.8 5.8 %collective-permute-start.35 = (bf16[2,96,192]{2,1,0:T(8,128)(2,1)S(1)}, bf16[2,96,192]{2,1,0:T(8,128)(2,1)S(1)}, u32[]{:S(2)}, u32[]{:S(2)}) collective-permute-start(bf16[2,96,192]{2,1,0:T(8,128)(2,1)S(1)} %get-tuple-element.223), channel_id=1, source_target_pairs={{0,1},{1,0},{2,3},{3,2},{4,5},{5,4},{6,7},{7,6},{8,9},{9,8},{10,11... | collective-permute-start | bytes 221192 | tf_op jit(solution)/shard_map/ppermute | solution.py:1010
  171.8 5.8 %collective-permute-start.36 = (bf16[2,96,192]{2,1,0:T(8,128)(2,1)S(1)}, bf16[2,96,192]{2,1,0:T(8,128)(2,1)S(1)}, u32[]{:S(2)}, u32[]{:S(2)}) collective-permute-start(bf16[2,96,192]{2,1,0:T(8,128)(2,1)S(1)} %get-tuple-element.224), channel_id=1, source_target_pairs={{0,2},{1,3},{2,0},{3,1},{4,6},{5,7},{6,4},{7,5},{8,10},{9,11},{10,... | collective-permute-start | bytes 221192 | tf_op jit(solution)/shard_map/ppermute | solution.py:1010
  173.5 5.3 %collective-permute-start.37 = (bf16[2,96,192]{2,1,0:T(8,128)(2,1)S(1)}, bf16[2,96,192]{2,1,0:T(8,128)(2,1)S(1)}, u32[]{:S(2)}, u32[]{:S(2)}) collective-permute-start(bf16[2,96,192]{2,1,0:T(8,128)(2,1)S(1)} %get-tuple-element.225), channel_id=1, source_target_pairs={{0,3},{1,2},{2,1},{3,0},{4,7},{5,6},{6,5},{7,4},{8,11},{9,10},{10,... | collective-permute-start | bytes 221192 | tf_op jit(solution)/shard_map/ppermute | solution.py:1010
  (17 other events, 107.1 us)

commit v6 on v5

--- a/solution.py
+++ b/solution.py
@@ -16,9 +16,10 @@
 SCALE = DH**-0.5
 BLOCK = 256
 UNIT = 128
+WINDOWED = (0, 2)
 SIZES = (5, 8)
 VMEM = 18
-CHUNKS = 1
+CHUNKS = 2
 ROOT_HALF = 0.5**0.5
 ROOT_TWO_PI = 0.3989422804014327
 
@@ -261,7 +262,10 @@
             o_out[:, here] = mixed
             ctx[here, :] = mixed.T.astype(LOW)
 
-        each_window(info, b, run)
+        if project:
+            each_window(info, b, run)
+        else:
+            run(pl.ds(0, tokens), tokens)
         return 0
 
     lax.fori_loop(0, len(parts) * each, step, 0)
@@ -389,7 +393,10 @@
             d_query = own_heads(dot_nn(kt[:, window], d_scores)) * SCALE
             dq_out[rows, :] = d_query.T.astype(LOW)
 
-        each_window(info, b, run)
+        if n in WINDOWED:
+            each_window(info, b, run)
+        else:
+            run(pl.ds(0, tokens), tokens)
         return 0
 
     lax.fori_loop(0, tokens // BLOCK, step, 0)
@@ -726,26 +733,28 @@
 
 
 def down_kernel(info, mine, theirs, act, act_pair, *outs):
-    rel = pl.program_id(0)
     left = jnp.concatenate([mine[0], mine[1]], axis=0)
-    grad = dot_nn(left, act[...]) + dot_nn(theirs[...], act_pair[...])
-    size = grad.shape[0] // 4
-    for n, order in enumerate(DOWN_ORDERS):
-        for flip in range(2):
-            start = (2 * flip + n) * size
-            put(grad[start : start + size], rel, flip, order, outs[2 * n], outs[2 * n + 1])
+    both = dot_nn(left, act[...]) + dot_nn(theirs[...], act_pair[...])
+    size, block = both.shape[0] // 4, both.shape[1] // 2
+    for side in range(2):
+        rel = 2 * pl.program_id(0) + (side ^ (info[3] % 2))
+        grad = both[:, side * block : (side + 1) * block]
+        for n, order in enumerate(DOWN_ORDERS):
+            for flip in range(2):
+                start = (2 * flip + n) * size
+                put(grad[start : start + size], rel, flip, order, outs[2 * n], outs[2 * n + 1])
 
 
 def down_grad(info, mine, theirs, act, act_pair, after):
     _, size, count = mine.shape
     block = act.shape[1] // 8
     part = (8, size // 2, block)
-    spec = pl.BlockSpec((count, block), lambda r, i: (0, r ^ i[3]))
+    spec = pl.BlockSpec((count, 2 * block), lambda r, i: (0, r ^ (i[3] // 2)))
     return pl.pallas_call(
         ordered(down_kernel, after),
         grid_spec=pltpu.PrefetchScalarGridSpec(
             num_scalar_prefetch=1,
-            grid=(8,),
+            grid=(4,),
             in_specs=waiting(after) + [full(mine.shape), full(theirs.shape), spec, spec],
             out_specs=[full(part)] * 4,
         ),
@@ -765,17 +774,16 @@
     me = info[3]
     step = pl.program_id(0)
 
-    @pl.when(step < 4)
-    def _():
-        grad = dot_nn(left[0], mine[0]) + dot_nn(left_pair[0], theirs[...])
-        for n, flip in ((0, 0), (1, 0), (0, 1), (1, 1)):
-
-            @pl.when(step == 2 * flip + n)
-            def _():
-                send, keep = ((send_a, keep_a), (send_b, keep_b))[n]
-                put_rows(grad, rows, me, flip, UP_ORDERS[n], send, keep)
-
-    @pl.when(step == 4)
+    for flip in range(2):
+
+        @pl.when(step == flip)
+        def _():
+            both = dot_nn(left[0], mine[0]) + dot_nn(left_pair[0], theirs[...])
+            wide = both.shape[1] // 2
+            put_rows(both[:, :wide], rows, me, flip, UP_ORDERS[0], send_a, keep_a)
+            put_rows(both[:, wide:], rows, me, flip, UP_ORDERS[1], send_b, keep_b)
+
+    @pl.when(step == 2)
     def _():
         right = jnp.concatenate([mine_d[0], mine_d[1]], axis=0)
         grad = dot_nt(left[1], right) + dot_nt(left_pair[1], theirs_d[...])
@@ -799,7 +807,7 @@
     half = width // 2
 
     def at(s):
-        return jnp.minimum(s, 3)
+        return jnp.minimum(s, 1)
 
     shapes = [
         shaped((lead, width // 8, half), dtype) for lead in (8, 12) for dtype in (LOW, F32)
@@ -808,12 +816,12 @@
         ordered(up_kernel, after),
         grid_spec=pltpu.PrefetchScalarGridSpec(
             num_scalar_prefetch=1,
-            grid=(5,),
+            grid=(3,),
             in_specs=waiting(after)
             + [full(left.shape)] * 2
             + [
-                pl.BlockSpec((1, count, half), lambda s, i: (at(s) // 2, 0, at(s) % 2)),
-                pl.BlockSpec((count, half), lambda s, i: (1 + at(s) // 2, at(s) % 2)),
+                pl.BlockSpec((1, count, width), lambda s, i: (at(s), 0, 0)),
+                pl.BlockSpec((count, width), lambda s, i: (1 + at(s), 0)),
                 full(mine_d.shape),
                 pl.BlockSpec((half, count), lambda s, i: (0, 0)),
             ],

time: 181 us -> 180 us (level)
  waiting for transfers between devices: 31.8 us -> 41.4 us
  Pallas kernels: 89.3 us -> 83.8 us
  starting transfers between devices: 41.4 us -> 36.6 us
    ppermute x16, waiting for transfers between devices: 10.1 us -> 17.9 us  [over_batch(): lax.ppermute(array, 'batch', [(i, i ^ flip) for i in range(batch_size)])]
    ppermute x16, starting transfers between devices: 25.2 us -> 22.1 us  [over_batch(): lax.ppermute(array, 'batch', [(i, i ^ flip) for i in range(batch_size)])]
    pallas_call x1, Pallas kernels: 7.84 us -> 5.63 us  [down_grad(): pl.pallas_call(ordered(down_kernel, after), grid_spec=pltpu.PrefetchScala...]
    ppermute x23, waiting for transfers between devices: 21.6 us -> 23.5 us  [over_seq(): return lax.ppermute(array, 'seq', [(i, i ^ flip) for i in range(seq_size)])]
    pallas_call x1, Pallas kernels: 6.95 us -> 5.12 us  [up_grad(): pl.pallas_call(ordered(up_kernel, after), grid_spec=pltpu.PrefetchScalarG...]
  transfers between devices with their start and end apart: 39 -> 39, of which waited for: 14 -> 15; matrix products, arithmetic and copies ran while one was open for 6% -> 6% of each run, Pallas kernels for 33% -> 31%
where the time goes in v6:
time: 180 us
  Pallas kernels  83.8 us (47%)
  waiting for transfers between devices  41.4 us (23%)
  starting transfers between devices  36.6 us (20%)
  local copies, waits for them, and re-layouts  11.5 us (6%)
  other arithmetic  4.9 us (3%)
    ppermute x23, waiting for transfers between devices, over_seq(): return lax.ppermute(array, 'seq', [(i, i ^ flip) for i in range(seq_size)])  23.5 us
    pallas_call x3, Pallas kernels, attend_backward(): pl.pallas_call(ordered(functools.partial(backward_kernel, n), after), gri...  22.8 us
    ppermute x16, starting transfers between devices, over_batch(): lax.ppermute(array, 'batch', [(i, i ^ flip) for i in range(batch_size)])  22.1 us
    ppermute x16, waiting for transfers between devices, over_batch(): lax.ppermute(array, 'batch', [(i, i ^ flip) for i in range(batch_size)])  17.9 us
    ppermute x23, starting transfers between devices, over_seq(): return lax.ppermute(array, 'seq', [(i, i ^ flip) for i in range(seq_size)])  14.5 us
    pallas_call x1, Pallas kernels, attend_forward(): pl.pallas_call(functools.partial(forward_kernel, True), grid_spec=pltpu.P...  13.7 us
    pallas_call x1, Pallas kernels, middle_forward(): pl.pallas_call(ordered(middle_forward_kernel, after), grid_spec=pltpu.Pre...  11.8 us
    pallas_call x1, Pallas kernels, middle_backward(): pl.pallas_call(middle_backward_kernel, grid_spec=pltpu.PrefetchScalarGrid...  10.3 us
  transfers between devices with their start and end apart: 39, of which 15 were waited for; matrix products, arithmetic and copies ran while one was open for 6% of the time, Pallas kernels for 31%

profile of v6, /device:TPU:0, one launch (start us, length us, event | category | flops | bytes accessed | tf_op | source)
XLA Modules:
  0.0 179.5 jit_solution(15933970919575612748)
XLA Ops:
  0.8 1.2 dynamic-slice_bitcast_fusion
  2.0 3.0 %collective-permute-start.1 = (bf16[256,768]{1,0:T(8,128)(2,1)S(1)}, bf16[256,768]{1,0:T(8,128)(2,1)S(1)}, u32[]{:S(2)}, u32[]{:S(2)}) collective-permute-start(bf16[256,768]{1,0:T(8,128)(2,1)S(1)} %get-tuple-element.245), channel_id=1, source_target_pairs={{0,2},{1,3},{2,0},{3,1},{4,6},{5,7},{6,4},{7,5},{8,10},{9,11},{10,... | collective-permute-start | bytes 1179656 | tf_op jit(solution)/shard_map/ppermute | solution.py:1018
  6.2 7.9 %collective-permute-done.1.x2.refs_2_ = bf16[256,768]{1,0:T(8,128)(2,1)S(1)} collective-permute-done((bf16[256,768]{1,0:T(8,128)(2,1)S(1)}, bf16[256,768]{1,0:T(8,128)(2,1)S(1)}, u32[]{:S(2)}, u32[]{:S(2)}) %collective-permute-start.1) | collective-permute-done | bytes 393248 | tf_op jit(solution)/shard_map/ppermute | solution.py:1018
  14.8 1.0 collective-permute-done.2.x3.refs_3_
  15.8 2.0 %copy-done.3 = bf16[768,2304]{1,0:T(8,128)(2,1)S(1)} copy-done((bf16[768,2304]{1,0:T(8,128)(2,1)S(1)}, bf16[768,2304]{1,0:T(8,128)(2,1)}, u32[]{:S(2)}) %copy-start.3) | copy-done | bytes 3538968
  17.8 13.7 %attend_forward.1 = (bf16[1024,384]{1,0:T(8,128)(2,1)S(1)}, bf16[1024,384]{1,0:T(8,128)(2,1)S(1)}, bf16[1024,384]{1,0:T(8,128)(2,1)S(1)}, bf16[256,384]{1,0:T(8,...) custom-call(s32[12]{0:T(128)S(1)} %concatenate.6.info, ...), custom_call_target="tpu_custom_call" | custom-call | flops 9600000000 | tf_op jit(solution)/shard_map/attend_forward/pallas_call | solution.py:313
  31.7 2.5 %collective-permute-start.4 = (bf16[256,384]{1,0:T(8,128)(2,1)S(1)}, bf16[256,384]{1,0:T(8,128)(2,1)S(1)}, u32[]{:S(2)}, u32[]{:S(2)}) collective-permute-start(bf16[256,384]{1,0:T(8,128)(2,1)S(1)} %get-tuple-element.126), channel_id=1, source_target_pairs={{0,2},{1,3},{2,0},{3,1},{4,6},{5,7},{6,4},{7,5},{8,10},{9,11},{10,... | collective-permute-start | bytes 589832 | tf_op jit(solution)/shard_map/ppermute | solution.py:1018
  34.3 1.0 turn.1.refs_0_.refs_14_
  35.4 4.8 %attend_own.1 = (bf16[256,384]{1,0:T(8,128)(2,1)S(1)}, f32[384,256]{1,0:T(8,128)S(1)}, f32[3,1,512]{2,1,0:T(1,128)S(1)}) custom-call(s32[12]{0:T(128)S(1)} %concatenate.6.info, bf16[1024,384]{1,0:T(8,128)(2,1)S(1)} %get-tuple-element.121.refs_0_.refs_1_, bf16[1024,384]{1,0:T(8,128)(2,1)S(1)} %get-tuple-element.122.refs_1_.refs_2_, ...), custom_call_target="tpu_custom_call" | custom-call | flops 3000000000 | tf_op jit(solution)/shard_map/attend_own/pallas_call | solution.py:330
  40.2 3.5 %collective-permute-done.5.refs_4_ = bf16[256,384]{1,0:T(8,128)(2,1)S(1)} collective-permute-done((bf16[256,384]{1,0:T(8,128)(2,1)S(1)}, bf16[256,384]{1,0:T(8,128)(2,1)S(1)}, u32[]{:S(2)}, u32[]{:S(2)}) %collective-permute-start.5) | collective-permute-done | bytes 196640 | tf_op jit(solution)/shard_map/ppermute | solution.py:1018
  43.8 11.8 %middle_forward.1 = (bf16[2,256,768]{2,1,0:T(8,128)(2,1)}, f32[512,768]{1,0:T(8,128)S(1)}, f32[512,768]{1,0:T(8,128)S(1)}, f32[512,1]{1,0:T(8,128)S(1)}, bf16[2,...) custom-call(s32[12]{0:T(128)S(1)} %concatenate.6.info, ...), custom_call_target="tpu_custom_call" | custom-call | flops 10800000000 | tf_op jit(solution)/shard_map/middle_forward/pallas_call | solution.py:577
  56.2 10.3 %middle_backward.1 = (bf16[1536,768]{1,0:T(8,128)(2,1)S(1)}, bf16[2,512,768]{2,1,0:T(8,128)(2,1)S(1)}, f32[512,768]{1,0:T(8,128)S(1)}, bf16[256,384]{1,0:T(8,128...) custom-call(s32[12]{0:T(128)S(1)} %concatenate.6.info, ...), custom_call_target="tpu_custom_call" | custom-call | flops 9600000000 | tf_op jit(solution)/shard_map/middle_backward/pallas_call | solution.py:691
  67.1 1.6 collective-permute-start.10
  68.6 5.6 %down_grad.1 = (bf16[8,96,384]{2,1,0:T(8,128)(2,1)S(1)}, f32[8,96,384]{2,1,0:T(8,128)S(1)}, bf16[8,96,384]{2,1,0:T(8,128)(2,1)S(1)}, f32[8,96,384]{2,1,0:T(8,128)S(1)}) custom-call(s32[12]{0:T(128)S(1)} %concatenate.6.info, f32[8,128]{1,0:T(8,128)S(1)} %mark.1.refs_0_, bf16[2,192,512]{2,1,0:T(8,128)(2,1)S(1)} %get-tuple-element.142.refs_1_, ...), custom_call_target="tpu_custom_call" | custom-call | flops 4800000000 | tf_op jit(solution)/shard_map/down_grad/pallas_call | solution.py:753
  74.3 1.2 collective-permute-start.12
  76.0 2.4 %collective-permute-done.10.refs_7_ = bf16[2,256,384]{2,1,0:T(8,128)(2,1)S(1)} collective-permute-done((bf16[2,256,384]{2,1,0:T(8,128)(2,1)S(1)}, bf16[2,256,384]{2,1,0:T(8,128)(2,1)S(1)}, u32[]{:S(2)}, u32[]{:S(2)}) %collective-permute-start.10) | collective-permute-done | bytes 393248 | tf_op jit(solution)/shard_map/ppermute | solution.py:1018
  78.5 5.1 %up_grad.1 = (bf16[8,96,384]{2,1,0:T(8,128)(2,1)S(1)}, f32[8,96,384]{2,1,0:T(8,128)S(1)}, bf16[12,96,384]{2,1,0:T(8,128)(2,1)S(1)}, f32[12,96,384]{2,1,0:T(8,128)S(1)}) custom-call(s32[12]{0:T(128)S(1)} %concatenate.6.info, f32[8,96,384]{2,1,0:T(8,128)S(1)} %get-tuple-element.143.refs_0_.refs_1_, bf16[2,768,512]{2,1,0:T(8,128)(2,1)S(1)} %get-tuple-element.137.refs_1_, ...), custom_call_target="tpu_custom_call" | custom-call | flops 6000000000 | tf_op jit(solution)/shard_map/up_grad/pallas_call | solution.py:815
  83.6 1.8 %collective-permute-start.15 = (bf16[12,96,384]{2,1,0:T(8,128)(2,1)S(1)}, bf16[12,96,384]{2,1,0:T(8,128)(2,1)S(1)}, u32[]{:S(2)}, u32[]{:S(2)}) collective-permute-start(bf16[12,96,384]{2,1,0:T(8,128)(2,1)S(1)} %get-tuple-element.165), channel_id=1, source_target_pairs={{0,4},{4,0},{8,12},{12,8},{16,20},{20,16},{24,28},{28,24},{1,5},{5... | collective-permute-start | bytes 2654216 | tf_op jit(solution)/shard_map/ppermute | solution.py:1021
  86.4 7.3 %attend_backward.3 = (bf16[1024,128]{1,0:T(8,128)(2,1)S(1)}, bf16[1024,128]{1,0:T(8,128)(2,1)S(1)}, bf16[1024,128]{1,0:T(8,128)(2,1)S(1)}, f32[16,768]{1,0:T(8,1...) custom-call(s32[12]{0:T(128)S(1)} %concatenate.6.info, ...), custom_call_target="tpu_custom_call" | custom-call | flops 4800000000 | tf_op jit(solution)/shard_map/attend_backward/pallas_call | solution.py:434
  94.0 3.0 %collective-permute-start.18 = (bf16[4,96,384]{2,1,0:T(8,128)(2,1)S(1)}, bf16[4,96,384]{2,1,0:T(8,128)(2,1)S(1)}, u32[]{:S(2)}, u32[]{:S(2)}) collective-permute-start(bf16[4,96,384]{2,1,0:T(8,128)(2,1)S(1)} %get-tuple-element.171), channel_id=1, source_target_pairs={{0,8},{4,12},{8,0},{12,4},{16,24},{20,28},{24,16},{28,20},{1,9},{5... | collective-permute-start | bytes 884744 | tf_op jit(solution)/shard_map/ppermute | solution.py:1021
  97.6 8.3 %attend_backward.4 = (bf16[1024,128]{1,0:T(8,128)(2,1)S(1)}, bf16[1024,128]{1,0:T(8,128)(2,1)S(1)}, bf16[1024,128]{1,0:T(8,128)(2,1)S(1)}, f32[16,768]{1,0:T(8,1...) custom-call(s32[12]{0:T(128)S(1)} %concatenate.6.info, f32[8,128]{1,0:T(8,128)S(1)} %get-tuple-element.160.refs_0_, ...), custom_call_target="tpu_custom_call" | custom-call | flops 4800000000 | tf_op jit(solution)/shard_map/attend_backward/pallas_call | solution.py:434
  105.9 3.9 %collective-permute-done.16.refs_6_ = bf16[4,96,384]{2,1,0:T(8,128)(2,1)S(1)} collective-permute-done((bf16[4,96,384]{2,1,0:T(8,128)(2,1)S(1)}, bf16[4,96,384]{2,1,0:T(8,128)(2,1)S(1)}, u32[]{:S(2)}, u32[]{:S(2)}) %collective-permute-start.16) | collective-permute-done | bytes 294944 | tf_op jit(solution)/shard_map/ppermute | solution.py:1018
  110.8 1.2 collective-permute-start.19
  112.7 2.4 %collective-permute-start.22 = (bf16[4,96,384]{2,1,0:T(8,128)(2,1)S(1)}, bf16[4,96,384]{2,1,0:T(8,128)(2,1)S(1)}, u32[]{:S(2)}, u32[]{:S(2)}) collective-permute-start(bf16[4,96,384]{2,1,0:T(8,128)(2,1)S(1)} %get-tuple-element.182), channel_id=1, source_target_pairs={{0,8},{4,12},{8,0},{12,4},{16,24},{20,28},{24,16},{28,20},{1,9},{5... | collective-permute-start | bytes 884744 | tf_op jit(solution)/shard_map/ppermute | solution.py:1021
  115.1 1.1 collective-permute-start.21
  116.2 7.1 %attend_backward.5 = (bf16[1024,128]{1,0:T(8,128)(2,1)S(1)}, bf16[1024,128]{1,0:T(8,128)(2,1)S(1)}, bf16[1024,128]{1,0:T(8,128)(2,1)S(1)}, f32[16,768]{1,0:T(8,1...) custom-call(s32[12]{0:T(128)S(1)} %concatenate.6.info, f32[8,128]{1,0:T(8,128)S(1)} %get-tuple-element.173.refs_0_, ...), custom_call_target="tpu_custom_call" | custom-call | flops 4800000000 | tf_op jit(solution)/shard_map/attend_backward/pallas_call | solution.py:434
  123.4 3.9 %collective-permute-done.22.refs_8_ = bf16[4,96,384]{2,1,0:T(8,128)(2,1)S(1)} collective-permute-done((bf16[4,96,384]{2,1,0:T(8,128)(2,1)S(1)}, bf16[4,96,384]{2,1,0:T(8,128)(2,1)S(1)}, u32[]{:S(2)}, u32[]{:S(2)}) %collective-permute-start.22) | collective-permute-done | bytes 294944 | tf_op jit(solution)/shard_map/ppermute | solution.py:1021
  127.3 2.6 %collective-permute-done.21.refs_6_ = bf16[4,96,384]{2,1,0:T(8,128)(2,1)S(1)} collective-permute-done((bf16[4,96,384]{2,1,0:T(8,128)(2,1)S(1)}, bf16[4,96,384]{2,1,0:T(8,128)(2,1)S(1)}, u32[]{:S(2)}, u32[]{:S(2)}) %collective-permute-start.21) | collective-permute-done | bytes 294944 | tf_op jit(solution)/shard_map/ppermute | solution.py:1021
  131.2 2.6 %collective-permute-start.26 = (bf16[3,96,384]{2,1,0:T(8,128)(2,1)S(1)}, bf16[3,96,384]{2,1,0:T(8,128)(2,1)S(1)}, u32[]{:S(2)}, u32[]{:S(2)}) collective-permute-start(bf16[3,96,384]{2,1,0:T(8,128)(2,1)S(1)} %get-tuple-element.204), channel_id=1, source_target_pairs={{0,16},{4,20},{8,24},{12,28},{16,0},{20,4},{24,8},{28,12},{1,17},{... | collective-permute-start | bytes 663560 | tf_op jit(solution)/shard_map/ppermute | solution.py:1021
  133.8 5.1 %input_part.1 = (f32[256,768]{1,0:T(8,128)S(1)}, f32[256,768]{1,0:T(8,128)S(1)}, f32[2,256,768]{2,1,0:T(8,128)}) custom-call(s32[12]{0:T(128)S(1)} %concatenate.6.info, f32[8,128]{1,0:T(8,128)S(1)} %get-tuple-element.186.refs_0_, bf16[1024,128]{1,0:T(8,128)(2,1)S(1)} %get-tuple-element.187.refs_1_, bf16[1024,128]{1,0:T(8,128)(2,1)S(1)} %get-tuple-element.188.refs_2_, ...), custom_call_target="tpu_custom_call" | custom-call | flops 3600000000 | tf_op jit(solution)/shard_map/input_part/pallas_call | solution.py:869
  139.0 2.7 %collective-permute-done.26.refs_6_ = bf16[3,96,384]{2,1,0:T(8,128)(2,1)S(1)} collective-permute-done((bf16[3,96,384]{2,1,0:T(8,128)(2,1)S(1)}, bf16[3,96,384]{2,1,0:T(8,128)(2,1)S(1)}, u32[]{:S(2)}, u32[]{:S(2)}) %collective-permute-start.26) | collective-permute-done | bytes 221216 | tf_op jit(solution)/shard_map/ppermute | solution.py:1021
  145.5 3.7 %collective-permute-done.29 = f32[16,768]{1,0:T(8,128)S(1)} collective-permute-done((f32[16,768]{1,0:T(8,128)S(1)}, f32[16,768]{1,0:T(8,128)S(1)}, u32[]{:S(2)}, u32[]{:S(2)}) %collective-permute-start.29) | collective-permute-done | bytes 49184 | tf_op jit(solution)/shard_map/ppermute | solution.py:1018
  149.2 1.6 collective-permute-start.30
  150.8 1.1 collective-permute-start.31
  151.9 1.3 collective-permute-start.32
  153.2 1.7 slice.76
  154.9 1.2 fusion.1.refs_2_
  156.1 1.0 collective-permute-start.28
  157.1 5.8 %collective-permute-done.31.refs_4_ = bf16[3,96,384]{2,1,0:T(8,128)(2,1)S(1)} collective-permute-done((bf16[3,96,384]{2,1,0:T(8,128)(2,1)}, bf16[3,96,384]{2,1,0:T(8,128)(2,1)S(1)}, u32[]{:S(2)}, u32[]{:S(2)}) %collective-permute-start.31) | collective-permute-done | bytes 221216 | tf_op jit(solution)/shard_map/ppermute | solution.py:1021
  163.1 1.3 collective-permute-start.34
  164.4 1.2 collective-permute-start.33
  167.0 1.5 collective-permute-done.33.refs_1_
  170.1 1.2 collective-permute-start.38
  171.6 1.5 collective-permute-start.37
  173.1 1.4 select_bitcast_fusion.1
  174.5 1.2 pad_maximum_fusion
  177.0 1.1 collective-permute-done.37.three
  178.2 1.4 gather.1
  (136 shorter events, 17.1 us)
Async XLA Ops:
  0.7 13.6 %copy-start.14 = (bf16[768]{0:T(1024)(128)(2,1)S(1)}, bf16[768]{0:T(1024)(128)(2,1)}, u32[]{:S(2)}) copy-start(bf16[768]{0:T(1024)(128)(2,1)} %param.19) | copy-start | bytes 4612
  0.7 13.6 %copy-start.15 = (bf16[768]{0:T(1024)(128)(2,1)S(1)}, bf16[768]{0:T(1024)(128)(2,1)}, u32[]{:S(2)}) copy-start(bf16[768]{0:T(1024)(128)(2,1)} %param.20) | copy-start | bytes 4612
  0.7 13.7 %copy-start.16 = (bf16[768]{0:T(1024)(128)(2,1)S(1)}, bf16[768]{0:T(1024)(128)(2,1)}, u32[]{:S(2)}) copy-start(bf16[768]{0:T(1024)(128)(2,1)} %param.23) | copy-start | bytes 4612
  0.7 13.7 %copy-start.12 = (bf16[3072]{0:T(1024)(128)(2,1)S(1)}, bf16[3072]{0:T(1024)(128)(2,1)}, u32[]{:S(2)}) copy-start(bf16[3072]{0:T(1024)(128)(2,1)} %param.26) | copy-start | bytes 18436
  0.7 13.7 %copy-start.17 = (bf16[768]{0:T(1024)(128)(2,1)S(1)}, bf16[768]{0:T(1024)(128)(2,1)}, u32[]{:S(2)}) copy-start(bf16[768]{0:T(1024)(128)(2,1)} %param.22) | copy-start | bytes 4612
  0.7 13.7 %copy-start.18 = (bf16[768]{0:T(1024)(128)(2,1)S(1)}, bf16[768]{0:T(1024)(128)(2,1)}, u32[]{:S(2)}) copy-start(bf16[768]{0:T(1024)(128)(2,1)} %param.24) | copy-start | bytes 4612
  0.7 13.7 %copy-start.19 = (bf16[768]{0:T(1024)(128)(2,1)S(1)}, bf16[768]{0:T(1024)(128)(2,1)}, u32[]{:S(2)}) copy-start(bf16[768]{0:T(1024)(128)(2,1)} %param.28) | copy-start | bytes 4612
  0.7 13.7 %copy-start.20 = (bf16[768]{0:T(1024)(128)(2,1)S(1)}, bf16[768]{0:T(1024)(128)(2,1)}, u32[]{:S(2)}) copy-start(bf16[768]{0:T(1024)(128)(2,1)} %param.29) | copy-start | bytes 4612
  0.7 13.7 %copy-start.21 = (bf16[768]{0:T(1024)(128)(2,1)S(1)}, bf16[768]{0:T(1024)(128)(2,1)}, u32[]{:S(2)}) copy-start(bf16[768]{0:T(1024)(128)(2,1)} %param.30) | copy-start | bytes 4612
  2.0 12.1 %collective-permute-start.1 = (bf16[256,768]{1,0:T(8,128)(2,1)S(1)}, bf16[256,768]{1,0:T(8,128)(2,1)S(1)}, u32[]{:S(2)}, u32[]{:S(2)}) collective-permute-start(bf16[256,768]{1,0:T(8,128)(2,1)S(1)} %get-tuple-element.245), channel_id=1, source_target_pairs={{0,2},{1,3},{2,0},{3,1},{4,6},{5,7},{6,4},{7,5},{8,10},{9,11},{10,... | collective-permute-start | bytes 1179656 | tf_op jit(solution)/shard_map/ppermute | solution.py:1018
  5.0 9.9 %collective-permute-start = (bf16[256,768]{1,0:T(8,128)(2,1)S(1)}, bf16[256,768]{1,0:T(8,128)(2,1)S(1)}, u32[]{:S(2)}, u32[]{:S(2)}) collective-permute-start(bf16[256,768]{1,0:T(8,128)(2,1)S(1)} %get-tuple-element.246.x0.refs_0_), channel_id=1, source_target_pairs={{0,1},{1,0},{2,3},{3,2},{4,5},{5,4},{6,7},{7,6},{8,9},{9,8},{10,11... | collective-permute-start | bytes 1179656 | tf_op jit(solution)/shard_map/ppermute | solution.py:1018
  14.1 1.7 collective-permute-start.2
  31.5 8.7 %collective-permute-start.3 = (bf16[256,384]{1,0:T(8,128)(2,1)S(1)}, bf16[256,384]{1,0:T(8,128)(2,1)S(1)}, u32[]{:S(2)}, u32[]{:S(2)}) collective-permute-start(bf16[256,384]{1,0:T(8,128)(2,1)S(1)} %get-tuple-element.125), channel_id=1, source_target_pairs={{0,1},{1,0},{2,3},{3,2},{4,5},{5,4},{6,7},{7,6},{8,9},{9,8},{10,11... | collective-permute-start | bytes 589832 | tf_op jit(solution)/shard_map/ppermute | solution.py:1018
  31.7 8.5 %collective-permute-start.4 = (bf16[256,384]{1,0:T(8,128)(2,1)S(1)}, bf16[256,384]{1,0:T(8,128)(2,1)S(1)}, u32[]{:S(2)}, u32[]{:S(2)}) collective-permute-start(bf16[256,384]{1,0:T(8,128)(2,1)S(1)} %get-tuple-element.126), channel_id=1, source_target_pairs={{0,2},{1,3},{2,0},{3,1},{4,6},{5,7},{6,4},{7,5},{8,10},{9,11},{10,... | collective-permute-start | bytes 589832 | tf_op jit(solution)/shard_map/ppermute | solution.py:1018
  34.3 9.4 %collective-permute-start.5 = (bf16[256,384]{1,0:T(8,128)(2,1)S(1)}, bf16[256,384]{1,0:T(8,128)(2,1)S(1)}, u32[]{:S(2)}, u32[]{:S(2)}) collective-permute-start(bf16[256,384]{1,0:T(8,128)(2,1)S(1)} %get-tuple-element.127), channel_id=1, source_target_pairs={{0,3},{1,2},{2,1},{3,0},{4,7},{5,6},{6,5},{7,4},{8,11},{9,10},{10,... | collective-permute-start | bytes 589832 | tf_op jit(solution)/shard_map/ppermute | solution.py:1018
  55.6 11.0 %collective-permute-start.7 = (bf16[512,3072]{1,0:T(8,128)(2,1)}, bf16[512,3072]{1,0:T(8,128)(2,1)S(1)}, u32[]{:S(2)}, u32[]{:S(2)}) collective-permute-start(bf16[512,3072]{1,0:T(8,128)(2,1)} %get-tuple-element.138.refs_3_), channel_id=1, source_target_pairs={{0,1},{1,0},{2,3},{3,2},{4,5},{5,4},{6,7},{7,6},{8,9},{9,8},{10,11... | collective-permute-start | bytes 9437192 | tf_op jit(solution)/shard_map/ppermute | solution.py:1018
  55.7 10.9 %collective-permute-start.6 = (bf16[2,768,512]{2,1,0:T(8,128)(2,1)S(1)}, bf16[2,768,512]{2,1,0:T(8,128)(2,1)S(1)}, u32[]{:S(2)}, u32[]{:S(2)}) collective-permute-start(bf16[2,768,512]{2,1,0:T(8,128)(2,1)S(1)} %get-tuple-element.137.refs_1_), channel_id=1, source_target_pairs={{0,1},{1,0},{2,3},{3,2},{4,5},{5,4},{6,7},{7,6},{8,9},{9,8},{10,11... | collective-permute-start | bytes 4718600 | tf_op jit(solution)/shard_map/ppermute | solution.py:1018
  56.1 10.5 %collective-permute-start.8 = (bf16[384,512]{1,0:T(8,128)(2,1)S(1)}, bf16[384,512]{1,0:T(8,128)(2,1)S(1)}, u32[]{:S(2)}, u32[]{:S(2)}) collective-permute-start(bf16[384,512]{1,0:T(8,128)(2,1)S(1)} %get-tuple-element.139), channel_id=1, source_target_pairs={{0,1},{1,0},{2,3},{3,2},{4,5},{5,4},{6,7},{7,6},{8,9},{9,8},{10,11... | collective-permute-start | bytes 1179656 | tf_op jit(solution)/shard_map/ppermute | solution.py:1018
  66.6 11.9 %collective-permute-start.9 = (bf16[1536,768]{1,0:T(8,128)(2,1)S(1)}, bf16[1536,768]{1,0:T(8,128)(2,1)S(1)}, u32[]{:S(2)}, u32[]{:S(2)}) collective-permute-start(bf16[1536,768]{1,0:T(8,128)(2,1)S(1)} %get-tuple-element.145), channel_id=1, source_target_pairs={{0,1},{1,0},{2,3},{3,2},{4,5},{5,4},{6,7},{7,6},{8,9},{9,8},{10,11... | collective-permute-start | bytes 7077896 | tf_op jit(solution)/shard_map/ppermute | solution.py:1018
  67.1 11.3 %collective-permute-start.10 = (bf16[2,256,384]{2,1,0:T(8,128)(2,1)S(1)}, bf16[2,256,384]{2,1,0:T(8,128)(2,1)S(1)}, u32[]{:S(2)}, u32[]{:S(2)}) collective-permute-start(bf16[2,256,384]{2,1,0:T(8,128)(2,1)S(1)} %get-tuple-element.149), channel_id=1, source_target_pairs={{0,2},{1,3},{2,0},{3,1},{4,6},{5,7},{6,4},{7,5},{8,10},{9,11},{10,... | collective-permute-start | bytes 1179656 | tf_op jit(solution)/shard_map/ppermute | solution.py:1018
  74.3 19.5 %collective-permute-start.12 = (bf16[8,96,384]{2,1,0:T(8,128)(2,1)S(1)}, bf16[8,96,384]{2,1,0:T(8,128)(2,1)S(1)}, u32[]{:S(2)}, u32[]{:S(2)}) collective-permute-start(bf16[8,96,384]{2,1,0:T(8,128)(2,1)S(1)} %get-tuple-element.156), channel_id=1, source_target_pairs={{0,8},{4,12},{8,0},{12,4},{16,24},{20,28},{24,16},{28,20},{1,9},{5... | collective-permute-start | bytes 1769480 | tf_op jit(solution)/shard_map/ppermute | solution.py:1021
  75.5 18.3 %collective-permute-start.13 = (bf16[8,96,384]{2,1,0:T(8,128)(2,1)S(1)}, bf16[8,96,384]{2,1,0:T(8,128)(2,1)S(1)}, u32[]{:S(2)}, u32[]{:S(2)}) collective-permute-start(bf16[8,96,384]{2,1,0:T(8,128)(2,1)S(1)} %get-tuple-element.158), channel_id=1, source_target_pairs={{0,2},{1,3},{2,0},{3,1},{4,6},{5,7},{6,4},{7,5},{8,10},{9,11},{10,... | collective-permute-start | bytes 1769480 | tf_op jit(solution)/shard_map/ppermute | solution.py:1018
  78.4 8.0 %collective-permute-start.11 = (bf16[256,384]{1,0:T(8,128)(2,1)S(1)}, bf16[256,384]{1,0:T(8,128)(2,1)S(1)}, u32[]{:S(2)}, u32[]{:S(2)}) collective-permute-start(bf16[256,384]{1,0:T(8,128)(2,1)S(1)} %slice_bitcast_fusion.2), channel_id=1, source_target_pairs={{0,1},{1,0},{2,3},{3,2},{4,5},{5,4},{6,7},{7,6},{8,9},{9,8},{10,11... | collective-permute-start | bytes 589832 | tf_op jit(solution)/shard_map/ppermute | solution.py:1018
  83.6 26.8 %collective-permute-start.15 = (bf16[12,96,384]{2,1,0:T(8,128)(2,1)S(1)}, bf16[12,96,384]{2,1,0:T(8,128)(2,1)S(1)}, u32[]{:S(2)}, u32[]{:S(2)}) collective-permute-start(bf16[12,96,384]{2,1,0:T(8,128)(2,1)S(1)} %get-tuple-element.165), channel_id=1, source_target_pairs={{0,4},{4,0},{8,12},{12,8},{16,20},{20,16},{24,28},{28,24},{1,5},{5... | collective-permute-start | bytes 2654216 | tf_op jit(solution)/shard_map/ppermute | solution.py:1021
  85.5 25.0 %collective-permute-start.14 = (bf16[8,96,384]{2,1,0:T(8,128)(2,1)S(1)}, bf16[8,96,384]{2,1,0:T(8,128)(2,1)S(1)}, u32[]{:S(2)}, u32[]{:S(2)}) collective-permute-start(bf16[8,96,384]{2,1,0:T(8,128)(2,1)S(1)} %get-tuple-element.163), channel_id=1, source_target_pairs={{0,2},{1,3},{2,0},{3,1},{4,6},{5,7},{6,4},{7,5},{8,10},{9,11},{10,... | collective-permute-start | bytes 1769480 | tf_op jit(solution)/shard_map/ppermute | solution.py:1018
  94.0 11.9 %collective-permute-start.18 = (bf16[4,96,384]{2,1,0:T(8,128)(2,1)S(1)}, bf16[4,96,384]{2,1,0:T(8,128)(2,1)S(1)}, u32[]{:S(2)}, u32[]{:S(2)}) collective-permute-start(bf16[4,96,384]{2,1,0:T(8,128)(2,1)S(1)} %get-tuple-element.171), channel_id=1, source_target_pairs={{0,8},{4,12},{8,0},{12,4},{16,24},{20,28},{24,16},{28,20},{1,9},{5... | collective-permute-start | bytes 884744 | tf_op jit(solution)/shard_map/ppermute | solution.py:1021
  97.0 12.8 %collective-permute-start.16 = (bf16[4,96,384]{2,1,0:T(8,128)(2,1)S(1)}, bf16[4,96,384]{2,1,0:T(8,128)(2,1)S(1)}, u32[]{:S(2)}, u32[]{:S(2)}) collective-permute-start(bf16[4,96,384]{2,1,0:T(8,128)(2,1)S(1)} %get-tuple-element.167), channel_id=1, source_target_pairs={{0,2},{1,3},{2,0},{3,1},{4,6},{5,7},{6,4},{7,5},{8,10},{9,11},{10,... | collective-permute-start | bytes 884744 | tf_op jit(solution)/shard_map/ppermute | solution.py:1018
  97.5 13.0 %collective-permute-start.17 = (bf16[4,96,384]{2,1,0:T(8,128)(2,1)S(1)}, bf16[4,96,384]{2,1,0:T(8,128)(2,1)S(1)}, u32[]{:S(2)}, u32[]{:S(2)}) collective-permute-start(bf16[4,96,384]{2,1,0:T(8,128)(2,1)S(1)} %get-tuple-element.169), channel_id=1, source_target_pairs={{0,8},{4,12},{8,0},{12,4},{16,24},{20,28},{24,16},{28,20},{1,9},{5... | collective-permute-start | bytes 884744 | tf_op jit(solution)/shard_map/ppermute | solution.py:1021
  110.8 19.1 %collective-permute-start.19 = (bf16[6,96,384]{2,1,0:T(8,128)(2,1)S(1)}, bf16[6,96,384]{2,1,0:T(8,128)(2,1)S(1)}, u32[]{:S(2)}, u32[]{:S(2)}) collective-permute-start(bf16[6,96,384]{2,1,0:T(8,128)(2,1)S(1)} %get-tuple-element.176), channel_id=1, source_target_pairs={{0,4},{4,0},{8,12},{12,8},{16,20},{20,16},{24,28},{28,24},{1,5},{5... | collective-permute-start | bytes 1327112 | tf_op jit(solution)/shard_map/ppermute | solution.py:1021
  112.1 17.8 %collective-permute-start.20 = (bf16[6,96,384]{2,1,0:T(8,128)(2,1)S(1)}, bf16[6,96,384]{2,1,0:T(8,128)(2,1)S(1)}, u32[]{:S(2)}, u32[]{:S(2)}) collective-permute-start(bf16[6,96,384]{2,1,0:T(8,128)(2,1)S(1)} %get-tuple-element.178), channel_id=1, source_target_pairs={{0,2},{1,3},{2,0},{3,1},{4,6},{5,7},{6,4},{7,5},{8,10},{9,11},{10,... | collective-permute-start | bytes 1327112 | tf_op jit(solution)/shard_map/ppermute | solution.py:1018
  112.7 14.6 %collective-permute-start.22 = (bf16[4,96,384]{2,1,0:T(8,128)(2,1)S(1)}, bf16[4,96,384]{2,1,0:T(8,128)(2,1)S(1)}, u32[]{:S(2)}, u32[]{:S(2)}) collective-permute-start(bf16[4,96,384]{2,1,0:T(8,128)(2,1)S(1)} %get-tuple-element.182), channel_id=1, source_target_pairs={{0,8},{4,12},{8,0},{12,4},{16,24},{20,28},{24,16},{28,20},{1,9},{5... | collective-permute-start | bytes 884744 | tf_op jit(solution)/shard_map/ppermute | solution.py:1021
  115.1 14.8 %collective-permute-start.21 = (bf16[4,96,384]{2,1,0:T(8,128)(2,1)S(1)}, bf16[4,96,384]{2,1,0:T(8,128)(2,1)S(1)}, u32[]{:S(2)}, u32[]{:S(2)}) collective-permute-start(bf16[4,96,384]{2,1,0:T(8,128)(2,1)S(1)} %get-tuple-element.180), channel_id=1, source_target_pairs={{0,16},{4,20},{8,24},{12,28},{16,0},{20,4},{24,8},{28,12},{1,17},{... | collective-permute-start | bytes 884744 | tf_op jit(solution)/shard_map/ppermute | solution.py:1021
  130.2 11.5 %collective-permute-start.24 = (bf16[8,96,384]{2,1,0:T(8,128)(2,1)S(1)}, bf16[8,96,384]{2,1,0:T(8,128)(2,1)S(1)}, u32[]{:S(2)}, u32[]{:S(2)}) collective-permute-start(bf16[8,96,384]{2,1,0:T(8,128)(2,1)S(1)} %get-tuple-element.200), channel_id=1, source_target_pairs={{0,4},{4,0},{8,12},{12,8},{16,20},{20,16},{24,28},{28,24},{1,5},{5... | collective-permute-start | bytes 1769480 | tf_op jit(solution)/shard_map/ppermute | solution.py:1021
  130.7 8.3 %collective-permute-start.25 = (bf16[3,96,384]{2,1,0:T(8,128)(2,1)S(1)}, bf16[3,96,384]{2,1,0:T(8,128)(2,1)S(1)}, u32[]{:S(2)}, u32[]{:S(2)}) collective-permute-start(bf16[3,96,384]{2,1,0:T(8,128)(2,1)S(1)} %get-tuple-element.202), channel_id=1, source_target_pairs={{0,8},{4,12},{8,0},{12,4},{16,24},{20,28},{24,16},{28,20},{1,9},{5... | collective-permute-start | bytes 663560 | tf_op jit(solution)/shard_map/ppermute | solution.py:1021
  131.2 10.6 %collective-permute-start.26 = (bf16[3,96,384]{2,1,0:T(8,128)(2,1)S(1)}, bf16[3,96,384]{2,1,0:T(8,128)(2,1)S(1)}, u32[]{:S(2)}, u32[]{:S(2)}) collective-permute-start(bf16[3,96,384]{2,1,0:T(8,128)(2,1)S(1)} %get-tuple-element.204), channel_id=1, source_target_pairs={{0,16},{4,20},{8,24},{12,28},{16,0},{20,4},{24,8},{28,12},{1,17},{... | collective-permute-start | bytes 663560 | tf_op jit(solution)/shard_map/ppermute | solution.py:1021
  133.8 11.2 %collective-permute-start.23 = (f32[16,768]{1,0:T(8,128)S(1)}, f32[16,768]{1,0:T(8,128)S(1)}, u32[]{:S(2)}, u32[]{:S(2)}) collective-permute-start(f32[16,768]{1,0:T(8,128)S(1)} %get-tuple-element.198.refs_0_), channel_id=1, source_target_pairs={{0,1},{1,0},{2,3},{3,2},{4,5},{5,4},{6,7},{7,6},{8,9},{9,8},{10,11... | collective-permute-start | bytes 147464 | tf_op jit(solution)/shard_map/ppermute | solution.py:1018
  145.0 9.9 %collective-permute-start.27 = (f32[2,256,768]{2,1,0:T(8,128)}, f32[2,256,768]{2,1,0:T(8,128)}, u32[]{:S(2)}, u32[]{:S(2)}) collective-permute-start(f32[2,256,768]{2,1,0:T(8,128)} %get-tuple-element.206), channel_id=1, source_target_pairs={{0,1},{1,0},{2,3},{3,2},{4,5},{5,4},{6,7},{7,6},{8,9},{9,8},{10,11... | collective-permute-start | bytes 4718600 | tf_op jit(solution)/shard_map/ppermute | solution.py:1018
  145.0 4.2 %collective-permute-start.29 = (f32[16,768]{1,0:T(8,128)S(1)}, f32[16,768]{1,0:T(8,128)S(1)}, u32[]{:S(2)}, u32[]{:S(2)}) collective-permute-start(f32[16,768]{1,0:T(8,128)S(1)} %add.61), channel_id=1, source_target_pairs={{0,2},{1,3},{2,0},{3,1},{4,6},{5,7},{6,4},{7,5},{8,10},{9,11},{10,... | collective-permute-start | bytes 147464 | tf_op jit(solution)/shard_map/ppermute | solution.py:1018
  149.2 5.7 %collective-permute-start.30 = (f32[16,768]{1,0:T(8,128)S(1)}, f32[16,768]{1,0:T(8,128)S(1)}, u32[]{:S(2)}, u32[]{:S(2)}) collective-permute-start(f32[16,768]{1,0:T(8,128)S(1)} %add.62), channel_id=1, source_target_pairs={{0,4},{4,0},{8,12},{12,8},{16,20},{20,16},{24,28},{28,24},{1,5},{5... | collective-permute-start | bytes 147464 | tf_op jit(solution)/shard_map/ppermute | solution.py:1021
  150.8 12.2 %collective-permute-start.31 = (bf16[3,96,384]{2,1,0:T(8,128)(2,1)}, bf16[3,96,384]{2,1,0:T(8,128)(2,1)S(1)}, u32[]{:S(2)}, u32[]{:S(2)}) collective-permute-start(bf16[3,96,384]{2,1,0:T(8,128)(2,1)} %copy-done.11), channel_id=1, source_target_pairs={{0,16},{4,20},{8,24},{12,28},{16,0},{20,4},{24,8},{28,12},{1,17},{... | collective-permute-start | bytes 663560 | tf_op jit(solution)/shard_map/ppermute | solution.py:1021
  151.9 11.1 %collective-permute-start.32 = (bf16[3,96,384]{2,1,0:T(8,128)(2,1)S(1)}, bf16[3,96,384]{2,1,0:T(8,128)(2,1)S(1)}, u32[]{:S(2)}, u32[]{:S(2)}) collective-permute-start(bf16[3,96,384]{2,1,0:T(8,128)(2,1)S(1)} %get-tuple-element.213), channel_id=1, source_target_pairs={{0,8},{4,12},{8,0},{12,4},{16,24},{20,28},{24,16},{28,20},{1,9},{5... | collective-permute-start | bytes 663560 | tf_op jit(solution)/shard_map/ppermute | solution.py:1021
  156.1 12.9 %collective-permute-start.28 = (bf16[256,768]{1,0:T(8,128)(2,1)S(1)}, bf16[256,768]{1,0:T(8,128)(2,1)S(1)}, u32[]{:S(2)}, u32[]{:S(2)}) collective-permute-start(bf16[256,768]{1,0:T(8,128)(2,1)S(1)} %fusion.1.refs_2_), channel_id=1, source_target_pairs={{0,2},{1,3},{2,0},{3,1},{4,6},{5,7},{6,4},{7,5},{8,10},{9,11},{10,... | collective-permute-start | bytes 1179656 | tf_op jit(solution)/shard_map/ppermute | solution.py:1018
  163.1 6.0 %collective-permute-start.34 = (bf16[1,96,384]{2,1,0:T(8,128)(2,1)S(1)}, bf16[1,96,384]{2,1,0:T(8,128)(2,1)S(1)}, u32[]{:S(2)}, u32[]{:S(2)}) collective-permute-start(bf16[1,96,384]{2,1,0:T(8,128)(2,1)S(1)} %get-tuple-element.220), channel_id=1, source_target_pairs={{0,16},{4,20},{8,24},{12,28},{16,0},{20,4},{24,8},{28,12},{1,17},{... | collective-permute-start | bytes 221192 | tf_op jit(solution)/shard_map/ppermute | solution.py:1021
  164.4 4.1 %collective-permute-start.33 = (f32[16,768]{1,0:T(8,128)S(1)}, f32[16,768]{1,0:T(8,128)S(1)}, u32[]{:S(2)}, u32[]{:S(2)}) collective-permute-start(f32[16,768]{1,0:T(8,128)S(1)} %add.63.refs_1_), channel_id=1, source_target_pairs={{0,8},{4,12},{8,0},{12,4},{16,24},{20,28},{24,16},{28,20},{1,9},{5... | collective-permute-start | bytes 147464 | tf_op jit(solution)/shard_map/ppermute | solution.py:1021
  170.1 5.7 %collective-permute-start.38 = (f32[16,768]{1,0:T(8,128)S(1)}, f32[16,768]{1,0:T(8,128)S(1)}, u32[]{:S(2)}, u32[]{:S(2)}) collective-permute-start(f32[16,768]{1,0:T(8,128)S(1)} %add.64), channel_id=1, source_target_pairs={{0,16},{4,20},{8,24},{12,28},{16,0},{20,4},{24,8},{28,12},{1,17},{... | collective-permute-start | bytes 147464 | tf_op jit(solution)/shard_map/ppermute | solution.py:1021
  171.2 5.8 %collective-permute-start.35 = (bf16[2,96,192]{2,1,0:T(8,128)(2,1)S(1)}, bf16[2,96,192]{2,1,0:T(8,128)(2,1)S(1)}, u32[]{:S(2)}, u32[]{:S(2)}) collective-permute-start(bf16[2,96,192]{2,1,0:T(8,128)(2,1)S(1)} %get-tuple-element.223), channel_id=1, source_target_pairs={{0,1},{1,0},{2,3},{3,2},{4,5},{5,4},{6,7},{7,6},{8,9},{9,8},{10,11... | collective-permute-start | bytes 221192 | tf_op jit(solution)/shard_map/ppermute | solution.py:1018
  171.2 5.8 %collective-permute-start.36 = (bf16[2,96,192]{2,1,0:T(8,128)(2,1)S(1)}, bf16[2,96,192]{2,1,0:T(8,128)(2,1)S(1)}, u32[]{:S(2)}, u32[]{:S(2)}) collective-permute-start(bf16[2,96,192]{2,1,0:T(8,128)(2,1)S(1)} %get-tuple-element.224), channel_id=1, source_target_pairs={{0,2},{1,3},{2,0},{3,1},{4,6},{5,7},{6,4},{7,5},{8,10},{9,11},{10,... | collective-permute-start | bytes 221192 | tf_op jit(solution)/shard_map/ppermute | solution.py:1018
  171.6 6.5 %collective-permute-start.37 = (bf16[2,96,192]{2,1,0:T(8,128)(2,1)S(1)}, bf16[2,96,192]{2,1,0:T(8,128)(2,1)S(1)}, u32[]{:S(2)}, u32[]{:S(2)}) collective-permute-start(bf16[2,96,192]{2,1,0:T(8,128)(2,1)S(1)} %get-tuple-element.225), channel_id=1, source_target_pairs={{0,3},{1,2},{2,1},{3,0},{4,7},{5,6},{6,5},{7,4},{8,11},{9,10},{10,... | collective-permute-start | bytes 221192 | tf_op jit(solution)/shard_map/ppermute | solution.py:1018
  (17 other events, 104.7 us)

commit v7 on v6

--- a/solution.py
+++ b/solution.py
@@ -1129,29 +1129,32 @@
     grads = [*zero[:3], *one[:3], *two[:3]]
     vectors, token = tie(two[3], token)
     flights = launch(others, up_a, up_b)
-    vectors_got = over_seq(vectors, 1)
+    vectors = vectors + over_seq(vectors, 1)
 
     near, far, send = input_part(info, grads, qkv_weight, [token])
-    (up_a, up_b, down), token = land(
-        [near],
+    vectors, token = tie(vectors, mark(near))
+    vectors = vectors + over_seq(vectors, 2)
+    (up_a, up_b, down, first), token = land(
+        [token, vectors],
         flights,
         ("w", (1, 0), (0, 2), (1, 1)),
         ("z", (2, 0), (0, 3)),
-        ("", (0, 0), (0, 1), (2, 1)),
+        ("", (0, 0), (0, 1)),
+        ("", (2, 1)),
     )
     down_total = down[3]
     up_a, up_b = launch(up_a, up_b)
-    send, vectors_got, token = tie(send, vectors_got, token)
+    send, vectors, token = tie(send, vectors, token)
     d_row_got = over_seq(send, 1)
     far = (far + d_row_got[1]).astype(LOW)
     d_far = over_seq(far, 2)
-    vectors = vectors + vectors_got
-    vectors = vectors + over_seq(vectors, 2)
     vectors = vectors + swap(vectors, "y")
-    (up, third), token = land(
+    (up, out_total, second, third), token = land(
         [token, vectors, far],
         [up_a, up_b],
-        ("", (0, 0), (1, 0), (0, 2), (0, 1)),
+        ("", (0, 0), (1, 0)),
+        ("", (0, 2)),
+        ("", (0, 1)),
         ("w", (1, 1)),
     )
     up_total = up[3]
@@ -1159,13 +1162,13 @@
     vectors, token = tie(vectors, token)
     (third,) = launch(third)
     vectors_got = swap(vectors, "z")
-    own, *others = share(info, down[3], up[3], third[2], third[3], [token, vectors_got, d_far])
+    own, *others = share(info, first[3], second[3], third[2], third[3], [token, vectors_got, d_far])
     vectors_got, own = tie(vectors_got, own)
     vectors = vectors + vectors_got
     qkv_total = gather(info, own, *[over_seq(other, 1 + j) for j, other in enumerate(others)])
     qkv_total = finish(qkv_total)
-    out_total = finish(up_total[2, :, :wide])
-    down_total = finish(down_total[:2].reshape(wide, half).T)
+    out_total = finish(out_total[3][0, :, :wide])
+    down_total = finish(down_total.reshape(wide, half).T)
     up_total = finish(jnp.concatenate([up_total[0], up_total[1]], axis=1))
 
     vectors = vectors + swap(vectors, "w")

time: 180 us -> 179 us (level)
    unnamed x52 -> x56, local copies, waits for them, and re-layouts: 5.11 us -> 6.18 us
  transfers between devices with their start and end apart: 39 -> 39, of which waited for: 15 -> 13; matrix products, arithmetic and copies ran while one was open for 6% -> 5% of each run, Pallas kernels for 31% -> 31%
where the time goes in v7:
time: 179 us
  Pallas kernels  85 us (47%)
  waiting for transfers between devices  41.2 us (23%)
  starting transfers between devices  36 us (20%)
  local copies, waits for them, and re-layouts  10.8 us (6%)
  other arithmetic  4.9 us (3%)
    ppermute x23, waiting for transfers between devices, over_seq(): return lax.ppermute(array, 'seq', [(i, i ^ flip) for i in range(seq_size)])  23.9 us
    pallas_call x3, Pallas kernels, attend_backward(): pl.pallas_call(ordered(functools.partial(backward_kernel, n), after), gri...  23.6 us
    ppermute x16, starting transfers between devices, over_batch(): lax.ppermute(array, 'batch', [(i, i ^ flip) for i in range(batch_size)])  22.2 us
    ppermute x16, waiting for transfers between devices, over_batch(): lax.ppermute(array, 'batch', [(i, i ^ flip) for i in range(batch_size)])  17.3 us
    pallas_call x1, Pallas kernels, attend_forward(): pl.pallas_call(functools.partial(forward_kernel, True), grid_spec=pltpu.P...  14.6 us
    ppermute x23, starting transfers between devices, over_seq(): return lax.ppermute(array, 'seq', [(i, i ^ flip) for i in range(seq_size)])  13.7 us
    pallas_call x1, Pallas kernels, middle_forward(): pl.pallas_call(ordered(middle_forward_kernel, after), grid_spec=pltpu.Pre...  11.6 us
    pallas_call x1, Pallas kernels, middle_backward(): pl.pallas_call(middle_backward_kernel, grid_spec=pltpu.PrefetchScalarGrid...  10.3 us
  transfers between devices with their start and end apart: 39, of which 13 were waited for; matrix products, arithmetic and copies ran while one was open for 5% of the time, Pallas kernels for 31%

profile of v7, /device:TPU:0, one launch (start us, length us, event | category | flops | bytes accessed | tf_op | source)
XLA Modules:
  0.0 179.3 jit_solution(9020153095063577015)
XLA Ops:
  0.8 1.2 dynamic-slice_bitcast_fusion
  2.0 3.0 %collective-permute-start.1 = (bf16[256,768]{1,0:T(8,128)(2,1)S(1)}, bf16[256,768]{1,0:T(8,128)(2,1)S(1)}, u32[]{:S(2)}, u32[]{:S(2)}) collective-permute-start(bf16[256,768]{1,0:T(8,128)(2,1)S(1)} %get-tuple-element.255), channel_id=1, source_target_pairs={{0,2},{1,3},{2,0},{3,1},{4,6},{5,7},{6,4},{7,5},{8,10},{9,11},{10,... | collective-permute-start | bytes 1179656 | tf_op jit(solution)/shard_map/ppermute | solution.py:1018
  6.2 7.9 %collective-permute-done.1.x2.refs_2_ = bf16[256,768]{1,0:T(8,128)(2,1)S(1)} collective-permute-done((bf16[256,768]{1,0:T(8,128)(2,1)S(1)}, bf16[256,768]{1,0:T(8,128)(2,1)S(1)}, u32[]{:S(2)}, u32[]{:S(2)}) %collective-permute-start.1) | collective-permute-done | bytes 393248 | tf_op jit(solution)/shard_map/ppermute | solution.py:1018
  14.8 1.0 collective-permute-done.2.x3.refs_3_
  15.8 2.0 %copy-done.1 = bf16[768,2304]{1,0:T(8,128)(2,1)S(1)} copy-done((bf16[768,2304]{1,0:T(8,128)(2,1)S(1)}, bf16[768,2304]{1,0:T(8,128)(2,1)}, u32[]{:S(2)}) %copy-start.1) | copy-done | bytes 3538968
  17.8 14.6 %attend_forward.1 = (bf16[1024,384]{1,0:T(8,128)(2,1)S(1)}, bf16[1024,384]{1,0:T(8,128)(2,1)S(1)}, bf16[1024,384]{1,0:T(8,128)(2,1)S(1)}, bf16[256,384]{1,0:T(8,...) custom-call(s32[12]{0:T(128)S(1)} %concatenate.6.info, ...), custom_call_target="tpu_custom_call" | custom-call | flops 9600000000 | tf_op jit(solution)/shard_map/attend_forward/pallas_call | solution.py:313
  32.5 1.0 collective-permute-start.4
  33.5 0.9 collective-permute-start.5
  34.4 1.0 turn.1.refs_0_.refs_14_
  35.5 4.8 %attend_own.1 = (bf16[256,384]{1,0:T(8,128)(2,1)S(1)}, f32[384,256]{1,0:T(8,128)S(1)}, f32[3,1,512]{2,1,0:T(1,128)S(1)}) custom-call(s32[12]{0:T(128)S(1)} %concatenate.6.info, bf16[1024,384]{1,0:T(8,128)(2,1)S(1)} %get-tuple-element.126.refs_0_.refs_1_, bf16[1024,384]{1,0:T(8,128)(2,1)S(1)} %get-tuple-element.127.refs_1_.refs_2_, ...), custom_call_target="tpu_custom_call" | custom-call | flops 3000000000 | tf_op jit(solution)/shard_map/attend_own/pallas_call | solution.py:330
  40.3 3.3 %collective-permute-done.5.refs_4_ = bf16[256,384]{1,0:T(8,128)(2,1)S(1)} collective-permute-done((bf16[256,384]{1,0:T(8,128)(2,1)S(1)}, bf16[256,384]{1,0:T(8,128)(2,1)S(1)}, u32[]{:S(2)}, u32[]{:S(2)}) %collective-permute-start.5) | collective-permute-done | bytes 196640 | tf_op jit(solution)/shard_map/ppermute | solution.py:1018
  43.6 11.6 %middle_forward.1 = (bf16[2,256,768]{2,1,0:T(8,128)(2,1)}, f32[512,768]{1,0:T(8,128)S(1)}, f32[512,768]{1,0:T(8,128)S(1)}, f32[512,1]{1,0:T(8,128)S(1)}, bf16[2,...) custom-call(s32[12]{0:T(128)S(1)} %concatenate.6.info, ...), custom_call_target="tpu_custom_call" | custom-call | flops 10800000000 | tf_op jit(solution)/shard_map/middle_forward/pallas_call | solution.py:577
  56.0 10.3 %middle_backward.1 = (bf16[1536,768]{1,0:T(8,128)(2,1)S(1)}, bf16[2,512,768]{2,1,0:T(8,128)(2,1)S(1)}, f32[512,768]{1,0:T(8,128)S(1)}, bf16[256,384]{1,0:T(8,128...) custom-call(s32[12]{0:T(128)S(1)} %concatenate.6.info, ...), custom_call_target="tpu_custom_call" | custom-call | flops 9600000000 | tf_op jit(solution)/shard_map/middle_backward/pallas_call | solution.py:691
  67.1 1.2 copy-done.4
  68.3 4.7 %down_grad.1 = (bf16[8,96,384]{2,1,0:T(8,128)(2,1)S(1)}, f32[8,96,384]{2,1,0:T(8,128)S(1)}, bf16[8,96,384]{2,1,0:T(8,128)(2,1)S(1)}, f32[8,96,384]{2,1,0:T(8,128)S(1)}) custom-call(s32[12]{0:T(128)S(1)} %concatenate.6.info, f32[8,128]{1,0:T(8,128)S(1)} %mark.2.refs_0_, bf16[2,192,512]{2,1,0:T(8,128)(2,1)S(1)} %get-tuple-element.147.refs_1_, ...), custom_call_target="tpu_custom_call" | custom-call | flops 4800000000 | tf_op jit(solution)/shard_map/down_grad/pallas_call | solution.py:753
  73.0 1.8 collective-permute-start.12
  74.8 1.6 collective-permute-start.13
  76.3 2.3 %collective-permute-done.10.refs_7_ = bf16[2,256,384]{2,1,0:T(8,128)(2,1)S(1)} collective-permute-done((bf16[2,256,384]{2,1,0:T(8,128)(2,1)S(1)}, bf16[2,256,384]{2,1,0:T(8,128)(2,1)S(1)}, u32[]{:S(2)}, u32[]{:S(2)}) %collective-permute-start.10) | collective-permute-done | bytes 393248 | tf_op jit(solution)/shard_map/ppermute | solution.py:1018
  78.8 5.1 %up_grad.1 = (bf16[8,96,384]{2,1,0:T(8,128)(2,1)S(1)}, f32[8,96,384]{2,1,0:T(8,128)S(1)}, bf16[12,96,384]{2,1,0:T(8,128)(2,1)S(1)}, f32[12,96,384]{2,1,0:T(8,128)S(1)}) custom-call(s32[12]{0:T(128)S(1)} %concatenate.6.info, f32[8,96,384]{2,1,0:T(8,128)S(1)} %get-tuple-element.148.refs_0_.refs_1_, bf16[2,768,512]{2,1,0:T(8,128)(2,1)S(1)} %get-tuple-element.142.refs_1_, ...), custom_call_target="tpu_custom_call" | custom-call | flops 6000000000 | tf_op jit(solution)/shard_map/up_grad/pallas_call | solution.py:815
  84.0 0.9 collective-permute-start.14
  84.8 7.8 %attend_backward.3 = (bf16[1024,128]{1,0:T(8,128)(2,1)S(1)}, bf16[1024,128]{1,0:T(8,128)(2,1)S(1)}, bf16[1024,128]{1,0:T(8,128)(2,1)S(1)}, f32[16,768]{1,0:T(8,1...) custom-call(s32[12]{0:T(128)S(1)} %concatenate.6.info, ...), custom_call_target="tpu_custom_call" | custom-call | flops 4800000000 | tf_op jit(solution)/shard_map/attend_backward/pallas_call | solution.py:434
  92.8 2.7 %collective-permute-start.18 = (bf16[4,96,384]{2,1,0:T(8,128)(2,1)S(1)}, bf16[4,96,384]{2,1,0:T(8,128)(2,1)S(1)}, u32[]{:S(2)}, u32[]{:S(2)}) collective-permute-start(bf16[4,96,384]{2,1,0:T(8,128)(2,1)S(1)} %get-tuple-element.176), channel_id=1, source_target_pairs={{0,8},{4,12},{8,0},{12,4},{16,24},{20,28},{24,16},{28,20},{1,9},{5... | collective-permute-start | bytes 884744 | tf_op jit(solution)/shard_map/ppermute | solution.py:1021
  95.6 1.0 collective-permute-start.16
  96.6 8.3 %attend_backward.4 = (bf16[1024,128]{1,0:T(8,128)(2,1)S(1)}, bf16[1024,128]{1,0:T(8,128)(2,1)S(1)}, bf16[1024,128]{1,0:T(8,128)(2,1)S(1)}, f32[16,768]{1,0:T(8,1...) custom-call(s32[12]{0:T(128)S(1)} %concatenate.6.info, f32[8,128]{1,0:T(8,128)S(1)} %get-tuple-element.165.refs_0_, ...), custom_call_target="tpu_custom_call" | custom-call | flops 4800000000 | tf_op jit(solution)/shard_map/attend_backward/pallas_call | solution.py:434
  105.0 4.7 %collective-permute-done.16.refs_6_ = bf16[4,96,384]{2,1,0:T(8,128)(2,1)S(1)} collective-permute-done((bf16[4,96,384]{2,1,0:T(8,128)(2,1)S(1)}, bf16[4,96,384]{2,1,0:T(8,128)(2,1)S(1)}, u32[]{:S(2)}, u32[]{:S(2)}) %collective-permute-start.16) | collective-permute-done | bytes 294944 | tf_op jit(solution)/shard_map/ppermute | solution.py:1018
  111.6 2.5 %collective-permute-start.22 = (bf16[4,96,384]{2,1,0:T(8,128)(2,1)S(1)}, bf16[4,96,384]{2,1,0:T(8,128)(2,1)S(1)}, u32[]{:S(2)}, u32[]{:S(2)}) collective-permute-start(bf16[4,96,384]{2,1,0:T(8,128)(2,1)S(1)} %get-tuple-element.187), channel_id=1, source_target_pairs={{0,8},{4,12},{8,0},{12,4},{16,24},{20,28},{24,16},{28,20},{1,9},{5... | collective-permute-start | bytes 884744 | tf_op jit(solution)/shard_map/ppermute | solution.py:1021
  114.1 3.1 %collective-permute-start.21 = (bf16[4,96,384]{2,1,0:T(8,128)(2,1)S(1)}, bf16[4,96,384]{2,1,0:T(8,128)(2,1)S(1)}, u32[]{:S(2)}, u32[]{:S(2)}) collective-permute-start(bf16[4,96,384]{2,1,0:T(8,128)(2,1)S(1)} %get-tuple-element.185), channel_id=1, source_target_pairs={{0,16},{4,20},{8,24},{12,28},{16,0},{20,4},{24,8},{28,12},{1,17},{... | collective-permute-start | bytes 884744 | tf_op jit(solution)/shard_map/ppermute | solution.py:1021
  117.2 7.5 %attend_backward.5 = (bf16[1024,128]{1,0:T(8,128)(2,1)S(1)}, bf16[1024,128]{1,0:T(8,128)(2,1)S(1)}, bf16[1024,128]{1,0:T(8,128)(2,1)S(1)}, f32[16,768]{1,0:T(8,1...) custom-call(s32[12]{0:T(128)S(1)} %concatenate.6.info, f32[8,128]{1,0:T(8,128)S(1)} %get-tuple-element.178.refs_0_, ...), custom_call_target="tpu_custom_call" | custom-call | flops 4800000000 | tf_op jit(solution)/shard_map/attend_backward/pallas_call | solution.py:434
  124.8 1.7 collective-permute-done.22.refs_8_
  126.4 3.1 %collective-permute-done.21.refs_6_ = bf16[4,96,384]{2,1,0:T(8,128)(2,1)S(1)} collective-permute-done((bf16[4,96,384]{2,1,0:T(8,128)(2,1)S(1)}, bf16[4,96,384]{2,1,0:T(8,128)(2,1)S(1)}, u32[]{:S(2)}, u32[]{:S(2)}) %collective-permute-start.21) | collective-permute-done | bytes 294944 | tf_op jit(solution)/shard_map/ppermute | solution.py:1021
  130.8 2.6 %collective-permute-start.27 = (bf16[3,96,384]{2,1,0:T(8,128)(2,1)S(1)}, bf16[3,96,384]{2,1,0:T(8,128)(2,1)S(1)}, u32[]{:S(2)}, u32[]{:S(2)}) collective-permute-start(bf16[3,96,384]{2,1,0:T(8,128)(2,1)S(1)} %get-tuple-element.211), channel_id=1, source_target_pairs={{0,16},{4,20},{8,24},{12,28},{16,0},{20,4},{24,8},{28,12},{1,17},{... | collective-permute-start | bytes 663560 | tf_op jit(solution)/shard_map/ppermute | solution.py:1021
  133.4 5.1 %input_part.1 = (f32[256,768]{1,0:T(8,128)S(1)}, f32[256,768]{1,0:T(8,128)S(1)}, f32[2,256,768]{2,1,0:T(8,128)}) custom-call(s32[12]{0:T(128)S(1)} %concatenate.6.info, f32[8,128]{1,0:T(8,128)S(1)} %get-tuple-element.191.refs_0_, bf16[1024,128]{1,0:T(8,128)(2,1)S(1)} %get-tuple-element.192.refs_1_, bf16[1024,128]{1,0:T(8,128)(2,1)S(1)} %get-tuple-element.193.refs_2_, ...), custom_call_target="tpu_custom_call" | custom-call | flops 3600000000 | tf_op jit(solution)/shard_map/input_part/pallas_call | solution.py:869
  139.2 3.5 %collective-permute-done.24 = f32[16,768]{1,0:T(8,128)S(1)} collective-permute-done((f32[16,768]{1,0:T(8,128)S(1)}, f32[16,768]{1,0:T(8,128)S(1)}, u32[]{:S(2)}, u32[]{:S(2)}) %collective-permute-start.24) | collective-permute-done | bytes 49184 | tf_op jit(solution)/shard_map/ppermute | solution.py:1018
  142.8 1.3 collective-permute-done.27.refs_7_
  144.1 0.9 join.8
  147.9 1.6 collective-permute-start.30
  149.9 2.5 %collective-permute-start.32 = (bf16[3,96,384]{2,1,0:T(8,128)(2,1)S(1)}, bf16[3,96,384]{2,1,0:T(8,128)(2,1)S(1)}, u32[]{:S(2)}, u32[]{:S(2)}) collective-permute-start(bf16[3,96,384]{2,1,0:T(8,128)(2,1)S(1)} %get-tuple-element.220), channel_id=1, source_target_pairs={{0,8},{4,12},{8,0},{12,4},{16,24},{20,28},{24,16},{28,20},{1,9},{5... | collective-permute-start | bytes 663560 | tf_op jit(solution)/shard_map/ppermute | solution.py:1021
  152.4 1.2 fusion.1.refs_2_
  154.2 8.5 %collective-permute-done.31.refs_4_ = bf16[3,96,384]{2,1,0:T(8,128)(2,1)S(1)} collective-permute-done((bf16[3,96,384]{2,1,0:T(8,128)(2,1)}, bf16[3,96,384]{2,1,0:T(8,128)(2,1)S(1)}, u32[]{:S(2)}, u32[]{:S(2)}) %collective-permute-start.31) | collective-permute-done | bytes 221216 | tf_op jit(solution)/shard_map/ppermute | solution.py:1021
  163.5 1.5 collective-permute-start.33
  166.4 2.5 %collective-permute-done.33.refs_1_ = f32[16,768]{1,0:T(8,128)S(1)} collective-permute-done((f32[16,768]{1,0:T(8,128)S(1)}, f32[16,768]{1,0:T(8,128)S(1)}, u32[]{:S(2)}, u32[]{:S(2)}) %collective-permute-start.33) | collective-permute-done | bytes 49184 | tf_op jit(solution)/shard_map/ppermute | solution.py:1021
  168.9 1.0 share.1
  169.9 1.0 collective-permute-start.38
  171.4 1.4 collective-permute-start.37
  172.8 1.4 select_bitcast_fusion.1
  174.2 1.2 pad_maximum_fusion
  176.8 1.1 collective-permute-done.37.three
  177.9 1.4 gather.1
  (140 shorter events, 15.6 us)
Async XLA Ops:
  0.7 13.6 %copy-start.16 = (bf16[768]{0:T(1024)(128)(2,1)S(1)}, bf16[768]{0:T(1024)(128)(2,1)}, u32[]{:S(2)}) copy-start(bf16[768]{0:T(1024)(128)(2,1)} %param.19) | copy-start | bytes 4612
  0.7 13.6 %copy-start.17 = (bf16[768]{0:T(1024)(128)(2,1)S(1)}, bf16[768]{0:T(1024)(128)(2,1)}, u32[]{:S(2)}) copy-start(bf16[768]{0:T(1024)(128)(2,1)} %param.20) | copy-start | bytes 4612
  0.7 13.7 %copy-start.18 = (bf16[768]{0:T(1024)(128)(2,1)S(1)}, bf16[768]{0:T(1024)(128)(2,1)}, u32[]{:S(2)}) copy-start(bf16[768]{0:T(1024)(128)(2,1)} %param.23) | copy-start | bytes 4612
  0.7 13.7 %copy-start.14 = (bf16[3072]{0:T(1024)(128)(2,1)S(1)}, bf16[3072]{0:T(1024)(128)(2,1)}, u32[]{:S(2)}) copy-start(bf16[3072]{0:T(1024)(128)(2,1)} %param.26) | copy-start | bytes 18436
  0.7 13.7 %copy-start.19 = (bf16[768]{0:T(1024)(128)(2,1)S(1)}, bf16[768]{0:T(1024)(128)(2,1)}, u32[]{:S(2)}) copy-start(bf16[768]{0:T(1024)(128)(2,1)} %param.22) | copy-start | bytes 4612
  0.7 13.7 %copy-start.20 = (bf16[768]{0:T(1024)(128)(2,1)S(1)}, bf16[768]{0:T(1024)(128)(2,1)}, u32[]{:S(2)}) copy-start(bf16[768]{0:T(1024)(128)(2,1)} %param.24) | copy-start | bytes 4612
  0.7 13.7 %copy-start.21 = (bf16[768]{0:T(1024)(128)(2,1)S(1)}, bf16[768]{0:T(1024)(128)(2,1)}, u32[]{:S(2)}) copy-start(bf16[768]{0:T(1024)(128)(2,1)} %param.28) | copy-start | bytes 4612
  0.7 13.7 %copy-start.22 = (bf16[768]{0:T(1024)(128)(2,1)S(1)}, bf16[768]{0:T(1024)(128)(2,1)}, u32[]{:S(2)}) copy-start(bf16[768]{0:T(1024)(128)(2,1)} %param.29) | copy-start | bytes 4612
  0.7 13.7 %copy-start.23 = (bf16[768]{0:T(1024)(128)(2,1)S(1)}, bf16[768]{0:T(1024)(128)(2,1)}, u32[]{:S(2)}) copy-start(bf16[768]{0:T(1024)(128)(2,1)} %param.30) | copy-start | bytes 4612
  2.0 12.1 %collective-permute-start.1 = (bf16[256,768]{1,0:T(8,128)(2,1)S(1)}, bf16[256,768]{1,0:T(8,128)(2,1)S(1)}, u32[]{:S(2)}, u32[]{:S(2)}) collective-permute-start(bf16[256,768]{1,0:T(8,128)(2,1)S(1)} %get-tuple-element.255), channel_id=1, source_target_pairs={{0,2},{1,3},{2,0},{3,1},{4,6},{5,7},{6,4},{7,5},{8,10},{9,11},{10,... | collective-permute-start | bytes 1179656 | tf_op jit(solution)/shard_map/ppermute | solution.py:1018
  5.0 9.9 %collective-permute-start = (bf16[256,768]{1,0:T(8,128)(2,1)S(1)}, bf16[256,768]{1,0:T(8,128)(2,1)S(1)}, u32[]{:S(2)}, u32[]{:S(2)}) collective-permute-start(bf16[256,768]{1,0:T(8,128)(2,1)S(1)} %get-tuple-element.256.x0.refs_0_), channel_id=1, source_target_pairs={{0,1},{1,0},{2,3},{3,2},{4,5},{5,4},{6,7},{7,6},{8,9},{9,8},{10,11... | collective-permute-start | bytes 1179656 | tf_op jit(solution)/shard_map/ppermute | solution.py:1018
  14.1 1.7 collective-permute-start.2
  32.4 7.8 %collective-permute-start.3 = (bf16[256,384]{1,0:T(8,128)(2,1)S(1)}, bf16[256,384]{1,0:T(8,128)(2,1)S(1)}, u32[]{:S(2)}, u32[]{:S(2)}) collective-permute-start(bf16[256,384]{1,0:T(8,128)(2,1)S(1)} %get-tuple-element.130), channel_id=1, source_target_pairs={{0,1},{1,0},{2,3},{3,2},{4,5},{5,4},{6,7},{7,6},{8,9},{9,8},{10,11... | collective-permute-start | bytes 589832 | tf_op jit(solution)/shard_map/ppermute | solution.py:1018
  32.5 7.8 %collective-permute-start.4 = (bf16[256,384]{1,0:T(8,128)(2,1)S(1)}, bf16[256,384]{1,0:T(8,128)(2,1)S(1)}, u32[]{:S(2)}, u32[]{:S(2)}) collective-permute-start(bf16[256,384]{1,0:T(8,128)(2,1)S(1)} %get-tuple-element.131), channel_id=1, source_target_pairs={{0,2},{1,3},{2,0},{3,1},{4,6},{5,7},{6,4},{7,5},{8,10},{9,11},{10,... | collective-permute-start | bytes 589832 | tf_op jit(solution)/shard_map/ppermute | solution.py:1018
  33.5 10.1 %collective-permute-start.5 = (bf16[256,384]{1,0:T(8,128)(2,1)S(1)}, bf16[256,384]{1,0:T(8,128)(2,1)S(1)}, u32[]{:S(2)}, u32[]{:S(2)}) collective-permute-start(bf16[256,384]{1,0:T(8,128)(2,1)S(1)} %get-tuple-element.132), channel_id=1, source_target_pairs={{0,3},{1,2},{2,1},{3,0},{4,7},{5,6},{6,5},{7,4},{8,11},{9,10},{10,... | collective-permute-start | bytes 589832 | tf_op jit(solution)/shard_map/ppermute | solution.py:1018
  55.2 11.2 %collective-permute-start.7 = (bf16[512,3072]{1,0:T(8,128)(2,1)S(1)}, bf16[512,3072]{1,0:T(8,128)(2,1)S(1)}, u32[]{:S(2)}, u32[]{:S(2)}) collective-permute-start(bf16[512,3072]{1,0:T(8,128)(2,1)S(1)} %get-tuple-element.143.refs_3_), channel_id=1, source_target_pairs={{0,1},{1,0},{2,3},{3,2},{4,5},{5,4},{6,7},{7,6},{8,9},{9,8},{10,11... | collective-permute-start | bytes 9437192 | tf_op jit(solution)/shard_map/ppermute | solution.py:1018
  55.5 10.9 %collective-permute-start.6 = (bf16[2,768,512]{2,1,0:T(8,128)(2,1)S(1)}, bf16[2,768,512]{2,1,0:T(8,128)(2,1)S(1)}, u32[]{:S(2)}, u32[]{:S(2)}) collective-permute-start(bf16[2,768,512]{2,1,0:T(8,128)(2,1)S(1)} %get-tuple-element.142.refs_1_), channel_id=1, source_target_pairs={{0,1},{1,0},{2,3},{3,2},{4,5},{5,4},{6,7},{7,6},{8,9},{9,8},{10,11... | collective-permute-start | bytes 4718600 | tf_op jit(solution)/shard_map/ppermute | solution.py:1018
  55.8 10.6 %collective-permute-start.8 = (bf16[384,512]{1,0:T(8,128)(2,1)S(1)}, bf16[384,512]{1,0:T(8,128)(2,1)S(1)}, u32[]{:S(2)}, u32[]{:S(2)}) collective-permute-start(bf16[384,512]{1,0:T(8,128)(2,1)S(1)} %get-tuple-element.144), channel_id=1, source_target_pairs={{0,1},{1,0},{2,3},{3,2},{4,5},{5,4},{6,7},{7,6},{8,9},{9,8},{10,11... | collective-permute-start | bytes 1179656 | tf_op jit(solution)/shard_map/ppermute | solution.py:1018
  66.4 12.3 %collective-permute-start.9 = (bf16[1536,768]{1,0:T(8,128)(2,1)S(1)}, bf16[1536,768]{1,0:T(8,128)(2,1)S(1)}, u32[]{:S(2)}, u32[]{:S(2)}) collective-permute-start(bf16[1536,768]{1,0:T(8,128)(2,1)S(1)} %get-tuple-element.150), channel_id=1, source_target_pairs={{0,1},{1,0},{2,3},{3,2},{4,5},{5,4},{6,7},{7,6},{8,9},{9,8},{10,11... | collective-permute-start | bytes 7077896 | tf_op jit(solution)/shard_map/ppermute | solution.py:1018
  66.7 11.9 %collective-permute-start.10 = (bf16[2,256,384]{2,1,0:T(8,128)(2,1)S(1)}, bf16[2,256,384]{2,1,0:T(8,128)(2,1)S(1)}, u32[]{:S(2)}, u32[]{:S(2)}) collective-permute-start(bf16[2,256,384]{2,1,0:T(8,128)(2,1)S(1)} %get-tuple-element.154), channel_id=1, source_target_pairs={{0,2},{1,3},{2,0},{3,1},{4,6},{5,7},{6,4},{7,5},{8,10},{9,11},{10,... | collective-permute-start | bytes 1179656 | tf_op jit(solution)/shard_map/ppermute | solution.py:1018
  73.0 19.6 %collective-permute-start.12 = (bf16[8,96,384]{2,1,0:T(8,128)(2,1)S(1)}, bf16[8,96,384]{2,1,0:T(8,128)(2,1)S(1)}, u32[]{:S(2)}, u32[]{:S(2)}) collective-permute-start(bf16[8,96,384]{2,1,0:T(8,128)(2,1)S(1)} %get-tuple-element.161), channel_id=1, source_target_pairs={{0,8},{4,12},{8,0},{12,4},{16,24},{20,28},{24,16},{28,20},{1,9},{5... | collective-permute-start | bytes 1769480 | tf_op jit(solution)/shard_map/ppermute | solution.py:1021
  74.8 17.9 %collective-permute-start.13 = (bf16[8,96,384]{2,1,0:T(8,128)(2,1)S(1)}, bf16[8,96,384]{2,1,0:T(8,128)(2,1)S(1)}, u32[]{:S(2)}, u32[]{:S(2)}) collective-permute-start(bf16[8,96,384]{2,1,0:T(8,128)(2,1)S(1)} %get-tuple-element.163), channel_id=1, source_target_pairs={{0,2},{1,3},{2,0},{3,1},{4,6},{5,7},{6,4},{7,5},{8,10},{9,11},{10,... | collective-permute-start | bytes 1769480 | tf_op jit(solution)/shard_map/ppermute | solution.py:1018
  78.7 6.1 %collective-permute-start.11 = (bf16[256,384]{1,0:T(8,128)(2,1)S(1)}, bf16[256,384]{1,0:T(8,128)(2,1)S(1)}, u32[]{:S(2)}, u32[]{:S(2)}) collective-permute-start(bf16[256,384]{1,0:T(8,128)(2,1)S(1)} %slice_bitcast_fusion.2), channel_id=1, source_target_pairs={{0,1},{1,0},{2,3},{3,2},{4,5},{5,4},{6,7},{7,6},{8,9},{9,8},{10,11... | collective-permute-start | bytes 589832 | tf_op jit(solution)/shard_map/ppermute | solution.py:1018
  83.9 25.7 %collective-permute-start.15 = (bf16[12,96,384]{2,1,0:T(8,128)(2,1)S(1)}, bf16[12,96,384]{2,1,0:T(8,128)(2,1)S(1)}, u32[]{:S(2)}, u32[]{:S(2)}) collective-permute-start(bf16[12,96,384]{2,1,0:T(8,128)(2,1)S(1)} %get-tuple-element.170), channel_id=1, source_target_pairs={{0,4},{4,0},{8,12},{12,8},{16,20},{20,16},{24,28},{28,24},{1,5},{5... | collective-permute-start | bytes 2654216 | tf_op jit(solution)/shard_map/ppermute | solution.py:1021
  84.0 25.7 %collective-permute-start.14 = (bf16[8,96,384]{2,1,0:T(8,128)(2,1)S(1)}, bf16[8,96,384]{2,1,0:T(8,128)(2,1)S(1)}, u32[]{:S(2)}, u32[]{:S(2)}) collective-permute-start(bf16[8,96,384]{2,1,0:T(8,128)(2,1)S(1)} %get-tuple-element.168), channel_id=1, source_target_pairs={{0,2},{1,3},{2,0},{3,1},{4,6},{5,7},{6,4},{7,5},{8,10},{9,11},{10,... | collective-permute-start | bytes 1769480 | tf_op jit(solution)/shard_map/ppermute | solution.py:1018
  92.8 12.1 %collective-permute-start.18 = (bf16[4,96,384]{2,1,0:T(8,128)(2,1)S(1)}, bf16[4,96,384]{2,1,0:T(8,128)(2,1)S(1)}, u32[]{:S(2)}, u32[]{:S(2)}) collective-permute-start(bf16[4,96,384]{2,1,0:T(8,128)(2,1)S(1)} %get-tuple-element.176), channel_id=1, source_target_pairs={{0,8},{4,12},{8,0},{12,4},{16,24},{20,28},{24,16},{28,20},{1,9},{5... | collective-permute-start | bytes 884744 | tf_op jit(solution)/shard_map/ppermute | solution.py:1021
  95.6 14.1 %collective-permute-start.16 = (bf16[4,96,384]{2,1,0:T(8,128)(2,1)S(1)}, bf16[4,96,384]{2,1,0:T(8,128)(2,1)S(1)}, u32[]{:S(2)}, u32[]{:S(2)}) collective-permute-start(bf16[4,96,384]{2,1,0:T(8,128)(2,1)S(1)} %get-tuple-element.172), channel_id=1, source_target_pairs={{0,2},{1,3},{2,0},{3,1},{4,6},{5,7},{6,4},{7,5},{8,10},{9,11},{10,... | collective-permute-start | bytes 884744 | tf_op jit(solution)/shard_map/ppermute | solution.py:1018
  96.6 13.1 %collective-permute-start.17 = (bf16[4,96,384]{2,1,0:T(8,128)(2,1)S(1)}, bf16[4,96,384]{2,1,0:T(8,128)(2,1)S(1)}, u32[]{:S(2)}, u32[]{:S(2)}) collective-permute-start(bf16[4,96,384]{2,1,0:T(8,128)(2,1)S(1)} %get-tuple-element.174), channel_id=1, source_target_pairs={{0,8},{4,12},{8,0},{12,4},{16,24},{20,28},{24,16},{28,20},{1,9},{5... | collective-permute-start | bytes 884744 | tf_op jit(solution)/shard_map/ppermute | solution.py:1021
  110.0 19.6 %collective-permute-start.19 = (bf16[6,96,384]{2,1,0:T(8,128)(2,1)S(1)}, bf16[6,96,384]{2,1,0:T(8,128)(2,1)S(1)}, u32[]{:S(2)}, u32[]{:S(2)}) collective-permute-start(bf16[6,96,384]{2,1,0:T(8,128)(2,1)S(1)} %get-tuple-element.181), channel_id=1, source_target_pairs={{0,4},{4,0},{8,12},{12,8},{16,20},{20,16},{24,28},{28,24},{1,5},{5... | collective-permute-start | bytes 1327112 | tf_op jit(solution)/shard_map/ppermute | solution.py:1021
  110.8 18.8 %collective-permute-start.20 = (bf16[6,96,384]{2,1,0:T(8,128)(2,1)S(1)}, bf16[6,96,384]{2,1,0:T(8,128)(2,1)S(1)}, u32[]{:S(2)}, u32[]{:S(2)}) collective-permute-start(bf16[6,96,384]{2,1,0:T(8,128)(2,1)S(1)} %get-tuple-element.183), channel_id=1, source_target_pairs={{0,2},{1,3},{2,0},{3,1},{4,6},{5,7},{6,4},{7,5},{8,10},{9,11},{10,... | collective-permute-start | bytes 1327112 | tf_op jit(solution)/shard_map/ppermute | solution.py:1018
  111.6 14.8 %collective-permute-start.22 = (bf16[4,96,384]{2,1,0:T(8,128)(2,1)S(1)}, bf16[4,96,384]{2,1,0:T(8,128)(2,1)S(1)}, u32[]{:S(2)}, u32[]{:S(2)}) collective-permute-start(bf16[4,96,384]{2,1,0:T(8,128)(2,1)S(1)} %get-tuple-element.187), channel_id=1, source_target_pairs={{0,8},{4,12},{8,0},{12,4},{16,24},{20,28},{24,16},{28,20},{1,9},{5... | collective-permute-start | bytes 884744 | tf_op jit(solution)/shard_map/ppermute | solution.py:1021
  114.1 15.5 %collective-permute-start.21 = (bf16[4,96,384]{2,1,0:T(8,128)(2,1)S(1)}, bf16[4,96,384]{2,1,0:T(8,128)(2,1)S(1)}, u32[]{:S(2)}, u32[]{:S(2)}) collective-permute-start(bf16[4,96,384]{2,1,0:T(8,128)(2,1)S(1)} %get-tuple-element.185), channel_id=1, source_target_pairs={{0,16},{4,20},{8,24},{12,28},{16,0},{20,4},{24,8},{28,12},{1,17},{... | collective-permute-start | bytes 884744 | tf_op jit(solution)/shard_map/ppermute | solution.py:1021
  129.9 14.2 %collective-permute-start.25 = (bf16[8,96,384]{2,1,0:T(8,128)(2,1)S(1)}, bf16[8,96,384]{2,1,0:T(8,128)(2,1)S(1)}, u32[]{:S(2)}, u32[]{:S(2)}) collective-permute-start(bf16[8,96,384]{2,1,0:T(8,128)(2,1)S(1)} %get-tuple-element.207), channel_id=1, source_target_pairs={{0,4},{4,0},{8,12},{12,8},{16,20},{20,16},{24,28},{28,24},{1,5},{5... | collective-permute-start | bytes 1769480 | tf_op jit(solution)/shard_map/ppermute | solution.py:1021
  130.6 7.9 %collective-permute-start.23 = (f32[16,768]{1,0:T(8,128)S(1)}, f32[16,768]{1,0:T(8,128)S(1)}, u32[]{:S(2)}, u32[]{:S(2)}) collective-permute-start(f32[16,768]{1,0:T(8,128)S(1)} %get-tuple-element.203.refs_0_), channel_id=1, source_target_pairs={{0,1},{1,0},{2,3},{3,2},{4,5},{5,4},{6,7},{7,6},{8,9},{9,8},{10,11... | collective-permute-start | bytes 147464 | tf_op jit(solution)/shard_map/ppermute | solution.py:1018
  130.6 12.2 %collective-permute-start.26 = (bf16[3,96,384]{2,1,0:T(8,128)(2,1)S(1)}, bf16[3,96,384]{2,1,0:T(8,128)(2,1)S(1)}, u32[]{:S(2)}, u32[]{:S(2)}) collective-permute-start(bf16[3,96,384]{2,1,0:T(8,128)(2,1)S(1)} %get-tuple-element.209), channel_id=1, source_target_pairs={{0,8},{4,12},{8,0},{12,4},{16,24},{20,28},{24,16},{28,20},{1,9},{5... | collective-permute-start | bytes 663560 | tf_op jit(solution)/shard_map/ppermute | solution.py:1021
  130.8 13.3 %collective-permute-start.27 = (bf16[3,96,384]{2,1,0:T(8,128)(2,1)S(1)}, bf16[3,96,384]{2,1,0:T(8,128)(2,1)S(1)}, u32[]{:S(2)}, u32[]{:S(2)}) collective-permute-start(bf16[3,96,384]{2,1,0:T(8,128)(2,1)S(1)} %get-tuple-element.211), channel_id=1, source_target_pairs={{0,16},{4,20},{8,24},{12,28},{16,0},{20,4},{24,8},{28,12},{1,17},{... | collective-permute-start | bytes 663560 | tf_op jit(solution)/shard_map/ppermute | solution.py:1021
  138.5 4.2 %collective-permute-start.24 = (f32[16,768]{1,0:T(8,128)S(1)}, f32[16,768]{1,0:T(8,128)S(1)}, u32[]{:S(2)}, u32[]{:S(2)}) collective-permute-start(f32[16,768]{1,0:T(8,128)S(1)} %add.57), channel_id=1, source_target_pairs={{0,2},{1,3},{2,0},{3,1},{4,6},{5,7},{6,4},{7,5},{8,10},{9,11},{10,... | collective-permute-start | bytes 147464 | tf_op jit(solution)/shard_map/ppermute | solution.py:1018
  147.9 4.5 %collective-permute-start.28 = (f32[2,256,768]{2,1,0:T(8,128)}, f32[2,256,768]{2,1,0:T(8,128)}, u32[]{:S(2)}, u32[]{:S(2)}) collective-permute-start(f32[2,256,768]{2,1,0:T(8,128)} %get-tuple-element.213), channel_id=1, source_target_pairs={{0,1},{1,0},{2,3},{3,2},{4,5},{5,4},{6,7},{7,6},{8,9},{9,8},{10,11... | collective-permute-start | bytes 4718600 | tf_op jit(solution)/shard_map/ppermute | solution.py:1018
  147.9 4.5 %collective-permute-start.30 = (f32[16,768]{1,0:T(8,128)S(1)}, f32[16,768]{1,0:T(8,128)S(1)}, u32[]{:S(2)}, u32[]{:S(2)}) collective-permute-start(f32[16,768]{1,0:T(8,128)S(1)} %add.58.refs_1_), channel_id=1, source_target_pairs={{0,4},{4,0},{8,12},{12,8},{16,20},{20,16},{24,28},{28,24},{1,5},{5... | collective-permute-start | bytes 147464 | tf_op jit(solution)/shard_map/ppermute | solution.py:1021
  149.5 13.2 %collective-permute-start.31 = (bf16[3,96,384]{2,1,0:T(8,128)(2,1)}, bf16[3,96,384]{2,1,0:T(8,128)(2,1)S(1)}, u32[]{:S(2)}, u32[]{:S(2)}) collective-permute-start(bf16[3,96,384]{2,1,0:T(8,128)(2,1)} %copy-done.11), channel_id=1, source_target_pairs={{0,16},{4,20},{8,24},{12,28},{16,0},{20,4},{24,8},{28,12},{1,17},{... | collective-permute-start | bytes 663560 | tf_op jit(solution)/shard_map/ppermute | solution.py:1021
  149.9 12.8 %collective-permute-start.32 = (bf16[3,96,384]{2,1,0:T(8,128)(2,1)S(1)}, bf16[3,96,384]{2,1,0:T(8,128)(2,1)S(1)}, u32[]{:S(2)}, u32[]{:S(2)}) collective-permute-start(bf16[3,96,384]{2,1,0:T(8,128)(2,1)S(1)} %get-tuple-element.220), channel_id=1, source_target_pairs={{0,8},{4,12},{8,0},{12,4},{16,24},{20,28},{24,16},{28,20},{1,9},{5... | collective-permute-start | bytes 663560 | tf_op jit(solution)/shard_map/ppermute | solution.py:1021
  153.7 15.2 %collective-permute-start.29 = (bf16[256,768]{1,0:T(8,128)(2,1)S(1)}, bf16[256,768]{1,0:T(8,128)(2,1)S(1)}, u32[]{:S(2)}, u32[]{:S(2)}) collective-permute-start(bf16[256,768]{1,0:T(8,128)(2,1)S(1)} %fusion.1.refs_2_), channel_id=1, source_target_pairs={{0,2},{1,3},{2,0},{3,1},{4,6},{5,7},{6,4},{7,5},{8,10},{9,11},{10,... | collective-permute-start | bytes 1179656 | tf_op jit(solution)/shard_map/ppermute | solution.py:1018
  162.8 6.1 %collective-permute-start.34 = (bf16[1,96,384]{2,1,0:T(8,128)(2,1)S(1)}, bf16[1,96,384]{2,1,0:T(8,128)(2,1)S(1)}, u32[]{:S(2)}, u32[]{:S(2)}) collective-permute-start(bf16[1,96,384]{2,1,0:T(8,128)(2,1)S(1)} %get-tuple-element.227), channel_id=1, source_target_pairs={{0,16},{4,20},{8,24},{12,28},{16,0},{20,4},{24,8},{28,12},{1,17},{... | collective-permute-start | bytes 221192 | tf_op jit(solution)/shard_map/ppermute | solution.py:1021
  163.5 5.5 %collective-permute-start.33 = (f32[16,768]{1,0:T(8,128)S(1)}, f32[16,768]{1,0:T(8,128)S(1)}, u32[]{:S(2)}, u32[]{:S(2)}) collective-permute-start(f32[16,768]{1,0:T(8,128)S(1)} %add.63.refs_1_), channel_id=1, source_target_pairs={{0,8},{4,12},{8,0},{12,4},{16,24},{20,28},{24,16},{28,20},{1,9},{5... | collective-permute-start | bytes 147464 | tf_op jit(solution)/shard_map/ppermute | solution.py:1021
  169.9 5.6 %collective-permute-start.38 = (f32[16,768]{1,0:T(8,128)S(1)}, f32[16,768]{1,0:T(8,128)S(1)}, u32[]{:S(2)}, u32[]{:S(2)}) collective-permute-start(f32[16,768]{1,0:T(8,128)S(1)} %add.64), channel_id=1, source_target_pairs={{0,16},{4,20},{8,24},{12,28},{16,0},{20,4},{24,8},{28,12},{1,17},{... | collective-permute-start | bytes 147464 | tf_op jit(solution)/shard_map/ppermute | solution.py:1021
  171.0 5.8 %collective-permute-start.35 = (bf16[2,96,192]{2,1,0:T(8,128)(2,1)S(1)}, bf16[2,96,192]{2,1,0:T(8,128)(2,1)S(1)}, u32[]{:S(2)}, u32[]{:S(2)}) collective-permute-start(bf16[2,96,192]{2,1,0:T(8,128)(2,1)S(1)} %get-tuple-element.230), channel_id=1, source_target_pairs={{0,1},{1,0},{2,3},{3,2},{4,5},{5,4},{6,7},{7,6},{8,9},{9,8},{10,11... | collective-permute-start | bytes 221192 | tf_op jit(solution)/shard_map/ppermute | solution.py:1018
  171.0 5.8 %collective-permute-start.36 = (bf16[2,96,192]{2,1,0:T(8,128)(2,1)S(1)}, bf16[2,96,192]{2,1,0:T(8,128)(2,1)S(1)}, u32[]{:S(2)}, u32[]{:S(2)}) collective-permute-start(bf16[2,96,192]{2,1,0:T(8,128)(2,1)S(1)} %get-tuple-element.231), channel_id=1, source_target_pairs={{0,2},{1,3},{2,0},{3,1},{4,6},{5,7},{6,4},{7,5},{8,10},{9,11},{10,... | collective-permute-start | bytes 221192 | tf_op jit(solution)/shard_map/ppermute | solution.py:1018
  171.4 6.5 %collective-permute-start.37 = (bf16[2,96,192]{2,1,0:T(8,128)(2,1)S(1)}, bf16[2,96,192]{2,1,0:T(8,128)(2,1)S(1)}, u32[]{:S(2)}, u32[]{:S(2)}) collective-permute-start(bf16[2,96,192]{2,1,0:T(8,128)(2,1)S(1)} %get-tuple-element.232), channel_id=1, source_target_pairs={{0,3},{1,2},{2,1},{3,0},{4,7},{5,6},{6,5},{7,4},{8,11},{9,10},{10,... | collective-permute-start | bytes 221192 | tf_op jit(solution)/shard_map/ppermute | solution.py:1018
  (19 other events, 118.4 us)
